TPU v7x, 256 devices: a whole 4x4x8 slice. The times are simulated.
256 devices in a mesh: leaf: 32 (over z, y), samp: 8 (over x, core).
Axes of the slice: x: 4, y: 4, z: 8, core: 2. Of those that a mesh axis runs over, the one named last changes fastest.
Arguments:
- samples: bfloat16 [131072, 512], P('leaf', 'samp'), may hold values from -6 to 6
- omega: bfloat16 [131072, 512], P('leaf', 'samp'), may hold values from -6 to 6
- leaf_basis: bfloat16 [1024, 64, 128], P('leaf'), may hold values from -0.5 to 0.5
- near_blocks: bfloat16 [1024, 8, 128, 128], P('leaf'), may hold values from -0.1875 to 0.1875
- near_index: int32 [1024, 8], P('leaf'), may hold values from 0 to 1023, as said below
- near_count: int32 [1024], P('leaf'), may hold values from 2 to 8, as said below
- inner_transfer: bfloat16 [1984, 4096], P('leaf'), may hold values from -0.5 to 0.5
- upper_transfer: bfloat16 [62, 4096], replicated, may hold values from -0.5 to 0.5
Outputs:
- leaf_coeffs: float32 [1024, 64, 512], P('leaf', None, 'samp')
- leaf_gram: float32 [1024, 4096], P('leaf', 'samp')
- ancestor_coeffs: float32 [32, 5, 64, 512], P('leaf', None, None, 'samp')
Inputs may be any that keep to these rules, and one draw needn't show every extreme that they name: `near_index`: slot 0 of leaf i names i itself, slot 1 names a leaf exactly 32 away from i, and every slot names a leaf at most 32 away from i. `near_count`: every group of 32 consecutive leaves has a leaf with all 8 slots live.
All inputs are finite; a program needn't handle non-finite values.
Results may differ from a plain program's by a relative error of at most 0.0029.
Values may be sent and summed in bfloat16 or wider, within the bound.
No kernel may reach another device: no remote copies, remote signals or barrier semaphores. Data moves between devices by JAX's collectives and lax.ppermute only.
A program may use at most 64 MiB of HBM per device.

v0:
```python
import jax
import jax.numpy as jnp
from jax import lax
from jax.sharding import PartitionSpec as P


def with_halo(cells, sides, width):
    for axis, dim in sides:
        count = lax.axis_size(axis)
        ends = count - 1
        head = lax.slice_in_dim(cells, 0, width, axis=dim)
        tail = lax.slice_in_dim(cells, cells.shape[dim] - width, cells.shape[dim], axis=dim)
        cells = jnp.concatenate(
            [
                lax.ppermute(tail, axis, [(i, (i + 1) % count) for i in range(ends)]),
                cells,
                lax.ppermute(head, axis, [((i + 1) % count, i) for i in range(ends)]),
            ],
            axis=dim,
        )
    return cells


def partner(shard, axis, stride):
    return lax.ppermute(shard, axis, [(i, i ^ 1 << stride) for i in range(lax.axis_size(axis))])


def shards(
    samples, omega, leaf_basis, near_blocks, near_index, near_count, inner_transfer, upper_transfer
):
    leaf_count = near_count.shape[0]
    slot_count = near_index.shape[1]
    rank_size = leaf_basis.shape[1]
    leaf_size = leaf_basis.shape[2]
    column_count = samples.shape[1]
    widened = with_halo(omega, (("leaf", 0),), leaf_count * leaf_size)
    widened = widened.reshape(3 * leaf_count, leaf_size, column_count)
    device = lax.axis_index("leaf")
    anchor = device * leaf_count - leaf_count
    local_index = near_index - anchor
    fetched = widened[local_index]
    live_mask = (jnp.arange(slot_count)[None, :] < near_count[:, None]).astype(jnp.bfloat16)
    fetched = fetched * live_mask[:, :, None, None]
    near_sum = jnp.einsum(
        "gkab,gkbs->gas", near_blocks, fetched, preferred_element_type=jnp.float32
    )
    sample_rows = samples.reshape(leaf_count, leaf_size, column_count).astype(jnp.float32)
    far_part = (sample_rows - near_sum).astype(jnp.bfloat16)
    cluster_coefficient_array = jnp.einsum(
        "grb,gbs->grs", leaf_basis, far_part, preferred_element_type=jnp.float32
    )
    overall_column_count = column_count * lax.axis_size("samp")
    gram_term = (
        jnp.einsum(
            "ydb,ykb->ydk",
            cluster_coefficient_array,
            cluster_coefficient_array,
            precision=lax.Precision.HIGHEST,
        )
        / overall_column_count
    )
    gram_term = gram_term.reshape(leaf_count, rank_size * rank_size)
    leaf_gram = lax.psum_scatter(gram_term, "samp", scatter_dimension=1, tiled=True)
    inner = inner_transfer.astype(jnp.float32).reshape(-1, rank_size, rank_size)
    current = cluster_coefficient_array
    offset = 0
    width_now = leaf_count
    while width_now > 1:
        mats = inner[offset : offset + width_now]
        projected = jnp.einsum("nab,nas->nbs", mats, current, precision=lax.Precision.HIGHEST)
        projected = projected.reshape(width_now // 2, 2, rank_size, column_count)
        current = projected[:, 0] + projected[:, 1]
        offset = offset + width_now
        width_now = width_now // 2
    accum = current[0]
    upper = upper_transfer.astype(jnp.float32).reshape(-1, rank_size, rank_size)
    group_total = lax.axis_size("leaf")
    heights = group_total.bit_length() - 1
    offset = 0
    width_now = group_total
    levels = []
    for height in range(heights):
        node_index = offset + jnp.right_shift(device, height)
        matrix = lax.dynamic_index_in_dim(upper, node_index, 0, keepdims=False)
        own_part = jnp.dot(matrix.T, accum, precision=lax.Precision.HIGHEST)
        accum = own_part + partner(own_part, "leaf", height)
        levels.append(accum)
        offset = offset + width_now
        width_now = width_now // 2
    ancestor_coeffs = jnp.stack(levels, axis=0)[None]
    return (cluster_coefficient_array, leaf_gram, ancestor_coeffs)


def solution(mesh):
    return jax.shard_map(
        shards,
        mesh=mesh,
        in_specs=(
            P("leaf", "samp"),
            P("leaf", "samp"),
            P("leaf", None, None),
            P("leaf", None, None, None),
            P("leaf", None),
            P("leaf"),
            P("leaf", None),
            P(),
        ),
        out_specs=(P("leaf", None, "samp"), P("leaf", "samp"), P("leaf", None, None, "samp")),
        check_vma=False,
    )
```

profile of v0, /device:TPU:16, one launch (start us, length us, event | category | flops | bytes accessed | tf_op | source)
XLA Modules:
  0.0 91.2 jit_solution(5975317132888699407)
XLA Ops:
  7.2 2.5 %collective-permute-start.1 = (bf16[4096,64]{0,1:T(8,128)(2,1)}, bf16[4096,64]{0,1:T(8,128)(2,1)S(1)}, u32[]{:S(2)}, u32[]{:S(2)}) collective-permute-start(bf16[4096,64]{0,1:T(8,128)(2,1)} %param.9), channel_id=1, source_target_pairs={{8,0},{16,8},{24,16},{32,24},{40,32},{48,40},{56,48},{64,56},{72,6... | collective-permute-start | bytes 1572872 | tf_op jit(solution)/shard_map/ppermute | solution.py:17
  9.7 3.5 %collective-permute-start = (bf16[4096,64]{0,1:T(8,128)(2,1)}, bf16[4096,64]{0,1:T(8,128)(2,1)}, u32[]{:S(2)}, u32[]{:S(2)}) collective-permute-start(bf16[4096,64]{0,1:T(8,128)(2,1)} %param.9), channel_id=1, source_target_pairs={{0,8},{8,16},{16,24},{24,32},{32,40},{40,48},{48,56},{56,64},{64,7... | collective-permute-start | bytes 1572872 | tf_op jit(solution)/shard_map/ppermute | solution.py:15
  16.7 1.0 %slice.60 = bf16[32,4096]{1,0:T(8,128)(2,1)S(1)} slice(bf16[62,4096]{1,0:T(8,128)(2,1)} %param.14), slice={[0:32], [0:4096]} | slice | bytes 524288 | tf_op jit(solution)/shard_map/slice | solution.py:69
  21.0 2.7 %reshape.75 = bf16[62,64,64]{2,1,0:T(8,128)(2,1)} reshape(bf16[62,4096]{1,0:T(8,128)(2,1)} %param.15) | data formatting | bytes 1015808 | tf_op jit(solution)/shard_map/reshape | solution.py:76
  25.3 1.6 %copy_bitcast_fusion = bf16[96,128,64]{1,2,0:T(8,128)(2,1)S(1)} fusion(bf16[4096,64]{0,1:T(8,128)(2,1)} %copy-done.2, bf16[4096,64]{0,1:T(8,128)(2,1)S(1)} %copy-done.1, bf16[4096,64]{0,1:T(8,128)(2,1)} %collective-permute-done), kind=kLoop, calls=%fused_computation.4 | loop fusion | flops 4718592 | bytes 3145728 | tf_op jit(solution)/shard_map/reshape | solution.py:37
  27.0 3.0 %gather_fusion = bf16[256,128,64]{1,2,0:T(8,128)(2,1)} fusion(bf16[96,128,64]{1,2,0:T(8,128)(2,1)S(1)} %copy_bitcast_fusion, s32[1024]{0:T(1024)S(1)} %pad_clamp_fusion), kind=kCustom, calls=%fused_computation | custom fusion | bytes 8389632 | tf_op jit(solution)/shard_map/gather | solution.py:41
  30.0 6.4 %fusion.13 = f32[32,64,64]{2,1,0:T(8,128)S(1)} fusion(bf16[32,64,128]{2,1,0:T(8,128)(2,1)S(1)} %copy-done, bf16[32,8,128,128]{3,2,1,0:T(8,128)(2,1)} %param.11, bf16[32,8,128,64]{2,3,1,0:T(8,128)(2,1)} %bitcast.142, bf16[32,8]{1,0:T(8,128)(2,1)S(1)} %fusion.50, bf16[4096,64]{0,1:T(8,128)(2,1)S(1)} %copy-done.6), kind=kOutput, calls=%fused_computation.10 | convolution fusion | flops 573308928 | bytes 14156288 | tf_op jit(solution)/shard_map/grb,gbs->grs/dot_general | solution.py:49
  38.2 0.9 %fusion.33 = f32[64,64]{1,0:T(8,128)S(1)} fusion(f32[1,2,64,64]{2,3,1,0:T(8,128)S(1)} %convolution_bitcast_fusion, bf16[62,64,64]{2,1,0:T(8,128)(2,1)} %reshape.75, s32[]{:T(128)S(6)} %select_n.20), kind=kOutput, calls=%fused_computation.36 | convolution fusion | flops 3149824 | bytes 65540 | tf_op jit(solution)/shard_map/dot_general | solution.py:85
  39.1 3.4 %collective-permute-start.2 = (f32[64,64]{1,0:T(8,128)S(1)}, f32[64,64]{1,0:T(8,128)S(1)}, u32[]{:S(2)}, u32[]{:S(2)}) collective-permute-start(f32[64,64]{1,0:T(8,128)S(1)} %fusion.33), channel_id=1, source_target_pairs={{0,8},{8,0},{16,24},{24,16},{32,40},{40,32},{48,56},{56,48},{64,72... | collective-permute-start | bytes 49160 | tf_op jit(solution)/shard_map/ppermute | solution.py:25
  42.5 1.8 %convolution_multiply_fusion = f32[32,64,64]{2,1,0:T(8,128)S(1)} fusion(f32[32,64,64]{2,1,0:T(8,128)S(1)} %fusion.13), kind=kOutput, calls=%fused_computation.7 | convolution fusion | flops 100794368 | bytes 1048576 | tf_op jit(solution)/shard_map/ydb,ykb->ydk/dot_general | solution.py:54
  44.3 1.3 %copy.58 = f32[32,64,64]{2,1,0:T(8,128)} copy(f32[32,64,64]{1,2,0:T(8,128)S(1)} %bitcast.143) | data formatting | bytes 1048576
  45.7 1.1 %reshape.74 = f32[32,4096]{1,0:T(8,128)} reshape(f32[32,64,64]{2,1,0:T(8,128)S(1)} %convolution_multiply_fusion) | data formatting | bytes 1048576 | tf_op jit(solution)/shard_map/reshape | solution.py:62
  46.8 0.9 %fusion.42 = f32[64,64]{1,0:T(8,128)S(1)} fusion(bf16[62,64,64]{2,1,0:T(8,128)(2,1)} %reshape.75, s32[]{:T(128)S(6)} %select_n.21, f32[64,64]{1,0:T(8,128)S(1)} %fusion.33, f32[64,64]{1,0:T(8,128)S(1)} %collective-permute-done.2), kind=kOutput, calls=%fused_computation.49 | convolution fusion | flops 3149824 | bytes 65540 | tf_op jit(solution)/shard_map/dot_general | solution.py:85
  47.9 5.4 %collective-permute-done.3 = f32[64,64]{1,0:T(8,128)S(1)} collective-permute-done((f32[64,64]{1,0:T(8,128)S(1)}, f32[64,64]{1,0:T(8,128)S(1)}, u32[]{:S(2)}, u32[]{:S(2)}) %collective-permute-start.3) | collective-permute-done | bytes 16416 | tf_op jit(solution)/shard_map/ppermute | solution.py:25
  53.3 0.9 %fusion.40 = f32[64,64]{1,0:T(8,128)S(1)} fusion(bf16[62,64,64]{2,1,0:T(8,128)(2,1)} %reshape.75, s32[]{:T(128)S(6)} %select_n.22, f32[64,64]{1,0:T(8,128)S(1)} %fusion.42, f32[64,64]{1,0:T(8,128)S(1)} %collective-permute-done.3), kind=kOutput, calls=%fused_computation.47 | convolution fusion | flops 3149824 | bytes 65540 | tf_op jit(solution)/shard_map/dot_general | solution.py:85
  54.2 2.0 %collective-permute-start.4 = (f32[64,64]{1,0:T(8,128)S(1)}, f32[64,64]{1,0:T(8,128)S(1)}, u32[]{:S(2)}, u32[]{:S(2)}) collective-permute-start(f32[64,64]{1,0:T(8,128)S(1)} %fusion.40), channel_id=1, source_target_pairs={{0,32},{8,40},{16,48},{24,56},{32,0},{40,8},{48,16},{56,24},{64,96... | collective-permute-start | bytes 49160 | tf_op jit(solution)/shard_map/ppermute | solution.py:25
  56.2 2.0 %collective-permute-done.4 = f32[64,64]{1,0:T(8,128)S(1)} collective-permute-done((f32[64,64]{1,0:T(8,128)S(1)}, f32[64,64]{1,0:T(8,128)S(1)}, u32[]{:S(2)}, u32[]{:S(2)}) %collective-permute-start.4) | collective-permute-done | bytes 16416 | tf_op jit(solution)/shard_map/ppermute | solution.py:25
  58.2 0.9 %fusion.38 = f32[64,64]{1,0:T(8,128)S(1)} fusion(bf16[62,64,64]{2,1,0:T(8,128)(2,1)} %reshape.75, s32[]{:T(128)S(6)} %select_n.23, f32[64,64]{1,0:T(8,128)S(1)} %fusion.40, f32[64,64]{1,0:T(8,128)S(1)} %collective-permute-done.4), kind=kOutput, calls=%fused_computation.45 | convolution fusion | flops 3149824 | bytes 65540 | tf_op jit(solution)/shard_map/dot_general | solution.py:85
  59.1 4.5 %collective-permute-start.5 = (f32[64,64]{1,0:T(8,128)S(1)}, f32[64,64]{1,0:T(8,128)S(1)}, u32[]{:S(2)}, u32[]{:S(2)}) collective-permute-start(f32[64,64]{1,0:T(8,128)S(1)} %fusion.38), channel_id=1, source_target_pairs={{0,64},{8,72},{16,80},{24,88},{32,96},{40,104},{48,112},{56,120},{... | collective-permute-start | bytes 49160 | tf_op jit(solution)/shard_map/ppermute | solution.py:25
  63.6 1.9 %collective-permute-done.5 = f32[64,64]{1,0:T(8,128)S(1)} collective-permute-done((f32[64,64]{1,0:T(8,128)S(1)}, f32[64,64]{1,0:T(8,128)S(1)}, u32[]{:S(2)}, u32[]{:S(2)}) %collective-permute-start.5) | collective-permute-done | bytes 16416 | tf_op jit(solution)/shard_map/ppermute | solution.py:25
  65.5 0.9 %fusion.36 = f32[64,64]{1,0:T(8,128)S(1)} fusion(bf16[62,64,64]{2,1,0:T(8,128)(2,1)} %reshape.75, s32[]{:T(128)S(6)} %select_n.24, f32[64,64]{1,0:T(8,128)S(1)} %fusion.38, f32[64,64]{1,0:T(8,128)S(1)} %collective-permute-done.5), kind=kOutput, calls=%fused_computation.43 | convolution fusion | flops 3149824 | bytes 65540 | tf_op jit(solution)/shard_map/dot_general | solution.py:85
  66.4 5.9 %collective-permute-start.6 = (f32[64,64]{1,0:T(8,128)S(1)}, f32[64,64]{1,0:T(8,128)S(1)}, u32[]{:S(2)}, u32[]{:S(2)}) collective-permute-start(f32[64,64]{1,0:T(8,128)S(1)} %fusion.36), channel_id=1, source_target_pairs={{0,128},{8,136},{16,144},{24,152},{32,160},{40,168},{48,176},{56,1... | collective-permute-start | bytes 49160 | tf_op jit(solution)/shard_map/ppermute | solution.py:25
  72.4 2.0 %collective-permute-done.6 = f32[64,64]{1,0:T(8,128)S(1)} collective-permute-done((f32[64,64]{1,0:T(8,128)S(1)}, f32[64,64]{1,0:T(8,128)S(1)}, u32[]{:S(2)}, u32[]{:S(2)}) %collective-permute-start.6) | collective-permute-done | bytes 16416 | tf_op jit(solution)/shard_map/ppermute | solution.py:25
  74.4 10.0 %reduce-scatter.2.cloned.1.call-done = f32[32,512]{1,0:T(8,128)} async-done(((f32[32,4096]{1,0:T(8,128)}), f32[32,512]{1,0:T(8,128)}) %reduce-scatter.2.cloned.1.call-update) | async-done | bytes 65552 | tf_op jit(solution)/shard_map/reduce_scatter | solution.py:63
  (44 shorter events, 10.2 us)
Async XLA Ops:
  7.2 22.9 %copy-start = (bf16[32,64,128]{2,1,0:T(8,128)(2,1)S(1)}, bf16[32,64,128]{2,1,0:T(8,128)(2,1)}, u32[]{:S(2)}) copy-start(bf16[32,64,128]{2,1,0:T(8,128)(2,1)} %param.10) | copy-start | bytes 1572868
  7.2 18.1 %copy-start.1 = (bf16[4096,64]{0,1:T(8,128)(2,1)S(1)}, bf16[4096,64]{0,1:T(8,128)(2,1)}, u32[]{:S(2)}) copy-start(bf16[4096,64]{0,1:T(8,128)(2,1)} %param.9) | copy-start | bytes 1572868
  7.2 77.2 %reduce-scatter.2.cloned.1.call-start = ((), (), s32[]{:S(2)}) async-start(), calls=%async_computation.1 | async-start | bytes 589824 | tf_op jit(solution)/shard_map/reduce_scatter | solution.py:63
  7.2 17.2 %collective-permute-start.1 = (bf16[4096,64]{0,1:T(8,128)(2,1)}, bf16[4096,64]{0,1:T(8,128)(2,1)S(1)}, u32[]{:S(2)}, u32[]{:S(2)}) collective-permute-start(bf16[4096,64]{0,1:T(8,128)(2,1)} %param.9), channel_id=1, source_target_pairs={{8,0},{16,8},{24,16},{32,24},{40,32},{48,40},{56,48},{64,56},{72,6... | collective-permute-start | bytes 1572872 | tf_op jit(solution)/shard_map/ppermute | solution.py:17
  9.7 15.6 %collective-permute-start = (bf16[4096,64]{0,1:T(8,128)(2,1)}, bf16[4096,64]{0,1:T(8,128)(2,1)}, u32[]{:S(2)}, u32[]{:S(2)}) collective-permute-start(bf16[4096,64]{0,1:T(8,128)(2,1)} %param.9), channel_id=1, source_target_pairs={{0,8},{8,16},{16,24},{24,32},{32,40},{40,48},{48,56},{56,64},{64,7... | collective-permute-start | bytes 1572872 | tf_op jit(solution)/shard_map/ppermute | solution.py:15
  24.5 0.8 copy-start.2
  27.0 3.1 %copy-start.6 = (bf16[4096,64]{0,1:T(8,128)(2,1)S(1)}, bf16[4096,64]{0,1:T(8,128)(2,1)}, u32[]{:S(2)}) copy-start(bf16[4096,64]{0,1:T(8,128)(2,1)} %param.8) | copy-start | bytes 1572868
  36.4 1.3 %copy-start.3 = (bf16[4,64,64]{2,1,0:T(8,128)(2,1)S(1)}, bf16[4,64,64]{2,1,0:T(8,128)(2,1)}, u32[]{:S(2)}) copy-start(bf16[4,64,64]{2,1,0:T(8,128)(2,1)} %slice.73) | copy-start | bytes 98308
  36.5 1.5 %copy-start.4 = (bf16[2,64,64]{2,1,0:T(8,128)(2,1)S(1)}, bf16[2,64,64]{2,1,0:T(8,128)(2,1)}, u32[]{:S(2)}) copy-start(bf16[2,64,64]{2,1,0:T(8,128)(2,1)} %slice.77) | copy-start | bytes 49156
  39.1 7.7 %collective-permute-start.2 = (f32[64,64]{1,0:T(8,128)S(1)}, f32[64,64]{1,0:T(8,128)S(1)}, u32[]{:S(2)}, u32[]{:S(2)}) collective-permute-start(f32[64,64]{1,0:T(8,128)S(1)} %fusion.33), channel_id=1, source_target_pairs={{0,8},{8,0},{16,24},{24,16},{32,40},{40,32},{48,56},{56,48},{64,72... | collective-permute-start | bytes 49160 | tf_op jit(solution)/shard_map/ppermute | solution.py:25
  47.8 5.5 %collective-permute-start.3 = (f32[64,64]{1,0:T(8,128)S(1)}, f32[64,64]{1,0:T(8,128)S(1)}, u32[]{:S(2)}, u32[]{:S(2)}) collective-permute-start(f32[64,64]{1,0:T(8,128)S(1)} %fusion.42), channel_id=1, source_target_pairs={{0,16},{8,24},{16,0},{24,8},{32,48},{40,56},{48,32},{56,40},{64,80... | collective-permute-start | bytes 49160 | tf_op jit(solution)/shard_map/ppermute | solution.py:25
  54.2 4.0 %collective-permute-start.4 = (f32[64,64]{1,0:T(8,128)S(1)}, f32[64,64]{1,0:T(8,128)S(1)}, u32[]{:S(2)}, u32[]{:S(2)}) collective-permute-start(f32[64,64]{1,0:T(8,128)S(1)} %fusion.40), channel_id=1, source_target_pairs={{0,32},{8,40},{16,48},{24,56},{32,0},{40,8},{48,16},{56,24},{64,96... | collective-permute-start | bytes 49160 | tf_op jit(solution)/shard_map/ppermute | solution.py:25
  59.1 6.4 %collective-permute-start.5 = (f32[64,64]{1,0:T(8,128)S(1)}, f32[64,64]{1,0:T(8,128)S(1)}, u32[]{:S(2)}, u32[]{:S(2)}) collective-permute-start(f32[64,64]{1,0:T(8,128)S(1)} %fusion.38), channel_id=1, source_target_pairs={{0,64},{8,72},{16,80},{24,88},{32,96},{40,104},{48,112},{56,120},{... | collective-permute-start | bytes 49160 | tf_op jit(solution)/shard_map/ppermute | solution.py:25
  66.4 7.9 %collective-permute-start.6 = (f32[64,64]{1,0:T(8,128)S(1)}, f32[64,64]{1,0:T(8,128)S(1)}, u32[]{:S(2)}, u32[]{:S(2)}) collective-permute-start(f32[64,64]{1,0:T(8,128)S(1)} %fusion.36), channel_id=1, source_target_pairs={{0,128},{8,136},{16,144},{24,152},{32,160},{40,168},{48,176},{56,1... | collective-permute-start | bytes 49160 | tf_op jit(solution)/shard_map/ppermute | solution.py:25
  74.3 10.0 %copy-start.5 = (f32[5,64,64]{2,1,0:T(8,128)}, f32[5,64,64]{2,1,0:T(8,128)S(1)}, u32[]{:S(2)}) copy-start(f32[5,64,64]{2,1,0:T(8,128)S(1)} %bitcast_dynamic-update-slice_fusion) | copy-start | bytes 245764
Sparse Core Ops, SparseCore 0:
  46.9 37.3 reduce-scatter.1
where the time goes:
time: 91.9 us; the launch traced here: 91.2 us
  starting transfers between devices  21.9 us (24%)
  waiting for transfers between devices  21.3 us (23%)
  local copies, waits for them, and re-layouts  16.1 us (18%)
  matrix products  14.5 us (16%)
  between operations  14.3 us (16%)
  other arithmetic  3.09 us (3%)
    ppermute x5, starting transfers between devices, partner(): lax.ppermute(shard, axis, [(i, i ^ 1 << stride) for i in range(lax.axis_s...  15.9 us
    ppermute x5, waiting for transfers between devices, partner(): lax.ppermute(shard, axis, [(i, i ^ 1 << stride) for i in range(lax.axis_s...  11.3 us
    reduce_scatter x1, waiting for transfers between devices, shards(): lax.psum_scatter(gram_term, 'samp', scatter_dimension=1, tiled=True)  10 us
    slice x10, local copies, waits for them, and re-layouts, shards(): mats = inner[offset:offset + width_now]  6.87 us
    dot_general x1, matrix products, shards(): jnp.einsum('grb,gbs->grs', leaf_basis, far_part, preferred_element_type=j...  6.4 us
    dot_general x5, matrix products, shards(): own_part = jnp.dot(matrix.T, accum, precision=lax.Precision.HIGHEST)  4.63 us
    ppermute x1, starting transfers between devices, with_halo(): lax.ppermute(tail, axis, [(i, (i + 1) % count) for i in range(ends)])  3.49 us
    gather x1, local copies, waits for them, and re-layouts, shards(): fetched = widened[local_index]  3.04 us
  transfers between devices with their start and end apart: 8, of which 6 were waited for; matrix products, arithmetic and copies ran while one was open for 21% of the time, Pallas kernels for 0%

commit v1 on v0

v1 whole, which is shorter than its diff:
```python
import functools

import jax
import jax.numpy as jnp
from jax import lax
from jax.experimental import pallas as pl
from jax.experimental.pallas import tpu as pltpu
from jax.sharding import PartitionSpec as P

NT = (((1,), (1,)), ((), ()))
NN = (((1,), (0,)), ((), ()))


def dot(a, b, dims):
    return lax.dot_general(a, b, dims, preferred_element_type=jnp.float32)


def split(value):
    high = value.astype(jnp.bfloat16)
    return high, (value - high.astype(jnp.float32)).astype(jnp.bfloat16)


def leaf_kernel(
    scale,
    slot_ref,
    place_ref,
    left_ref,
    own_ref,
    right_ref,
    samples_ref,
    blocks_ref,
    basis_ref,
    path_high_ref,
    path_low_ref,
    coeff_ref,
    keep_ref,
    send_ref,
    part_ref,
    source,
    gram,
):
    step = pl.program_id(0)
    pairs = pl.num_programs(0)
    slots = blocks_ref.shape[2]
    size = blocks_ref.shape[3]
    columns = own_ref.shape[0]
    count = own_ref.shape[1] // size
    rank = basis_ref.shape[1]

    @pl.when(step == 0)
    def _():
        for place, ref in enumerate((left_ref, own_ref, right_ref)):
            for leaf in range(count):
                source[place * count + leaf] = ref[:, leaf * size : (leaf + 1) * size]
        source[3 * count] = jnp.zeros((columns, size), source.dtype)
        part_ref[...] = jnp.zeros_like(part_ref)

    both = []
    for half in range(2):
        leaf = step + half * pairs
        fetched = jnp.concatenate(
            [source[slot_ref[leaf * slots + k]] for k in range(slots)], axis=1
        )
        matrix = jnp.concatenate([blocks_ref[half, 0, k] for k in range(slots)], axis=1)
        near = dot(fetched, matrix, NT)
        start = pl.multiple_of(leaf * size, size)
        far = (samples_ref[:, pl.ds(start, size)].astype(jnp.float32) - near).astype(jnp.bfloat16)
        coeff = dot(basis_ref[leaf], far, NT)
        coeff_ref[leaf] = coeff
        both.append(coeff)
    stacked = jnp.concatenate(both, axis=0)
    high, low = split(stacked)
    product = dot(high, high, NT) + (dot(high, low, NT) + dot(low, high, NT))
    lane = lax.broadcasted_iota(jnp.int32, (rank, 2 * rank), 1)
    value = jnp.where(lane < rank, product[:rank], product[rank:]) * scale
    gram[pl.ds(step, rank, stride=pairs), :] = value
    path = path_high_ref[step]
    part_ref[...] += dot(path, high, NN) + (dot(path, low, NN) + dot(path_low_ref[step], high, NN))

    @pl.when(step == pairs - 1)
    def _():
        rows = rank // (2 * keep_ref.shape[0])
        for relative in range(2 * keep_ref.shape[0]):
            first = jnp.bitwise_xor(place_ref[0], relative) * rows
            for row in range(rows):
                at = pl.multiple_of((first + row) * pairs, pairs)
                tile = gram[pl.ds(at, pairs), :]
                if relative % 2:
                    send_ref[relative // 2, row] = tile.astype(send_ref.dtype)
                else:
                    keep_ref[relative // 2, row] = tile


def finish_kernel(total_ref, last_ref, out_ref):
    rows, pairs, width = total_ref.shape
    half = width // 2
    lane = lax.broadcasted_iota(jnp.int32, (pairs, width), 1)
    for row in range(0, rows, 2):
        even = total_ref[row] + last_ref[row].astype(jnp.float32)
        odd = total_ref[row + 1] + last_ref[row + 1].astype(jnp.float32)
        at = slice(row * half, (row + 2) * half)
        out_ref[:pairs, at] = jnp.where(lane < half, even, pltpu.roll(odd, half, 1))
        out_ref[pairs:, at] = jnp.where(lane < half, pltpu.roll(even, half, 1), odd)


def whole(shape):
    return pl.BlockSpec(shape, lambda step, *_: (0,) * len(shape))


def leaf_pass(slot, place, left, own, right, samples, blocks, basis, path_high, path_low, parts):
    count, slots, size, _ = blocks.shape
    rank = basis.shape[1]
    columns = own.shape[0]
    pairs = count // 2
    rows = rank // parts
    grid_spec = pltpu.PrefetchScalarGridSpec(
        num_scalar_prefetch=2,
        grid=(pairs,),
        in_specs=[
            whole(left.shape),
            whole(own.shape),
            whole(right.shape),
            whole(samples.shape),
            pl.BlockSpec((2, 1, slots, size, size), lambda step, *_: (0, step, 0, 0, 0)),
            whole(basis.shape),
            whole(path_high.shape),
            whole(path_low.shape),
        ],
        out_specs=[
            whole((count, rank, columns)),
            whole((parts // 2, rows, pairs, 2 * rank)),
            whole((parts // 2, rows, pairs, 2 * rank)),
            whole((rank, columns)),
        ],
        scratch_shapes=[
            pltpu.VMEM((3 * count + 1, columns, size), jnp.bfloat16),
            pltpu.VMEM((rank * pairs, 2 * rank), jnp.float32),
        ],
    )
    return pl.pallas_call(
        functools.partial(leaf_kernel, 1.0 / (columns * parts)),
        grid_spec=grid_spec,
        out_shape=(
            jax.ShapeDtypeStruct((count, rank, columns), jnp.float32),
            jax.ShapeDtypeStruct((parts // 2, rows, pairs, 2 * rank), jnp.float32),
            jax.ShapeDtypeStruct((parts // 2, rows, pairs, 2 * rank), jnp.bfloat16),
            jax.ShapeDtypeStruct((rank, columns), jnp.float32),
        ),
        name="leaf_pass",
    )(slot, place, left, own, right, samples, blocks.reshape(2, pairs, slots, size, size), basis, path_high, path_low)


def exchange(value, axis, flip):
    return lax.ppermute(value, axis, [(i, i ^ flip) for i in range(lax.axis_size(axis))])


def shards(
    samples, omega, leaf_basis, near_blocks, near_index, near_count, inner_transfer, upper_transfer
):
    count = near_count.shape[0]
    slots = near_index.shape[1]
    rank = leaf_basis.shape[1]
    groups = lax.axis_size("leaf")
    parts = lax.axis_size("samp")
    device = lax.axis_index("leaf")
    place = lax.axis_index("samp")

    own = omega.T
    left = lax.ppermute(own, "leaf", [(i, i + 1) for i in range(groups - 1)])
    right = lax.ppermute(own, "leaf", [(i + 1, i) for i in range(groups - 1)])

    live = jnp.arange(slots)[None, :] < near_count[:, None]
    slot = jnp.where(live, near_index - (device * count - count), 3 * count).reshape(-1)

    heights = groups.bit_length() - 1
    upper = []
    offset, width = 0, groups
    for height in range(heights):
        row = lax.dynamic_slice_in_dim(
            upper_transfer, offset + jnp.right_shift(device, height), 1, axis=0
        )
        upper.append(row.reshape(rank, rank).astype(jnp.float32))
        offset, width = offset + width, width // 2

    levels = []
    offset, width = 0, count
    while width > 1:
        levels.append(inner_transfer[offset : offset + width].reshape(width, rank, rank))
        offset, width = offset + width, width // 2
    path = upper[0][None]
    for mats in reversed(levels):
        path = jnp.einsum(
            "nmab,nbc->nmac",
            mats.astype(jnp.float32).reshape(-1, 2, rank, rank)
            if mats.shape[0] > 1
            else mats,
            path,
            precision=lax.Precision.HIGHEST,
        ).reshape(-1, rank, rank)
    path = path.reshape(2, count // 2, rank, rank).transpose(1, 3, 0, 2)
    path = path.reshape(count // 2, rank, 2 * rank)
    path_high, path_low = split(path)

    coeffs, keep, send, part = leaf_pass(
        slot.astype(jnp.int32),
        place.astype(jnp.int32).reshape(1),
        left,
        own,
        right,
        samples.T,
        near_blocks,
        leaf_basis,
        path_high,
        path_low,
        parts,
    )

    flips = (1, 3, 4, 8, 24)
    ancestors = []
    accum = part
    gram = None
    for height in range(heights):
        if height:
            accum = jnp.dot(upper[height].T, accum, precision=lax.Precision.HIGHEST)
        accum = accum + exchange(accum, "leaf", flips[height])
        ancestors.append(accum)
    gram = keep + exchange(send, "samp", 1).astype(jnp.float32)
    got = exchange(gram[1:3].astype(jnp.bfloat16), "samp", 2).astype(jnp.float32)
    near_total = gram[0] + got[0]
    far_total = gram[3] + got[1]
    last = exchange(far_total.astype(jnp.bfloat16), "samp", 6)
    leaf_gram = pl.pallas_call(
        finish_kernel,
        out_shape=jax.ShapeDtypeStruct((count, rank * rank // parts), jnp.float32),
        name="finish",
    )(near_total, last)
    return coeffs, leaf_gram, jnp.stack(ancestors, axis=0)[None]


def solution(mesh):
    return jax.shard_map(
        shards,
        mesh=mesh,
        in_specs=(
            P("leaf", "samp"),
            P("leaf", "samp"),
            P("leaf", None, None),
            P("leaf", None, None, None),
            P("leaf", None),
            P("leaf"),
            P("leaf", None),
            P(),
        ),
        out_specs=(P("leaf", None, "samp"), P("leaf", "samp"), P("leaf", None, None, "samp")),
        check_vma=False,
    )
```

time: 91.9 us -> 83.7 us (0.911)
  the two profiles are of different devices: /device:TPU:16 before, /device:TPU:6 now
where the time goes in v1:
time: 83.7 us; the launch traced here: 82.8 us
  starting transfers between devices  26.3 us (31%)
  Pallas kernels  21.2 us (25%)
  waiting for transfers between devices  15.3 us (18%)
  local copies, waits for them, and re-layouts  10.8 us (13%)
  matrix products  5.07 us (6%)
  other arithmetic  3.34 us (4%)
  between operations  0.85 us (1%)
    ppermute x8, starting transfers between devices, exchange(): lax.ppermute(value, axis, [(i, i ^ flip) for i in range(lax.axis_size(axi...  21.4 us
    pallas_call x1, Pallas kernels, leaf_pass(): pl.pallas_call(functools.partial(leaf_kernel, 1.0 / (columns * parts)), g...  19.6 us
    ppermute x8, waiting for transfers between devices, exchange(): lax.ppermute(value, axis, [(i, i ^ flip) for i in range(lax.axis_size(axi...  14.7 us
    slice x5, local copies, waits for them, and re-layouts, shards(): inner_transfer[offset:offset + width].reshape(width, rank, rank)  4.45 us
    ppermute x1, starting transfers between devices, shards(): left = lax.ppermute(own, 'leaf', [(i, i + 1) for i in range(groups - 1)])  3.65 us
    dot_general x5, matrix products, shards(): jnp.einsum('nmab,nbc->nmac', mats.astype(jnp.float32).reshape(-1, 2, rank...  3.49 us
  transfers between devices with their start and end apart: 10, of which 7 were waited for; matrix products, arithmetic and copies ran while one was open for 22% of the time, Pallas kernels for 0%

profile of v1, /device:TPU:6, one launch (start us, length us, event | category | flops | bytes accessed | tf_op | source)
XLA Modules:
  0.0 82.8 jit_solution(9828496820438638299)
XLA Ops:
  0.7 3.6 %collective-permute-start = (bf16[64,4096]{1,0:T(8,128)(2,1)}, bf16[64,4096]{1,0:T(8,128)(2,1)S(1)}, u32[]{:S(2)}, u32[]{:S(2)}) collective-permute-start(bf16[64,4096]{1,0:T(8,128)(2,1)} %bitcast.71), channel_id=1, source_target_pairs={{0,8},{8,16},{16,24},{24,32},{32,40},{40,48},{48,56},{56,64},{64,7... | collective-permute-start | bytes 1572872 | tf_op jit(solution)/shard_map/ppermute | solution.py:169
  4.3 1.3 %collective-permute-start.1 = (bf16[64,4096]{1,0:T(8,128)(2,1)}, bf16[64,4096]{1,0:T(8,128)(2,1)S(1)}, u32[]{:S(2)}, u32[]{:S(2)}) collective-permute-start(bf16[64,4096]{1,0:T(8,128)(2,1)} %bitcast.72), channel_id=1, source_target_pairs={{8,0},{16,8},{24,16},{32,24},{40,32},{48,40},{56,48},{64,56},{72,6... | collective-permute-start | bytes 1572872 | tf_op jit(solution)/shard_map/ppermute | solution.py:170
  8.2 0.9 %slice.34 = bf16[16,4096]{1,0:T(8,128)(2,1)S(1)} slice(bf16[62,4096]{1,0:T(8,128)(2,1)} %param.14), slice={[32:48], [0:4096]} | slice | bytes 262144 | tf_op jit(solution)/shard_map/slice | solution.py:188
  9.1 1.0 %slice.35 = bf16[32,4096]{1,0:T(8,128)(2,1)S(1)} slice(bf16[62,4096]{1,0:T(8,128)(2,1)} %param.14), slice={[0:32], [0:4096]} | slice | bytes 524288 | tf_op jit(solution)/shard_map/slice | solution.py:188
  10.1 1.2 %dynamic-slice_reduce_fusion = (bf16[4096]{0:T(1024)(128)(2,1)S(1)}, bf16[4096]{0:T(1024)(128)(2,1)S(1)}, bf16[4096]{0:T(1024)(128)(2,1)S(1)}, bf16[4096]{0:T(1024)(128)(2,1)S(1)}, bf16[4096]{0:T(1024)(128)(2,1)S(1)}) fusion(bf16[62,4096]{1,0:T(8,128)(2,1)} %param.15, s32[]{:T(128)S(6)} %select_n.24, s32[]{:T(128)S(6)} %select_n.22, s32[]{:T(128)S(6)} %select_n.21, ...), kind=kLoop, calls=%fused_computation.15 | loop fusion | bytes 81940 | tf_op jit(solution)/shard_map/dynamic_slice | solution.py:179
  13.6 0.9 %fusion.13 = f32[8,64,2,64]{3,1,2,0:T(8,128)S(1)} fusion(f32[8,64,64,1]{1,2,3,0:T(8,128)S(1)} %bitcast.70, bf16[8,2,64,64]{3,2,1,0:T(8,128)(2,1)S(1)} %reshape.88), kind=kOutput, calls=%fused_computation.32 | convolution fusion | flops 50331648 | bytes 524288 | tf_op jit(solution)/shard_map/nmab,nbc->nmac/dot_general | solution.py:192
  14.5 1.6 %fusion.14 = f32[16,64,2,64]{3,1,2,0:T(8,128)S(1)} fusion(f32[16,64,64,1]{1,2,3,0:T(8,128)S(1)} %bitcast.69, bf16[16,2,64,64]{3,2,1,0:T(8,128)(2,1)S(1)} %reshape.90), kind=kOutput, calls=%fused_computation.33 | convolution fusion | flops 100663296 | bytes 1048576 | tf_op jit(solution)/shard_map/nmab,nbc->nmac/dot_general | solution.py:192
  18.3 0.9 %subtract_convert_fusion = (bf16[16,64,128]{2,1,0:T(8,128)(2,1)}, bf16[16,64,128]{2,1,0:T(8,128)(2,1)}) fusion(f32[16,64,128]{2,1,0:T(8,128)S(1)} %reshape.91), kind=kLoop, calls=%fused_computation.2 | loop fusion | flops 524288 | bytes 1048576 | tf_op jit(solution)/shard_map/convert_element_type | solution.py:20
  20.6 19.6 %leaf_pass.1 = (f32[32,64,64]{2,1,0:T(8,128)}, f32[4,8,16,128]{3,2,1,0:T(8,128)}, bf16[4,8,16,128]{3,2,1,0:T(8,128)(2,1)}, f32[64,64]{1,0:T(8,128)}) custom-call(s32[256]{0:T(256)} %reshape.79.slot_ref, s32[1]{0:T(128)} %bitcast.place_ref, bf16[64,4096]{1,0:T(8,128)(2,1)} %copy-done, bf16[64,4096]{1,0:T(8,128)(2,1)} %bitcast.73, bf16[64,4096]{1,0:T(8,128)(2,1)} %copy-done.1, ...), custom_call_target="tpu_custom_call" | custom-call | tf_op jit(solution)/shard_map/leaf_pass/pallas_call | solution.py:140
  40.2 2.2 %collective-permute-start.5 = (f32[64,64]{1,0:T(8,128)}, f32[64,64]{1,0:T(8,128)S(1)}, u32[]{:S(2)}, u32[]{:S(2)}) collective-permute-start(f32[64,64]{1,0:T(8,128)} %get-tuple-element.10), channel_id=1, source_target_pairs={{0,8},{8,0},{16,24},{24,16},{32,40},{40,32},{48,56},{56,48},{64,72... | collective-permute-start | bytes 49160 | tf_op jit(solution)/shard_map/ppermute | solution.py:154
  42.8 1.7 %collective-permute-done.5 = f32[64,64]{1,0:T(8,128)S(1)} collective-permute-done((f32[64,64]{1,0:T(8,128)}, f32[64,64]{1,0:T(8,128)S(1)}, u32[]{:S(2)}, u32[]{:S(2)}) %collective-permute-start.5) | collective-permute-done | bytes 16416 | tf_op jit(solution)/shard_map/ppermute | solution.py:154
  44.5 1.0 %fusion.9 = f32[64,64]{1,0:T(8,128)S(1)} fusion(bf16[64,64]{1,0:T(8,128)(2,1)S(1)} %reshape.92, f32[64,64]{1,0:T(8,128)} %get-tuple-element.10, f32[64,64]{1,0:T(8,128)S(1)} %collective-permute-done.5), kind=kOutput, calls=%fused_computation.26 | convolution fusion | flops 3149824 | bytes 57344 | tf_op jit(solution)/shard_map/dot_general | solution.py:224
  45.5 5.0 %collective-permute-start.6 = (f32[64,64]{1,0:T(8,128)S(1)}, f32[64,64]{1,0:T(8,128)S(1)}, u32[]{:S(2)}, u32[]{:S(2)}) collective-permute-start(f32[64,64]{1,0:T(8,128)S(1)} %fusion.9), channel_id=1, source_target_pairs={{0,24},{8,16},{16,8},{24,0},{32,56},{40,48},{48,40},{56,32},{64,88... | collective-permute-start | bytes 49160 | tf_op jit(solution)/shard_map/ppermute | solution.py:154
  51.3 1.1 %collective-permute-done.6 = f32[64,64]{1,0:T(8,128)S(1)} collective-permute-done((f32[64,64]{1,0:T(8,128)S(1)}, f32[64,64]{1,0:T(8,128)S(1)}, u32[]{:S(2)}, u32[]{:S(2)}) %collective-permute-start.6) | collective-permute-done | bytes 16416 | tf_op jit(solution)/shard_map/ppermute | solution.py:154
  52.6 2.9 %collective-permute-start.7 = (f32[64,64]{1,0:T(8,128)S(1)}, f32[64,64]{1,0:T(8,128)S(1)}, u32[]{:S(2)}, u32[]{:S(2)}) collective-permute-start(f32[64,64]{1,0:T(8,128)S(1)} %fusion.7), channel_id=1, source_target_pairs={{0,32},{8,40},{16,48},{24,56},{32,0},{40,8},{48,16},{56,24},{64,96... | collective-permute-start | bytes 49160 | tf_op jit(solution)/shard_map/ppermute | solution.py:154
  55.5 1.9 %collective-permute-done.7 = f32[64,64]{1,0:T(8,128)S(1)} collective-permute-done((f32[64,64]{1,0:T(8,128)S(1)}, f32[64,64]{1,0:T(8,128)S(1)}, u32[]{:S(2)}, u32[]{:S(2)}) %collective-permute-start.7) | collective-permute-done | bytes 16416 | tf_op jit(solution)/shard_map/ppermute | solution.py:154
  57.6 4.9 %collective-permute-start.8 = (f32[64,64]{1,0:T(8,128)S(1)}, f32[64,64]{1,0:T(8,128)S(1)}, u32[]{:S(2)}, u32[]{:S(2)}) collective-permute-start(f32[64,64]{1,0:T(8,128)S(1)} %fusion.5), channel_id=1, source_target_pairs={{0,64},{8,72},{16,80},{24,88},{32,96},{40,104},{48,112},{56,120},{... | collective-permute-start | bytes 49160 | tf_op jit(solution)/shard_map/ppermute | solution.py:154
  62.5 1.9 %collective-permute-done.8 = f32[64,64]{1,0:T(8,128)S(1)} collective-permute-done((f32[64,64]{1,0:T(8,128)S(1)}, f32[64,64]{1,0:T(8,128)S(1)}, u32[]{:S(2)}, u32[]{:S(2)}) %collective-permute-start.8) | collective-permute-done | bytes 16416 | tf_op jit(solution)/shard_map/ppermute | solution.py:154
  64.6 4.9 %collective-permute-start.9 = (f32[64,64]{1,0:T(8,128)S(1)}, f32[64,64]{1,0:T(8,128)S(1)}, u32[]{:S(2)}, u32[]{:S(2)}) collective-permute-start(f32[64,64]{1,0:T(8,128)S(1)} %fusion.3), channel_id=1, source_target_pairs={{0,192},{8,200},{16,208},{24,216},{32,224},{40,232},{48,240},{56,2... | collective-permute-start | bytes 49160 | tf_op jit(solution)/shard_map/ppermute | solution.py:154
  69.5 1.0 %convert_add_fusion = f32[4,8,16,128]{3,2,1,0:T(8,128)S(1)} fusion(f32[4,8,16,128]{3,2,1,0:T(8,128)} %get-tuple-element.8, bf16[4,8,16,128]{3,2,1,0:T(8,128)(2,1)S(1)} %collective-permute-done.2), kind=kLoop, calls=%fused_computation.3 | loop fusion | flops 131072 | bytes 655360 | tf_op jit(solution)/shard_map/add | solution.py:227
  70.5 0.9 %collective-permute-start.3 = (bf16[2,8,16,128]{3,2,1,0:T(8,128)(2,1)S(1)}, bf16[2,8,16,128]{3,2,1,0:T(8,128)(2,1)S(1)}, u32[]{:S(2)}, u32[]{:S(2)}) collective-permute-start(bf16[2,8,16,128]{3,2,1,0:T(8,128)(2,1)S(1)} %slice.59), channel_id=1, source_target_pairs={{0,2},{1,3},{2,0},{3,1},{4,6},{5,7},{6,4},{7,5},{8,10},{9,11},{10,... | collective-permute-start | bytes 196616 | tf_op jit(solution)/shard_map/ppermute | solution.py:154
  71.5 3.4 %collective-permute-done.3 = bf16[2,8,16,128]{3,2,1,0:T(8,128)(2,1)S(1)} collective-permute-done((bf16[2,8,16,128]{3,2,1,0:T(8,128)(2,1)S(1)}, bf16[2,8,16,128]{3,2,1,0:T(8,128)(2,1)S(1)}, u32[]{:S(2)}, u32[]{:S(2)}) %collective-permute-start.3) | collective-permute-done | bytes 65568 | tf_op jit(solution)/shard_map/ppermute | solution.py:154
  76.0 4.6 %collective-permute-done.4.last_ref = bf16[8,16,128]{2,1,0:T(8,128)(2,1)S(1)} collective-permute-done((bf16[8,16,128]{2,1,0:T(8,128)(2,1)S(1)}, bf16[8,16,128]{2,1,0:T(8,128)(2,1)S(1)}, u32[]{:S(2)}, u32[]{:S(2)}) %collective-permute-start.4) | collective-permute-done | bytes 32800 | tf_op jit(solution)/shard_map/ppermute | solution.py:154
  81.3 1.6 %finish.1 = f32[32,512]{1,0:T(8,128)} custom-call(f32[8,16,128]{2,1,0:T(8,128)} %get-tuple-element.19.total_ref, bf16[8,16,128]{2,1,0:T(8,128)(2,1)} %copy-done.2), custom_call_target="tpu_custom_call" | custom-call | tf_op jit(solution)/shard_map/finish/pallas_call | solution.py:232
  (50 shorter events, 11.9 us)
Async XLA Ops:
  0.6 16.9 %copy-start.4 = (s32[32,8]{0,1:T(8,128)S(1)}, s32[32,8]{0,1:T(8,128)}, u32[]{:S(2)}) copy-start(s32[32,8]{0,1:T(8,128)} %param.12) | copy-start | bytes 3076
  0.6 16.9 %copy-start.5 = (s32[32]{0:T(128)S(1)}, s32[32]{0:T(128)}, u32[]{:S(2)}) copy-start(s32[32]{0:T(128)} %param.13) | copy-start | bytes 388
  0.7 18.6 %collective-permute-start = (bf16[64,4096]{1,0:T(8,128)(2,1)}, bf16[64,4096]{1,0:T(8,128)(2,1)S(1)}, u32[]{:S(2)}, u32[]{:S(2)}) collective-permute-start(bf16[64,4096]{1,0:T(8,128)(2,1)} %bitcast.71), channel_id=1, source_target_pairs={{0,8},{8,16},{16,24},{24,32},{32,40},{40,48},{48,56},{56,64},{64,7... | collective-permute-start | bytes 1572872 | tf_op jit(solution)/shard_map/ppermute | solution.py:169
  4.3 15.5 %collective-permute-start.1 = (bf16[64,4096]{1,0:T(8,128)(2,1)}, bf16[64,4096]{1,0:T(8,128)(2,1)S(1)}, u32[]{:S(2)}, u32[]{:S(2)}) collective-permute-start(bf16[64,4096]{1,0:T(8,128)(2,1)} %bitcast.72), channel_id=1, source_target_pairs={{8,0},{16,8},{24,16},{32,24},{40,32},{48,40},{56,48},{64,56},{72,6... | collective-permute-start | bytes 1572872 | tf_op jit(solution)/shard_map/ppermute | solution.py:170
  19.2 0.8 copy-start
  19.8 0.8 copy-start.1
  40.2 4.3 %collective-permute-start.5 = (f32[64,64]{1,0:T(8,128)}, f32[64,64]{1,0:T(8,128)S(1)}, u32[]{:S(2)}, u32[]{:S(2)}) collective-permute-start(f32[64,64]{1,0:T(8,128)} %get-tuple-element.10), channel_id=1, source_target_pairs={{0,8},{8,0},{16,24},{24,16},{32,40},{40,32},{48,56},{56,48},{64,72... | collective-permute-start | bytes 49160 | tf_op jit(solution)/shard_map/ppermute | solution.py:154
  42.8 26.8 %collective-permute-start.2 = (bf16[4,8,16,128]{3,2,1,0:T(8,128)(2,1)}, bf16[4,8,16,128]{3,2,1,0:T(8,128)(2,1)S(1)}, u32[]{:S(2)}, u32[]{:S(2)}) collective-permute-start(bf16[4,8,16,128]{3,2,1,0:T(8,128)(2,1)} %get-tuple-element.9), channel_id=1, source_target_pairs={{0,1},{1,0},{2,3},{3,2},{4,5},{5,4},{6,7},{7,6},{8,9},{9,8},{10,11... | collective-permute-start | bytes 393224 | tf_op jit(solution)/shard_map/ppermute | solution.py:154
  45.5 6.9 %collective-permute-start.6 = (f32[64,64]{1,0:T(8,128)S(1)}, f32[64,64]{1,0:T(8,128)S(1)}, u32[]{:S(2)}, u32[]{:S(2)}) collective-permute-start(f32[64,64]{1,0:T(8,128)S(1)} %fusion.9), channel_id=1, source_target_pairs={{0,24},{8,16},{16,8},{24,0},{32,56},{40,48},{48,40},{56,32},{64,88... | collective-permute-start | bytes 49160 | tf_op jit(solution)/shard_map/ppermute | solution.py:154
  52.6 4.8 %collective-permute-start.7 = (f32[64,64]{1,0:T(8,128)S(1)}, f32[64,64]{1,0:T(8,128)S(1)}, u32[]{:S(2)}, u32[]{:S(2)}) collective-permute-start(f32[64,64]{1,0:T(8,128)S(1)} %fusion.7), channel_id=1, source_target_pairs={{0,32},{8,40},{16,48},{24,56},{32,0},{40,8},{48,16},{56,24},{64,96... | collective-permute-start | bytes 49160 | tf_op jit(solution)/shard_map/ppermute | solution.py:154
  57.6 6.8 %collective-permute-start.8 = (f32[64,64]{1,0:T(8,128)S(1)}, f32[64,64]{1,0:T(8,128)S(1)}, u32[]{:S(2)}, u32[]{:S(2)}) collective-permute-start(f32[64,64]{1,0:T(8,128)S(1)} %fusion.5), channel_id=1, source_target_pairs={{0,64},{8,72},{16,80},{24,88},{32,96},{40,104},{48,112},{56,120},{... | collective-permute-start | bytes 49160 | tf_op jit(solution)/shard_map/ppermute | solution.py:154
  64.6 11.4 %collective-permute-start.9 = (f32[64,64]{1,0:T(8,128)S(1)}, f32[64,64]{1,0:T(8,128)S(1)}, u32[]{:S(2)}, u32[]{:S(2)}) collective-permute-start(f32[64,64]{1,0:T(8,128)S(1)} %fusion.3), channel_id=1, source_target_pairs={{0,192},{8,200},{16,208},{24,216},{32,224},{40,232},{48,240},{56,2... | collective-permute-start | bytes 49160 | tf_op jit(solution)/shard_map/ppermute | solution.py:154
  70.5 4.4 %collective-permute-start.3 = (bf16[2,8,16,128]{3,2,1,0:T(8,128)(2,1)S(1)}, bf16[2,8,16,128]{3,2,1,0:T(8,128)(2,1)S(1)}, u32[]{:S(2)}, u32[]{:S(2)}) collective-permute-start(bf16[2,8,16,128]{3,2,1,0:T(8,128)(2,1)S(1)} %slice.59), channel_id=1, source_target_pairs={{0,2},{1,3},{2,0},{3,1},{4,6},{5,7},{6,4},{7,5},{8,10},{9,11},{10,... | collective-permute-start | bytes 196616 | tf_op jit(solution)/shard_map/ppermute | solution.py:154
  75.5 5.1 %collective-permute-start.4 = (bf16[8,16,128]{2,1,0:T(8,128)(2,1)S(1)}, bf16[8,16,128]{2,1,0:T(8,128)(2,1)S(1)}, u32[]{:S(2)}, u32[]{:S(2)}) collective-permute-start(bf16[8,16,128]{2,1,0:T(8,128)(2,1)S(1)} %get-tuple-element.18), channel_id=1, source_target_pairs={{0,6},{1,7},{2,4},{3,5},{4,2},{5,3},{6,0},{7,1},{8,14},{9,15},{10,... | collective-permute-start | bytes 98312 | tf_op jit(solution)/shard_map/ppermute | solution.py:154
  76.0 6.8 %copy-start.3 = (f32[5,64,64]{2,1,0:T(8,128)}, f32[5,64,64]{2,1,0:T(8,128)S(1)}, u32[]{:S(2)}) copy-start(f32[5,64,64]{2,1,0:T(8,128)S(1)} %bitcast_dynamic-update-slice_fusion) | copy-start | bytes 245764
  80.7 0.6 copy-start.2

commit v2 on v0

v2 whole, which is shorter than its diff:
```python
import functools

import jax
import jax.numpy as jnp
from jax import lax
from jax.experimental import pallas as pl
from jax.experimental.pallas import tpu as pltpu
from jax.sharding import PartitionSpec as P

NT = (((1,), (1,)), ((), ()))
NN = (((1,), (0,)), ((), ()))
PER_STEP = 8
TAIL = 2 * PER_STEP
VMEM = pl.BlockSpec(memory_space=pltpu.VMEM)
SMEM = pl.BlockSpec(memory_space=pltpu.SMEM)


def dot(a, b, dims):
    return lax.dot_general(a, b, dims, preferred_element_type=jnp.float32)


def split(value):
    high = value.astype(jnp.bfloat16)
    return high, (value - high.astype(jnp.float32)).astype(jnp.bfloat16)


def resident(value):
    return pltpu.with_memory_space_constraint(value, pltpu.VMEM)


def spread(source, first, ref, size):
    for leaf in range(ref.shape[1] // size):
        source[first + leaf] = ref[:, leaf * size : (leaf + 1) * size]


def subtract_near(total, steps, task_ref, source, blocks_ref, acc_ref, slots):
    shift = total.bit_length()
    low = (1 << shift) - 1

    def body(step, carry):
        done = []
        for task in range(PER_STEP):
            one = task_ref[(step * PER_STEP + task) * 2]
            two = task_ref[(step * PER_STEP + task) * 2 + 1]
            left, right = jnp.right_shift(one, shift), jnp.right_shift(two, shift)
            fetched = jnp.concatenate(
                [source[jnp.bitwise_and(one, low)], source[jnp.bitwise_and(two, low)]], axis=1
            )
            matrix = jnp.concatenate([blocks_ref[left], blocks_ref[right]], axis=1)
            done.append((lax.div(left, slots), dot(fetched, matrix, NT)))
        for leaf, near in done:
            acc_ref[leaf] = acc_ref[leaf] - near
        return carry

    lax.fori_loop(0, steps, body, 0)


def own_kernel(
    index_ref,
    number_ref,
    anchor_ref,
    own_ref,
    samples_ref,
    blocks_ref,
    acc_ref,
    far_task_ref,
    far_steps_ref,
    own_task,
    source,
):
    slots, count = index_ref.shape
    size = blocks_ref.shape[1]
    total = 2 * count
    shift = total.bit_length()
    for leaf in range(count):
        acc_ref[leaf] = samples_ref[:, leaf * size : (leaf + 1) * size].astype(jnp.float32)
    spread(source, 0, own_ref, size)
    source[count] = jnp.zeros_like(source[count])

    def sort_leaf(leaf, places):
        own_place, far_place = places
        live = number_ref[leaf]
        for slot in range(slots):
            block = jnp.left_shift(leaf * slots + slot, shift)
            at = index_ref[slot, leaf] - anchor_ref[0]
            inside = jnp.logical_and(at >= count, at < total)
            alive = slot < live
            own_task[own_place] = block + (at - count)
            far_task_ref[far_place] = block + jnp.where(at < count, at, at - count)
            own_place = own_place + jnp.where(jnp.logical_and(alive, inside), 1, 0)
            far_place = far_place + jnp.where(
                jnp.logical_and(alive, jnp.logical_not(inside)), 1, 0
            )
        block = jnp.left_shift(leaf * slots, shift)
        own_task[own_place] = block + count
        far_task_ref[far_place] = block + total
        return (
            own_place + jnp.bitwise_and(own_place, 1),
            far_place + jnp.bitwise_and(far_place, 1),
        )

    own_place, far_place = lax.fori_loop(0, count, sort_leaf, (0, 0))
    for place in range(TAIL):
        own_task[own_place + place] = count
        far_task_ref[far_place + place] = total
    far_steps_ref[0] = lax.div(far_place + TAIL - 1, TAIL)
    steps = lax.div(own_place + TAIL - 1, TAIL)
    subtract_near(total, steps, own_task, source, blocks_ref, acc_ref, slots)


def far_kernel(
    task_ref,
    steps_ref,
    left_ref,
    right_ref,
    near_ref,
    blocks_ref,
    basis_ref,
    path_high_ref,
    path_low_ref,
    coeff_ref,
    high_ref,
    part_ref,
    source,
    acc,
    low_ref,
):
    count, rank, size = basis_ref.shape
    slots = blocks_ref.shape[0] // count
    spread(source, 0, left_ref, size)
    spread(source, count, right_ref, size)
    source[2 * count] = jnp.zeros_like(source[2 * count])
    acc[...] = near_ref[...]
    subtract_near(2 * count, steps_ref[0], task_ref, source, blocks_ref, acc, slots)

    def leaf_step(step, carry):
        for inner in range(PER_STEP):
            leaf = step * PER_STEP + inner
            coeff = dot(basis_ref[leaf], acc[leaf].astype(jnp.bfloat16), NT)
            coeff_ref[leaf] = coeff
            high, low = split(coeff)
            rows = pl.ds(pl.multiple_of(leaf * rank, rank), rank)
            high_ref[rows, :] = high
            low_ref[rows, :] = low
        return carry

    lax.fori_loop(0, count // PER_STEP, leaf_step, 0)
    part = dot(path_high_ref[...], high_ref[...], NN)
    part += dot(path_low_ref[...], high_ref[...], NN)
    part += dot(path_high_ref[...], low_ref[...], NN)
    turned = part.T
    half = turned.shape[0] // 2
    part_ref[...] = jnp.concatenate([turned[:half], turned[half:]], axis=1)


def gram_kernel(scale, place_ref, high_ref, keep_ref, send_ref, gram):
    parts, rows, pairs, width = keep_ref.shape
    parts = 2 * parts
    rank = width // 2
    lane = lax.broadcasted_iota(jnp.int32, (rank, width), 1)

    def pair_step(step, carry):
        for inner in range(PER_STEP):
            pair = step * PER_STEP + inner
            one = high_ref[pl.ds(pl.multiple_of(pair * rank, rank), rank), :]
            two = high_ref[pl.ds(pl.multiple_of((pair + pairs) * rank, rank), rank), :]
            stacked = jnp.concatenate([one, two], axis=0)
            product = dot(stacked, stacked, NT)
            value = jnp.where(lane < rank, product[:rank], product[rank:]) * scale
            gram[pl.ds(pair, rank, stride=pairs), :] = value
        return carry

    lax.fori_loop(0, pairs // PER_STEP, pair_step, 0)
    for relative in range(parts):
        first = jnp.bitwise_xor(place_ref[0], relative) * rows
        target = send_ref if relative % 2 else keep_ref
        for row in range(rows):
            at = pl.multiple_of((first + row) * pairs, pairs)
            target[relative // 2, row] = gram[pl.ds(at, pairs), :]


def path_kernel(top_ref, mats_ref, high_ref, low_ref, work):
    rank = top_ref.shape[0]
    count = high_ref.shape[1] // rank
    top = top_ref[...].astype(jnp.float32).T
    nodes = [split(top)]
    width = 2
    offset = 2 * count - 2
    while width <= count:
        offset = offset - width
        later = []
        for parent, (high, low) in enumerate(nodes):
            first = (offset + 2 * parent) * rank
            pair = mats_ref[first : first + 2 * rank, :]
            product = dot(high, pair, NT) + dot(low, pair, NT)
            pair_high, pair_low = split(product)
            if width == count:
                high_ref[:, 2 * parent * rank : 2 * (parent + 1) * rank] = pair_high
                low_ref[:, 2 * parent * rank : 2 * (parent + 1) * rank] = pair_low
            else:
                later.append((pair_high[:, :rank], pair_low[:, :rank]))
                later.append((pair_high[:, rank:], pair_low[:, rank:]))
        nodes = later
        width = 2 * width


def finish_kernel(total_ref, last_ref, out_ref):
    rows, pairs, width = total_ref.shape
    half = width // 2
    lane = lax.broadcasted_iota(jnp.int32, (pairs, width), 1)
    for row in range(0, rows, 2):
        even = total_ref[row] + last_ref[row]
        odd = total_ref[row + 1] + last_ref[row + 1]
        at = slice(row * half, (row + 2) * half)
        out_ref[:pairs, at] = jnp.where(lane < half, even, pltpu.roll(odd, half, 1))
        out_ref[pairs:, at] = jnp.where(lane < half, pltpu.roll(even, half, 1), odd)


def params(mib):
    return pltpu.CompilerParams(vmem_limit_bytes=mib * 2**20)


def own_pass(index, number, anchor, own, samples, blocks):
    slots, count = index.shape
    size = blocks.shape[1]
    columns = own.shape[0]
    tasks = slots * count + TAIL
    return pl.pallas_call(
        own_kernel,
        in_specs=[SMEM, SMEM, SMEM, VMEM, VMEM, VMEM],
        out_specs=(VMEM, SMEM, SMEM),
        out_shape=(
            pltpu.VMEM((count, columns, size), jnp.float32),
            jax.ShapeDtypeStruct((tasks,), jnp.int32),
            jax.ShapeDtypeStruct((1,), jnp.int32),
        ),
        scratch_shapes=[
            pltpu.SMEM((tasks,), jnp.int32),
            pltpu.VMEM((count + 1, columns, size), jnp.bfloat16),
        ],
        compiler_params=params(8),
        name="own_pass",
    )(index, number, anchor, resident(own), resident(samples), resident(blocks))


def far_pass(tasks, steps, left, right, near, blocks, basis, path_high, path_low):
    count, rank, size = basis.shape
    columns = left.shape[0]
    return pl.pallas_call(
        far_kernel,
        in_specs=[SMEM, SMEM] + [VMEM] * 7,
        out_specs=(VMEM, VMEM, VMEM),
        out_shape=(
            pltpu.VMEM((count, rank, columns), jnp.float32),
            pltpu.VMEM((count * rank, columns), jnp.bfloat16),
            pltpu.VMEM((columns // 2, 2 * rank), jnp.float32),
        ),
        scratch_shapes=[
            pltpu.VMEM((2 * count + 1, columns, size), jnp.bfloat16),
            pltpu.VMEM((count, columns, size), jnp.float32),
            pltpu.VMEM((count * rank, columns), jnp.bfloat16),
        ],
        compiler_params=params(8),
        name="far_pass",
    )(
        tasks,
        steps,
        resident(left),
        resident(right),
        near,
        resident(blocks),
        resident(basis),
        path_high,
        path_low,
    )


def gram_pass(place, high, count, parts):
    columns = high.shape[1]
    rank = high.shape[0] // count
    pairs = count // 2
    shape = (parts // 2, rank // parts, pairs, 2 * rank)
    return pl.pallas_call(
        functools.partial(gram_kernel, 1.0 / (columns * parts)),
        in_specs=[SMEM, VMEM],
        out_specs=(VMEM, VMEM),
        out_shape=(pltpu.VMEM(shape, jnp.float32), pltpu.VMEM(shape, jnp.float32)),
        scratch_shapes=[pltpu.VMEM((rank * pairs, 2 * rank), jnp.float32)],
        compiler_params=params(8),
        name="gram_pass",
    )(place, high)


def path_pass(top, mats, count):
    rank = top.shape[0]
    shape = (rank, count * rank)
    return pl.pallas_call(
        path_kernel,
        in_specs=[VMEM, VMEM],
        out_specs=(VMEM, VMEM),
        out_shape=(pltpu.VMEM(shape, jnp.bfloat16), pltpu.VMEM(shape, jnp.bfloat16)),
        scratch_shapes=[pltpu.VMEM((8, 128), jnp.float32)],
        compiler_params=params(8),
        name="path_pass",
    )(resident(top), resident(mats))


def exchange(value, axis, flip):
    return lax.ppermute(value, axis, [(i, i ^ flip) for i in range(lax.axis_size(axis))])


def shards(
    samples, omega, leaf_basis, near_blocks, near_index, near_count, inner_transfer, upper_transfer
):
    count = near_count.shape[0]
    slots = near_index.shape[1]
    rank = leaf_basis.shape[1]
    size = leaf_basis.shape[2]
    groups = lax.axis_size("leaf")
    parts = lax.axis_size("samp")
    device = lax.axis_index("leaf")
    place = lax.axis_index("samp")

    own = omega.T
    left = lax.ppermute(own, "leaf", [(i, i + 1) for i in range(groups - 1)])
    right = lax.ppermute(own, "leaf", [(i + 1, i) for i in range(groups - 1)])

    blocks = near_blocks.reshape(count * slots, size, size)
    anchor = (device * count - count).astype(jnp.int32).reshape(1)
    near, tasks, steps = own_pass(near_index.T, near_count, anchor, own, samples.T, blocks)

    heights = groups.bit_length() - 1
    rows = []
    offset, width = 0, groups
    for height in range(heights):
        rows.append(
            lax.dynamic_slice_in_dim(
                upper_transfer, offset + jnp.right_shift(device, height), 1, axis=0
            )
        )
        offset, width = offset + width, width // 2
    upper = jnp.concatenate(rows, axis=0).reshape(heights, rank, rank)
    path_high, path_low = path_pass(upper[0], inner_transfer.reshape(-1, rank), count)
    both = jnp.zeros((heights, 2, rank, 2, rank), jnp.float32)
    both = both.at[:, 0, :, 0].set(upper.astype(jnp.float32))
    both = both.at[:, 1, :, 1].set(upper.astype(jnp.float32))
    both = both.reshape(heights, 2 * rank, 2 * rank)

    coeffs, high, part = far_pass(
        tasks, steps, left, right, near, blocks, leaf_basis, path_high, path_low
    )
    keep, send = gram_pass(place.astype(jnp.int32).reshape(1), high, count, parts)

    flips = (1, 3, 4, 8, 24)
    ancestors = []
    accum = part
    for height in range(heights):
        if height:
            accum = jnp.dot(accum, both[height], precision=lax.Precision.HIGHEST)
        accum = accum + exchange(accum, "leaf", flips[height])
        turned = accum.reshape(-1, 2, rank).transpose(2, 1, 0).reshape(rank, -1)
        ancestors.append(turned)
    gram = keep + exchange(send, "samp", 1)
    got = exchange(gram[1:3].astype(jnp.bfloat16), "samp", 2).astype(jnp.float32)
    near_total = gram[0] + got[0]
    far_total = gram[3] + got[1]
    last = exchange(far_total, "samp", 6)
    leaf_gram = pl.pallas_call(
        finish_kernel,
        in_specs=[VMEM, VMEM],
        out_specs=VMEM,
        out_shape=jax.ShapeDtypeStruct((count, rank * rank // parts), jnp.float32),
        compiler_params=params(8),
        name="finish",
    )(resident(near_total), resident(last))
    return coeffs, leaf_gram, jnp.stack(ancestors, axis=0)[None]


def solution(mesh):
    return jax.shard_map(
        shards,
        mesh=mesh,
        in_specs=(
            P("leaf", "samp"),
            P("leaf", "samp"),
            P("leaf", None, None),
            P("leaf", None, None, None),
            P("leaf", None),
            P("leaf"),
            P("leaf", None),
            P(),
        ),
        out_specs=(P("leaf", None, "samp"), P("leaf", "samp"), P("leaf", None, None, "samp")),
        check_vma=False,
    )
```

time: 91.9 us -> 74.6 us (0.81)
  the two profiles are of different devices: /device:TPU:16 before, /device:TPU:6 now
where the time goes in v2:
time: 74.6 us; the launch traced here: 73.9 us
  starting transfers between devices  24.8 us (33%)
  local copies, waits for them, and re-layouts  21.4 us (29%)
  Pallas kernels  13.1 us (18%)
  waiting for transfers between devices  13.1 us (18%)
  between operations  0.89 us (1%)
    ppermute x8, starting transfers between devices, exchange(): lax.ppermute(value, axis, [(i, i ^ flip) for i in range(lax.axis_size(axi...  19.8 us
    ppermute x8, waiting for transfers between devices, exchange(): lax.ppermute(value, axis, [(i, i ^ flip) for i in range(lax.axis_size(axi...  13.1 us
    unnamed x24, local copies, waits for them, and re-layouts  9.63 us
    pallas_call x1, Pallas kernels, own_pass(): pl.pallas_call(own_kernel, in_specs=[SMEM, SMEM, SMEM, VMEM, VMEM, VMEM],...  5.36 us
    scatter x1, local copies, waits for them, and re-layouts, shards(): both = both.at[:, 1, :, 1].set(upper.astype(jnp.float32))  5.12 us
    pallas_call x1, Pallas kernels, far_pass(): pl.pallas_call(far_kernel, in_specs=[SMEM, SMEM] + [VMEM] * 7, out_specs=...  4.62 us
    ppermute x1, starting transfers between devices, shards(): left = lax.ppermute(own, 'leaf', [(i, i + 1) for i in range(groups - 1)])  3.65 us
    reshape x1, local copies, waits for them, and re-layouts, shards(): inner_transfer.reshape(-1, rank)  2.02 us
  transfers between devices with their start and end apart: 10, of which 6 were waited for; matrix products, arithmetic and copies ran while one was open for 19% of the time, Pallas kernels for 10%

profile of v2, /device:TPU:6, one launch (start us, length us, event | category | flops | bytes accessed | tf_op | source)
XLA Modules:
  0.0 73.9 jit_solution(889312073268480067)
XLA Ops:
  0.6 3.6 %collective-permute-start = (bf16[64,4096]{1,0:T(8,128)(2,1)}, bf16[64,4096]{1,0:T(8,128)(2,1)S(1)}, u32[]{:S(2)}, u32[]{:S(2)}) collective-permute-start(bf16[64,4096]{1,0:T(8,128)(2,1)} %bitcast.39), channel_id=1, source_target_pairs={{0,8},{8,16},{16,24},{24,32},{32,40},{40,48},{48,56},{56,64},{64,7... | collective-permute-start | bytes 1572872 | tf_op jit(solution)/shard_map/ppermute | solution.py:325
  4.3 1.3 %collective-permute-start.1 = (bf16[64,4096]{1,0:T(8,128)(2,1)}, bf16[64,4096]{1,0:T(8,128)(2,1)S(1)}, u32[]{:S(2)}, u32[]{:S(2)}) collective-permute-start(bf16[64,4096]{1,0:T(8,128)(2,1)} %bitcast.40), channel_id=1, source_target_pairs={{8,0},{16,8},{24,16},{32,24},{40,32},{48,40},{56,48},{64,56},{72,6... | collective-permute-start | bytes 1572872 | tf_op jit(solution)/shard_map/ppermute | solution.py:326
  5.6 1.1 %constant_dynamic-slice_fusion = (bf16[1,4096]{1,0:T(2,128)(2,1)S(1)}, bf16[1,4096]{1,0:T(2,128)(2,1)S(1)}, bf16[1,4096]{1,0:T(2,128)(2,1)S(1)}, bf16[4096]{0:T(...) fusion(bf16[62,4096]{1,0:T(8,128)(2,1)} %param.19, s32[]{:T(128)S(6)} %select_n.19, ...), kind=kLoop, calls=%fused_computation.10 | loop fusion | bytes 90132 | tf_op jit(solution)/shard_map/dynamic_slice | solution.py:337
  6.8 2.0 %reshape.143.mats_ref = bf16[3968,64]{1,0:T(8,128)(2,1)S(1)} reshape(bf16[62,4096]{1,0:T(8,128)(2,1)} %param.18) | data formatting | bytes 1015808 | tf_op jit(solution)/shard_map/reshape | solution.py:343
  9.1 1.0 %scatter.6 = f32[5,2,64,2,64]{4,3,2,1,0:T(2,128)} pad(f32[5,1,64,1,64]{4,3,2,1,0:T(1,128)S(1)} %bitcast.43, f32[]{:T(128)} %constant.97.clone.1), padding=0_0x0_1x0_0x0_1x0_0 | pad | bytes 409604 | tf_op jit(solution)/shard_map/scatter | solution.py:345
  10.1 5.1 %scatter.9 = f32[5,2,64,2,64]{4,3,2,1,0:T(2,128)} dynamic-update-slice(f32[5,2,64,2,64]{4,3,2,1,0:T(2,128)} %scatter.6, f32[5,1,64,1,64]{4,3,2,1,0:T(1,128)S(1)} %bitcast.44, s32[]{:T(128)} %constant.83.clone.1, s32[]{:T(128)} %constant.86.clone.1, s32[]{:T(128)} %constant.83.clone.1, s32[]{:T(128)} %constant.86.clone.1, s32[]{:T(128)} %constant.83.clone.1) | dynamic-update-slice | bytes 163844 | tf_op jit(solution)/shard_map/scatter | solution.py:346
  15.2 1.7 %path_pass.1 = (bf16[64,2048]{1,0:T(8,128)(2,1)S(1)}, bf16[64,2048]{1,0:T(8,128)(2,1)S(1)}) custom-call(bf16[64,64]{1,0:T(8,128)(2,1)S(1)} %squeeze.19.top_ref, bf16[3968,64]{1,0:T(8,128)(2,1)S(1)} %reshape.143.mats_ref), custom_call_target="tpu_custom_call" | custom-call | tf_op jit(solution)/shard_map/path_pass/pallas_call | solution.py:297
  17.0 3.5 %copy-done = bf16[32,8,128,128]{3,2,1,0:T(8,128)(2,1)S(1)} copy-done((bf16[32,8,128,128]{3,2,1,0:T(8,128)(2,1)S(1)}, bf16[32,8,128,128]{3,2,1,0:T(8,128)(2,1)}, u32[]{:S(2)}) %copy-start) | copy-done | bytes 8388632
  20.4 1.0 %copy-done.2 = bf16[4096,64]{0,1:T(8,128)(2,1)S(1)} copy-done((bf16[4096,64]{0,1:T(8,128)(2,1)S(1)}, bf16[4096,64]{0,1:T(8,128)(2,1)}, u32[]{:S(2)}) %copy-start.2) | copy-done | bytes 524312
  21.5 1.0 %copy-done.3 = bf16[4096,64]{0,1:T(8,128)(2,1)S(1)} copy-done((bf16[4096,64]{0,1:T(8,128)(2,1)S(1)}, bf16[4096,64]{0,1:T(8,128)(2,1)}, u32[]{:S(2)}) %copy-start.3) | copy-done | bytes 524312
  23.9 5.4 %own_pass.1 = (f32[32,64,128]{2,1,0:T(8,128)S(1)}, s32[272]{0:T(512)S(1)}, s32[1]{0:T(128)}) custom-call(s32[8,32]{1,0:T(8,128)S(1)} %bitcast.42, s32[32]{0:T(128)S(1)} %copy-done.8, s32[1]{0:T(128)} %bitcast.1.anchor_ref, bf16[64,4096]{1,0:T(8,128)(2,1)S(1)} %bitcast.41, bf16[64,4096]{1,0:T(8,128)(2,1)S(1)} %bitcast.38, bf16[256,128,128]{2,1,0:T(8,128)(2,1)S(1)} %bitcast.36), custom_call_target="tpu_custom_call" | custom-call | tf_op jit(solution)/shard_map/own_pass/pallas_call | solution.py:228
  30.2 4.6 %far_pass.1 = (f32[32,64,64]{2,1,0:T(8,128)S(1)}, bf16[2048,64]{1,0:T(8,128)(2,1)S(1)}, f32[32,128]{1,0:T(8,128)S(1)}) custom-call(s32[272]{0:T(512)S(1)} %get-tuple-element.37.task_ref, s32[1]{0:T(128)} %get-tuple-element.38.steps_ref, bf16[64,4096]{1,0:T(8,128)(2,1)S(1)} %collective-permute-done.left_ref, ...), custom_call_target="tpu_custom_call" | custom-call | tf_op jit(solution)/shard_map/far_pass/pallas_call | solution.py:249
  34.9 2.7 %collective-permute-start.5 = (f32[32,128]{1,0:T(8,128)S(1)}, f32[32,128]{1,0:T(8,128)S(1)}, u32[]{:S(2)}, u32[]{:S(2)}) collective-permute-start(f32[32,128]{1,0:T(8,128)S(1)} %get-tuple-element.46), channel_id=1, source_target_pairs={{0,8},{8,0},{16,24},{24,16},{32,40},{40,32},{48,56},{56,48},{64,72... | collective-permute-start | bytes 49160 | tf_op jit(solution)/shard_map/ppermute | solution.py:309
  37.6 1.1 %fusion.3 = (f32[1,2,64,2,64]{4,3,2,1,0:T(2,128)S(1)}, f32[1,2,64,2,64]{4,3,2,1,0:T(2,128)S(1)}, f32[1,2,64,2,64]{4,3,2,1,0:T(2,128)S(1)}, f32[1,2,64,2,64]{4,3,2,1,0:T(2,128)S(1)}) fusion(f32[5,2,64,2,64]{4,3,2,1,0:T(2,128)} %scatter.9), kind=kLoop, calls=%fused_computation.16 | loop fusion | bytes 524288 | tf_op jit(solution)/shard_map/slice | solution.py:359
  40.0 1.0 %copy.29 = f32[32,64,64]{2,1,0:T(8,128)} copy(f32[32,64,64]{2,1,0:T(8,128)S(1)} %get-tuple-element.64) | data formatting | bytes 1048576
  41.3 2.9 %collective-permute-start.6 = (f32[32,128]{1,0:T(8,128)S(1)}, f32[32,128]{1,0:T(8,128)S(1)}, u32[]{:S(2)}, u32[]{:S(2)}) collective-permute-start(f32[32,128]{1,0:T(8,128)S(1)} %fusion.4), channel_id=1, source_target_pairs={{0,24},{8,16},{16,8},{24,0},{32,56},{40,48},{48,40},{56,32},{64,88... | collective-permute-start | bytes 49160 | tf_op jit(solution)/shard_map/ppermute | solution.py:309
  44.2 2.2 %collective-permute-done.6 = f32[32,128]{1,0:T(8,128)S(1)} collective-permute-done((f32[32,128]{1,0:T(8,128)S(1)}, f32[32,128]{1,0:T(8,128)S(1)}, u32[]{:S(2)}, u32[]{:S(2)}) %collective-permute-start.6) | collective-permute-done | bytes 16416 | tf_op jit(solution)/shard_map/ppermute | solution.py:309
  46.6 3.8 %collective-permute-start.7 = (f32[32,128]{1,0:T(8,128)S(1)}, f32[32,128]{1,0:T(8,128)S(1)}, u32[]{:S(2)}, u32[]{:S(2)}) collective-permute-start(f32[32,128]{1,0:T(8,128)S(1)} %fusion.5), channel_id=1, source_target_pairs={{0,32},{8,40},{16,48},{24,56},{32,0},{40,8},{48,16},{56,24},{64,96... | collective-permute-start | bytes 49160 | tf_op jit(solution)/shard_map/ppermute | solution.py:309
  50.4 1.7 %collective-permute-done.7 = f32[32,128]{1,0:T(8,128)S(1)} collective-permute-done((f32[32,128]{1,0:T(8,128)S(1)}, f32[32,128]{1,0:T(8,128)S(1)}, u32[]{:S(2)}, u32[]{:S(2)}) %collective-permute-start.7) | collective-permute-done | bytes 16416 | tf_op jit(solution)/shard_map/ppermute | solution.py:309
  52.3 3.1 %collective-permute-start.8 = (f32[32,128]{1,0:T(8,128)S(1)}, f32[32,128]{1,0:T(8,128)S(1)}, u32[]{:S(2)}, u32[]{:S(2)}) collective-permute-start(f32[32,128]{1,0:T(8,128)S(1)} %fusion.6), channel_id=1, source_target_pairs={{0,64},{8,72},{16,80},{24,88},{32,96},{40,104},{48,112},{56,120},{... | collective-permute-start | bytes 49160 | tf_op jit(solution)/shard_map/ppermute | solution.py:309
  55.5 1.7 %collective-permute-done.8 = f32[32,128]{1,0:T(8,128)S(1)} collective-permute-done((f32[32,128]{1,0:T(8,128)S(1)}, f32[32,128]{1,0:T(8,128)S(1)}, u32[]{:S(2)}, u32[]{:S(2)}) %collective-permute-start.8) | collective-permute-done | bytes 16416 | tf_op jit(solution)/shard_map/ppermute | solution.py:309
  57.4 5.7 %collective-permute-start.9 = (f32[32,128]{1,0:T(8,128)S(1)}, f32[32,128]{1,0:T(8,128)S(1)}, u32[]{:S(2)}, u32[]{:S(2)}) collective-permute-start(f32[32,128]{1,0:T(8,128)S(1)} %fusion.7), channel_id=1, source_target_pairs={{0,192},{8,200},{16,208},{24,216},{32,224},{40,232},{48,240},{56,2... | collective-permute-start | bytes 49160 | tf_op jit(solution)/shard_map/ppermute | solution.py:309
  65.0 2.6 %collective-permute-done.3 = bf16[2,8,16,128]{3,2,1,0:T(8,128)(2,1)S(1)} collective-permute-done((bf16[2,8,16,128]{3,2,1,0:T(8,128)(2,1)S(1)}, bf16[2,8,16,128]{3,2,1,0:T(8,128)(2,1)S(1)}, u32[]{:S(2)}, u32[]{:S(2)}) %collective-permute-start.3) | collective-permute-done | bytes 65568 | tf_op jit(solution)/shard_map/ppermute | solution.py:309
  69.0 4.2 %collective-permute-done.4.last_ref = f32[8,16,128]{2,1,0:T(8,128)S(1)} collective-permute-done((f32[8,16,128]{2,1,0:T(8,128)S(1)}, f32[8,16,128]{2,1,0:T(8,128)S(1)}, u32[]{:S(2)}, u32[]{:S(2)}) %collective-permute-start.4) | collective-permute-done | bytes 65568 | tf_op jit(solution)/shard_map/ppermute | solution.py:309
  (61 shorter events, 8.9 us)
Async XLA Ops:
  0.6 28.6 %copy-start.4 = (bf16[32,64,128]{2,1,0:T(8,128)(2,1)S(1)}, bf16[32,64,128]{2,1,0:T(8,128)(2,1)}, u32[]{:S(2)}) copy-start(bf16[32,64,128]{2,1,0:T(8,128)(2,1)} %basis_ref.1) | copy-start | bytes 1572868
  0.6 28.6 %collective-permute-start = (bf16[64,4096]{1,0:T(8,128)(2,1)}, bf16[64,4096]{1,0:T(8,128)(2,1)S(1)}, u32[]{:S(2)}, u32[]{:S(2)}) collective-permute-start(bf16[64,4096]{1,0:T(8,128)(2,1)} %bitcast.39), channel_id=1, source_target_pairs={{0,8},{8,16},{16,24},{24,32},{32,40},{40,48},{48,56},{56,64},{64,7... | collective-permute-start | bytes 1572872 | tf_op jit(solution)/shard_map/ppermute | solution.py:325
  4.3 24.9 %collective-permute-start.1 = (bf16[64,4096]{1,0:T(8,128)(2,1)}, bf16[64,4096]{1,0:T(8,128)(2,1)S(1)}, u32[]{:S(2)}, u32[]{:S(2)}) collective-permute-start(bf16[64,4096]{1,0:T(8,128)(2,1)} %bitcast.40), channel_id=1, source_target_pairs={{8,0},{16,8},{24,16},{32,24},{40,32},{48,40},{56,48},{64,56},{72,6... | collective-permute-start | bytes 1572872 | tf_op jit(solution)/shard_map/ppermute | solution.py:326
  16.9 12.3 %copy-start.5 = (bf16[64,2048]{1,0:T(8,128)(2,1)}, bf16[64,2048]{1,0:T(8,128)(2,1)S(1)}, u32[]{:S(2)}) copy-start(bf16[64,2048]{1,0:T(8,128)(2,1)S(1)} %get-tuple-element.41.path_low_ref) | copy-start | bytes 786436
  17.0 3.5 %copy-start = (bf16[32,8,128,128]{3,2,1,0:T(8,128)(2,1)S(1)}, bf16[32,8,128,128]{3,2,1,0:T(8,128)(2,1)}, u32[]{:S(2)}) copy-start(bf16[32,8,128,128]{3,2,1,0:T(8,128)(2,1)} %param.15) | copy-start | bytes 25165828
  20.4 1.0 %copy-start.2 = (bf16[4096,64]{0,1:T(8,128)(2,1)S(1)}, bf16[4096,64]{0,1:T(8,128)(2,1)}, u32[]{:S(2)}) copy-start(bf16[4096,64]{0,1:T(8,128)(2,1)} %param.12) | copy-start | bytes 1572868
  21.5 1.0 %copy-start.3 = (bf16[4096,64]{0,1:T(8,128)(2,1)S(1)}, bf16[4096,64]{0,1:T(8,128)(2,1)}, u32[]{:S(2)}) copy-start(bf16[4096,64]{0,1:T(8,128)(2,1)} %param.13) | copy-start | bytes 1572868
  22.5 0.7 copy-start.7
  23.2 0.7 copy-start.8
  23.9 5.4 %copy-start.1 = (bf16[32,8,128,128]{3,2,1,0:T(8,128)(2,1)S(1)}, bf16[32,8,128,128]{3,2,1,0:T(8,128)(2,1)}, u32[]{:S(2)}) copy-start(bf16[32,8,128,128]{3,2,1,0:T(8,128)(2,1)} %param.15) | copy-start | bytes 25165828
  29.3 1.0 %copy-start.6 = (bf16[64,2048]{1,0:T(8,128)(2,1)S(1)}, bf16[64,2048]{1,0:T(8,128)(2,1)}, u32[]{:S(2)}) copy-start(bf16[64,2048]{1,0:T(8,128)(2,1)} %copy-done.5) | copy-start | bytes 786436
  34.9 6.2 %collective-permute-start.5 = (f32[32,128]{1,0:T(8,128)S(1)}, f32[32,128]{1,0:T(8,128)S(1)}, u32[]{:S(2)}, u32[]{:S(2)}) collective-permute-start(f32[32,128]{1,0:T(8,128)S(1)} %get-tuple-element.46), channel_id=1, source_target_pairs={{0,8},{8,0},{16,24},{24,16},{32,40},{40,32},{48,56},{56,48},{64,72... | collective-permute-start | bytes 49160 | tf_op jit(solution)/shard_map/ppermute | solution.py:309
  39.9 23.2 %collective-permute-start.2 = (f32[4,8,16,128]{3,2,1,0:T(8,128)S(1)}, f32[4,8,16,128]{3,2,1,0:T(8,128)S(1)}, u32[]{:S(2)}, u32[]{:S(2)}) collective-permute-start(f32[4,8,16,128]{3,2,1,0:T(8,128)S(1)} %get-tuple-element.45), channel_id=1, source_target_pairs={{0,1},{1,0},{2,3},{3,2},{4,5},{5,4},{6,7},{7,6},{8,9},{9,8},{10,11... | collective-permute-start | bytes 786440 | tf_op jit(solution)/shard_map/ppermute | solution.py:309
  41.3 5.0 %collective-permute-start.6 = (f32[32,128]{1,0:T(8,128)S(1)}, f32[32,128]{1,0:T(8,128)S(1)}, u32[]{:S(2)}, u32[]{:S(2)}) collective-permute-start(f32[32,128]{1,0:T(8,128)S(1)} %fusion.4), channel_id=1, source_target_pairs={{0,24},{8,16},{16,8},{24,0},{32,56},{40,48},{48,40},{56,32},{64,88... | collective-permute-start | bytes 49160 | tf_op jit(solution)/shard_map/ppermute | solution.py:309
  46.6 5.5 %collective-permute-start.7 = (f32[32,128]{1,0:T(8,128)S(1)}, f32[32,128]{1,0:T(8,128)S(1)}, u32[]{:S(2)}, u32[]{:S(2)}) collective-permute-start(f32[32,128]{1,0:T(8,128)S(1)} %fusion.5), channel_id=1, source_target_pairs={{0,32},{8,40},{16,48},{24,56},{32,0},{40,8},{48,16},{56,24},{64,96... | collective-permute-start | bytes 49160 | tf_op jit(solution)/shard_map/ppermute | solution.py:309
  52.3 4.9 %collective-permute-start.8 = (f32[32,128]{1,0:T(8,128)S(1)}, f32[32,128]{1,0:T(8,128)S(1)}, u32[]{:S(2)}, u32[]{:S(2)}) collective-permute-start(f32[32,128]{1,0:T(8,128)S(1)} %fusion.6), channel_id=1, source_target_pairs={{0,64},{8,72},{16,80},{24,88},{32,96},{40,104},{48,112},{56,120},{... | collective-permute-start | bytes 49160 | tf_op jit(solution)/shard_map/ppermute | solution.py:309
  57.4 7.4 %collective-permute-start.9 = (f32[32,128]{1,0:T(8,128)S(1)}, f32[32,128]{1,0:T(8,128)S(1)}, u32[]{:S(2)}, u32[]{:S(2)}) collective-permute-start(f32[32,128]{1,0:T(8,128)S(1)} %fusion.7), channel_id=1, source_target_pairs={{0,192},{8,200},{16,208},{24,216},{32,224},{40,232},{48,240},{56,2... | collective-permute-start | bytes 49160 | tf_op jit(solution)/shard_map/ppermute | solution.py:309
  63.2 4.4 %collective-permute-start.3 = (bf16[2,8,16,128]{3,2,1,0:T(8,128)(2,1)S(1)}, bf16[2,8,16,128]{3,2,1,0:T(8,128)(2,1)S(1)}, u32[]{:S(2)}, u32[]{:S(2)}) collective-permute-start(bf16[2,8,16,128]{3,2,1,0:T(8,128)(2,1)S(1)} %slice.124), channel_id=1, source_target_pairs={{0,2},{1,3},{2,0},{3,1},{4,6},{5,7},{6,4},{7,5},{8,10},{9,11},{10,... | collective-permute-start | bytes 196616 | tf_op jit(solution)/shard_map/ppermute | solution.py:309
  67.6 5.6 %collective-permute-start.4 = (f32[8,16,128]{2,1,0:T(8,128)S(1)}, f32[8,16,128]{2,1,0:T(8,128)S(1)}, u32[]{:S(2)}, u32[]{:S(2)}) collective-permute-start(f32[8,16,128]{2,1,0:T(8,128)S(1)} %get-tuple-element.62), channel_id=1, source_target_pairs={{0,6},{1,7},{2,4},{3,5},{4,2},{5,3},{6,0},{7,1},{8,14},{9,15},{10,... | collective-permute-start | bytes 196616 | tf_op jit(solution)/shard_map/ppermute | solution.py:309

commit v3 on v2

--- a/solution.py
+++ b/solution.py
@@ -13,6 +13,7 @@
 TAIL = 2 * PER_STEP
 VMEM = pl.BlockSpec(memory_space=pltpu.VMEM)
 SMEM = pl.BlockSpec(memory_space=pltpu.SMEM)
+ANY = pl.BlockSpec(memory_space=pl.ANY)
 
 
 def dot(a, b, dims):
@@ -55,27 +56,82 @@
     lax.fori_loop(0, steps, body, 0)
 
 
+def path_products(upper_ref, mats_ref, high_ref, low_ref):
+    rank = upper_ref.shape[1]
+    count = high_ref.shape[1] // rank
+    top = upper_ref[0].astype(jnp.float32).T
+    nodes = [split(top)]
+    width = 2
+    offset = 2 * count - 2
+    while width <= count:
+        offset = offset - width
+        later = []
+        for parent, (high, low) in enumerate(nodes):
+            first = (offset + 2 * parent) * rank
+            pair = mats_ref[first : first + 2 * rank, :]
+            product = dot(high, pair, NT) + dot(low, pair, NT)
+            pair_high, pair_low = split(product)
+            if width == count:
+                high_ref[:, 2 * parent * rank : 2 * (parent + 1) * rank] = pair_high
+                low_ref[:, 2 * parent * rank : 2 * (parent + 1) * rank] = pair_low
+            else:
+                later.append((pair_high[:, :rank], pair_low[:, :rank]))
+                later.append((pair_high[:, rank:], pair_low[:, rank:]))
+        nodes = later
+        width = 2 * width
+
+
 def own_kernel(
+    anchor_ref,
+    index_any,
+    number_any,
+    upper_ref,
+    mats_ref,
+    own_any,
+    samples_any,
+    blocks_any,
+    acc_ref,
+    blocks_ref,
+    path_high_ref,
+    path_low_ref,
+    twice_ref,
+    far_task_ref,
+    far_steps_ref,
     index_ref,
     number_ref,
-    anchor_ref,
+    own_task,
     own_ref,
     samples_ref,
-    blocks_ref,
-    acc_ref,
-    far_task_ref,
-    far_steps_ref,
-    own_task,
     source,
+    sems,
 ):
+    copies = [
+        pltpu.make_async_copy(origin, target, sems.at[place])
+        for place, (origin, target) in enumerate(
+            (
+                (index_any, index_ref),
+                (number_any, number_ref),
+                (own_any, own_ref),
+                (samples_any, samples_ref),
+                (blocks_any, blocks_ref),
+            )
+        )
+    ]
+    for copy in copies:
+        copy.start()
     slots, count = index_ref.shape
     size = blocks_ref.shape[1]
     total = 2 * count
     shift = total.bit_length()
-    for leaf in range(count):
-        acc_ref[leaf] = samples_ref[:, leaf * size : (leaf + 1) * size].astype(jnp.float32)
-    spread(source, 0, own_ref, size)
-    source[count] = jnp.zeros_like(source[count])
+    path_products(upper_ref, mats_ref, path_high_ref, path_low_ref)
+    for height in range(1, upper_ref.shape[0]):
+        matrix = upper_ref[height].astype(jnp.float32)
+        blank = jnp.zeros_like(matrix)
+        rank = matrix.shape[0]
+        twice_ref[height - 1, :rank] = jnp.concatenate([matrix, blank], axis=1)
+        twice_ref[height - 1, rank:] = jnp.concatenate([blank, matrix], axis=1)
+    copies[0].wait()
+    copies[1].wait()
 
     def sort_leaf(leaf, places):
         own_place, far_place = places
@@ -105,6 +161,13 @@
         far_task_ref[far_place + place] = total
     far_steps_ref[0] = lax.div(far_place + TAIL - 1, TAIL)
     steps = lax.div(own_place + TAIL - 1, TAIL)
+    copies[2].wait()
+    spread(source, 0, own_ref, size)
+    source[count] = jnp.zeros_like(source[count])
+    copies[3].wait()
+    for leaf in range(count):
+        acc_ref[leaf] = samples_ref[:, leaf * size : (leaf + 1) * size].astype(jnp.float32)
+    copies[4].wait()
     subtract_near(total, steps, own_task, source, blocks_ref, acc_ref, slots)
 
 
@@ -121,16 +184,16 @@
     coeff_ref,
     high_ref,
     part_ref,
+    acc,
     source,
-    acc,
     low_ref,
 ):
+    del near_ref
     count, rank, size = basis_ref.shape
     slots = blocks_ref.shape[0] // count
     spread(source, 0, left_ref, size)
     spread(source, count, right_ref, size)
     source[2 * count] = jnp.zeros_like(source[2 * count])
-    acc[...] = near_ref[...]
     subtract_near(2 * count, steps_ref[0], task_ref, source, blocks_ref, acc, slots)
 
     def leaf_step(step, carry):
@@ -154,8 +217,7 @@
 
 
 def gram_kernel(scale, place_ref, high_ref, keep_ref, send_ref, gram):
-    parts, rows, pairs, width = keep_ref.shape
-    parts = 2 * parts
+    hops, cores, rows, pairs, width = keep_ref.shape
     rank = width // 2
     lane = lax.broadcasted_iota(jnp.int32, (rank, width), 1)
 
@@ -171,76 +233,85 @@
         return carry
 
     lax.fori_loop(0, pairs // PER_STEP, pair_step, 0)
-    for relative in range(parts):
-        first = jnp.bitwise_xor(place_ref[0], relative) * rows
-        target = send_ref if relative % 2 else keep_ref
-        for row in range(rows):
-            at = pl.multiple_of((first + row) * pairs, pairs)
-            target[relative // 2, row] = gram[pl.ds(at, pairs), :]
-
-
-def path_kernel(top_ref, mats_ref, high_ref, low_ref, work):
-    rank = top_ref.shape[0]
-    count = high_ref.shape[1] // rank
-    top = top_ref[...].astype(jnp.float32).T
-    nodes = [split(top)]
-    width = 2
-    offset = 2 * count - 2
-    while width <= count:
-        offset = offset - width
-        later = []
-        for parent, (high, low) in enumerate(nodes):
-            first = (offset + 2 * parent) * rank
-            pair = mats_ref[first : first + 2 * rank, :]
-            product = dot(high, pair, NT) + dot(low, pair, NT)
-            pair_high, pair_low = split(product)
-            if width == count:
-                high_ref[:, 2 * parent * rank : 2 * (parent + 1) * rank] = pair_high
-                low_ref[:, 2 * parent * rank : 2 * (parent + 1) * rank] = pair_low
-            else:
-                later.append((pair_high[:, :rank], pair_low[:, :rank]))
-                later.append((pair_high[:, rank:], pair_low[:, rank:]))
-        nodes = later
-        width = 2 * width
-
-
-def finish_kernel(total_ref, last_ref, out_ref):
+    for hop in range(hops):
+        for core in range(cores):
+            first = (jnp.bitwise_xor(place_ref[0], hop) * cores + core) * rows
+            for row in range(rows):
+                at = pl.multiple_of((first + row) * pairs, pairs)
+                tile = gram[pl.ds(at, pairs), :]
+                keep_ref[hop, core, row] = tile
+                send_ref[hop, core, row] = tile.astype(send_ref.dtype)
+
+
+def finish_kernel(core_ref, total_ref, other_ref, out_ref):
     rows, pairs, width = total_ref.shape
     half = width // 2
     lane = lax.broadcasted_iota(jnp.int32, (pairs, width), 1)
+    first = jnp.broadcast_to(core_ref[0], (pairs, width)) == 0
     for row in range(0, rows, 2):
-        even = total_ref[row] + last_ref[row]
-        odd = total_ref[row + 1] + last_ref[row + 1]
+        even = jnp.where(first, total_ref[row], other_ref[row])
+        odd = jnp.where(first, total_ref[row + 1], other_ref[row + 1])
         at = slice(row * half, (row + 2) * half)
         out_ref[:pairs, at] = jnp.where(lane < half, even, pltpu.roll(odd, half, 1))
         out_ref[pairs:, at] = jnp.where(lane < half, pltpu.roll(even, half, 1), odd)
 
 
+def turn_kernel(core_ref, lower_ref, last_ref, *refs):
+    levels, out_ref = refs[:-1], refs[-1]
+    half, width = last_ref.shape
+    first = jnp.broadcast_to(core_ref[0], (half, width)) == 0
+    for height, held in enumerate(levels):
+        at = slice(height * half, (height + 1) * half)
+        sent = last_ref[...] if held is levels[-1] else lower_ref[at]
+        turned = jnp.where(first, sent, held[:half]).T
+        out_ref[height] = jnp.concatenate([turned[: width // 2], turned[width // 2 :]], axis=1)
+
+
 def params(mib):
     return pltpu.CompilerParams(vmem_limit_bytes=mib * 2**20)
 
 
-def own_pass(index, number, anchor, own, samples, blocks):
+def own_pass(anchor, index, number, upper, mats, own, samples, blocks):
     slots, count = index.shape
     size = blocks.shape[1]
     columns = own.shape[0]
+    heights, rank, _ = upper.shape
     tasks = slots * count + TAIL
+    far = lambda value: pltpu.with_memory_space_constraint(value, pltpu.HBM)
     return pl.pallas_call(
         own_kernel,
-        in_specs=[SMEM, SMEM, SMEM, VMEM, VMEM, VMEM],
-        out_specs=(VMEM, SMEM, SMEM),
+        in_specs=[SMEM, ANY, ANY, VMEM, VMEM, ANY, ANY, ANY],
+        out_specs=(VMEM, VMEM, VMEM, VMEM, VMEM, SMEM, SMEM),
         out_shape=(
             pltpu.VMEM((count, columns, size), jnp.float32),
+            pltpu.VMEM(blocks.shape, blocks.dtype),
+            pltpu.VMEM((rank, count * rank), jnp.bfloat16),
+            pltpu.VMEM((rank, count * rank), jnp.bfloat16),
+            pltpu.VMEM((heights - 1, 2 * rank, 2 * rank), jnp.float32),
             jax.ShapeDtypeStruct((tasks,), jnp.int32),
             jax.ShapeDtypeStruct((1,), jnp.int32),
         ),
         scratch_shapes=[
+            pltpu.SMEM((slots, count), jnp.int32),
+            pltpu.SMEM((count,), jnp.int32),
             pltpu.SMEM((tasks,), jnp.int32),
+            pltpu.VMEM(own.shape, own.dtype),
+            pltpu.VMEM(samples.shape, samples.dtype),
             pltpu.VMEM((count + 1, columns, size), jnp.bfloat16),
+            pltpu.SemaphoreType.DMA((5,)),
         ],
         compiler_params=params(8),
         name="own_pass",
-    )(index, number, anchor, resident(own), resident(samples), resident(blocks))
+    )(
+        anchor,
+        far(index),
+        far(number),
+        resident(upper),
+        resident(mats),
+        far(own),
+        far(samples),
+        far(blocks),
+    )
 
 
 def far_pass(tasks, steps, left, right, near, blocks, basis, path_high, path_low):
@@ -249,15 +320,16 @@
     return pl.pallas_call(
         far_kernel,
         in_specs=[SMEM, SMEM] + [VMEM] * 7,
-        out_specs=(VMEM, VMEM, VMEM),
+        out_specs=(VMEM, VMEM, VMEM, VMEM),
         out_shape=(
             pltpu.VMEM((count, rank, columns), jnp.float32),
             pltpu.VMEM((count * rank, columns), jnp.bfloat16),
             pltpu.VMEM((columns // 2, 2 * rank), jnp.float32),
+            pltpu.VMEM((count, columns, size), jnp.float32),
         ),
+        input_output_aliases={4: 3},
         scratch_shapes=[
             pltpu.VMEM((2 * count + 1, columns, size), jnp.bfloat16),
-            pltpu.VMEM((count, columns, size), jnp.float32),
             pltpu.VMEM((count * rank, columns), jnp.bfloat16),
         ],
         compiler_params=params(8),
@@ -268,45 +340,44 @@
         resident(left),
         resident(right),
         near,
-        resident(blocks),
+        blocks,
         resident(basis),
         path_high,
         path_low,
     )
 
 
-def gram_pass(place, high, count, parts):
+def gram_pass(place, high, count, hops, cores):
     columns = high.shape[1]
     rank = high.shape[0] // count
     pairs = count // 2
-    shape = (parts // 2, rank // parts, pairs, 2 * rank)
+    parts = hops * cores
+    shape = (hops, cores, rank // parts, pairs, 2 * rank)
     return pl.pallas_call(
         functools.partial(gram_kernel, 1.0 / (columns * parts)),
         in_specs=[SMEM, VMEM],
         out_specs=(VMEM, VMEM),
-        out_shape=(pltpu.VMEM(shape, jnp.float32), pltpu.VMEM(shape, jnp.float32)),
+        out_shape=(pltpu.VMEM(shape, jnp.float32), pltpu.VMEM(shape, jnp.bfloat16)),
         scratch_shapes=[pltpu.VMEM((rank * pairs, 2 * rank), jnp.float32)],
         compiler_params=params(8),
         name="gram_pass",
     )(place, high)
 
 
-def path_pass(top, mats, count):
-    rank = top.shape[0]
-    shape = (rank, count * rank)
-    return pl.pallas_call(
-        path_kernel,
-        in_specs=[VMEM, VMEM],
-        out_specs=(VMEM, VMEM),
-        out_shape=(pltpu.VMEM(shape, jnp.bfloat16), pltpu.VMEM(shape, jnp.bfloat16)),
-        scratch_shapes=[pltpu.VMEM((8, 128), jnp.float32)],
-        compiler_params=params(8),
-        name="path_pass",
-    )(resident(top), resident(mats))
-
-
-def exchange(value, axis, flip):
-    return lax.ppermute(value, axis, [(i, i ^ flip) for i in range(lax.axis_size(axis))])
+def exchange(value, core, leaf=0, samp=0):
+    groups, parts = lax.axis_size("leaf"), lax.axis_size("samp")
+    pairs = [
+        (g * parts + s, (g ^ leaf) * parts + (s ^ samp))
+        for g in range(groups)
+        for s in range(core, parts, 2)
+    ]
+    return lax.ppermute(value, ("leaf", "samp"), pairs)
+
+
+def hand_over(value, core):
+    return lax.ppermute(
+        value, "samp", [(s, s ^ 1) for s in range(core, lax.axis_size("samp"), 2)]
+    )
 
 
 def shards(
@@ -319,15 +390,12 @@
     groups = lax.axis_size("leaf")
     parts = lax.axis_size("samp")
     device = lax.axis_index("leaf")
-    place = lax.axis_index("samp")
+    place = lax.axis_index("samp").astype(jnp.int32)
+    hop, core = jnp.right_shift(place, 1).reshape(1), jnp.bitwise_and(place, 1).reshape(1)
 
     own = omega.T
     left = lax.ppermute(own, "leaf", [(i, i + 1) for i in range(groups - 1)])
     right = lax.ppermute(own, "leaf", [(i + 1, i) for i in range(groups - 1)])
-
-    blocks = near_blocks.reshape(count * slots, size, size)
-    anchor = (device * count - count).astype(jnp.int32).reshape(1)
-    near, tasks, steps = own_pass(near_index.T, near_count, anchor, own, samples.T, blocks)
 
     heights = groups.bit_length() - 1
     rows = []
@@ -340,40 +408,58 @@
         )
         offset, width = offset + width, width // 2
     upper = jnp.concatenate(rows, axis=0).reshape(heights, rank, rank)
-    path_high, path_low = path_pass(upper[0], inner_transfer.reshape(-1, rank), count)
-    both = jnp.zeros((heights, 2, rank, 2, rank), jnp.float32)
-    both = both.at[:, 0, :, 0].set(upper.astype(jnp.float32))
-    both = both.at[:, 1, :, 1].set(upper.astype(jnp.float32))
-    both = both.reshape(heights, 2 * rank, 2 * rank)
-
-    coeffs, high, part = far_pass(
+
+    blocks = near_blocks.reshape(count * slots, size, size)
+    anchor = (device * count - count).astype(jnp.int32).reshape(1)
+    near, blocks, path_high, path_low, twice, tasks, steps = own_pass(
+        anchor,
+        near_index.T,
+        near_count,
+        upper,
+        inner_transfer.reshape(-1, rank),
+        own,
+        samples.T,
+        blocks,
+    )
+    coeffs, high, part, _ = far_pass(
         tasks, steps, left, right, near, blocks, leaf_basis, path_high, path_low
     )
-    keep, send = gram_pass(place.astype(jnp.int32).reshape(1), high, count, parts)
-
+
+    accum = jnp.concatenate([part, hand_over(part, 0)], axis=0)
+    keep, send = gram_pass(hop, high, count, parts // 2, 2)
     flips = (1, 3, 4, 8, 24)
-    ancestors = []
-    accum = part
+    held = []
     for height in range(heights):
         if height:
-            accum = jnp.dot(accum, both[height], precision=lax.Precision.HIGHEST)
-        accum = accum + exchange(accum, "leaf", flips[height])
-        turned = accum.reshape(-1, 2, rank).transpose(2, 1, 0).reshape(rank, -1)
-        ancestors.append(turned)
-    gram = keep + exchange(send, "samp", 1)
-    got = exchange(gram[1:3].astype(jnp.bfloat16), "samp", 2).astype(jnp.float32)
+            accum = jnp.dot(accum, twice[height - 1], precision=lax.Precision.HIGHEST)
+        accum = accum + exchange(accum, 1, leaf=flips[height])
+        held.append(accum)
+        if height == heights - 2:
+            lower = hand_over(jnp.concatenate([a[part.shape[0] :] for a in held], axis=0), 1)
+    last = hand_over(accum[part.shape[0] :], 1)
+    ancestors = pl.pallas_call(
+        turn_kernel,
+        in_specs=[SMEM] + [VMEM] * (heights + 2),
+        out_specs=VMEM,
+        out_shape=jax.ShapeDtypeStruct((heights, rank, part.shape[0] * 2), jnp.float32),
+        compiler_params=params(8),
+        name="turn",
+    )(core, resident(lower), resident(last), *map(resident, held))
+
+    gram = keep + hand_over(send, 1).astype(jnp.float32)
+    got = exchange(gram[1:3].astype(jnp.bfloat16), 0, samp=2).astype(jnp.float32)
     near_total = gram[0] + got[0]
-    far_total = gram[3] + got[1]
-    last = exchange(far_total, "samp", 6)
+    total = near_total + exchange(gram[3] + got[1], 0, samp=6)
+    other = hand_over(total[1], 0)
     leaf_gram = pl.pallas_call(
         finish_kernel,
-        in_specs=[VMEM, VMEM],
+        in_specs=[SMEM, VMEM, VMEM],
         out_specs=VMEM,
         out_shape=jax.ShapeDtypeStruct((count, rank * rank // parts), jnp.float32),
         compiler_params=params(8),
         name="finish",
-    )(resident(near_total), resident(last))
-    return coeffs, leaf_gram, jnp.stack(ancestors, axis=0)[None]
+    )(core, resident(total[0]), resident(other))
+    return coeffs, leaf_gram, ancestors[None]
 
 
 def solution(mesh):

time: 74.6 us -> 71.3 us (0.956)
  the two profiles are of different devices: /device:TPU:6 before, /device:TPU:97 now
where the time goes in v3:
time: 71.3 us; the launch traced here: 70.8 us
  starting transfers between devices  35.2 us (49%)
  waiting for transfers between devices  15.3 us (21%)
  Pallas kernels  14.1 us (20%)
  local copies, waits for them, and re-layouts  4.36 us (6%)
  between operations  0.98 us (1%)
  matrix products  0.73 us (1%)
    ppermute x7, starting transfers between devices, exchange(): return lax.ppermute(value, ('leaf', 'samp'), pairs)  19.1 us
    ppermute x7, waiting for transfers between devices, exchange(): return lax.ppermute(value, ('leaf', 'samp'), pairs)  12.4 us
    ppermute x5, starting transfers between devices, hand_over(): lax.ppermute(value, 'samp', [(s, s ^ 1) for s in range(core, lax.axis_siz...  8.62 us
    pallas_call x1, Pallas kernels, own_pass(): pl.pallas_call(own_kernel, in_specs=[SMEM, ANY, ANY, VMEM, VMEM, ANY, ANY...  6.86 us
    pallas_call x1, Pallas kernels, far_pass(): pl.pallas_call(far_kernel, in_specs=[SMEM, SMEM] + [VMEM] * 7, out_specs=...  4.89 us
    ppermute x1, starting transfers between devices, shards(): right = lax.ppermute(own, 'leaf', [(i + 1, i) for i in range(groups - 1)])  4.19 us
    ppermute x1, starting transfers between devices, shards(): left = lax.ppermute(own, 'leaf', [(i, i + 1) for i in range(groups - 1)])  3.34 us
    ppermute x5, waiting for transfers between devices, hand_over(): lax.ppermute(value, 'samp', [(s, s ^ 1) for s in range(core, lax.axis_siz...  2.52 us
  transfers between devices with their start and end apart: 14, of which 6 were waited for; matrix products, arithmetic and copies ran while one was open for 7% of the time, Pallas kernels for 12%

profile of v3, /device:TPU:97, one launch (start us, length us, event | category | flops | bytes accessed | tf_op | source)
XLA Modules:
  0.0 70.8 jit_solution(15985005728321215549)
XLA Ops:
  0.6 3.3 %collective-permute-start = (bf16[64,4096]{1,0:T(8,128)(2,1)}, bf16[64,4096]{1,0:T(8,128)(2,1)S(1)}, u32[]{:S(2)}, u32[]{:S(2)}) collective-permute-start(bf16[64,4096]{1,0:T(8,128)(2,1)} %bitcast.36), channel_id=1, source_target_pairs={{0,8},{8,16},{16,24},{24,32},{32,40},{40,48},{48,56},{56,64},{64,7... | collective-permute-start | bytes 1572872 | tf_op jit(solution)/shard_map/ppermute | solution.py:397
  4.0 4.2 %collective-permute-start.1 = (bf16[64,4096]{1,0:T(8,128)(2,1)}, bf16[64,4096]{1,0:T(8,128)(2,1)S(1)}, u32[]{:S(2)}, u32[]{:S(2)}) collective-permute-start(bf16[64,4096]{1,0:T(8,128)(2,1)} %bitcast.37), channel_id=1, source_target_pairs={{8,0},{16,8},{24,16},{32,24},{40,32},{48,40},{56,48},{64,56},{72,6... | collective-permute-start | bytes 1572872 | tf_op jit(solution)/shard_map/ppermute | solution.py:398
  8.2 1.1 %constant_dynamic-slice_fusion = (bf16[1,4096]{1,0:T(2,128)(2,1)S(1)}, bf16[1,4096]{1,0:T(2,128)(2,1)S(1)}, bf16[1,4096]{1,0:T(2,128)(2,1)S(1)}, bf16[1,4096]{1,0:T(2,128)(2,1)S(1)}, bf16[1,4096]{1,0:T(2,128)(2,1)S(1)}) fusion(bf16[62,4096]{1,0:T(8,128)(2,1)} %param.15, s32[]{:T(128)S(6)} %select_n.19, s32[]{:T(128)S(6)} %select_n.17, s32[]{:T(128)S(6)} %select_n.16, ...), kind=kLoop, calls=%fused_computation.24 | loop fusion | bytes 81940 | tf_op jit(solution)/shard_map/dynamic_slice | solution.py:405
  9.5 2.0 %reshape.28.mats_ref = bf16[3968,64]{1,0:T(8,128)(2,1)S(1)} reshape(bf16[62,4096]{1,0:T(8,128)(2,1)} %param.14) | data formatting | bytes 1015808 | tf_op jit(solution)/shard_map/reshape | solution.py:419
  11.5 6.9 %own_pass.1 = (f32[32,64,128]{2,1,0:T(8,128)S(1)}, bf16[256,128,128]{2,1,0:T(8,128)(2,1)S(1)}, bf16[64,2048]{1,0:T(8,128)(2,1)S(1)}, bf16[64,2048]{1,0:T(8,128)(...) custom-call(s32[1]{0:T(128)} %bitcast.anchor_ref, s32[8,32]{1,0:T(8,128)} %bitcast.40, ...), custom_call_target="tpu_custom_call" | custom-call | tf_op jit(solution)/shard_map/own_pass/pallas_call | solution.py:281
  18.8 4.9 %far_pass.1 = (f32[32,64,64]{2,1,0:T(8,128)S(1)}, bf16[2048,64]{1,0:T(8,128)(2,1)S(1)}, f32[32,128]{1,0:T(8,128)S(1)}, f32[32,64,128]{2,1,0:T(8,128)S(1)}) custom-call(s32[272]{0:T(512)S(1)} %get-tuple-element.15.task_ref, s32[1]{0:T(128)} %get-tuple-element.16.steps_ref, ...), custom_call_target="tpu_custom_call", output_to_operand_aliasing={{3}: (4, {})} | custom-call | tf_op jit(solution)/shard_map/far_pass/pallas_call | solution.py:320
  23.6 1.3 %collective-permute-start.6 = (f32[32,128]{1,0:T(8,128)S(1)}, f32[32,128]{1,0:T(8,128)S(1)}, u32[]{:S(2)}, u32[]{:S(2)}) collective-permute-start(f32[32,128]{1,0:T(8,128)S(1)} %get-tuple-element.25), channel_id=1, source_target_pairs={{0,1},{2,3},{4,5},{6,7},{8,9},{10,11},{12,13},{14,15},{16,17},{18,... | collective-permute-start | bytes 49160 | tf_op jit(solution)/shard_map/ppermute | solution.py:378
  25.0 2.5 %collective-permute-done.6 = f32[32,128]{1,0:T(8,128)S(1)} collective-permute-done((f32[32,128]{1,0:T(8,128)S(1)}, f32[32,128]{1,0:T(8,128)S(1)}, u32[]{:S(2)}, u32[]{:S(2)}) %collective-permute-start.6) | collective-permute-done | bytes 16416 | tf_op jit(solution)/shard_map/ppermute | solution.py:378
  27.5 2.7 %collective-permute-start.7 = (f32[64,128]{1,0:T(8,128)S(1)}, f32[64,128]{1,0:T(8,128)S(1)}, u32[]{:S(2)}, u32[]{:S(2)}) collective-permute-start(f32[64,128]{1,0:T(8,128)S(1)} %constant_dynamic-update-slice_fusion), channel_id=1, source_target_pairs={{1,9},{3,11},{5,13},{7,15},{9,1},{11,3},{13,5},{15,7},{17,25},{19,... | collective-permute-start | bytes 98312 | tf_op jit(solution)/shard_map/ppermute | solution.py:374
  30.2 1.9 %collective-permute-done.7 = f32[64,128]{1,0:T(8,128)S(1)} collective-permute-done((f32[64,128]{1,0:T(8,128)S(1)}, f32[64,128]{1,0:T(8,128)S(1)}, u32[]{:S(2)}, u32[]{:S(2)}) %collective-permute-start.7) | collective-permute-done | bytes 32800 | tf_op jit(solution)/shard_map/ppermute | solution.py:374
  32.4 9.0 %collective-permute-start.8 = (f32[64,128]{1,0:T(8,128)S(1)}, f32[64,128]{1,0:T(8,128)S(1)}, u32[]{:S(2)}, u32[]{:S(2)}) collective-permute-start(f32[64,128]{1,0:T(8,128)S(1)} %fusion.9), channel_id=1, source_target_pairs={{1,25},{3,27},{5,29},{7,31},{9,17},{11,19},{13,21},{15,23},{17,9},... | collective-permute-start | bytes 98312 | tf_op jit(solution)/shard_map/ppermute | solution.py:374
  42.1 1.3 %collective-permute-start.2 = (bf16[4,2,8,16,128]{4,3,2,1,0:T(8,128)(2,1)S(1)}, bf16[4,2,8,16,128]{4,3,2,1,0:T(8,128)(2,1)S(1)}, u32[]{:S(2)}, u32[]{:S(2)}) collective-permute-start(bf16[4,2,8,16,128]{4,3,2,1,0:T(8,128)(2,1)S(1)} %get-tuple-element.24), channel_id=1, source_target_pairs={{1,0},{3,2},{5,4},{7,6},{9,8},{11,10},{13,12},{15,14},{17,16},{19,... | collective-permute-start | bytes 786440 | tf_op jit(solution)/shard_map/ppermute | solution.py:378
  43.6 1.9 %collective-permute-start.9 = (f32[64,128]{1,0:T(8,128)S(1)}, f32[64,128]{1,0:T(8,128)S(1)}, u32[]{:S(2)}, u32[]{:S(2)}) collective-permute-start(f32[64,128]{1,0:T(8,128)S(1)} %fusion.7), channel_id=1, source_target_pairs={{1,33},{3,35},{5,37},{7,39},{9,41},{11,43},{13,45},{15,47},{17,49}... | collective-permute-start | bytes 98312 | tf_op jit(solution)/shard_map/ppermute | solution.py:374
  45.5 2.7 %collective-permute-done.9 = f32[64,128]{1,0:T(8,128)S(1)} collective-permute-done((f32[64,128]{1,0:T(8,128)S(1)}, f32[64,128]{1,0:T(8,128)S(1)}, u32[]{:S(2)}, u32[]{:S(2)}) %collective-permute-start.9) | collective-permute-done | bytes 32800 | tf_op jit(solution)/shard_map/ppermute | solution.py:374
  49.2 1.9 %collective-permute-start.10 = (f32[64,128]{1,0:T(8,128)S(1)}, f32[64,128]{1,0:T(8,128)S(1)}, u32[]{:S(2)}, u32[]{:S(2)}) collective-permute-start(f32[64,128]{1,0:T(8,128)S(1)} %fusion.5), channel_id=1, source_target_pairs={{1,65},{3,67},{5,69},{7,71},{9,73},{11,75},{13,77},{15,79},{17,81}... | collective-permute-start | bytes 98312 | tf_op jit(solution)/shard_map/ppermute | solution.py:374
  51.9 3.2 %collective-permute-done.10 = f32[64,128]{1,0:T(8,128)S(1)} collective-permute-done((f32[64,128]{1,0:T(8,128)S(1)}, f32[64,128]{1,0:T(8,128)S(1)}, u32[]{:S(2)}, u32[]{:S(2)}) %collective-permute-start.10) | collective-permute-done | bytes 32800 | tf_op jit(solution)/shard_map/ppermute | solution.py:374
  55.2 3.4 %collective-permute-start.11 = (f32[128,128]{1,0:T(8,128)S(1)}, f32[128,128]{1,0:T(8,128)S(1)}, u32[]{:S(2)}, u32[]{:S(2)}) collective-permute-start(f32[128,128]{1,0:T(8,128)S(1)} %pad_maximum_fusion), channel_id=1, source_target_pairs={{1,0},{3,2},{5,4},{7,6},{9,8},{11,10},{13,12},{15,14},{17,16},{19,... | collective-permute-start | bytes 196616 | tf_op jit(solution)/shard_map/ppermute | solution.py:378
  58.6 1.3 %collective-permute-start.5 = (f32[8,16,128]{2,1,0:T(8,128)S(1)}, f32[8,16,128]{2,1,0:T(8,128)S(1)}, u32[]{:S(2)}, u32[]{:S(2)}) collective-permute-start(f32[8,16,128]{2,1,0:T(8,128)S(1)} %get-tuple-element.32), channel_id=1, source_target_pairs={{0,1},{2,3},{4,5},{6,7},{8,9},{10,11},{12,13},{14,15},{16,17},{18,... | collective-permute-start | bytes 196616 | tf_op jit(solution)/shard_map/ppermute | solution.py:378
  60.1 2.2 %collective-permute-start.12 = (f32[64,128]{1,0:T(8,128)S(1)}, f32[64,128]{1,0:T(8,128)S(1)}, u32[]{:S(2)}, u32[]{:S(2)}) collective-permute-start(f32[64,128]{1,0:T(8,128)S(1)} %fusion.3), channel_id=1, source_target_pairs={{1,193},{3,195},{5,197},{7,199},{9,201},{11,203},{13,205},{15,207}... | collective-permute-start | bytes 98312 | tf_op jit(solution)/shard_map/ppermute | solution.py:374
  62.3 4.6 %collective-permute-done.12 = f32[64,128]{1,0:T(8,128)S(1)} collective-permute-done((f32[64,128]{1,0:T(8,128)S(1)}, f32[64,128]{1,0:T(8,128)S(1)}, u32[]{:S(2)}, u32[]{:S(2)}) %collective-permute-start.12) | collective-permute-done | bytes 32800 | tf_op jit(solution)/shard_map/ppermute | solution.py:374
  66.9 1.3 %collective-permute-start.13 = (f32[32,128]{1,0:T(8,128)S(1)}, f32[32,128]{1,0:T(8,128)S(1)}, u32[]{:S(2)}, u32[]{:S(2)}) collective-permute-start(f32[32,128]{1,0:T(8,128)S(1)} %slice.76), channel_id=1, source_target_pairs={{1,0},{3,2},{5,4},{7,6},{9,8},{11,10},{13,12},{15,14},{17,16},{19,... | collective-permute-start | bytes 49160 | tf_op jit(solution)/shard_map/ppermute | solution.py:378
  68.2 1.0 %copy.14 = f32[32,64,64]{2,1,0:T(8,128)} copy(f32[32,64,64]{2,1,0:T(8,128)S(1)} %get-tuple-element.34) | data formatting | bytes 1048576
  69.2 0.9 %turn.1 = f32[5,64,64]{2,1,0:T(8,128)} custom-call(s32[1]{0:T(128)} %bitcast.5.core_ref, f32[128,128]{1,0:T(8,128)S(1)} %collective-permute-done.11.lower_ref, f32[32,128]{1,0:T(8,128)S(1)} %collective-permute-done.13.last_ref, f32[64,128]{1,0:T(8,128)S(1)} %add.72.refs_0_, f32[64,128]{1,0:T(8,128)S(1)} %add.73.refs_1_, f32[64,128]{1,0:T(8,128)S(1)} %add.74.refs_2_, ...), custom_call_target="tpu_custom_call" | custom-call | tf_op jit(solution)/shard_map/turn/pallas_call | solution.py:440
  70.1 0.7 %finish.1 = f32[32,512]{1,0:T(8,128)} custom-call(s32[1]{0:T(128)} %bitcast.5.core_ref, f32[8,16,128]{2,1,0:T(8,128)S(1)} %get-tuple-element.33.total_ref, f32[8,16,128]{2,1,0:T(8,128)S(1)} %collective-permute-done.5.other_ref), custom_call_target="tpu_custom_call" | custom-call | tf_op jit(solution)/shard_map/finish/pallas_call | solution.py:454
  (39 shorter events, 3.6 us)
Async XLA Ops:
  0.6 18.1 %copy-start = (bf16[32,64,128]{2,1,0:T(8,128)(2,1)S(1)}, bf16[32,64,128]{2,1,0:T(8,128)(2,1)}, u32[]{:S(2)}) copy-start(bf16[32,64,128]{2,1,0:T(8,128)(2,1)} %basis_ref.1) | copy-start | bytes 1572868
  0.6 17.8 %collective-permute-start = (bf16[64,4096]{1,0:T(8,128)(2,1)}, bf16[64,4096]{1,0:T(8,128)(2,1)S(1)}, u32[]{:S(2)}, u32[]{:S(2)}) collective-permute-start(bf16[64,4096]{1,0:T(8,128)(2,1)} %bitcast.36), channel_id=1, source_target_pairs={{0,8},{8,16},{16,24},{24,32},{32,40},{40,48},{48,56},{56,64},{64,7... | collective-permute-start | bytes 1572872 | tf_op jit(solution)/shard_map/ppermute | solution.py:397
  4.0 14.8 %collective-permute-start.1 = (bf16[64,4096]{1,0:T(8,128)(2,1)}, bf16[64,4096]{1,0:T(8,128)(2,1)S(1)}, u32[]{:S(2)}, u32[]{:S(2)}) collective-permute-start(bf16[64,4096]{1,0:T(8,128)(2,1)} %bitcast.37), channel_id=1, source_target_pairs={{8,0},{16,8},{24,16},{32,24},{40,32},{48,40},{56,48},{64,56},{72,6... | collective-permute-start | bytes 1572872 | tf_op jit(solution)/shard_map/ppermute | solution.py:398
  23.6 3.9 %collective-permute-start.6 = (f32[32,128]{1,0:T(8,128)S(1)}, f32[32,128]{1,0:T(8,128)S(1)}, u32[]{:S(2)}, u32[]{:S(2)}) collective-permute-start(f32[32,128]{1,0:T(8,128)S(1)} %get-tuple-element.25), channel_id=1, source_target_pairs={{0,1},{2,3},{4,5},{6,7},{8,9},{10,11},{12,13},{14,15},{16,17},{18,... | collective-permute-start | bytes 49160 | tf_op jit(solution)/shard_map/ppermute | solution.py:378
  27.5 4.6 %collective-permute-start.7 = (f32[64,128]{1,0:T(8,128)S(1)}, f32[64,128]{1,0:T(8,128)S(1)}, u32[]{:S(2)}, u32[]{:S(2)}) collective-permute-start(f32[64,128]{1,0:T(8,128)S(1)} %constant_dynamic-update-slice_fusion), channel_id=1, source_target_pairs={{1,9},{3,11},{5,13},{7,15},{9,1},{11,3},{13,5},{15,7},{17,25},{19,... | collective-permute-start | bytes 98312 | tf_op jit(solution)/shard_map/ppermute | solution.py:374
  32.4 11.0 %collective-permute-start.8 = (f32[64,128]{1,0:T(8,128)S(1)}, f32[64,128]{1,0:T(8,128)S(1)}, u32[]{:S(2)}, u32[]{:S(2)}) collective-permute-start(f32[64,128]{1,0:T(8,128)S(1)} %fusion.9), channel_id=1, source_target_pairs={{1,25},{3,27},{5,29},{7,31},{9,17},{11,19},{13,21},{15,23},{17,9},... | collective-permute-start | bytes 98312 | tf_op jit(solution)/shard_map/ppermute | solution.py:374
  42.1 6.2 %collective-permute-start.2 = (bf16[4,2,8,16,128]{4,3,2,1,0:T(8,128)(2,1)S(1)}, bf16[4,2,8,16,128]{4,3,2,1,0:T(8,128)(2,1)S(1)}, u32[]{:S(2)}, u32[]{:S(2)}) collective-permute-start(bf16[4,2,8,16,128]{4,3,2,1,0:T(8,128)(2,1)S(1)} %get-tuple-element.24), channel_id=1, source_target_pairs={{1,0},{3,2},{5,4},{7,6},{9,8},{11,10},{13,12},{15,14},{17,16},{19,... | collective-permute-start | bytes 786440 | tf_op jit(solution)/shard_map/ppermute | solution.py:378
  43.6 4.7 %collective-permute-start.9 = (f32[64,128]{1,0:T(8,128)S(1)}, f32[64,128]{1,0:T(8,128)S(1)}, u32[]{:S(2)}, u32[]{:S(2)}) collective-permute-start(f32[64,128]{1,0:T(8,128)S(1)} %fusion.7), channel_id=1, source_target_pairs={{1,33},{3,35},{5,37},{7,39},{9,41},{11,43},{13,45},{15,47},{17,49}... | collective-permute-start | bytes 98312 | tf_op jit(solution)/shard_map/ppermute | solution.py:374
  48.4 2.8 %collective-permute-start.3 = (bf16[2,2,8,16,128]{4,3,2,1,0:T(8,128)(2,1)S(1)}, bf16[2,2,8,16,128]{4,3,2,1,0:T(8,128)(2,1)S(1)}, u32[]{:S(2)}, u32[]{:S(2)}) collective-permute-start(bf16[2,2,8,16,128]{4,3,2,1,0:T(8,128)(2,1)S(1)} %slice.106), channel_id=1, source_target_pairs={{0,2},{2,0},{4,6},{6,4},{8,10},{10,8},{12,14},{14,12},{16,18},{18,... | collective-permute-start | bytes 393224 | tf_op jit(solution)/shard_map/ppermute | solution.py:374
  49.2 5.9 %collective-permute-start.10 = (f32[64,128]{1,0:T(8,128)S(1)}, f32[64,128]{1,0:T(8,128)S(1)}, u32[]{:S(2)}, u32[]{:S(2)}) collective-permute-start(f32[64,128]{1,0:T(8,128)S(1)} %fusion.5), channel_id=1, source_target_pairs={{1,65},{3,67},{5,69},{7,71},{9,73},{11,75},{13,77},{15,79},{17,81}... | collective-permute-start | bytes 98312 | tf_op jit(solution)/shard_map/ppermute | solution.py:374
  51.2 7.3 %collective-permute-start.4 = (f32[2,8,16,128]{3,2,1,0:T(8,128)S(1)}, f32[2,8,16,128]{3,2,1,0:T(8,128)S(1)}, u32[]{:S(2)}, u32[]{:S(2)}) collective-permute-start(f32[2,8,16,128]{3,2,1,0:T(8,128)S(1)} %fusion), channel_id=1, source_target_pairs={{0,6},{2,4},{4,2},{6,0},{8,14},{10,12},{12,10},{14,8},{16,22},{18,... | collective-permute-start | bytes 393224 | tf_op jit(solution)/shard_map/ppermute | solution.py:374
  55.2 14.0 %collective-permute-start.11 = (f32[128,128]{1,0:T(8,128)S(1)}, f32[128,128]{1,0:T(8,128)S(1)}, u32[]{:S(2)}, u32[]{:S(2)}) collective-permute-start(f32[128,128]{1,0:T(8,128)S(1)} %pad_maximum_fusion), channel_id=1, source_target_pairs={{1,0},{3,2},{5,4},{7,6},{9,8},{11,10},{13,12},{15,14},{17,16},{19,... | collective-permute-start | bytes 196616 | tf_op jit(solution)/shard_map/ppermute | solution.py:378
  58.6 11.5 %collective-permute-start.5 = (f32[8,16,128]{2,1,0:T(8,128)S(1)}, f32[8,16,128]{2,1,0:T(8,128)S(1)}, u32[]{:S(2)}, u32[]{:S(2)}) collective-permute-start(f32[8,16,128]{2,1,0:T(8,128)S(1)} %get-tuple-element.32), channel_id=1, source_target_pairs={{0,1},{2,3},{4,5},{6,7},{8,9},{10,11},{12,13},{14,15},{16,17},{18,... | collective-permute-start | bytes 196616 | tf_op jit(solution)/shard_map/ppermute | solution.py:378
  60.1 6.8 %collective-permute-start.12 = (f32[64,128]{1,0:T(8,128)S(1)}, f32[64,128]{1,0:T(8,128)S(1)}, u32[]{:S(2)}, u32[]{:S(2)}) collective-permute-start(f32[64,128]{1,0:T(8,128)S(1)} %fusion.3), channel_id=1, source_target_pairs={{1,193},{3,195},{5,197},{7,199},{9,201},{11,203},{13,205},{15,207}... | collective-permute-start | bytes 98312 | tf_op jit(solution)/shard_map/ppermute | solution.py:374
  66.9 2.3 %collective-permute-start.13 = (f32[32,128]{1,0:T(8,128)S(1)}, f32[32,128]{1,0:T(8,128)S(1)}, u32[]{:S(2)}, u32[]{:S(2)}) collective-permute-start(f32[32,128]{1,0:T(8,128)S(1)} %slice.76), channel_id=1, source_target_pairs={{1,0},{3,2},{5,4},{7,6},{9,8},{11,10},{13,12},{15,14},{17,16},{19,... | collective-permute-start | bytes 49160 | tf_op jit(solution)/shard_map/ppermute | solution.py:378

commit v4 on v3

v4 whole, which is shorter than its diff:
```python
import functools

import jax
import jax.numpy as jnp
from jax import lax
from jax.experimental import pallas as pl
from jax.experimental.pallas import tpu as pltpu
from jax.sharding import PartitionSpec as P

NT = (((1,), (1,)), ((), ()))
NN = (((1,), (0,)), ((), ()))
PER_STEP = 8
TAIL = 2 * PER_STEP
VMEM = pl.BlockSpec(memory_space=pltpu.VMEM)
SMEM = pl.BlockSpec(memory_space=pltpu.SMEM)
ANY = pl.BlockSpec(memory_space=pl.ANY)


def dot(a, b, dims):
    return lax.dot_general(a, b, dims, preferred_element_type=jnp.float32)


def split(value):
    high = value.astype(jnp.bfloat16)
    return high, (value - high.astype(jnp.float32)).astype(jnp.bfloat16)


def resident(value):
    return pltpu.with_memory_space_constraint(value, pltpu.VMEM)


def spread(source, first, ref, size):
    for leaf in range(ref.shape[1] // size):
        source[first + leaf] = ref[:, leaf * size : (leaf + 1) * size]


def subtract_near(total, steps, task_ref, source, blocks_ref, acc_ref, slots):
    shift = total.bit_length()
    low = (1 << shift) - 1

    def body(step, carry):
        done = []
        for task in range(PER_STEP):
            one = task_ref[(step * PER_STEP + task) * 2]
            two = task_ref[(step * PER_STEP + task) * 2 + 1]
            left, right = jnp.right_shift(one, shift), jnp.right_shift(two, shift)
            fetched = jnp.concatenate(
                [source[jnp.bitwise_and(one, low)], source[jnp.bitwise_and(two, low)]], axis=1
            )
            matrix = jnp.concatenate([blocks_ref[left], blocks_ref[right]], axis=1)
            done.append((lax.div(left, slots), dot(fetched, matrix, NT)))
        for leaf, near in done:
            acc_ref[leaf] = acc_ref[leaf] - near
        return carry

    lax.fori_loop(0, steps, body, 0)


def path_products(upper_ref, mats_ref, high_ref, low_ref):
    rank = upper_ref.shape[1]
    count = high_ref.shape[1] // rank
    top = upper_ref[0].astype(jnp.float32).T
    nodes = [split(top)]
    width = 2
    offset = 2 * count - 2
    while width <= count:
        offset = offset - width
        later = []
        for parent, (high, low) in enumerate(nodes):
            first = (offset + 2 * parent) * rank
            pair = mats_ref[first : first + 2 * rank, :]
            product = dot(high, pair, NT) + dot(low, pair, NT)
            pair_high, pair_low = split(product)
            if width == count:
                high_ref[:, 2 * parent * rank : 2 * (parent + 1) * rank] = pair_high
                low_ref[:, 2 * parent * rank : 2 * (parent + 1) * rank] = pair_low
            else:
                later.append((pair_high[:, :rank], pair_low[:, :rank]))
                later.append((pair_high[:, rank:], pair_low[:, rank:]))
        nodes = later
        width = 2 * width


def own_kernel(
    anchor_ref,
    index_any,
    number_any,
    upper_ref,
    mats_ref,
    own_any,
    samples_any,
    blocks_any,
    acc_ref,
    blocks_ref,
    path_high_ref,
    path_low_ref,
    twice_ref,
    first_task_ref,
    first_steps_ref,
    second_task_ref,
    second_steps_ref,
    index_ref,
    number_ref,
    own_task,
    own_ref,
    samples_ref,
    source,
    sems,
):
    copies = [
        pltpu.make_async_copy(origin, target, sems.at[place])
        for place, (origin, target) in enumerate(
            (
                (index_any, index_ref),
                (number_any, number_ref),
                (own_any, own_ref),
                (samples_any, samples_ref),
                (blocks_any, blocks_ref),
            )
        )
    ]
    for copy in copies:
        copy.start()
    slots, count = index_ref.shape
    size = blocks_ref.shape[1]
    total = 2 * count
    shift = count.bit_length()
    path_products(upper_ref, mats_ref, path_high_ref, path_low_ref)
    for height in range(1, upper_ref.shape[0]):
        matrix = upper_ref[height].astype(jnp.float32)
        blank = jnp.zeros_like(matrix)
        rank = matrix.shape[0]
        twice_ref[height - 1, :rank] = jnp.concatenate([matrix, blank], axis=1)
        twice_ref[height - 1, rank:] = jnp.concatenate([blank, matrix], axis=1)
    copies[0].wait()
    copies[1].wait()

    lists = (own_task, first_task_ref, second_task_ref)
    odd = anchor_ref[1]

    def sort_leaf(leaf, places):
        places = list(places)
        live = number_ref[leaf]
        for slot in range(slots):
            block = jnp.left_shift(leaf * slots + slot, shift)
            at = index_ref[slot, leaf] - anchor_ref[0]
            before, after = at < count, at >= total
            alive = slot < live
            code = block + jnp.bitwise_and(at, count - 1)
            inside = jnp.logical_not(jnp.logical_or(before, after))
            chosen = (
                inside,
                jnp.where(odd == 1, after, before),
                jnp.where(odd == 1, before, after),
            )
            for which, (tasks, here) in enumerate(zip(lists, chosen)):
                tasks[places[which]] = code
                places[which] = places[which] + jnp.where(jnp.logical_and(alive, here), 1, 0)
        blank = jnp.left_shift(leaf * slots, shift) + count
        for which, tasks in enumerate(lists):
            tasks[places[which]] = blank
            places[which] = places[which] + jnp.bitwise_and(places[which], 1)
        return tuple(places)

    places = lax.fori_loop(0, count, sort_leaf, (0, 0, 0))
    for place in range(TAIL):
        for which, tasks in enumerate(lists):
            tasks[places[which] + place] = count
    steps = [lax.div(place + TAIL - 1, TAIL) for place in places]
    first_steps_ref[0] = steps[1]
    second_steps_ref[0] = steps[2]
    copies[2].wait()
    spread(source, 0, own_ref, size)
    source[count] = jnp.zeros_like(source[count])
    copies[3].wait()
    for leaf in range(count):
        acc_ref[leaf] = samples_ref[:, leaf * size : (leaf + 1) * size].astype(jnp.float32)
    copies[4].wait()
    subtract_near(count, steps[0], own_task, source, blocks_ref, acc_ref, slots)


def side_kernel(task_ref, steps_ref, side_ref, near_ref, blocks_ref, slots, acc, source):
    del near_ref
    count, _, size = acc.shape
    spread(source, 0, side_ref, size)
    source[count] = jnp.zeros_like(source[count])
    subtract_near(count, steps_ref[0], task_ref, source, blocks_ref, acc, slots)


def far_kernel(
    task_ref,
    steps_ref,
    side_ref,
    near_ref,
    blocks_ref,
    basis_ref,
    path_high_ref,
    path_low_ref,
    coeff_any,
    high_ref,
    part_ref,
    acc,
    source,
    low_ref,
    coeff_ref,
    sems,
):
    count, rank, size = basis_ref.shape
    slots = blocks_ref.shape[0] // count
    side_kernel(task_ref, steps_ref, side_ref, near_ref, blocks_ref, slots, acc, source)

    copies = []
    for step in range(count // PER_STEP):
        for leaf in range(step * PER_STEP, (step + 1) * PER_STEP):
            coeff = dot(basis_ref[leaf], acc[leaf].astype(jnp.bfloat16), NT)
            coeff_ref[leaf] = coeff
            high, low = split(coeff)
            rows = slice(leaf * rank, (leaf + 1) * rank)
            high_ref[rows, :] = high
            low_ref[rows, :] = low
        these = pl.ds(step * PER_STEP, PER_STEP)
        copies.append(
            pltpu.make_async_copy(coeff_ref.at[these], coeff_any.at[these], sems.at[step])
        )
        copies[-1].start()
    part = dot(path_high_ref[...], high_ref[...], NN)
    part += dot(path_low_ref[...], high_ref[...], NN)
    part += dot(path_high_ref[...], low_ref[...], NN)
    turned = part.T
    half = turned.shape[0] // 2
    part_ref[...] = jnp.concatenate([turned[:half], turned[half:]], axis=1)
    for copy in copies:
        copy.wait()


def gram_kernel(scale, place_ref, high_ref, keep_ref, send_ref, gram):
    parts, rows, pairs, width = keep_ref.shape
    parts = 2 * parts
    rank = width // 2
    lane = lax.broadcasted_iota(jnp.int32, (rank, width), 1)

    def pair_step(step, carry):
        for inner in range(PER_STEP):
            pair = step * PER_STEP + inner
            one = high_ref[pl.ds(pl.multiple_of(pair * rank, rank), rank), :]
            two = high_ref[pl.ds(pl.multiple_of((pair + pairs) * rank, rank), rank), :]
            stacked = jnp.concatenate([one, two], axis=0)
            product = dot(stacked, stacked, NT)
            value = jnp.where(lane < rank, product[:rank], product[rank:]) * scale
            gram[pl.ds(pair, rank, stride=pairs), :] = value
        return carry

    lax.fori_loop(0, pairs // PER_STEP, pair_step, 0)
    for relative in range(parts):
        first = jnp.bitwise_xor(place_ref[0], relative) * rows
        target = send_ref if relative % 2 else keep_ref
        for row in range(rows):
            at = pl.multiple_of((first + row) * pairs, pairs)
            target[relative // 2, row] = gram[pl.ds(at, pairs), :]


def finish_kernel(total_ref, last_ref, out_ref):
    rows, pairs, width = total_ref.shape
    half = width // 2
    lane = lax.broadcasted_iota(jnp.int32, (pairs, width), 1)
    for row in range(0, rows, 2):
        even = total_ref[row] + last_ref[row]
        odd = total_ref[row + 1] + last_ref[row + 1]
        at = slice(row * half, (row + 2) * half)
        out_ref[:pairs, at] = jnp.where(lane < half, even, pltpu.roll(odd, half, 1))
        out_ref[pairs:, at] = jnp.where(lane < half, pltpu.roll(even, half, 1), odd)


def turn_kernel(*refs):
    levels, out_ref = refs[:-1], refs[-1]
    for height, level in enumerate(levels):
        turned = level[...].T
        half = turned.shape[0] // 2
        out_ref[height] = jnp.concatenate([turned[:half], turned[half:]], axis=1)


def params(mib):
    return pltpu.CompilerParams(vmem_limit_bytes=mib * 2**20)


def own_pass(anchor, index, number, upper, mats, own, samples, blocks):
    slots, count = index.shape
    size = blocks.shape[1]
    columns = own.shape[0]
    heights, rank, _ = upper.shape
    tasks = slots * count + TAIL
    far = lambda value: pltpu.with_memory_space_constraint(value, pltpu.HBM)
    return pl.pallas_call(
        own_kernel,
        in_specs=[SMEM, ANY, ANY, VMEM, VMEM, ANY, ANY, ANY],
        out_specs=(VMEM, VMEM, VMEM, VMEM, VMEM, SMEM, SMEM, SMEM, SMEM),
        out_shape=(
            pltpu.VMEM((count, columns, size), jnp.float32),
            pltpu.VMEM(blocks.shape, blocks.dtype),
            pltpu.VMEM((rank, count * rank), jnp.bfloat16),
            pltpu.VMEM((rank, count * rank), jnp.bfloat16),
            pltpu.VMEM((heights - 1, 2 * rank, 2 * rank), jnp.float32),
            jax.ShapeDtypeStruct((tasks,), jnp.int32),
            jax.ShapeDtypeStruct((1,), jnp.int32),
            jax.ShapeDtypeStruct((tasks,), jnp.int32),
            jax.ShapeDtypeStruct((1,), jnp.int32),
        ),
        scratch_shapes=[
            pltpu.SMEM((slots, count), jnp.int32),
            pltpu.SMEM((count,), jnp.int32),
            pltpu.SMEM((tasks,), jnp.int32),
            pltpu.VMEM(own.shape, own.dtype),
            pltpu.VMEM(samples.shape, samples.dtype),
            pltpu.VMEM((count + 1, columns, size), jnp.bfloat16),
            pltpu.SemaphoreType.DMA((5,)),
        ],
        compiler_params=params(8),
        name="own_pass",
    )(
        anchor,
        far(index),
        far(number),
        resident(upper),
        resident(mats),
        far(own),
        far(samples),
        far(blocks),
    )


def side_pass(tasks, steps, side, near, blocks):
    count, columns, size = near.shape
    slots = blocks.shape[0] // count

    def kernel(task_ref, steps_ref, side_ref, near_ref, blocks_ref, acc, source):
        side_kernel(task_ref, steps_ref, side_ref, near_ref, blocks_ref, slots, acc, source)

    return pl.pallas_call(
        kernel,
        in_specs=[SMEM, SMEM] + [VMEM] * 3,
        out_specs=VMEM,
        out_shape=pltpu.VMEM((count, columns, size), jnp.float32),
        input_output_aliases={3: 0},
        scratch_shapes=[pltpu.VMEM((count + 1, columns, size), jnp.bfloat16)],
        compiler_params=params(8),
        name="side_pass",
    )(tasks, steps, resident(side), near, blocks)


def far_pass(tasks, steps, side, near, blocks, basis, path_high, path_low):
    count, rank, size = basis.shape
    columns = side.shape[0]
    return pl.pallas_call(
        far_kernel,
        in_specs=[SMEM, SMEM] + [VMEM] * 6,
        out_specs=(ANY, VMEM, VMEM, VMEM),
        out_shape=(
            pltpu.HBM((count, rank, columns), jnp.float32),
            pltpu.VMEM((count * rank, columns), jnp.bfloat16),
            pltpu.VMEM((columns // 2, 2 * rank), jnp.float32),
            pltpu.VMEM((count, columns, size), jnp.float32),
        ),
        input_output_aliases={3: 3},
        scratch_shapes=[
            pltpu.VMEM((count + 1, columns, size), jnp.bfloat16),
            pltpu.VMEM((count * rank, columns), jnp.bfloat16),
            pltpu.VMEM((count, rank, columns), jnp.float32),
            pltpu.SemaphoreType.DMA((count // PER_STEP,)),
        ],
        compiler_params=params(8),
        name="far_pass",
    )(tasks, steps, resident(side), near, blocks, resident(basis), path_high, path_low)


def gram_pass(place, high, count, parts):
    columns = high.shape[1]
    rank = high.shape[0] // count
    pairs = count // 2
    shape = (parts // 2, rank // parts, pairs, 2 * rank)
    return pl.pallas_call(
        functools.partial(gram_kernel, 1.0 / (columns * parts)),
        in_specs=[SMEM, VMEM],
        out_specs=(VMEM, VMEM),
        out_shape=(pltpu.VMEM(shape, jnp.float32), pltpu.VMEM(shape, jnp.float32)),
        scratch_shapes=[pltpu.VMEM((rank * pairs, 2 * rank), jnp.float32)],
        compiler_params=params(8),
        name="gram_pass",
    )(place, high)


def exchange(value, axis, flip):
    return lax.ppermute(value, axis, [(i, i ^ flip) for i in range(lax.axis_size(axis))])


def swap(value, axis, first):
    pairs = [(i, i + 1) for i in range(first, lax.axis_size(axis) - 1, 2)]
    return lax.ppermute(value, axis, pairs + [(j, i) for i, j in pairs])


def shards(
    samples, omega, leaf_basis, near_blocks, near_index, near_count, inner_transfer, upper_transfer
):
    count = near_count.shape[0]
    slots = near_index.shape[1]
    rank = leaf_basis.shape[1]
    size = leaf_basis.shape[2]
    groups = lax.axis_size("leaf")
    parts = lax.axis_size("samp")
    device = lax.axis_index("leaf")
    place = lax.axis_index("samp").astype(jnp.int32)

    own = omega.T
    first = swap(own, "leaf", 1)
    second = swap(own, "leaf", 0)

    heights = groups.bit_length() - 1
    rows = []
    offset, width = 0, groups
    for height in range(heights):
        rows.append(
            lax.dynamic_slice_in_dim(
                upper_transfer, offset + jnp.right_shift(device, height), 1, axis=0
            )
        )
        offset, width = offset + width, width // 2
    upper = jnp.concatenate(rows, axis=0).reshape(heights, rank, rank)

    blocks = near_blocks.reshape(count * slots, size, size)
    anchor = jnp.stack([device * count - count, jnp.bitwise_and(device, 1)]).astype(jnp.int32)
    near, blocks, path_high, path_low, twice, tasks, steps, later_tasks, later_steps = own_pass(
        anchor,
        near_index.T,
        near_count,
        upper,
        inner_transfer.reshape(-1, rank),
        own,
        samples.T,
        blocks,
    )
    near = side_pass(tasks, steps, first, near, blocks)
    coeffs, high, part, _ = far_pass(
        later_tasks, later_steps, second, near, blocks, leaf_basis, path_high, path_low
    )

    flips = (1, 3, 4, 8, 24)
    levels = []
    accum = part
    gram, middle = None, None
    for height in range(heights):
        if height:
            accum = jnp.dot(accum, twice[height - 1], precision=lax.Precision.HIGHEST)
        other = exchange(accum, "leaf", flips[height])
        if height == 0:
            keep, send = gram_pass(place.reshape(1), high, count, parts)
            got = exchange(send, "samp", 1)
        elif height == 1:
            gram = keep + got
            middle = gram[1:3].astype(jnp.bfloat16)
            other, _ = lax.optimization_barrier((other, middle))
            got = exchange(middle, "samp", 2).astype(jnp.float32)
        elif height == 2:
            near_total = gram[0] + got[0]
            far_total = gram[3] + got[1]
            other, _ = lax.optimization_barrier((other, far_total))
            got = exchange(far_total, "samp", 6)
        elif height == 3:
            leaf_gram = pl.pallas_call(
                finish_kernel,
                in_specs=[VMEM, VMEM],
                out_specs=VMEM,
                out_shape=jax.ShapeDtypeStruct((count, rank * rank // parts), jnp.float32),
                compiler_params=params(8),
                name="finish",
            )(resident(near_total), resident(got))
            other, _ = lax.optimization_barrier((other, leaf_gram))
        accum = accum + other
        levels.append(accum)
    ancestors = pl.pallas_call(
        turn_kernel,
        in_specs=[VMEM] * heights,
        out_specs=VMEM,
        out_shape=jax.ShapeDtypeStruct((heights, rank, 2 * part.shape[0]), jnp.float32),
        compiler_params=params(8),
        name="turn",
    )(*map(resident, levels))
    return coeffs, leaf_gram, ancestors[None]


def solution(mesh):
    return jax.shard_map(
        shards,
        mesh=mesh,
        in_specs=(
            P("leaf", "samp"),
            P("leaf", "samp"),
            P("leaf", None, None),
            P("leaf", None, None, None),
            P("leaf", None),
            P("leaf"),
            P("leaf", None),
            P(),
        ),
        out_specs=(P("leaf", None, "samp"), P("leaf", "samp"), P("leaf", None, None, "samp")),
        check_vma=False,
    )
```

time: 71.3 us -> 53.7 us (0.75)
  the two profiles are of different devices: /device:TPU:97 before, /device:TPU:6 now
where the time goes in v4:
time: 53.7 us; the launch traced here: 53 us
  starting transfers between devices  24.6 us (46%)
  Pallas kernels  16.3 us (30%)
  waiting for transfers between devices  7.24 us (13%)
  local copies, waits for them, and re-layouts  3.32 us (6%)
  between operations  0.79 us (1%)
  matrix products  0.62 us (1%)
    ppermute x8, starting transfers between devices, exchange(): lax.ppermute(value, axis, [(i, i ^ flip) for i in range(lax.axis_size(axi...  19.4 us
    pallas_call x1, Pallas kernels, own_pass(): pl.pallas_call(own_kernel, in_specs=[SMEM, ANY, ANY, VMEM, VMEM, ANY, ANY...  8.31 us
    ppermute x8, waiting for transfers between devices, exchange(): lax.ppermute(value, axis, [(i, i ^ flip) for i in range(lax.axis_size(axi...  7.23 us
    ppermute x2, starting transfers between devices, swap(): return lax.ppermute(value, axis, pairs + [(j, i) for i, j in pairs])  5.15 us
    pallas_call x1, Pallas kernels, far_pass(): pl.pallas_call(far_kernel, in_specs=[SMEM, SMEM] + [VMEM] * 6, out_specs=...  4.38 us
    reshape x1, local copies, waits for them, and re-layouts, shards(): inner_transfer.reshape(-1, rank)  2.03 us
    pallas_call x1, Pallas kernels, side_pass(): pl.pallas_call(kernel, in_specs=[SMEM, SMEM] + [VMEM] * 3, out_specs=VMEM...  1.3 us
  transfers between devices with their start and end apart: 10, of which 6 were waited for; matrix products, arithmetic and copies ran while one was open for 7% of the time, Pallas kernels for 19%

profile of v4, /device:TPU:6, one launch (start us, length us, event | category | flops | bytes accessed | tf_op | source)
XLA Modules:
  0.0 53.0 jit_solution(16581599745165348853)
XLA Ops:
  0.6 0.7 %collective-permute-start.1 = (bf16[64,4096]{1,0:T(8,128)(2,1)}, bf16[64,4096]{1,0:T(8,128)(2,1)S(1)}, u32[]{:S(2)}, u32[]{:S(2)}) collective-permute-start(bf16[64,4096]{1,0:T(8,128)(2,1)} %bitcast.30), channel_id=1, source_target_pairs={{8,16},{24,32},{40,48},{56,64},{72,80},{88,96},{104,112},{120,128}... | collective-permute-start | bytes 1572872 | tf_op jit(solution)/shard_map/ppermute | solution.py:397
  1.3 4.5 %collective-permute-start = (bf16[64,4096]{1,0:T(8,128)(2,1)}, bf16[64,4096]{1,0:T(8,128)(2,1)S(1)}, u32[]{:S(2)}, u32[]{:S(2)}) collective-permute-start(bf16[64,4096]{1,0:T(8,128)(2,1)} %bitcast.31), channel_id=1, source_target_pairs={{0,8},{16,24},{32,40},{48,56},{64,72},{80,88},{96,104},{112,120},{... | collective-permute-start | bytes 1572872 | tf_op jit(solution)/shard_map/ppermute | solution.py:397
  5.8 1.1 %constant_dynamic-slice_fusion = (bf16[1,4096]{1,0:T(2,128)(2,1)S(1)}, bf16[1,4096]{1,0:T(2,128)(2,1)S(1)}, bf16[1,4096]{1,0:T(2,128)(2,1)S(1)}, bf16[1,4096]{1,0:T(2,128)(2,1)S(1)}, bf16[1,4096]{1,0:T(2,128)(2,1)S(1)}) fusion(bf16[62,4096]{1,0:T(8,128)(2,1)} %param.15, s32[]{:T(128)S(6)} %select_n.19, s32[]{:T(128)S(6)} %select_n.17, s32[]{:T(128)S(6)} %select_n.16, ...), kind=kLoop, calls=%fused_computation.17 | loop fusion | bytes 81940 | tf_op jit(solution)/shard_map/dynamic_slice | solution.py:421
  7.1 2.0 %reshape.21.mats_ref = bf16[3968,64]{1,0:T(8,128)(2,1)S(1)} reshape(bf16[62,4096]{1,0:T(8,128)(2,1)} %param.14) | data formatting | bytes 1015808 | tf_op jit(solution)/shard_map/reshape | solution.py:435
  9.2 8.3 %own_pass.1 = (f32[32,64,128]{2,1,0:T(8,128)S(1)}, bf16[256,128,128]{2,1,0:T(8,128)(2,1)S(1)}, bf16[64,2048]{1,0:T(8,128)(2,1)S(1)}, bf16[64,2048]{1,0:T(8,128)(...) custom-call(s32[2]{0:T(128)S(1)} %pad_add_fusion.anchor_ref, ...), custom_call_target="tpu_custom_call" | custom-call | tf_op jit(solution)/shard_map/own_pass/pallas_call | solution.py:293
  17.5 1.3 %side_pass.1.near_ref = f32[32,64,128]{2,1,0:T(8,128)S(1)} custom-call(s32[272]{0:T(512)S(1)} %get-tuple-element.22.task_ref, s32[1]{0:T(128)} %get-tuple-element.23.steps_ref, bf16[64,4096]{1,0:T(8,128)(2,1)S(1)} %collective-permute-done.1.side_ref, f32[32,64,128]{2,1,0:T(8,128)S(1)} %get-tuple-element.24.near_ref, ...), custom_call_target="tpu_custom_call", output_to_operand_aliasing={{}: (3, {})} | custom-call | tf_op jit(solution)/shard_map/side_pass/pallas_call | solution.py:338
  18.8 4.4 %far_pass.1 = (f32[32,64,64]{2,1,0:T(8,128)}, bf16[2048,64]{1,0:T(8,128)(2,1)S(1)}, f32[32,128]{1,0:T(8,128)S(1)}, f32[32,64,128]{2,1,0:T(8,128)S(1)}) custom-call(s32[272]{0:T(512)S(1)} %get-tuple-element.20.task_ref, s32[1]{0:T(128)} %get-tuple-element.21.steps_ref, ...), custom_call_target="tpu_custom_call", output_to_operand_aliasing={{3}: (3, {})} | custom-call | tf_op jit(solution)/shard_map/far_pass/pallas_call | solution.py:353
  23.2 0.7 %gram_pass.1 = (f32[4,8,16,128]{3,2,1,0:T(8,128)S(1)}, f32[4,8,16,128]{3,2,1,0:T(8,128)S(1)}) custom-call(s32[1]{0:T(128)} %bitcast.6.place_ref, bf16[2048,64]{1,0:T(8,128)(2,1)S(1)} %get-tuple-element.29.high_ref), custom_call_target="tpu_custom_call" | custom-call | tf_op jit(solution)/shard_map/gram_pass/pallas_call | solution.py:380
  24.0 1.2 %collective-permute-start.5 = (f32[32,128]{1,0:T(8,128)S(1)}, f32[32,128]{1,0:T(8,128)S(1)}, u32[]{:S(2)}, u32[]{:S(2)}) collective-permute-start(f32[32,128]{1,0:T(8,128)S(1)} %get-tuple-element.32), channel_id=1, source_target_pairs={{0,8},{8,0},{16,24},{24,16},{32,40},{40,32},{48,56},{56,48},{64,72... | collective-permute-start | bytes 49160 | tf_op jit(solution)/shard_map/ppermute | solution.py:392
  25.2 2.7 %collective-permute-done.5 = f32[32,128]{1,0:T(8,128)S(1)} collective-permute-done((f32[32,128]{1,0:T(8,128)S(1)}, f32[32,128]{1,0:T(8,128)S(1)}, u32[]{:S(2)}, u32[]{:S(2)}) %collective-permute-start.5) | collective-permute-done | bytes 16416 | tf_op jit(solution)/shard_map/ppermute | solution.py:392
  28.0 4.7 %collective-permute-start.6 = (f32[32,128]{1,0:T(8,128)S(1)}, f32[32,128]{1,0:T(8,128)S(1)}, u32[]{:S(2)}, u32[]{:S(2)}) collective-permute-start(f32[32,128]{1,0:T(8,128)S(1)} %fusion.8), channel_id=1, source_target_pairs={{0,24},{8,16},{16,8},{24,0},{32,56},{40,48},{48,40},{56,32},{64,88... | collective-permute-start | bytes 49160 | tf_op jit(solution)/shard_map/ppermute | solution.py:392
  32.8 0.9 %collective-permute-start.3 = (bf16[2,8,16,128]{3,2,1,0:T(8,128)(2,1)S(1)}, bf16[2,8,16,128]{3,2,1,0:T(8,128)(2,1)S(1)}, u32[]{:S(2)}, u32[]{:S(2)}) collective-permute-start(bf16[2,8,16,128]{3,2,1,0:T(8,128)(2,1)S(1)} %slice.67), channel_id=1, source_target_pairs={{0,2},{1,3},{2,0},{3,1},{4,6},{5,7},{6,4},{7,5},{8,10},{9,11},{10,... | collective-permute-start | bytes 196616 | tf_op jit(solution)/shard_map/ppermute | solution.py:392
  33.7 0.7 %collective-permute-done.6 = f32[32,128]{1,0:T(8,128)S(1)} collective-permute-done((f32[32,128]{1,0:T(8,128)S(1)}, f32[32,128]{1,0:T(8,128)S(1)}, u32[]{:S(2)}, u32[]{:S(2)}) %collective-permute-start.6) | collective-permute-done | bytes 16416 | tf_op jit(solution)/shard_map/ppermute | solution.py:392
  34.6 2.2 %collective-permute-start.7 = (f32[32,128]{1,0:T(8,128)S(1)}, f32[32,128]{1,0:T(8,128)S(1)}, u32[]{:S(2)}, u32[]{:S(2)}) collective-permute-start(f32[32,128]{1,0:T(8,128)S(1)} %fusion.6), channel_id=1, source_target_pairs={{0,32},{8,40},{16,48},{24,56},{32,0},{40,8},{48,16},{56,24},{64,96... | collective-permute-start | bytes 49160 | tf_op jit(solution)/shard_map/ppermute | solution.py:392
  36.8 0.3 collective-permute-done.3
  37.2 0.6 %collective-permute-start.4 = (f32[8,16,128]{2,1,0:T(8,128)S(1)}, f32[8,16,128]{2,1,0:T(8,128)S(1)}, u32[]{:S(2)}, u32[]{:S(2)}) collective-permute-start(f32[8,16,128]{2,1,0:T(8,128)S(1)} %get-tuple-element.42), channel_id=1, source_target_pairs={{0,6},{1,7},{2,4},{3,5},{4,2},{5,3},{6,0},{7,1},{8,14},{9,15},{10,... | collective-permute-start | bytes 196616 | tf_op jit(solution)/shard_map/ppermute | solution.py:392
  37.8 0.8 %collective-permute-done.7 = f32[32,128]{1,0:T(8,128)S(1)} collective-permute-done((f32[32,128]{1,0:T(8,128)S(1)}, f32[32,128]{1,0:T(8,128)S(1)}, u32[]{:S(2)}, u32[]{:S(2)}) %collective-permute-start.7) | collective-permute-done | bytes 16416 | tf_op jit(solution)/shard_map/ppermute | solution.py:392
  38.7 4.4 %collective-permute-start.8 = (f32[32,128]{1,0:T(8,128)S(1)}, f32[32,128]{1,0:T(8,128)S(1)}, u32[]{:S(2)}, u32[]{:S(2)}) collective-permute-start(f32[32,128]{1,0:T(8,128)S(1)} %fusion.4), channel_id=1, source_target_pairs={{0,64},{8,72},{16,80},{24,88},{32,96},{40,104},{48,112},{56,120},{... | collective-permute-start | bytes 49160 | tf_op jit(solution)/shard_map/ppermute | solution.py:392
  43.1 0.7 %finish.1 = f32[32,512]{1,0:T(8,128)} custom-call(f32[8,16,128]{2,1,0:T(8,128)S(1)} %get-tuple-element.43.total_ref, f32[8,16,128]{2,1,0:T(8,128)S(1)} %collective-permute-done.4.last_ref), custom_call_target="tpu_custom_call" | custom-call | tf_op jit(solution)/shard_map/finish/pallas_call | solution.py:467
  43.8 1.0 %collective-permute-done.8 = f32[32,128]{1,0:T(8,128)S(1)} collective-permute-done((f32[32,128]{1,0:T(8,128)S(1)}, f32[32,128]{1,0:T(8,128)S(1)}, u32[]{:S(2)}, u32[]{:S(2)}) %collective-permute-start.8) | collective-permute-done | bytes 16416 | tf_op jit(solution)/shard_map/ppermute | solution.py:392
  44.8 0.2 fusion.2
  45.0 5.4 %collective-permute-start.9 = (f32[32,128]{1,0:T(8,128)S(1)}, f32[32,128]{1,0:T(8,128)S(1)}, u32[]{:S(2)}, u32[]{:S(2)}) collective-permute-start(f32[32,128]{1,0:T(8,128)S(1)} %fusion.2), channel_id=1, source_target_pairs={{0,192},{8,200},{16,208},{24,216},{32,224},{40,232},{48,240},{56,2... | collective-permute-start | bytes 49160 | tf_op jit(solution)/shard_map/ppermute | solution.py:392
  50.4 1.7 %collective-permute-done.9 = f32[32,128]{1,0:T(8,128)S(1)} collective-permute-done((f32[32,128]{1,0:T(8,128)S(1)}, f32[32,128]{1,0:T(8,128)S(1)}, u32[]{:S(2)}, u32[]{:S(2)}) %collective-permute-start.9) | collective-permute-done | bytes 16416 | tf_op jit(solution)/shard_map/ppermute | solution.py:392
  52.1 0.9 %turn.1 = f32[5,64,64]{2,1,0:T(8,128)} custom-call(f32[32,128]{1,0:T(8,128)S(1)} %add.67.refs_0_, f32[32,128]{1,0:T(8,128)S(1)} %add.68.refs_1_, f32[32,128]{1,0:T(8,128)S(1)} %add.69.refs_2_, f32[32,128]{1,0:T(8,128)S(1)} %add.70.refs_3_, f32[32,128]{1,0:T(8,128)S(1)} %add.71.refs_4_), custom_call_target="tpu_custom_call" | custom-call | tf_op jit(solution)/shard_map/turn/pallas_call | solution.py:478
  (22 shorter events, 1.0 us)
Async XLA Ops:
  0.6 16.9 %collective-permute-start.1 = (bf16[64,4096]{1,0:T(8,128)(2,1)}, bf16[64,4096]{1,0:T(8,128)(2,1)S(1)}, u32[]{:S(2)}, u32[]{:S(2)}) collective-permute-start(bf16[64,4096]{1,0:T(8,128)(2,1)} %bitcast.30), channel_id=1, source_target_pairs={{8,16},{24,32},{40,48},{56,64},{72,80},{88,96},{104,112},{120,128}... | collective-permute-start | bytes 1572872 | tf_op jit(solution)/shard_map/ppermute | solution.py:397
  1.3 17.5 %collective-permute-start = (bf16[64,4096]{1,0:T(8,128)(2,1)}, bf16[64,4096]{1,0:T(8,128)(2,1)S(1)}, u32[]{:S(2)}, u32[]{:S(2)}) collective-permute-start(bf16[64,4096]{1,0:T(8,128)(2,1)} %bitcast.31), channel_id=1, source_target_pairs={{0,8},{16,24},{32,40},{48,56},{64,72},{80,88},{96,104},{112,120},{... | collective-permute-start | bytes 1572872 | tf_op jit(solution)/shard_map/ppermute | solution.py:397
  9.2 9.6 %copy-start = (bf16[32,64,128]{2,1,0:T(8,128)(2,1)S(1)}, bf16[32,64,128]{2,1,0:T(8,128)(2,1)}, u32[]{:S(2)}) copy-start(bf16[32,64,128]{2,1,0:T(8,128)(2,1)} %basis_ref.1) | copy-start | bytes 1572868
  23.9 8.8 %collective-permute-start.2 = (f32[4,8,16,128]{3,2,1,0:T(8,128)S(1)}, f32[4,8,16,128]{3,2,1,0:T(8,128)S(1)}, u32[]{:S(2)}, u32[]{:S(2)}) collective-permute-start(f32[4,8,16,128]{3,2,1,0:T(8,128)S(1)} %get-tuple-element.31), channel_id=1, source_target_pairs={{0,1},{1,0},{2,3},{3,2},{4,5},{5,4},{6,7},{7,6},{8,9},{9,8},{10,11... | collective-permute-start | bytes 786440 | tf_op jit(solution)/shard_map/ppermute | solution.py:392
  24.0 3.8 %collective-permute-start.5 = (f32[32,128]{1,0:T(8,128)S(1)}, f32[32,128]{1,0:T(8,128)S(1)}, u32[]{:S(2)}, u32[]{:S(2)}) collective-permute-start(f32[32,128]{1,0:T(8,128)S(1)} %get-tuple-element.32), channel_id=1, source_target_pairs={{0,8},{8,0},{16,24},{24,16},{32,40},{40,32},{48,56},{56,48},{64,72... | collective-permute-start | bytes 49160 | tf_op jit(solution)/shard_map/ppermute | solution.py:392
  28.0 6.4 %collective-permute-start.6 = (f32[32,128]{1,0:T(8,128)S(1)}, f32[32,128]{1,0:T(8,128)S(1)}, u32[]{:S(2)}, u32[]{:S(2)}) collective-permute-start(f32[32,128]{1,0:T(8,128)S(1)} %fusion.8), channel_id=1, source_target_pairs={{0,24},{8,16},{16,8},{24,0},{32,56},{40,48},{48,40},{56,32},{64,88... | collective-permute-start | bytes 49160 | tf_op jit(solution)/shard_map/ppermute | solution.py:392
  32.8 4.4 %collective-permute-start.3 = (bf16[2,8,16,128]{3,2,1,0:T(8,128)(2,1)S(1)}, bf16[2,8,16,128]{3,2,1,0:T(8,128)(2,1)S(1)}, u32[]{:S(2)}, u32[]{:S(2)}) collective-permute-start(bf16[2,8,16,128]{3,2,1,0:T(8,128)(2,1)S(1)} %slice.67), channel_id=1, source_target_pairs={{0,2},{1,3},{2,0},{3,1},{4,6},{5,7},{6,4},{7,5},{8,10},{9,11},{10,... | collective-permute-start | bytes 196616 | tf_op jit(solution)/shard_map/ppermute | solution.py:392
  34.6 3.9 %collective-permute-start.7 = (f32[32,128]{1,0:T(8,128)S(1)}, f32[32,128]{1,0:T(8,128)S(1)}, u32[]{:S(2)}, u32[]{:S(2)}) collective-permute-start(f32[32,128]{1,0:T(8,128)S(1)} %fusion.6), channel_id=1, source_target_pairs={{0,32},{8,40},{16,48},{24,56},{32,0},{40,8},{48,16},{56,24},{64,96... | collective-permute-start | bytes 49160 | tf_op jit(solution)/shard_map/ppermute | solution.py:392
  37.2 5.9 %collective-permute-start.4 = (f32[8,16,128]{2,1,0:T(8,128)S(1)}, f32[8,16,128]{2,1,0:T(8,128)S(1)}, u32[]{:S(2)}, u32[]{:S(2)}) collective-permute-start(f32[8,16,128]{2,1,0:T(8,128)S(1)} %get-tuple-element.42), channel_id=1, source_target_pairs={{0,6},{1,7},{2,4},{3,5},{4,2},{5,3},{6,0},{7,1},{8,14},{9,15},{10,... | collective-permute-start | bytes 196616 | tf_op jit(solution)/shard_map/ppermute | solution.py:392
  38.7 6.1 %collective-permute-start.8 = (f32[32,128]{1,0:T(8,128)S(1)}, f32[32,128]{1,0:T(8,128)S(1)}, u32[]{:S(2)}, u32[]{:S(2)}) collective-permute-start(f32[32,128]{1,0:T(8,128)S(1)} %fusion.4), channel_id=1, source_target_pairs={{0,64},{8,72},{16,80},{24,88},{32,96},{40,104},{48,112},{56,120},{... | collective-permute-start | bytes 49160 | tf_op jit(solution)/shard_map/ppermute | solution.py:392
  45.0 7.1 %collective-permute-start.9 = (f32[32,128]{1,0:T(8,128)S(1)}, f32[32,128]{1,0:T(8,128)S(1)}, u32[]{:S(2)}, u32[]{:S(2)}) collective-permute-start(f32[32,128]{1,0:T(8,128)S(1)} %fusion.2), channel_id=1, source_target_pairs={{0,192},{8,200},{16,208},{24,216},{32,224},{40,232},{48,240},{56,2... | collective-permute-start | bytes 49160 | tf_op jit(solution)/shard_map/ppermute | solution.py:392

commit v5 on v4

--- a/solution.py
+++ b/solution.py
@@ -10,7 +10,10 @@
 NT = (((1,), (1,)), ((), ()))
 NN = (((1,), (0,)), ((), ()))
 PER_STEP = 8
-TAIL = 2 * PER_STEP
+PER_TASKS = 2 * PER_STEP
+LANES = 128
+TASK_ROWS = 8
+LIST_ROWS = 3
 VMEM = pl.BlockSpec(memory_space=pltpu.VMEM)
 SMEM = pl.BlockSpec(memory_space=pltpu.SMEM)
 ANY = pl.BlockSpec(memory_space=pl.ANY)
@@ -34,15 +37,18 @@
         source[first + leaf] = ref[:, leaf * size : (leaf + 1) * size]
 
 
-def subtract_near(total, steps, task_ref, source, blocks_ref, acc_ref, slots):
-    shift = total.bit_length()
+def subtract_near(count, task_ref, source, blocks_ref, acc_ref, slots):
+    shift = count.bit_length()
     low = (1 << shift) - 1
+    per_row = LANES // PER_TASKS
 
     def body(step, carry):
         done = []
+        row = lax.div(step, per_row)
+        at = lax.rem(step, per_row) * PER_TASKS
         for task in range(PER_STEP):
-            one = task_ref[(step * PER_STEP + task) * 2]
-            two = task_ref[(step * PER_STEP + task) * 2 + 1]
+            one = task_ref[row, at + 2 * task]
+            two = task_ref[row, at + 2 * task + 1]
             left, right = jnp.right_shift(one, shift), jnp.right_shift(two, shift)
             fetched = jnp.concatenate(
                 [source[jnp.bitwise_and(one, low)], source[jnp.bitwise_and(two, low)]], axis=1
@@ -53,7 +59,55 @@
             acc_ref[leaf] = acc_ref[leaf] - near
         return carry
 
-    lax.fori_loop(0, steps, body, 0)
+    lax.fori_loop(0, task_ref[LIST_ROWS - 1, LANES - 1], body, 0)
+
+
+def list_tasks(index, number, device, lists_ref):
+    slots, count = index.shape
+    shift = count.bit_length()
+    slot = lax.broadcasted_iota(jnp.int32, (slots, count), 0)
+    leaf = lax.broadcasted_iota(jnp.int32, (slots, count), 1)
+    at = index - (device * count - count)
+    alive = slot < number
+    before, after = at < count, at >= 2 * count
+    even = jnp.broadcast_to(jnp.bitwise_and(device, 1), at.shape) == 0
+    side = jnp.where(before == even, 1, 2)
+    kind = jnp.where(jnp.logical_or(before, after), side, 0)
+    code = jnp.left_shift(leaf * slots + slot, shift) + jnp.bitwise_and(at, count - 1)
+    blank = count
+    earlier_slot = (
+        lax.broadcasted_iota(jnp.int32, (slots, slots), 1)
+        < lax.broadcasted_iota(jnp.int32, (slots, slots), 0)
+    ).astype(jnp.bfloat16)
+    earlier_leaf = (
+        lax.broadcasted_iota(jnp.int32, (count, count), 0)
+        < lax.broadcasted_iota(jnp.int32, (count, count), 1)
+    ).astype(jnp.bfloat16)
+    place = jnp.full((slots, count), -1, jnp.int32)
+    steps = []
+    for which in range(3):
+        chosen = jnp.logical_and(alive, kind == which)
+        mark = jnp.where(chosen, 1.0, 0.0)
+        rank = dot(earlier_slot, mark.astype(jnp.bfloat16), NN)
+        number_here = jnp.sum(mark, axis=0, keepdims=True).astype(jnp.int32)
+        padded = (number_here + jnp.bitwise_and(number_here, 1)).astype(jnp.float32)
+        base = dot(jnp.broadcast_to(padded, (slots, count)).astype(jnp.bfloat16), earlier_leaf, NN)
+        here = (base + rank).astype(jnp.int32) + which * LIST_ROWS * LANES
+        place = jnp.where(chosen, here, place)
+        total = jnp.sum(padded, axis=1, keepdims=True).astype(jnp.int32)
+        steps.append(jnp.right_shift(total + PER_TASKS - 1, PER_TASKS.bit_length() - 1))
+    place, value = place.T, code.T - blank
+    lane = lax.broadcasted_iota(jnp.int32, (count, LANES), 1)
+    for which in range(3):
+        for row in range(LIST_ROWS):
+            target = lane + (which * LIST_ROWS + row) * LANES
+            total = jnp.zeros((count, LANES), jnp.int32)
+            for k in range(slots):
+                total += jnp.where(place[:, k : k + 1] == target, value[:, k : k + 1], 0)
+            line = jnp.sum(total, axis=0, keepdims=True) + blank
+            if row == LIST_ROWS - 1:
+                line = jnp.where(lane[:1] == LANES - 1, steps[which], line)
+            lists_ref[which, row : row + 1] = line
 
 
 def path_products(upper_ref, mats_ref, high_ref, low_ref):
@@ -82,7 +136,6 @@
 
 
 def own_kernel(
-    anchor_ref,
     index_any,
     number_any,
     upper_ref,
@@ -96,100 +149,67 @@
     path_low_ref,
     twice_ref,
     first_task_ref,
-    first_steps_ref,
     second_task_ref,
-    second_steps_ref,
+    own_task,
+    lists,
     index_ref,
     number_ref,
-    own_task,
     own_ref,
     samples_ref,
     source,
     sems,
 ):
+    pairs = (
+        (index_any, index_ref),
+        (number_any, number_ref),
+        (own_any, own_ref),
+        (samples_any, samples_ref),
+        (blocks_any, blocks_ref),
+        (lists.at[0], own_task),
+        (lists.at[1], first_task_ref),
+        (lists.at[2], second_task_ref),
+    )
     copies = [
         pltpu.make_async_copy(origin, target, sems.at[place])
-        for place, (origin, target) in enumerate(
-            (
-                (index_any, index_ref),
-                (number_any, number_ref),
-                (own_any, own_ref),
-                (samples_any, samples_ref),
-                (blocks_any, blocks_ref),
-            )
-        )
+        for place, (origin, target) in enumerate(pairs)
     ]
-    for copy in copies:
+    for copy in copies[:5]:
         copy.start()
     slots, count = index_ref.shape
     size = blocks_ref.shape[1]
-    total = 2 * count
-    shift = count.bit_length()
+    rank = upper_ref.shape[1]
+    copies[0].wait()
+    copies[1].wait()
+    list_tasks(index_ref[...], number_ref[...], lax.axis_index("leaf"), lists)
+    for copy in copies[5:]:
+        copy.start()
     path_products(upper_ref, mats_ref, path_high_ref, path_low_ref)
     for height in range(1, upper_ref.shape[0]):
         matrix = upper_ref[height].astype(jnp.float32)
         blank = jnp.zeros_like(matrix)
-        rank = matrix.shape[0]
         twice_ref[height - 1, :rank] = jnp.concatenate([matrix, blank], axis=1)
         twice_ref[height - 1, rank:] = jnp.concatenate([blank, matrix], axis=1)
-    copies[0].wait()
-    copies[1].wait()
-
-    lists = (own_task, first_task_ref, second_task_ref)
-    odd = anchor_ref[1]
-
-    def sort_leaf(leaf, places):
-        places = list(places)
-        live = number_ref[leaf]
-        for slot in range(slots):
-            block = jnp.left_shift(leaf * slots + slot, shift)
-            at = index_ref[slot, leaf] - anchor_ref[0]
-            before, after = at < count, at >= total
-            alive = slot < live
-            code = block + jnp.bitwise_and(at, count - 1)
-            inside = jnp.logical_not(jnp.logical_or(before, after))
-            chosen = (
-                inside,
-                jnp.where(odd == 1, after, before),
-                jnp.where(odd == 1, before, after),
-            )
-            for which, (tasks, here) in enumerate(zip(lists, chosen)):
-                tasks[places[which]] = code
-                places[which] = places[which] + jnp.where(jnp.logical_and(alive, here), 1, 0)
-        blank = jnp.left_shift(leaf * slots, shift) + count
-        for which, tasks in enumerate(lists):
-            tasks[places[which]] = blank
-            places[which] = places[which] + jnp.bitwise_and(places[which], 1)
-        return tuple(places)
-
-    places = lax.fori_loop(0, count, sort_leaf, (0, 0, 0))
-    for place in range(TAIL):
-        for which, tasks in enumerate(lists):
-            tasks[places[which] + place] = count
-    steps = [lax.div(place + TAIL - 1, TAIL) for place in places]
-    first_steps_ref[0] = steps[1]
-    second_steps_ref[0] = steps[2]
     copies[2].wait()
     spread(source, 0, own_ref, size)
     source[count] = jnp.zeros_like(source[count])
     copies[3].wait()
     for leaf in range(count):
         acc_ref[leaf] = samples_ref[:, leaf * size : (leaf + 1) * size].astype(jnp.float32)
-    copies[4].wait()
-    subtract_near(count, steps[0], own_task, source, blocks_ref, acc_ref, slots)
-
-
-def side_kernel(task_ref, steps_ref, side_ref, near_ref, blocks_ref, slots, acc, source):
+    for copy in copies[4:]:
+        copy.wait()
+    subtract_near(count, own_task, source, blocks_ref, acc_ref, slots)
+
+
+def side_kernel(task_ref, side_ref, near_ref, blocks_ref, slots, acc, source):
     del near_ref
     count, _, size = acc.shape
     spread(source, 0, side_ref, size)
     source[count] = jnp.zeros_like(source[count])
-    subtract_near(count, steps_ref[0], task_ref, source, blocks_ref, acc, slots)
+    subtract_near(count, task_ref, source, blocks_ref, acc, slots)
 
 
 def far_kernel(
     task_ref,
-    steps_ref,
     side_ref,
     near_ref,
     blocks_ref,
@@ -207,7 +227,7 @@
 ):
     count, rank, size = basis_ref.shape
     slots = blocks_ref.shape[0] // count
-    side_kernel(task_ref, steps_ref, side_ref, near_ref, blocks_ref, slots, acc, source)
+    side_kernel(task_ref, side_ref, near_ref, blocks_ref, slots, acc, source)
 
     copies = []
     for step in range(count // PER_STEP):
@@ -283,41 +303,39 @@
     return pltpu.CompilerParams(vmem_limit_bytes=mib * 2**20)
 
 
-def own_pass(anchor, index, number, upper, mats, own, samples, blocks):
+def own_pass(index, number, upper, mats, own, samples, blocks):
     slots, count = index.shape
     size = blocks.shape[1]
     columns = own.shape[0]
     heights, rank, _ = upper.shape
-    tasks = slots * count + TAIL
+    tasks = pltpu.SMEM((TASK_ROWS, LANES), jnp.int32)
     far = lambda value: pltpu.with_memory_space_constraint(value, pltpu.HBM)
     return pl.pallas_call(
         own_kernel,
-        in_specs=[SMEM, ANY, ANY, VMEM, VMEM, ANY, ANY, ANY],
-        out_specs=(VMEM, VMEM, VMEM, VMEM, VMEM, SMEM, SMEM, SMEM, SMEM),
+        in_specs=[ANY, ANY, VMEM, VMEM, ANY, ANY, ANY],
+        out_specs=(VMEM, VMEM, VMEM, VMEM, VMEM, SMEM, SMEM),
         out_shape=(
             pltpu.VMEM((count, columns, size), jnp.float32),
             pltpu.VMEM(blocks.shape, blocks.dtype),
             pltpu.VMEM((rank, count * rank), jnp.bfloat16),
             pltpu.VMEM((rank, count * rank), jnp.bfloat16),
             pltpu.VMEM((heights - 1, 2 * rank, 2 * rank), jnp.float32),
-            jax.ShapeDtypeStruct((tasks,), jnp.int32),
-            jax.ShapeDtypeStruct((1,), jnp.int32),
-            jax.ShapeDtypeStruct((tasks,), jnp.int32),
-            jax.ShapeDtypeStruct((1,), jnp.int32),
+            tasks,
+            tasks,
         ),
         scratch_shapes=[
-            pltpu.SMEM((slots, count), jnp.int32),
-            pltpu.SMEM((count,), jnp.int32),
-            pltpu.SMEM((tasks,), jnp.int32),
+            tasks,
+            pltpu.VMEM((3, TASK_ROWS, LANES), jnp.int32),
+            pltpu.VMEM((slots, count), jnp.int32),
+            pltpu.VMEM((1, count), jnp.int32),
             pltpu.VMEM(own.shape, own.dtype),
             pltpu.VMEM(samples.shape, samples.dtype),
             pltpu.VMEM((count + 1, columns, size), jnp.bfloat16),
-            pltpu.SemaphoreType.DMA((5,)),
+            pltpu.SemaphoreType.DMA((8,)),
         ],
         compiler_params=params(8),
         name="own_pass",
     )(
-        anchor,
         far(index),
         far(number),
         resident(upper),
@@ -328,31 +346,31 @@
     )
 
 
-def side_pass(tasks, steps, side, near, blocks):
+def side_pass(tasks, side, near, blocks):
     count, columns, size = near.shape
     slots = blocks.shape[0] // count
 
-    def kernel(task_ref, steps_ref, side_ref, near_ref, blocks_ref, acc, source):
-        side_kernel(task_ref, steps_ref, side_ref, near_ref, blocks_ref, slots, acc, source)
+    def kernel(task_ref, side_ref, near_ref, blocks_ref, acc, source):
+        side_kernel(task_ref, side_ref, near_ref, blocks_ref, slots, acc, source)
 
     return pl.pallas_call(
         kernel,
-        in_specs=[SMEM, SMEM] + [VMEM] * 3,
+        in_specs=[SMEM] + [VMEM] * 3,
         out_specs=VMEM,
         out_shape=pltpu.VMEM((count, columns, size), jnp.float32),
-        input_output_aliases={3: 0},
+        input_output_aliases={2: 0},
         scratch_shapes=[pltpu.VMEM((count + 1, columns, size), jnp.bfloat16)],
         compiler_params=params(8),
         name="side_pass",
-    )(tasks, steps, resident(side), near, blocks)
-
-
-def far_pass(tasks, steps, side, near, blocks, basis, path_high, path_low):
+    )(tasks, resident(side), near, blocks)
+
+
+def far_pass(tasks, side, near, blocks, basis, path_high, path_low):
     count, rank, size = basis.shape
     columns = side.shape[0]
     return pl.pallas_call(
         far_kernel,
-        in_specs=[SMEM, SMEM] + [VMEM] * 6,
+        in_specs=[SMEM] + [VMEM] * 6,
         out_specs=(ANY, VMEM, VMEM, VMEM),
         out_shape=(
             pltpu.HBM((count, rank, columns), jnp.float32),
@@ -360,7 +378,7 @@
             pltpu.VMEM((columns // 2, 2 * rank), jnp.float32),
             pltpu.VMEM((count, columns, size), jnp.float32),
         ),
-        input_output_aliases={3: 3},
+        input_output_aliases={2: 3},
         scratch_shapes=[
             pltpu.VMEM((count + 1, columns, size), jnp.bfloat16),
             pltpu.VMEM((count * rank, columns), jnp.bfloat16),
@@ -369,7 +387,7 @@
         ],
         compiler_params=params(8),
         name="far_pass",
-    )(tasks, steps, resident(side), near, blocks, resident(basis), path_high, path_low)
+    )(tasks, resident(side), near, blocks, resident(basis), path_high, path_low)
 
 
 def gram_pass(place, high, count, parts):
@@ -426,20 +444,18 @@
     upper = jnp.concatenate(rows, axis=0).reshape(heights, rank, rank)
 
     blocks = near_blocks.reshape(count * slots, size, size)
-    anchor = jnp.stack([device * count - count, jnp.bitwise_and(device, 1)]).astype(jnp.int32)
-    near, blocks, path_high, path_low, twice, tasks, steps, later_tasks, later_steps = own_pass(
-        anchor,
+    near, blocks, path_high, path_low, twice, tasks, later_tasks = own_pass(
         near_index.T,
-        near_count,
+        near_count.reshape(1, count),
         upper,
         inner_transfer.reshape(-1, rank),
         own,
         samples.T,
         blocks,
     )
-    near = side_pass(tasks, steps, first, near, blocks)
+    near = side_pass(tasks, first, near, blocks)
     coeffs, high, part, _ = far_pass(
-        later_tasks, later_steps, second, near, blocks, leaf_basis, path_high, path_low
+        later_tasks, second, near, blocks, leaf_basis, path_high, path_low
     )
 
     flips = (1, 3, 4, 8, 24)
@@ -453,17 +469,17 @@
         if height == 0:
             keep, send = gram_pass(place.reshape(1), high, count, parts)
             got = exchange(send, "samp", 1)
-        elif height == 1:
+        elif height == 2:
             gram = keep + got
             middle = gram[1:3].astype(jnp.bfloat16)
             other, _ = lax.optimization_barrier((other, middle))
             got = exchange(middle, "samp", 2).astype(jnp.float32)
-        elif height == 2:
+        elif height == 3:
             near_total = gram[0] + got[0]
             far_total = gram[3] + got[1]
             other, _ = lax.optimization_barrier((other, far_total))
             got = exchange(far_total, "samp", 6)
-        elif height == 3:
+        elif height == 4:
             leaf_gram = pl.pallas_call(
                 finish_kernel,
                 in_specs=[VMEM, VMEM],

time: 53.7 us -> 50.1 us (0.933)
  Pallas kernels: 16.3 us -> 11.9 us
  waiting for transfers between devices: 7.24 us -> 8.42 us
    pallas_call x3, Pallas kernels: 14 us -> 9.62 us  [the longest x1 6.38 us: own_pass(): pl.pallas_call(own_kernel, in_specs=[ANY, ANY, VMEM, VMEM, ANY, ANY, ANY]...]
    ppermute x2, waiting for transfers between devices: 0.01 us -> 2.02 us  [swap(): return lax.ppermute(value, axis, pairs + [(j, i) for i, j in pairs])]
    ppermute x8, waiting for transfers between devices: 7.23 us -> 6.4 us  [exchange(): lax.ppermute(value, axis, [(i, i ^ flip) for i in range(lax.axis_size(axi...]
  transfers between devices with their start and end apart: 10 -> 10, of which waited for: 6 -> 6; matrix products, arithmetic and copies ran while one was open for 7% -> 8% of each run, Pallas kernels for 19% -> 16%
where the time goes in v5:
time: 50.1 us; the launch traced here: 49.5 us
  starting transfers between devices  24.4 us (49%)
  Pallas kernels  11.9 us (24%)
  waiting for transfers between devices  8.42 us (17%)
  local copies, waits for them, and re-layouts  3.33 us (7%)
  between operations  0.78 us (2%)
  matrix products  0.62 us (1%)
    ppermute x8, starting transfers between devices, exchange(): lax.ppermute(value, axis, [(i, i ^ flip) for i in range(lax.axis_size(axi...  19.2 us
    ppermute x8, waiting for transfers between devices, exchange(): lax.ppermute(value, axis, [(i, i ^ flip) for i in range(lax.axis_size(axi...  6.4 us
    pallas_call x1, Pallas kernels, own_pass(): pl.pallas_call(own_kernel, in_specs=[ANY, ANY, VMEM, VMEM, ANY, ANY, ANY]...  6.38 us
    ppermute x2, starting transfers between devices, swap(): return lax.ppermute(value, axis, pairs + [(j, i) for i, j in pairs])  5.15 us
    pallas_call x1, Pallas kernels, far_pass(): pl.pallas_call(far_kernel, in_specs=[SMEM] + [VMEM] * 6, out_specs=(ANY,...  3.14 us
    reshape x1, local copies, waits for them, and re-layouts, shards(): inner_transfer.reshape(-1, rank)  2.03 us
    ppermute x2, waiting for transfers between devices, swap(): return lax.ppermute(value, axis, pairs + [(j, i) for i, j in pairs])  2.02 us
    dynamic_slice x1, local copies, waits for them, and re-layouts, shards(): lax.dynamic_slice_in_dim(upper_transfer, offset + jnp.right_shift(device,...  1.05 us
  transfers between devices with their start and end apart: 10, of which 6 were waited for; matrix products, arithmetic and copies ran while one was open for 8% of the time, Pallas kernels for 16%

profile of v5, /device:TPU:6, one launch (start us, length us, event | category | flops | bytes accessed | tf_op | source)
XLA Modules:
  0.0 49.5 jit_solution(6658929030081710323)
XLA Ops:
  0.6 0.7 %collective-permute-start.1 = (bf16[64,4096]{1,0:T(8,128)(2,1)}, bf16[64,4096]{1,0:T(8,128)(2,1)S(1)}, u32[]{:S(2)}, u32[]{:S(2)}) collective-permute-start(bf16[64,4096]{1,0:T(8,128)(2,1)} %bitcast.29), channel_id=1, source_target_pairs={{8,16},{24,32},{40,48},{56,64},{72,80},{88,96},{104,112},{120,128}... | collective-permute-start | bytes 1572872 | tf_op jit(solution)/shard_map/ppermute | solution.py:415
  1.3 4.5 %collective-permute-start = (bf16[64,4096]{1,0:T(8,128)(2,1)}, bf16[64,4096]{1,0:T(8,128)(2,1)S(1)}, u32[]{:S(2)}, u32[]{:S(2)}) collective-permute-start(bf16[64,4096]{1,0:T(8,128)(2,1)} %bitcast.30), channel_id=1, source_target_pairs={{0,8},{16,24},{32,40},{48,56},{64,72},{80,88},{96,104},{112,120},{... | collective-permute-start | bytes 1572872 | tf_op jit(solution)/shard_map/ppermute | solution.py:415
  5.8 1.1 %constant_dynamic-slice_fusion = (bf16[1,4096]{1,0:T(2,128)(2,1)S(1)}, bf16[1,4096]{1,0:T(2,128)(2,1)S(1)}, bf16[1,4096]{1,0:T(2,128)(2,1)S(1)}, bf16[1,4096]{1,0:T(2,128)(2,1)S(1)}, bf16[1,4096]{1,0:T(2,128)(2,1)S(1)}) fusion(bf16[62,4096]{1,0:T(8,128)(2,1)} %param.15, s32[]{:T(128)S(6)} %select_n.19, s32[]{:T(128)S(6)} %select_n.17, s32[]{:T(128)S(6)} %select_n.16, ...), kind=kLoop, calls=%fused_computation.17 | loop fusion | bytes 81940 | tf_op jit(solution)/shard_map/dynamic_slice | solution.py:439
  7.1 2.0 %reshape.25.mats_ref = bf16[3968,64]{1,0:T(8,128)(2,1)S(1)} reshape(bf16[62,4096]{1,0:T(8,128)(2,1)} %param.14) | data formatting | bytes 1015808 | tf_op jit(solution)/shard_map/reshape | solution.py:451
  9.1 6.4 %own_pass.1 = (f32[32,64,128]{2,1,0:T(8,128)S(1)}, bf16[256,128,128]{2,1,0:T(8,128)(2,1)S(1)}, bf16[64,2048]{1,0:T(8,128)(2,1)S(1)}, bf16[64,2048]{1,0:T(8,128)(...) custom-call(s32[8,32]{1,0:T(8,128)} %bitcast.33, s32[1,32]{1,0:T(1,128)} %bitcast.34, ...), custom_call_target="tpu_custom_call" | custom-call | tf_op jit(solution)/shard_map/own_pass/pallas_call | solution.py:313
  15.6 2.0 %collective-permute-done.side_ref = bf16[64,4096]{1,0:T(8,128)(2,1)S(1)} collective-permute-done((bf16[64,4096]{1,0:T(8,128)(2,1)}, bf16[64,4096]{1,0:T(8,128)(2,1)S(1)}, u32[]{:S(2)}, u32[]{:S(2)}) %collective-permute-start) | collective-permute-done | bytes 524320 | tf_op jit(solution)/shard_map/ppermute | solution.py:415
  17.6 3.1 %far_pass.1 = (f32[32,64,64]{2,1,0:T(8,128)}, bf16[2048,64]{1,0:T(8,128)(2,1)S(1)}, f32[32,128]{1,0:T(8,128)S(1)}, f32[32,64,128]{2,1,0:T(8,128)S(1)}) custom-call(s32[8,128]{1,0:T(8,128)S(4)} %get-tuple-element.18.task_ref, bf16[64,4096]{1,0:T(8,128)(2,1)S(1)} %collective-permute-done.side_ref, ...), custom_call_target="tpu_custom_call", output_to_operand_aliasing={{3}: (2, {})} | custom-call | tf_op jit(solution)/shard_map/far_pass/pallas_call | solution.py:371
  20.8 1.2 %collective-permute-start.5 = (f32[32,128]{1,0:T(8,128)S(1)}, f32[32,128]{1,0:T(8,128)S(1)}, u32[]{:S(2)}, u32[]{:S(2)}) collective-permute-start(f32[32,128]{1,0:T(8,128)S(1)} %get-tuple-element.28), channel_id=1, source_target_pairs={{0,8},{8,0},{16,24},{24,16},{32,40},{40,32},{48,56},{56,48},{64,72... | collective-permute-start | bytes 49160 | tf_op jit(solution)/shard_map/ppermute | solution.py:410
  22.0 0.7 %gram_pass.1 = (f32[4,8,16,128]{3,2,1,0:T(8,128)S(1)}, f32[4,8,16,128]{3,2,1,0:T(8,128)S(1)}) custom-call(s32[1]{0:T(128)} %bitcast.5.place_ref, bf16[2048,64]{1,0:T(8,128)(2,1)S(1)} %get-tuple-element.25.high_ref), custom_call_target="tpu_custom_call" | custom-call | tf_op jit(solution)/shard_map/gram_pass/pallas_call | solution.py:398
  22.8 1.8 %collective-permute-done.5 = f32[32,128]{1,0:T(8,128)S(1)} collective-permute-done((f32[32,128]{1,0:T(8,128)S(1)}, f32[32,128]{1,0:T(8,128)S(1)}, u32[]{:S(2)}, u32[]{:S(2)}) %collective-permute-start.5) | collective-permute-done | bytes 16416 | tf_op jit(solution)/shard_map/ppermute | solution.py:410
  24.6 0.2 fusion.8
  24.8 4.7 %collective-permute-start.6 = (f32[32,128]{1,0:T(8,128)S(1)}, f32[32,128]{1,0:T(8,128)S(1)}, u32[]{:S(2)}, u32[]{:S(2)}) collective-permute-start(f32[32,128]{1,0:T(8,128)S(1)} %fusion.8), channel_id=1, source_target_pairs={{0,24},{8,16},{16,8},{24,0},{32,56},{40,48},{48,40},{56,32},{64,88... | collective-permute-start | bytes 49160 | tf_op jit(solution)/shard_map/ppermute | solution.py:410
  29.5 1.7 %collective-permute-done.6 = f32[32,128]{1,0:T(8,128)S(1)} collective-permute-done((f32[32,128]{1,0:T(8,128)S(1)}, f32[32,128]{1,0:T(8,128)S(1)}, u32[]{:S(2)}, u32[]{:S(2)}) %collective-permute-start.6) | collective-permute-done | bytes 16416 | tf_op jit(solution)/shard_map/ppermute | solution.py:410
  31.2 0.2 fusion.6
  31.4 2.3 %collective-permute-start.7 = (f32[32,128]{1,0:T(8,128)S(1)}, f32[32,128]{1,0:T(8,128)S(1)}, u32[]{:S(2)}, u32[]{:S(2)}) collective-permute-start(f32[32,128]{1,0:T(8,128)S(1)} %fusion.6), channel_id=1, source_target_pairs={{0,32},{8,40},{16,48},{24,56},{32,0},{40,8},{48,16},{56,24},{64,96... | collective-permute-start | bytes 49160 | tf_op jit(solution)/shard_map/ppermute | solution.py:410
  33.7 0.9 %collective-permute-start.3 = (bf16[2,8,16,128]{3,2,1,0:T(8,128)(2,1)S(1)}, bf16[2,8,16,128]{3,2,1,0:T(8,128)(2,1)S(1)}, u32[]{:S(2)}, u32[]{:S(2)}) collective-permute-start(bf16[2,8,16,128]{3,2,1,0:T(8,128)(2,1)S(1)} %slice.67), channel_id=1, source_target_pairs={{0,2},{1,3},{2,0},{3,1},{4,6},{5,7},{6,4},{7,5},{8,10},{9,11},{10,... | collective-permute-start | bytes 196616 | tf_op jit(solution)/shard_map/ppermute | solution.py:410
  34.7 0.7 %collective-permute-done.7 = f32[32,128]{1,0:T(8,128)S(1)} collective-permute-done((f32[32,128]{1,0:T(8,128)S(1)}, f32[32,128]{1,0:T(8,128)S(1)}, u32[]{:S(2)}, u32[]{:S(2)}) %collective-permute-start.7) | collective-permute-done | bytes 16416 | tf_op jit(solution)/shard_map/ppermute | solution.py:410
  35.6 4.3 %collective-permute-start.8 = (f32[32,128]{1,0:T(8,128)S(1)}, f32[32,128]{1,0:T(8,128)S(1)}, u32[]{:S(2)}, u32[]{:S(2)}) collective-permute-start(f32[32,128]{1,0:T(8,128)S(1)} %fusion.4), channel_id=1, source_target_pairs={{0,64},{8,72},{16,80},{24,88},{32,96},{40,104},{48,112},{56,120},{... | collective-permute-start | bytes 49160 | tf_op jit(solution)/shard_map/ppermute | solution.py:410
  39.9 0.6 %collective-permute-start.4 = (f32[8,16,128]{2,1,0:T(8,128)S(1)}, f32[8,16,128]{2,1,0:T(8,128)S(1)}, u32[]{:S(2)}, u32[]{:S(2)}) collective-permute-start(f32[8,16,128]{2,1,0:T(8,128)S(1)} %get-tuple-element.38), channel_id=1, source_target_pairs={{0,6},{1,7},{2,4},{3,5},{4,2},{5,3},{6,0},{7,1},{8,14},{9,15},{10,... | collective-permute-start | bytes 196616 | tf_op jit(solution)/shard_map/ppermute | solution.py:410
  40.4 1.1 %collective-permute-done.8 = f32[32,128]{1,0:T(8,128)S(1)} collective-permute-done((f32[32,128]{1,0:T(8,128)S(1)}, f32[32,128]{1,0:T(8,128)S(1)}, u32[]{:S(2)}, u32[]{:S(2)}) %collective-permute-start.8) | collective-permute-done | bytes 16416 | tf_op jit(solution)/shard_map/ppermute | solution.py:410
  41.7 5.2 %collective-permute-start.9 = (f32[32,128]{1,0:T(8,128)S(1)}, f32[32,128]{1,0:T(8,128)S(1)}, u32[]{:S(2)}, u32[]{:S(2)}) collective-permute-start(f32[32,128]{1,0:T(8,128)S(1)} %fusion.2), channel_id=1, source_target_pairs={{0,192},{8,200},{16,208},{24,216},{32,224},{40,232},{48,240},{56,2... | collective-permute-start | bytes 49160 | tf_op jit(solution)/shard_map/ppermute | solution.py:410
  46.9 0.7 %finish.1 = f32[32,512]{1,0:T(8,128)} custom-call(f32[8,16,128]{2,1,0:T(8,128)S(1)} %get-tuple-element.39.total_ref, f32[8,16,128]{2,1,0:T(8,128)S(1)} %collective-permute-done.4.last_ref), custom_call_target="tpu_custom_call" | custom-call | tf_op jit(solution)/shard_map/finish/pallas_call | solution.py:483
  47.6 1.0 %collective-permute-done.9 = f32[32,128]{1,0:T(8,128)S(1)} collective-permute-done((f32[32,128]{1,0:T(8,128)S(1)}, f32[32,128]{1,0:T(8,128)S(1)}, u32[]{:S(2)}, u32[]{:S(2)}) %collective-permute-start.9) | collective-permute-done | bytes 16416 | tf_op jit(solution)/shard_map/ppermute | solution.py:410
  48.6 0.9 %turn.1 = f32[5,64,64]{2,1,0:T(8,128)} custom-call(f32[32,128]{1,0:T(8,128)S(1)} %add.62.refs_0_, f32[32,128]{1,0:T(8,128)S(1)} %add.63.refs_1_, f32[32,128]{1,0:T(8,128)S(1)} %add.64.refs_2_, f32[32,128]{1,0:T(8,128)S(1)} %add.65.refs_3_, f32[32,128]{1,0:T(8,128)S(1)} %add.66.refs_4_), custom_call_target="tpu_custom_call" | custom-call | tf_op jit(solution)/shard_map/turn/pallas_call | solution.py:494
  (21 shorter events, 0.8 us)
Async XLA Ops:
  0.6 14.9 %collective-permute-start.1 = (bf16[64,4096]{1,0:T(8,128)(2,1)}, bf16[64,4096]{1,0:T(8,128)(2,1)S(1)}, u32[]{:S(2)}, u32[]{:S(2)}) collective-permute-start(bf16[64,4096]{1,0:T(8,128)(2,1)} %bitcast.29), channel_id=1, source_target_pairs={{8,16},{24,32},{40,48},{56,64},{72,80},{88,96},{104,112},{120,128}... | collective-permute-start | bytes 1572872 | tf_op jit(solution)/shard_map/ppermute | solution.py:415
  1.3 16.3 %collective-permute-start = (bf16[64,4096]{1,0:T(8,128)(2,1)}, bf16[64,4096]{1,0:T(8,128)(2,1)S(1)}, u32[]{:S(2)}, u32[]{:S(2)}) collective-permute-start(bf16[64,4096]{1,0:T(8,128)(2,1)} %bitcast.30), channel_id=1, source_target_pairs={{0,8},{16,24},{32,40},{48,56},{64,72},{80,88},{96,104},{112,120},{... | collective-permute-start | bytes 1572872 | tf_op jit(solution)/shard_map/ppermute | solution.py:415
  9.1 8.5 %copy-start = (bf16[32,64,128]{2,1,0:T(8,128)(2,1)S(1)}, bf16[32,64,128]{2,1,0:T(8,128)(2,1)}, u32[]{:S(2)}) copy-start(bf16[32,64,128]{2,1,0:T(8,128)(2,1)} %basis_ref.1) | copy-start | bytes 1572868
  20.8 3.8 %collective-permute-start.5 = (f32[32,128]{1,0:T(8,128)S(1)}, f32[32,128]{1,0:T(8,128)S(1)}, u32[]{:S(2)}, u32[]{:S(2)}) collective-permute-start(f32[32,128]{1,0:T(8,128)S(1)} %get-tuple-element.28), channel_id=1, source_target_pairs={{0,8},{8,0},{16,24},{24,16},{32,40},{40,32},{48,56},{56,48},{64,72... | collective-permute-start | bytes 49160 | tf_op jit(solution)/shard_map/ppermute | solution.py:410
  22.7 11.0 %collective-permute-start.2 = (f32[4,8,16,128]{3,2,1,0:T(8,128)S(1)}, f32[4,8,16,128]{3,2,1,0:T(8,128)S(1)}, u32[]{:S(2)}, u32[]{:S(2)}) collective-permute-start(f32[4,8,16,128]{3,2,1,0:T(8,128)S(1)} %get-tuple-element.27), channel_id=1, source_target_pairs={{0,1},{1,0},{2,3},{3,2},{4,5},{5,4},{6,7},{7,6},{8,9},{9,8},{10,11... | collective-permute-start | bytes 786440 | tf_op jit(solution)/shard_map/ppermute | solution.py:410
  24.8 6.4 %collective-permute-start.6 = (f32[32,128]{1,0:T(8,128)S(1)}, f32[32,128]{1,0:T(8,128)S(1)}, u32[]{:S(2)}, u32[]{:S(2)}) collective-permute-start(f32[32,128]{1,0:T(8,128)S(1)} %fusion.8), channel_id=1, source_target_pairs={{0,24},{8,16},{16,8},{24,0},{32,56},{40,48},{48,40},{56,32},{64,88... | collective-permute-start | bytes 49160 | tf_op jit(solution)/shard_map/ppermute | solution.py:410
  31.4 4.0 %collective-permute-start.7 = (f32[32,128]{1,0:T(8,128)S(1)}, f32[32,128]{1,0:T(8,128)S(1)}, u32[]{:S(2)}, u32[]{:S(2)}) collective-permute-start(f32[32,128]{1,0:T(8,128)S(1)} %fusion.6), channel_id=1, source_target_pairs={{0,32},{8,40},{16,48},{24,56},{32,0},{40,8},{48,16},{56,24},{64,96... | collective-permute-start | bytes 49160 | tf_op jit(solution)/shard_map/ppermute | solution.py:410
  33.7 6.1 %collective-permute-start.3 = (bf16[2,8,16,128]{3,2,1,0:T(8,128)(2,1)S(1)}, bf16[2,8,16,128]{3,2,1,0:T(8,128)(2,1)S(1)}, u32[]{:S(2)}, u32[]{:S(2)}) collective-permute-start(bf16[2,8,16,128]{3,2,1,0:T(8,128)(2,1)S(1)} %slice.67), channel_id=1, source_target_pairs={{0,2},{1,3},{2,0},{3,1},{4,6},{5,7},{6,4},{7,5},{8,10},{9,11},{10,... | collective-permute-start | bytes 196616 | tf_op jit(solution)/shard_map/ppermute | solution.py:410
  35.6 6.0 %collective-permute-start.8 = (f32[32,128]{1,0:T(8,128)S(1)}, f32[32,128]{1,0:T(8,128)S(1)}, u32[]{:S(2)}, u32[]{:S(2)}) collective-permute-start(f32[32,128]{1,0:T(8,128)S(1)} %fusion.4), channel_id=1, source_target_pairs={{0,64},{8,72},{16,80},{24,88},{32,96},{40,104},{48,112},{56,120},{... | collective-permute-start | bytes 49160 | tf_op jit(solution)/shard_map/ppermute | solution.py:410
  39.9 7.0 %collective-permute-start.4 = (f32[8,16,128]{2,1,0:T(8,128)S(1)}, f32[8,16,128]{2,1,0:T(8,128)S(1)}, u32[]{:S(2)}, u32[]{:S(2)}) collective-permute-start(f32[8,16,128]{2,1,0:T(8,128)S(1)} %get-tuple-element.38), channel_id=1, source_target_pairs={{0,6},{1,7},{2,4},{3,5},{4,2},{5,3},{6,0},{7,1},{8,14},{9,15},{10,... | collective-permute-start | bytes 196616 | tf_op jit(solution)/shard_map/ppermute | solution.py:410
  41.7 6.9 %collective-permute-start.9 = (f32[32,128]{1,0:T(8,128)S(1)}, f32[32,128]{1,0:T(8,128)S(1)}, u32[]{:S(2)}, u32[]{:S(2)}) collective-permute-start(f32[32,128]{1,0:T(8,128)S(1)} %fusion.2), channel_id=1, source_target_pairs={{0,192},{8,200},{16,208},{24,216},{32,224},{40,232},{48,240},{56,2... | collective-permute-start | bytes 49160 | tf_op jit(solution)/shard_map/ppermute | solution.py:410

commit v6 on v5

--- a/solution.py
+++ b/solution.py
@@ -110,11 +110,10 @@
             lists_ref[which, row : row + 1] = line
 
 
-def path_products(upper_ref, mats_ref, high_ref, low_ref):
-    rank = upper_ref.shape[1]
-    count = high_ref.shape[1] // rank
-    top = upper_ref[0].astype(jnp.float32).T
-    nodes = [split(top)]
+def path_products(upper_ref, mats_ref, basis_ref, weight_ref):
+    count, rank, size = basis_ref.shape
+    nodes = [split(upper_ref[0].astype(jnp.float32).T)]
+    blank = jnp.zeros((rank, size), basis_ref.dtype)
     width = 2
     offset = 2 * count - 2
     while width <= count:
@@ -126,8 +125,16 @@
             product = dot(high, pair, NT) + dot(low, pair, NT)
             pair_high, pair_low = split(product)
             if width == count:
-                high_ref[:, 2 * parent * rank : 2 * (parent + 1) * rank] = pair_high
-                low_ref[:, 2 * parent * rank : 2 * (parent + 1) * rank] = pair_low
+                bases = jnp.concatenate(
+                    [
+                        jnp.concatenate([basis_ref[2 * parent], blank], axis=1),
+                        jnp.concatenate([blank, basis_ref[2 * parent + 1]], axis=1),
+                    ],
+                    axis=0,
+                )
+                weight = split(dot(pair_high, bases, NN) + dot(pair_low, bases, NN))
+                at = slice(2 * parent * size, 2 * (parent + 1) * size)
+                weight_ref[:rank, at], weight_ref[rank:, at] = weight
             else:
                 later.append((pair_high[:, :rank], pair_low[:, :rank]))
                 later.append((pair_high[:, rank:], pair_low[:, rank:]))
@@ -143,10 +150,11 @@
     own_any,
     samples_any,
     blocks_any,
+    basis_any,
     acc_ref,
     blocks_ref,
-    path_high_ref,
-    path_low_ref,
+    basis_ref,
+    weight_ref,
     twice_ref,
     first_task_ref,
     second_task_ref,
@@ -165,6 +173,7 @@
         (own_any, own_ref),
         (samples_any, samples_ref),
         (blocks_any, blocks_ref),
+        (basis_any, basis_ref),
         (lists.at[0], own_task),
         (lists.at[1], first_task_ref),
         (lists.at[2], second_task_ref),
@@ -173,7 +182,7 @@
         pltpu.make_async_copy(origin, target, sems.at[place])
         for place, (origin, target) in enumerate(pairs)
     ]
-    for copy in copies[:5]:
+    for copy in copies[:6]:
         copy.start()
     slots, count = index_ref.shape
     size = blocks_ref.shape[1]
@@ -181,9 +190,8 @@
     copies[0].wait()
     copies[1].wait()
     list_tasks(index_ref[...], number_ref[...], lax.axis_index("leaf"), lists)
-    for copy in copies[5:]:
+    for copy in copies[6:]:
         copy.start()
-    path_products(upper_ref, mats_ref, path_high_ref, path_low_ref)
     for height in range(1, upper_ref.shape[0]):
         matrix = upper_ref[height].astype(jnp.float32)
         blank = jnp.zeros_like(matrix)
@@ -197,6 +205,7 @@
         acc_ref[leaf] = samples_ref[:, leaf * size : (leaf + 1) * size].astype(jnp.float32)
     for copy in copies[4:]:
         copy.wait()
+    path_products(upper_ref, mats_ref, basis_ref, weight_ref)
     subtract_near(count, own_task, source, blocks_ref, acc_ref, slots)
 
 
@@ -209,83 +218,70 @@
 
 
 def far_kernel(
-    task_ref,
-    side_ref,
-    near_ref,
-    blocks_ref,
-    basis_ref,
-    path_high_ref,
-    path_low_ref,
-    coeff_any,
-    high_ref,
-    part_ref,
-    acc,
-    source,
-    low_ref,
-    coeff_ref,
-    sems,
+    task_ref, side_ref, near_ref, blocks_ref, weight_ref, far_ref, part_ref, acc, source
 ):
-    count, rank, size = basis_ref.shape
+    count, _, size = acc.shape
     slots = blocks_ref.shape[0] // count
     side_kernel(task_ref, side_ref, near_ref, blocks_ref, slots, acc, source)
-
-    copies = []
-    for step in range(count // PER_STEP):
-        for leaf in range(step * PER_STEP, (step + 1) * PER_STEP):
-            coeff = dot(basis_ref[leaf], acc[leaf].astype(jnp.bfloat16), NT)
-            coeff_ref[leaf] = coeff
-            high, low = split(coeff)
-            rows = slice(leaf * rank, (leaf + 1) * rank)
-            high_ref[rows, :] = high
-            low_ref[rows, :] = low
-        these = pl.ds(step * PER_STEP, PER_STEP)
-        copies.append(
-            pltpu.make_async_copy(coeff_ref.at[these], coeff_any.at[these], sems.at[step])
-        )
-        copies[-1].start()
-    part = dot(path_high_ref[...], high_ref[...], NN)
-    part += dot(path_low_ref[...], high_ref[...], NN)
-    part += dot(path_high_ref[...], low_ref[...], NN)
-    turned = part.T
+    for leaf in range(count):
+        far_ref[:, leaf * size : (leaf + 1) * size] = acc[leaf].astype(jnp.bfloat16)
+    product = dot(weight_ref[...], far_ref[...], NT)
+    rank = product.shape[0] // 2
+    turned = (product[:rank] + product[rank:]).T
     half = turned.shape[0] // 2
     part_ref[...] = jnp.concatenate([turned[:half], turned[half:]], axis=1)
-    for copy in copies:
-        copy.wait()
-
-
-def gram_kernel(scale, place_ref, high_ref, keep_ref, send_ref, gram):
+
+
+def gram_kernel(
+    scale, place_ref, far_ref, basis_ref, coeff_any, keep_ref, send_ref, gram, coeff_ref, sems
+):
     parts, rows, pairs, width = keep_ref.shape
     parts = 2 * parts
     rank = width // 2
+    size = basis_ref.shape[2]
     lane = lax.broadcasted_iota(jnp.int32, (rank, width), 1)
-
-    def pair_step(step, carry):
-        for inner in range(PER_STEP):
-            pair = step * PER_STEP + inner
-            one = high_ref[pl.ds(pl.multiple_of(pair * rank, rank), rank), :]
-            two = high_ref[pl.ds(pl.multiple_of((pair + pairs) * rank, rank), rank), :]
-            stacked = jnp.concatenate([one, two], axis=0)
+    copies = []
+    for first in range(0, pairs, PER_STEP):
+        stacks = []
+        for pair in range(first, first + PER_STEP):
+            both = []
+            for leaf in (pair, pair + pairs):
+                far = far_ref[:, leaf * size : (leaf + 1) * size]
+                coeff = dot(basis_ref[leaf], far, NT)
+                coeff_ref[leaf] = coeff
+                both.append(coeff.astype(jnp.bfloat16))
+            stacks.append(jnp.concatenate(both, axis=0))
+        for start in (first, first + pairs):
+            these = pl.ds(start, PER_STEP)
+            copies.append(
+                pltpu.make_async_copy(
+                    coeff_ref.at[these], coeff_any.at[these], sems.at[len(copies)]
+                )
+            )
+            copies[-1].start()
+        for pair, stacked in enumerate(stacks, first):
             product = dot(stacked, stacked, NT)
             value = jnp.where(lane < rank, product[:rank], product[rank:]) * scale
             gram[pl.ds(pair, rank, stride=pairs), :] = value
-        return carry
-
-    lax.fori_loop(0, pairs // PER_STEP, pair_step, 0)
     for relative in range(parts):
         first = jnp.bitwise_xor(place_ref[0], relative) * rows
         target = send_ref if relative % 2 else keep_ref
         for row in range(rows):
             at = pl.multiple_of((first + row) * pairs, pairs)
             target[relative // 2, row] = gram[pl.ds(at, pairs), :]
-
-
-def finish_kernel(total_ref, last_ref, out_ref):
-    rows, pairs, width = total_ref.shape
+    for copy in copies:
+        copy.wait()
+
+
+def finish_kernel(keep_ref, got_ref, *refs):
+    others, out_ref = refs[:-1], refs[-1]
+    _, rows, pairs, width = keep_ref.shape
     half = width // 2
     lane = lax.broadcasted_iota(jnp.int32, (pairs, width), 1)
     for row in range(0, rows, 2):
-        even = total_ref[row] + last_ref[row]
-        odd = total_ref[row + 1] + last_ref[row + 1]
+        even, odd = (keep_ref[0, at] + got_ref[0, at] for at in (row, row + 1))
+        for other in others:
+            even, odd = even + other[row], odd + other[row + 1]
         at = slice(row * half, (row + 2) * half)
         out_ref[:pairs, at] = jnp.where(lane < half, even, pltpu.roll(odd, half, 1))
         out_ref[pairs:, at] = jnp.where(lane < half, pltpu.roll(even, half, 1), odd)
@@ -303,7 +299,7 @@
     return pltpu.CompilerParams(vmem_limit_bytes=mib * 2**20)
 
 
-def own_pass(index, number, upper, mats, own, samples, blocks):
+def own_pass(index, number, upper, mats, own, samples, blocks, basis):
     slots, count = index.shape
     size = blocks.shape[1]
     columns = own.shape[0]
@@ -312,13 +308,13 @@
     far = lambda value: pltpu.with_memory_space_constraint(value, pltpu.HBM)
     return pl.pallas_call(
         own_kernel,
-        in_specs=[ANY, ANY, VMEM, VMEM, ANY, ANY, ANY],
+        in_specs=[ANY, ANY, VMEM, VMEM, ANY, ANY, ANY, ANY],
         out_specs=(VMEM, VMEM, VMEM, VMEM, VMEM, SMEM, SMEM),
         out_shape=(
             pltpu.VMEM((count, columns, size), jnp.float32),
             pltpu.VMEM(blocks.shape, blocks.dtype),
-            pltpu.VMEM((rank, count * rank), jnp.bfloat16),
-            pltpu.VMEM((rank, count * rank), jnp.bfloat16),
+            pltpu.VMEM(basis.shape, basis.dtype),
+            pltpu.VMEM((2 * rank, count * size), jnp.bfloat16),
             pltpu.VMEM((heights - 1, 2 * rank, 2 * rank), jnp.float32),
             tasks,
             tasks,
@@ -331,7 +327,7 @@
             pltpu.VMEM(own.shape, own.dtype),
             pltpu.VMEM(samples.shape, samples.dtype),
             pltpu.VMEM((count + 1, columns, size), jnp.bfloat16),
-            pltpu.SemaphoreType.DMA((8,)),
+            pltpu.SemaphoreType.DMA((9,)),
         ],
         compiler_params=params(8),
         name="own_pass",
@@ -343,6 +339,7 @@
         far(own),
         far(samples),
         far(blocks),
+        far(basis),
     )
 
 
@@ -365,45 +362,47 @@
     )(tasks, resident(side), near, blocks)
 
 
-def far_pass(tasks, side, near, blocks, basis, path_high, path_low):
-    count, rank, size = basis.shape
-    columns = side.shape[0]
+def far_pass(tasks, side, near, blocks, weight):
+    count, columns, size = near.shape
+    rank = weight.shape[0] // 2
     return pl.pallas_call(
         far_kernel,
-        in_specs=[SMEM] + [VMEM] * 6,
-        out_specs=(ANY, VMEM, VMEM, VMEM),
+        in_specs=[SMEM] + [VMEM] * 4,
+        out_specs=(VMEM, VMEM, VMEM),
         out_shape=(
-            pltpu.HBM((count, rank, columns), jnp.float32),
-            pltpu.VMEM((count * rank, columns), jnp.bfloat16),
+            pltpu.VMEM((columns, count * size), jnp.bfloat16),
             pltpu.VMEM((columns // 2, 2 * rank), jnp.float32),
             pltpu.VMEM((count, columns, size), jnp.float32),
         ),
-        input_output_aliases={2: 3},
+        input_output_aliases={2: 2},
+        scratch_shapes=[pltpu.VMEM((count + 1, columns, size), jnp.bfloat16)],
+        compiler_params=params(8),
+        name="far_pass",
+    )(tasks, resident(side), near, blocks, weight)
+
+
+def gram_pass(place, far, basis, parts):
+    count, rank, _ = basis.shape
+    columns = far.shape[0]
+    pairs = count // 2
+    shape = (parts // 2, rank // parts, pairs, 2 * rank)
+    return pl.pallas_call(
+        functools.partial(gram_kernel, 1.0 / (columns * parts)),
+        in_specs=[SMEM, VMEM, VMEM],
+        out_specs=(ANY, VMEM, VMEM),
+        out_shape=(
+            pltpu.HBM((count, rank, columns), jnp.float32),
+            pltpu.VMEM(shape, jnp.float32),
+            pltpu.VMEM(shape, jnp.float32),
+        ),
         scratch_shapes=[
-            pltpu.VMEM((count + 1, columns, size), jnp.bfloat16),
-            pltpu.VMEM((count * rank, columns), jnp.bfloat16),
+            pltpu.VMEM((rank * pairs, 2 * rank), jnp.float32),
             pltpu.VMEM((count, rank, columns), jnp.float32),
             pltpu.SemaphoreType.DMA((count // PER_STEP,)),
         ],
         compiler_params=params(8),
-        name="far_pass",
-    )(tasks, resident(side), near, blocks, resident(basis), path_high, path_low)
-
-
-def gram_pass(place, high, count, parts):
-    columns = high.shape[1]
-    rank = high.shape[0] // count
-    pairs = count // 2
-    shape = (parts // 2, rank // parts, pairs, 2 * rank)
-    return pl.pallas_call(
-        functools.partial(gram_kernel, 1.0 / (columns * parts)),
-        in_specs=[SMEM, VMEM],
-        out_specs=(VMEM, VMEM),
-        out_shape=(pltpu.VMEM(shape, jnp.float32), pltpu.VMEM(shape, jnp.float32)),
-        scratch_shapes=[pltpu.VMEM((rank * pairs, 2 * rank), jnp.float32)],
-        compiler_params=params(8),
         name="gram_pass",
-    )(place, high)
+    )(place, far, basis)
 
 
 def exchange(value, axis, flip):
@@ -444,7 +443,7 @@
     upper = jnp.concatenate(rows, axis=0).reshape(heights, rank, rank)
 
     blocks = near_blocks.reshape(count * slots, size, size)
-    near, blocks, path_high, path_low, twice, tasks, later_tasks = own_pass(
+    near, blocks, basis, weight, twice, crossing_tasks, tasks = own_pass(
         near_index.T,
         near_count.reshape(1, count),
         upper,
@@ -452,42 +451,37 @@
         own,
         samples.T,
         blocks,
+        leaf_basis,
     )
-    near = side_pass(tasks, first, near, blocks)
-    coeffs, high, part, _ = far_pass(
-        later_tasks, second, near, blocks, leaf_basis, path_high, path_low
-    )
+    near = side_pass(tasks, second, near, blocks)
+    far, part, _ = far_pass(crossing_tasks, first, near, blocks, weight)
 
     flips = (1, 3, 4, 8, 24)
     levels = []
     accum = part
-    gram, middle = None, None
     for height in range(heights):
         if height:
             accum = jnp.dot(accum, twice[height - 1], precision=lax.Precision.HIGHEST)
         other = exchange(accum, "leaf", flips[height])
         if height == 0:
-            keep, send = gram_pass(place.reshape(1), high, count, parts)
+            coeffs, keep, send = gram_pass(place.reshape(1), far, basis, parts)
             got = exchange(send, "samp", 1)
         elif height == 2:
-            gram = keep + got
-            middle = gram[1:3].astype(jnp.bfloat16)
-            other, _ = lax.optimization_barrier((other, middle))
-            got = exchange(middle, "samp", 2).astype(jnp.float32)
+            leaving = keep[1] + got[1]
+            other, _ = lax.optimization_barrier((other, leaving))
+            received = [exchange(leaving, "samp", 2)]
         elif height == 3:
-            near_total = gram[0] + got[0]
-            far_total = gram[3] + got[1]
-            other, _ = lax.optimization_barrier((other, far_total))
-            got = exchange(far_total, "samp", 6)
+            received += [exchange(keep[x] + got[x], "samp", 2 * x) for x in (2, 3)]
+            other, _ = lax.optimization_barrier((other, received[0]))
         elif height == 4:
             leaf_gram = pl.pallas_call(
                 finish_kernel,
-                in_specs=[VMEM, VMEM],
+                in_specs=[VMEM] * 5,
                 out_specs=VMEM,
                 out_shape=jax.ShapeDtypeStruct((count, rank * rank // parts), jnp.float32),
                 compiler_params=params(8),
                 name="finish",
-            )(resident(near_total), resident(got))
+            )(keep, *map(resident, [got] + received))
             other, _ = lax.optimization_barrier((other, leaf_gram))
         accum = accum + other
         levels.append(accum)

time: 50.1 us -> 51.7 us (1.032)
  waiting for transfers between devices: 8.42 us -> 4.14 us
  Pallas kernels: 11.9 us -> 15.8 us
  starting transfers between devices: 24.4 us -> 26.1 us
    ppermute x8 -> x9, starting transfers between devices: 19.2 us -> 23.8 us  [exchange(): lax.ppermute(value, axis, [(i, i ^ flip) for i in range(lax.axis_size(axi...]
    ppermute x2, starting transfers between devices: 5.15 us -> 2.35 us  [swap(): return lax.ppermute(value, axis, pairs + [(j, i) for i, j in pairs])]
    ppermute x8 -> x9, waiting for transfers between devices: 6.4 us -> 4.13 us  [exchange(): lax.ppermute(value, axis, [(i, i ^ flip) for i in range(lax.axis_size(axi...]
    ppermute x2, waiting for transfers between devices: 2.02 us -> 0.01 us  [swap(): return lax.ppermute(value, axis, pairs + [(j, i) for i, j in pairs])]
    pallas_call x1, Pallas kernels: 0.1 us -> 1.93 us  [side_pass(): pl.pallas_call(kernel, in_specs=[SMEM] + [VMEM] * 3, out_specs=VMEM, out_...]
    pallas_call x3, Pallas kernels: 10.2 us -> 11.6 us  [the longest x1 10.2 us: own_pass(): pl.pallas_call(own_kernel, in_specs=[ANY, ANY, VMEM, VMEM, ANY, ANY, ANY,...]
    pallas_call x1, Pallas kernels: 0.68 us -> 1.43 us  [gram_pass(): pl.pallas_call(functools.partial(gram_kernel, 1.0 / (columns * parts)), i...]
  transfers between devices with their start and end apart: 10 -> 11, of which waited for: 6 -> 4; matrix products, arithmetic and copies ran while one was open for 8% -> 8% of each run, Pallas kernels for 16% -> 28%
where the time goes in v6:
time: 51.7 us; the launch traced here: 50.8 us
  starting transfers between devices  26.1 us (50%)
  Pallas kernels  15.8 us (31%)
  waiting for transfers between devices  4.14 us (8%)
  local copies, waits for them, and re-layouts  3.32 us (6%)
  between operations  0.76 us (1%)
  matrix products  0.62 us (1%)
    ppermute x9, starting transfers between devices, exchange(): lax.ppermute(value, axis, [(i, i ^ flip) for i in range(lax.axis_size(axi...  23.8 us
    pallas_call x1, Pallas kernels, own_pass(): pl.pallas_call(own_kernel, in_specs=[ANY, ANY, VMEM, VMEM, ANY, ANY, ANY,...  10.2 us
    ppermute x9, waiting for transfers between devices, exchange(): lax.ppermute(value, axis, [(i, i ^ flip) for i in range(lax.axis_size(axi...  4.13 us
    ppermute x2, starting transfers between devices, swap(): return lax.ppermute(value, axis, pairs + [(j, i) for i, j in pairs])  2.35 us
    reshape x1, local copies, waits for them, and re-layouts, shards(): inner_transfer.reshape(-1, rank)  2.03 us
    pallas_call x1, Pallas kernels, side_pass(): pl.pallas_call(kernel, in_specs=[SMEM] + [VMEM] * 3, out_specs=VMEM, out_...  1.93 us
    pallas_call x1, Pallas kernels, gram_pass(): pl.pallas_call(functools.partial(gram_kernel, 1.0 / (columns * parts)), i...  1.43 us
    dynamic_slice x1, local copies, waits for them, and re-layouts, shards(): lax.dynamic_slice_in_dim(upper_transfer, offset + jnp.right_shift(device,...  1.07 us
  transfers between devices with their start and end apart: 11, of which 4 were waited for; matrix products, arithmetic and copies ran while one was open for 8% of the time, Pallas kernels for 28%

profile of v6, /device:TPU:6, one launch (start us, length us, event | category | flops | bytes accessed | tf_op | source)
XLA Modules:
  0.0 50.8 jit_solution(3913727386054116670)
XLA Ops:
  0.6 1.7 %collective-permute-start.1 = (bf16[64,4096]{1,0:T(8,128)(2,1)}, bf16[64,4096]{1,0:T(8,128)(2,1)S(1)}, u32[]{:S(2)}, u32[]{:S(2)}) collective-permute-start(bf16[64,4096]{1,0:T(8,128)(2,1)} %bitcast.31), channel_id=1, source_target_pairs={{0,8},{16,24},{32,40},{48,56},{64,72},{80,88},{96,104},{112,120},{... | collective-permute-start | bytes 1572872 | tf_op jit(solution)/shard_map/ppermute | solution.py:414
  2.3 0.7 %collective-permute-start = (bf16[64,4096]{1,0:T(8,128)(2,1)}, bf16[64,4096]{1,0:T(8,128)(2,1)S(1)}, u32[]{:S(2)}, u32[]{:S(2)}) collective-permute-start(bf16[64,4096]{1,0:T(8,128)(2,1)} %bitcast.32), channel_id=1, source_target_pairs={{8,16},{24,32},{40,48},{56,64},{72,80},{88,96},{104,112},{120,128}... | collective-permute-start | bytes 1572872 | tf_op jit(solution)/shard_map/ppermute | solution.py:414
  3.0 1.1 %constant_dynamic-slice_fusion = (bf16[1,4096]{1,0:T(2,128)(2,1)S(1)}, bf16[1,4096]{1,0:T(2,128)(2,1)S(1)}, bf16[1,4096]{1,0:T(2,128)(2,1)S(1)}, bf16[1,4096]{1,0:T(2,128)(2,1)S(1)}, bf16[1,4096]{1,0:T(2,128)(2,1)S(1)}) fusion(bf16[62,4096]{1,0:T(8,128)(2,1)} %param.15, s32[]{:T(128)S(6)} %select_n.19, s32[]{:T(128)S(6)} %select_n.17, s32[]{:T(128)S(6)} %select_n.16, ...), kind=kLoop, calls=%fused_computation.18 | loop fusion | bytes 81940 | tf_op jit(solution)/shard_map/dynamic_slice | solution.py:438
  4.3 2.0 %reshape.27.mats_ref = bf16[3968,64]{1,0:T(8,128)(2,1)S(1)} reshape(bf16[62,4096]{1,0:T(8,128)(2,1)} %param.14) | data formatting | bytes 1015808 | tf_op jit(solution)/shard_map/reshape | solution.py:450
  6.3 10.2 %own_pass.1 = (f32[32,64,128]{2,1,0:T(8,128)S(1)}, bf16[256,128,128]{2,1,0:T(8,128)(2,1)S(1)}, bf16[32,64,128]{2,1,0:T(8,128)(2,1)S(1)}, bf16[128,4096]{1,0:T(8,...) custom-call(s32[8,32]{1,0:T(8,128)} %bitcast.35, s32[1,32]{1,0:T(1,128)} %bitcast.36, ...), custom_call_target="tpu_custom_call" | custom-call | tf_op jit(solution)/shard_map/own_pass/pallas_call | solution.py:309
  16.6 1.9 %side_pass.1.near_ref = f32[32,64,128]{2,1,0:T(8,128)S(1)} custom-call(s32[8,128]{1,0:T(8,128)S(4)} %get-tuple-element.19.task_ref, bf16[64,4096]{1,0:T(8,128)(2,1)S(1)} %collective-permute-done.1.side_ref, f32[32,64,128]{2,1,0:T(8,128)S(1)} %get-tuple-element.20.near_ref, ...), custom_call_target="tpu_custom_call", output_to_operand_aliasing={{}: (2, {})} | custom-call | tf_op jit(solution)/shard_map/side_pass/pallas_call | solution.py:353
  18.5 0.6 %far_pass.1 = (bf16[64,4096]{1,0:T(8,128)(2,1)S(1)}, f32[32,128]{1,0:T(8,128)S(1)}, f32[32,64,128]{2,1,0:T(8,128)S(1)}) custom-call(s32[8,128]{1,0:T(8,128)S(4)} %get-tuple-element.18.task_ref, bf16[64,4096]{1,0:T(8,128)(2,1)S(1)} %collective-permute-done.side_ref, f32[32,64,128]{2,1,0:T(8,128)S(1)} %side_pass.1.near_ref, ...), custom_call_target="tpu_custom_call", output_to_operand_aliasing={{2}: (2, {})} | custom-call | tf_op jit(solution)/shard_map/far_pass/pallas_call | solution.py:368
  19.2 4.5 %collective-permute-start.6 = (f32[32,128]{1,0:T(8,128)S(1)}, f32[32,128]{1,0:T(8,128)S(1)}, u32[]{:S(2)}, u32[]{:S(2)}) collective-permute-start(f32[32,128]{1,0:T(8,128)S(1)} %get-tuple-element.28), channel_id=1, source_target_pairs={{0,8},{8,0},{16,24},{24,16},{32,40},{40,32},{48,56},{56,48},{64,72... | collective-permute-start | bytes 49160 | tf_op jit(solution)/shard_map/ppermute | solution.py:409
  23.6 1.4 %gram_pass.1 = (f32[32,64,64]{2,1,0:T(8,128)}, f32[4,8,16,128]{3,2,1,0:T(8,128)S(1)}, f32[4,8,16,128]{3,2,1,0:T(8,128)S(1)}) custom-call(s32[1]{0:T(128)} %bitcast.place_ref, bf16[64,4096]{1,0:T(8,128)(2,1)S(1)} %get-tuple-element.23.far_ref, bf16[32,64,128]{2,1,0:T(8,128)(2,1)S(1)} %get-tuple-element.24.basis_ref), custom_call_target="tpu_custom_call" | custom-call | tf_op jit(solution)/shard_map/gram_pass/pallas_call | solution.py:389
  25.2 0.2 collective-permute-done.6
  25.4 0.2 fusion.9
  25.5 4.5 %collective-permute-start.7 = (f32[32,128]{1,0:T(8,128)S(1)}, f32[32,128]{1,0:T(8,128)S(1)}, u32[]{:S(2)}, u32[]{:S(2)}) collective-permute-start(f32[32,128]{1,0:T(8,128)S(1)} %fusion.9), channel_id=1, source_target_pairs={{0,24},{8,16},{16,8},{24,0},{32,56},{40,48},{48,40},{56,32},{64,88... | collective-permute-start | bytes 49160 | tf_op jit(solution)/shard_map/ppermute | solution.py:409
  30.0 1.7 %collective-permute-done.7 = f32[32,128]{1,0:T(8,128)S(1)} collective-permute-done((f32[32,128]{1,0:T(8,128)S(1)}, f32[32,128]{1,0:T(8,128)S(1)}, u32[]{:S(2)}, u32[]{:S(2)}) %collective-permute-start.7) | collective-permute-done | bytes 16416 | tf_op jit(solution)/shard_map/ppermute | solution.py:409
  31.9 2.1 %collective-permute-start.8 = (f32[32,128]{1,0:T(8,128)S(1)}, f32[32,128]{1,0:T(8,128)S(1)}, u32[]{:S(2)}, u32[]{:S(2)}) collective-permute-start(f32[32,128]{1,0:T(8,128)S(1)} %fusion.7), channel_id=1, source_target_pairs={{0,32},{8,40},{16,48},{24,56},{32,0},{40,8},{48,16},{56,24},{64,96... | collective-permute-start | bytes 49160 | tf_op jit(solution)/shard_map/ppermute | solution.py:409
  34.0 0.9 %collective-permute-start.3 = (f32[8,16,128]{2,1,0:T(8,128)S(1)}, f32[8,16,128]{2,1,0:T(8,128)S(1)}, u32[]{:S(2)}, u32[]{:S(2)}) collective-permute-start(f32[8,16,128]{2,1,0:T(8,128)S(1)} %get-tuple-element.35), channel_id=1, source_target_pairs={{0,2},{1,3},{2,0},{3,1},{4,6},{5,7},{6,4},{7,5},{8,10},{9,11},{10,... | collective-permute-start | bytes 196616 | tf_op jit(solution)/shard_map/ppermute | solution.py:409
  34.9 0.8 %collective-permute-done.8 = f32[32,128]{1,0:T(8,128)S(1)} collective-permute-done((f32[32,128]{1,0:T(8,128)S(1)}, f32[32,128]{1,0:T(8,128)S(1)}, u32[]{:S(2)}, u32[]{:S(2)}) %collective-permute-start.8) | collective-permute-done | bytes 16416 | tf_op jit(solution)/shard_map/ppermute | solution.py:409
  35.9 4.5 %collective-permute-start.9 = (f32[32,128]{1,0:T(8,128)S(1)}, f32[32,128]{1,0:T(8,128)S(1)}, u32[]{:S(2)}, u32[]{:S(2)}) collective-permute-start(f32[32,128]{1,0:T(8,128)S(1)} %fusion.5), channel_id=1, source_target_pairs={{0,64},{8,72},{16,80},{24,88},{32,96},{40,104},{48,112},{56,120},{... | collective-permute-start | bytes 49160 | tf_op jit(solution)/shard_map/ppermute | solution.py:409
  40.3 1.4 %collective-permute-start.4 = (f32[8,16,128]{2,1,0:T(8,128)S(1)}, f32[8,16,128]{2,1,0:T(8,128)S(1)}, u32[]{:S(2)}, u32[]{:S(2)}) collective-permute-start(f32[8,16,128]{2,1,0:T(8,128)S(1)} %get-tuple-element.34), channel_id=1, source_target_pairs={{0,4},{1,5},{2,6},{3,7},{4,0},{5,1},{6,2},{7,3},{8,12},{9,13},{10,... | collective-permute-start | bytes 196616 | tf_op jit(solution)/shard_map/ppermute | solution.py:409
  41.7 2.1 %collective-permute-start.5 = (f32[8,16,128]{2,1,0:T(8,128)S(1)}, f32[8,16,128]{2,1,0:T(8,128)S(1)}, u32[]{:S(2)}, u32[]{:S(2)}) collective-permute-start(f32[8,16,128]{2,1,0:T(8,128)S(1)} %get-tuple-element.33), channel_id=1, source_target_pairs={{0,6},{1,7},{2,4},{3,5},{4,2},{5,3},{6,0},{7,1},{8,14},{9,15},{10,... | collective-permute-start | bytes 196616 | tf_op jit(solution)/shard_map/ppermute | solution.py:409
  43.8 0.2 fusion.3
  44.0 3.8 %collective-permute-start.10 = (f32[32,128]{1,0:T(8,128)S(1)}, f32[32,128]{1,0:T(8,128)S(1)}, u32[]{:S(2)}, u32[]{:S(2)}) collective-permute-start(f32[32,128]{1,0:T(8,128)S(1)} %fusion.3), channel_id=1, source_target_pairs={{0,192},{8,200},{16,208},{24,216},{32,224},{40,232},{48,240},{56,2... | collective-permute-start | bytes 49160 | tf_op jit(solution)/shard_map/ppermute | solution.py:409
  47.8 0.7 %finish.1 = f32[32,512]{1,0:T(8,128)} custom-call(f32[4,8,16,128]{3,2,1,0:T(8,128)S(1)} %get-tuple-element.26.keep_ref, f32[4,8,16,128]{3,2,1,0:T(8,128)S(1)} %collective-permute-done.2.got_ref, f32[8,16,128]{2,1,0:T(8,128)S(1)} %collective-permute-done.3.refs_0_, f32[8,16,128]{2,1,0:T(8,128)S(1)} %collective-permute-done.4.refs_1_, ...), custom_call_target="tpu_custom_call" | custom-call | tf_op jit(solution)/shard_map/finish/pallas_call | solution.py:477
  48.5 1.4 %collective-permute-done.10 = f32[32,128]{1,0:T(8,128)S(1)} collective-permute-done((f32[32,128]{1,0:T(8,128)S(1)}, f32[32,128]{1,0:T(8,128)S(1)}, u32[]{:S(2)}, u32[]{:S(2)}) %collective-permute-start.10) | collective-permute-done | bytes 16416 | tf_op jit(solution)/shard_map/ppermute | solution.py:409
  49.9 0.9 %turn.1 = f32[5,64,64]{2,1,0:T(8,128)} custom-call(f32[32,128]{1,0:T(8,128)S(1)} %add.67.refs_0_, f32[32,128]{1,0:T(8,128)S(1)} %add.68.refs_1_, f32[32,128]{1,0:T(8,128)S(1)} %add.69.refs_2_, f32[32,128]{1,0:T(8,128)S(1)} %add.70.refs_3_, f32[32,128]{1,0:T(8,128)S(1)} %add.71.refs_4_), custom_call_target="tpu_custom_call" | custom-call | tf_op jit(solution)/shard_map/turn/pallas_call | solution.py:488
  (18 shorter events, 0.7 us)
Async XLA Ops:
  0.6 15.9 %collective-permute-start.1 = (bf16[64,4096]{1,0:T(8,128)(2,1)}, bf16[64,4096]{1,0:T(8,128)(2,1)S(1)}, u32[]{:S(2)}, u32[]{:S(2)}) collective-permute-start(bf16[64,4096]{1,0:T(8,128)(2,1)} %bitcast.31), channel_id=1, source_target_pairs={{0,8},{16,24},{32,40},{48,56},{64,72},{80,88},{96,104},{112,120},{... | collective-permute-start | bytes 1572872 | tf_op jit(solution)/shard_map/ppermute | solution.py:414
  2.3 16.2 %collective-permute-start = (bf16[64,4096]{1,0:T(8,128)(2,1)}, bf16[64,4096]{1,0:T(8,128)(2,1)S(1)}, u32[]{:S(2)}, u32[]{:S(2)}) collective-permute-start(bf16[64,4096]{1,0:T(8,128)(2,1)} %bitcast.32), channel_id=1, source_target_pairs={{8,16},{24,32},{40,48},{56,64},{72,80},{88,96},{104,112},{120,128}... | collective-permute-start | bytes 1572872 | tf_op jit(solution)/shard_map/ppermute | solution.py:414
  19.2 6.2 %collective-permute-start.6 = (f32[32,128]{1,0:T(8,128)S(1)}, f32[32,128]{1,0:T(8,128)S(1)}, u32[]{:S(2)}, u32[]{:S(2)}) collective-permute-start(f32[32,128]{1,0:T(8,128)S(1)} %get-tuple-element.28), channel_id=1, source_target_pairs={{0,8},{8,0},{16,24},{24,16},{32,40},{40,32},{48,56},{56,48},{64,72... | collective-permute-start | bytes 49160 | tf_op jit(solution)/shard_map/ppermute | solution.py:409
  25.1 8.9 %collective-permute-start.2 = (f32[4,8,16,128]{3,2,1,0:T(8,128)S(1)}, f32[4,8,16,128]{3,2,1,0:T(8,128)S(1)}, u32[]{:S(2)}, u32[]{:S(2)}) collective-permute-start(f32[4,8,16,128]{3,2,1,0:T(8,128)S(1)} %get-tuple-element.27), channel_id=1, source_target_pairs={{0,1},{1,0},{2,3},{3,2},{4,5},{5,4},{6,7},{7,6},{8,9},{9,8},{10,11... | collective-permute-start | bytes 786440 | tf_op jit(solution)/shard_map/ppermute | solution.py:409
  25.5 6.2 %collective-permute-start.7 = (f32[32,128]{1,0:T(8,128)S(1)}, f32[32,128]{1,0:T(8,128)S(1)}, u32[]{:S(2)}, u32[]{:S(2)}) collective-permute-start(f32[32,128]{1,0:T(8,128)S(1)} %fusion.9), channel_id=1, source_target_pairs={{0,24},{8,16},{16,8},{24,0},{32,56},{40,48},{48,40},{56,32},{64,88... | collective-permute-start | bytes 49160 | tf_op jit(solution)/shard_map/ppermute | solution.py:409
  31.9 3.8 %collective-permute-start.8 = (f32[32,128]{1,0:T(8,128)S(1)}, f32[32,128]{1,0:T(8,128)S(1)}, u32[]{:S(2)}, u32[]{:S(2)}) collective-permute-start(f32[32,128]{1,0:T(8,128)S(1)} %fusion.7), channel_id=1, source_target_pairs={{0,32},{8,40},{16,48},{24,56},{32,0},{40,8},{48,16},{56,24},{64,96... | collective-permute-start | bytes 49160 | tf_op jit(solution)/shard_map/ppermute | solution.py:409
  34.0 9.9 %collective-permute-start.3 = (f32[8,16,128]{2,1,0:T(8,128)S(1)}, f32[8,16,128]{2,1,0:T(8,128)S(1)}, u32[]{:S(2)}, u32[]{:S(2)}) collective-permute-start(f32[8,16,128]{2,1,0:T(8,128)S(1)} %get-tuple-element.35), channel_id=1, source_target_pairs={{0,2},{1,3},{2,0},{3,1},{4,6},{5,7},{6,4},{7,5},{8,10},{9,11},{10,... | collective-permute-start | bytes 196616 | tf_op jit(solution)/shard_map/ppermute | solution.py:409
  35.9 8.0 %collective-permute-start.9 = (f32[32,128]{1,0:T(8,128)S(1)}, f32[32,128]{1,0:T(8,128)S(1)}, u32[]{:S(2)}, u32[]{:S(2)}) collective-permute-start(f32[32,128]{1,0:T(8,128)S(1)} %fusion.5), channel_id=1, source_target_pairs={{0,64},{8,72},{16,80},{24,88},{32,96},{40,104},{48,112},{56,120},{... | collective-permute-start | bytes 49160 | tf_op jit(solution)/shard_map/ppermute | solution.py:409
  40.3 7.5 %collective-permute-start.4 = (f32[8,16,128]{2,1,0:T(8,128)S(1)}, f32[8,16,128]{2,1,0:T(8,128)S(1)}, u32[]{:S(2)}, u32[]{:S(2)}) collective-permute-start(f32[8,16,128]{2,1,0:T(8,128)S(1)} %get-tuple-element.34), channel_id=1, source_target_pairs={{0,4},{1,5},{2,6},{3,7},{4,0},{5,1},{6,2},{7,3},{8,12},{9,13},{10,... | collective-permute-start | bytes 196616 | tf_op jit(solution)/shard_map/ppermute | solution.py:409
  41.7 6.1 %collective-permute-start.5 = (f32[8,16,128]{2,1,0:T(8,128)S(1)}, f32[8,16,128]{2,1,0:T(8,128)S(1)}, u32[]{:S(2)}, u32[]{:S(2)}) collective-permute-start(f32[8,16,128]{2,1,0:T(8,128)S(1)} %get-tuple-element.33), channel_id=1, source_target_pairs={{0,6},{1,7},{2,4},{3,5},{4,2},{5,3},{6,0},{7,1},{8,14},{9,15},{10,... | collective-permute-start | bytes 196616 | tf_op jit(solution)/shard_map/ppermute | solution.py:409
  44.0 5.9 %collective-permute-start.10 = (f32[32,128]{1,0:T(8,128)S(1)}, f32[32,128]{1,0:T(8,128)S(1)}, u32[]{:S(2)}, u32[]{:S(2)}) collective-permute-start(f32[32,128]{1,0:T(8,128)S(1)} %fusion.3), channel_id=1, source_target_pairs={{0,192},{8,200},{16,208},{24,216},{32,224},{40,232},{48,240},{56,2... | collective-permute-start | bytes 49160 | tf_op jit(solution)/shard_map/ppermute | solution.py:409

commit v7 on v6

--- a/solution.py
+++ b/solution.py
@@ -170,10 +170,10 @@
     pairs = (
         (index_any, index_ref),
         (number_any, number_ref),
+        (basis_any, basis_ref),
         (own_any, own_ref),
         (samples_any, samples_ref),
         (blocks_any, blocks_ref),
-        (basis_any, basis_ref),
         (lists.at[0], own_task),
         (lists.at[1], first_task_ref),
         (lists.at[2], second_task_ref),
@@ -192,20 +192,21 @@
     list_tasks(index_ref[...], number_ref[...], lax.axis_index("leaf"), lists)
     for copy in copies[6:]:
         copy.start()
+    copies[2].wait()
+    path_products(upper_ref, mats_ref, basis_ref, weight_ref)
     for height in range(1, upper_ref.shape[0]):
         matrix = upper_ref[height].astype(jnp.float32)
         blank = jnp.zeros_like(matrix)
         twice_ref[height - 1, :rank] = jnp.concatenate([matrix, blank], axis=1)
         twice_ref[height - 1, rank:] = jnp.concatenate([blank, matrix], axis=1)
-    copies[2].wait()
+    copies[3].wait()
     spread(source, 0, own_ref, size)
     source[count] = jnp.zeros_like(source[count])
-    copies[3].wait()
+    copies[4].wait()
     for leaf in range(count):
         acc_ref[leaf] = samples_ref[:, leaf * size : (leaf + 1) * size].astype(jnp.float32)
-    for copy in copies[4:]:
+    for copy in copies[5:]:
         copy.wait()
-    path_products(upper_ref, mats_ref, basis_ref, weight_ref)
     subtract_near(count, own_task, source, blocks_ref, acc_ref, slots)
 
 
@@ -431,16 +432,16 @@
     second = swap(own, "leaf", 0)
 
     heights = groups.bit_length() - 1
-    rows = []
+    nodes = []
     offset, width = 0, groups
     for height in range(heights):
-        rows.append(
-            lax.dynamic_slice_in_dim(
-                upper_transfer, offset + jnp.right_shift(device, height), 1, axis=0
-            )
-        )
+        node = jnp.right_shift(device, height)
+        nodes.append(offset + node)
+        if height == 1:
+            sibling = offset + jnp.bitwise_xor(node, 1)
         offset, width = offset + width, width // 2
-    upper = jnp.concatenate(rows, axis=0).reshape(heights, rank, rank)
+    rows = [lax.dynamic_slice_in_dim(upper_transfer, n, 1, axis=0) for n in nodes + [sibling]]
+    upper = jnp.concatenate(rows, axis=0).reshape(heights + 1, rank, rank)
 
     blocks = near_blocks.reshape(count * slots, size, size)
     near, blocks, basis, weight, twice, crossing_tasks, tasks = own_pass(
@@ -456,17 +457,19 @@
     near = side_pass(tasks, second, near, blocks)
     far, part, _ = far_pass(crossing_tasks, first, near, blocks, weight)
 
-    flips = (1, 3, 4, 8, 24)
-    levels = []
-    accum = part
-    for height in range(heights):
-        if height:
-            accum = jnp.dot(accum, twice[height - 1], precision=lax.Precision.HIGHEST)
-        other = exchange(accum, "leaf", flips[height])
-        if height == 0:
-            coeffs, keep, send = gram_pass(place.reshape(1), far, basis, parts)
-            got = exchange(send, "samp", 1)
-        elif height == 2:
+    def step(value, matrix):
+        return jnp.dot(value, matrix, precision=lax.Precision.HIGHEST)
+
+    third, other, fourth = (exchange(part, "leaf", flip) for flip in (2, 1, 3))
+    coeffs, keep, send = gram_pass(place.reshape(1), far, basis, parts)
+    got = exchange(send, "samp", 1)
+    levels = [part + other]
+    levels.append(step(levels[0], twice[0]) + step(third + fourth, twice[heights - 1]))
+    flips = (4, 8, 24)
+    for height, flip in enumerate(flips, 2):
+        accum = step(levels[-1], twice[height - 1])
+        other = exchange(accum, "leaf", flip)
+        if height == 2:
             leaving = keep[1] + got[1]
             other, _ = lax.optimization_barrier((other, leaving))
             received = [exchange(leaving, "samp", 2)]
@@ -483,8 +486,7 @@
                 name="finish",
             )(keep, *map(resident, [got] + received))
             other, _ = lax.optimization_barrier((other, leaf_gram))
-        accum = accum + other
-        levels.append(accum)
+        levels.append(accum + other)
     ancestors = pl.pallas_call(
         turn_kernel,
         in_specs=[VMEM] * heights,

time: 51.7 us -> 50.9 us (0.985)
  the two profiles are of different devices: /device:TPU:6 before, /device:TPU:32 now
where the time goes in v7:
time: 50.9 us; the launch traced here: 50.8 us
  starting transfers between devices  22.8 us (45%)
  Pallas kernels  14 us (28%)
  waiting for transfers between devices  8.94 us (18%)
  local copies, waits for them, and re-layouts  3.4 us (7%)
  matrix products  0.8 us (2%)
  between operations  0.8 us (2%)
    ppermute x10, starting transfers between devices, exchange(): lax.ppermute(value, axis, [(i, i ^ flip) for i in range(lax.axis_size(axi...  17.5 us
    pallas_call x1, Pallas kernels, own_pass(): pl.pallas_call(own_kernel, in_specs=[ANY, ANY, VMEM, VMEM, ANY, ANY, ANY,...  7.47 us
    ppermute x10, waiting for transfers between devices, exchange(): lax.ppermute(value, axis, [(i, i ^ flip) for i in range(lax.axis_size(axi...  7.23 us
    ppermute x2, starting transfers between devices, swap(): return lax.ppermute(value, axis, pairs + [(j, i) for i, j in pairs])  5.29 us
    pallas_call x1, Pallas kernels, far_pass(): pl.pallas_call(far_kernel, in_specs=[SMEM] + [VMEM] * 4, out_specs=(VMEM,...  2.15 us
    reshape x1, local copies, waits for them, and re-layouts, shards(): inner_transfer.reshape(-1, rank)  2.03 us
    ppermute x2, waiting for transfers between devices, swap(): return lax.ppermute(value, axis, pairs + [(j, i) for i, j in pairs])  1.71 us
    pallas_call x1, Pallas kernels, gram_pass(): pl.pallas_call(functools.partial(gram_kernel, 1.0 / (columns * parts)), i...  1.44 us
  transfers between devices with their start and end apart: 12, of which 5 were waited for; matrix products, arithmetic and copies ran while one was open for 8% of the time, Pallas kernels for 22%

profile of v7, /device:TPU:32, one launch (start us, length us, event | category | flops | bytes accessed | tf_op | source)
XLA Modules:
  0.0 50.8 jit_solution(2847665187192534897)
XLA Ops:
  0.6 1.7 %collective-permute-start.1 = (bf16[64,4096]{1,0:T(8,128)(2,1)}, bf16[64,4096]{1,0:T(8,128)(2,1)S(1)}, u32[]{:S(2)}, u32[]{:S(2)}) collective-permute-start(bf16[64,4096]{1,0:T(8,128)(2,1)} %bitcast.34), channel_id=1, source_target_pairs={{0,8},{16,24},{32,40},{48,56},{64,72},{80,88},{96,104},{112,120},{... | collective-permute-start | bytes 1572872 | tf_op jit(solution)/shard_map/ppermute | solution.py:415
  2.3 3.6 %collective-permute-start = (bf16[64,4096]{1,0:T(8,128)(2,1)}, bf16[64,4096]{1,0:T(8,128)(2,1)S(1)}, u32[]{:S(2)}, u32[]{:S(2)}) collective-permute-start(bf16[64,4096]{1,0:T(8,128)(2,1)} %bitcast.35), channel_id=1, source_target_pairs={{8,16},{24,32},{40,48},{56,64},{72,80},{88,96},{104,112},{120,128}... | collective-permute-start | bytes 1572872 | tf_op jit(solution)/shard_map/ppermute | solution.py:415
  5.9 1.1 %constant_dynamic-slice_fusion = (bf16[1,4096]{1,0:T(2,128)(2,1)S(1)}, bf16[1,4096]{1,0:T(2,128)(2,1)S(1)}, bf16[1,4096]{1,0:T(2,128)(2,1)S(1)}, bf16[1,4096]{1,...) fusion(bf16[62,4096]{1,0:T(8,128)(2,1)} %param.15, s32[]{:T(128)S(6)} %select_n.23, ...), kind=kLoop, calls=%fused_computation.22 | loop fusion | bytes 98328 | tf_op jit(solution)/shard_map/dynamic_slice | solution.py:443
  7.3 2.0 %reshape.27.mats_ref = bf16[3968,64]{1,0:T(8,128)(2,1)S(1)} reshape(bf16[62,4096]{1,0:T(8,128)(2,1)} %param.14) | data formatting | bytes 1015808 | tf_op jit(solution)/shard_map/reshape | solution.py:451
  9.4 7.5 %own_pass.1 = (f32[32,64,128]{2,1,0:T(8,128)S(1)}, bf16[256,128,128]{2,1,0:T(8,128)(2,1)S(1)}, bf16[32,64,128]{2,1,0:T(8,128)(2,1)S(1)}, bf16[128,4096]{1,0:T(8,...) custom-call(s32[8,32]{1,0:T(8,128)} %bitcast.38, s32[1,32]{1,0:T(1,128)} %bitcast.39, ...), custom_call_target="tpu_custom_call" | custom-call | tf_op jit(solution)/shard_map/own_pass/pallas_call | solution.py:310
  16.9 1.3 %side_pass.1.near_ref = f32[32,64,128]{2,1,0:T(8,128)S(1)} custom-call(s32[8,128]{1,0:T(8,128)S(4)} %get-tuple-element.19.task_ref, bf16[64,4096]{1,0:T(8,128)(2,1)S(1)} %collective-permute-done.1.side_ref, f32[32,64,128]{2,1,0:T(8,128)S(1)} %get-tuple-element.20.near_ref, ...), custom_call_target="tpu_custom_call", output_to_operand_aliasing={{}: (2, {})} | custom-call | tf_op jit(solution)/shard_map/side_pass/pallas_call | solution.py:354
  18.2 1.7 %collective-permute-done.side_ref = bf16[64,4096]{1,0:T(8,128)(2,1)S(1)} collective-permute-done((bf16[64,4096]{1,0:T(8,128)(2,1)}, bf16[64,4096]{1,0:T(8,128)(2,1)S(1)}, u32[]{:S(2)}, u32[]{:S(2)}) %collective-permute-start) | collective-permute-done | bytes 524320 | tf_op jit(solution)/shard_map/ppermute | solution.py:415
  19.9 2.2 %far_pass.1 = (bf16[64,4096]{1,0:T(8,128)(2,1)S(1)}, f32[32,128]{1,0:T(8,128)S(1)}, f32[32,64,128]{2,1,0:T(8,128)S(1)}) custom-call(s32[8,128]{1,0:T(8,128)S(4)} %get-tuple-element.18.task_ref, bf16[64,4096]{1,0:T(8,128)(2,1)S(1)} %collective-permute-done.side_ref, f32[32,64,128]{2,1,0:T(8,128)S(1)} %side_pass.1.near_ref, ...), custom_call_target="tpu_custom_call", output_to_operand_aliasing={{2}: (2, {})} | custom-call | tf_op jit(solution)/shard_map/far_pass/pallas_call | solution.py:369
  22.1 3.3 %collective-permute-start.7 = (f32[32,128]{1,0:T(8,128)S(1)}, f32[32,128]{1,0:T(8,128)S(1)}, u32[]{:S(2)}, u32[]{:S(2)}) collective-permute-start(f32[32,128]{1,0:T(8,128)S(1)} %get-tuple-element.28), channel_id=1, source_target_pairs={{0,16},{8,24},{16,0},{24,8},{32,48},{40,56},{48,32},{56,40},{64,80... | collective-permute-start | bytes 49160 | tf_op jit(solution)/shard_map/ppermute | solution.py:410
  25.5 1.4 %collective-permute-start.8 = (f32[32,128]{1,0:T(8,128)S(1)}, f32[32,128]{1,0:T(8,128)S(1)}, u32[]{:S(2)}, u32[]{:S(2)}) collective-permute-start(f32[32,128]{1,0:T(8,128)S(1)} %get-tuple-element.28), channel_id=1, source_target_pairs={{0,24},{8,16},{16,8},{24,0},{32,56},{40,48},{48,40},{56,32},{64,88... | collective-permute-start | bytes 49160 | tf_op jit(solution)/shard_map/ppermute | solution.py:410
  26.8 1.4 %gram_pass.1 = (f32[32,64,64]{2,1,0:T(8,128)}, f32[4,8,16,128]{3,2,1,0:T(8,128)S(1)}, f32[4,8,16,128]{3,2,1,0:T(8,128)S(1)}) custom-call(s32[1]{0:T(128)} %bitcast.place_ref, bf16[64,4096]{1,0:T(8,128)(2,1)S(1)} %get-tuple-element.23.far_ref, bf16[32,64,128]{2,1,0:T(8,128)(2,1)S(1)} %get-tuple-element.24.basis_ref), custom_call_target="tpu_custom_call" | custom-call | tf_op jit(solution)/shard_map/gram_pass/pallas_call | solution.py:390
  28.4 2.0 %collective-permute-done.8 = f32[32,128]{1,0:T(8,128)S(1)} collective-permute-done((f32[32,128]{1,0:T(8,128)S(1)}, f32[32,128]{1,0:T(8,128)S(1)}, u32[]{:S(2)}, u32[]{:S(2)}) %collective-permute-start.8) | collective-permute-done | bytes 16416 | tf_op jit(solution)/shard_map/ppermute | solution.py:410
  30.6 0.2 convolution_add_fusion.refs_1_
  30.9 0.2 collective-permute-start.9
  31.2 1.6 %collective-permute-start.3 = (f32[8,16,128]{2,1,0:T(8,128)S(1)}, f32[8,16,128]{2,1,0:T(8,128)S(1)}, u32[]{:S(2)}, u32[]{:S(2)}) collective-permute-start(f32[8,16,128]{2,1,0:T(8,128)S(1)} %get-tuple-element.35), channel_id=1, source_target_pairs={{0,2},{1,3},{2,0},{3,1},{4,6},{5,7},{6,4},{7,5},{8,10},{9,11},{10,... | collective-permute-start | bytes 196616 | tf_op jit(solution)/shard_map/ppermute | solution.py:410
  32.7 2.0 %collective-permute-done.9 = f32[32,128]{1,0:T(8,128)S(1)} collective-permute-done((f32[32,128]{1,0:T(8,128)S(1)}, f32[32,128]{1,0:T(8,128)S(1)}, u32[]{:S(2)}, u32[]{:S(2)}) %collective-permute-start.9) | collective-permute-done | bytes 16416 | tf_op jit(solution)/shard_map/ppermute | solution.py:410
  34.9 4.7 %collective-permute-start.10 = (f32[32,128]{1,0:T(8,128)S(1)}, f32[32,128]{1,0:T(8,128)S(1)}, u32[]{:S(2)}, u32[]{:S(2)}) collective-permute-start(f32[32,128]{1,0:T(8,128)S(1)} %fusion.5), channel_id=1, source_target_pairs={{0,64},{8,72},{16,80},{24,88},{32,96},{40,104},{48,112},{56,120},{... | collective-permute-start | bytes 49160 | tf_op jit(solution)/shard_map/ppermute | solution.py:410
  39.7 3.0 %collective-permute-start.4 = (f32[8,16,128]{2,1,0:T(8,128)S(1)}, f32[8,16,128]{2,1,0:T(8,128)S(1)}, u32[]{:S(2)}, u32[]{:S(2)}) collective-permute-start(f32[8,16,128]{2,1,0:T(8,128)S(1)} %get-tuple-element.34), channel_id=1, source_target_pairs={{0,4},{1,5},{2,6},{3,7},{4,0},{5,1},{6,2},{7,3},{8,12},{9,13},{10,... | collective-permute-start | bytes 196616 | tf_op jit(solution)/shard_map/ppermute | solution.py:410
  42.6 1.1 %collective-permute-start.5 = (f32[8,16,128]{2,1,0:T(8,128)S(1)}, f32[8,16,128]{2,1,0:T(8,128)S(1)}, u32[]{:S(2)}, u32[]{:S(2)}) collective-permute-start(f32[8,16,128]{2,1,0:T(8,128)S(1)} %get-tuple-element.33), channel_id=1, source_target_pairs={{0,6},{1,7},{2,4},{3,5},{4,2},{5,3},{6,0},{7,1},{8,14},{9,15},{10,... | collective-permute-start | bytes 196616 | tf_op jit(solution)/shard_map/ppermute | solution.py:410
  44.0 2.0 %collective-permute-start.11 = (f32[32,128]{1,0:T(8,128)S(1)}, f32[32,128]{1,0:T(8,128)S(1)}, u32[]{:S(2)}, u32[]{:S(2)}) collective-permute-start(f32[32,128]{1,0:T(8,128)S(1)} %fusion.3), channel_id=1, source_target_pairs={{0,192},{8,200},{16,208},{24,216},{32,224},{40,232},{48,240},{56,2... | collective-permute-start | bytes 49160 | tf_op jit(solution)/shard_map/ppermute | solution.py:410
  46.0 2.1 %collective-permute-done.5.refs_2_ = f32[8,16,128]{2,1,0:T(8,128)S(1)} collective-permute-done((f32[8,16,128]{2,1,0:T(8,128)S(1)}, f32[8,16,128]{2,1,0:T(8,128)S(1)}, u32[]{:S(2)}, u32[]{:S(2)}) %collective-permute-start.5) | collective-permute-done | bytes 65568 | tf_op jit(solution)/shard_map/ppermute | solution.py:410
  48.1 0.7 %finish.1 = f32[32,512]{1,0:T(8,128)} custom-call(f32[4,8,16,128]{3,2,1,0:T(8,128)S(1)} %get-tuple-element.26.keep_ref, f32[4,8,16,128]{3,2,1,0:T(8,128)S(1)} %collective-permute-done.2.got_ref, f32[8,16,128]{2,1,0:T(8,128)S(1)} %collective-permute-done.3.refs_0_, f32[8,16,128]{2,1,0:T(8,128)S(1)} %collective-permute-done.4.refs_1_, ...), custom_call_target="tpu_custom_call" | custom-call | tf_op jit(solution)/shard_map/finish/pallas_call | solution.py:480
  48.8 1.1 %collective-permute-done.11 = f32[32,128]{1,0:T(8,128)S(1)} collective-permute-done((f32[32,128]{1,0:T(8,128)S(1)}, f32[32,128]{1,0:T(8,128)S(1)}, u32[]{:S(2)}, u32[]{:S(2)}) %collective-permute-start.11) | collective-permute-done | bytes 16416 | tf_op jit(solution)/shard_map/ppermute | solution.py:410
  49.9 0.9 %turn.1 = f32[5,64,64]{2,1,0:T(8,128)} custom-call(f32[32,128]{1,0:T(8,128)S(1)} %add.84.refs_0_, f32[32,128]{1,0:T(8,128)S(1)} %convolution_add_fusion.refs_1_, f32[32,128]{1,0:T(8,128)S(1)} %add.87.refs_2_, f32[32,128]{1,0:T(8,128)S(1)} %add.88.refs_3_, f32[32,128]{1,0:T(8,128)S(1)} %add.89.refs_4_), custom_call_target="tpu_custom_call" | custom-call | tf_op jit(solution)/shard_map/turn/pallas_call | solution.py:490
  (20 shorter events, 1.1 us)
Async XLA Ops:
  0.6 16.2 %collective-permute-start.1 = (bf16[64,4096]{1,0:T(8,128)(2,1)}, bf16[64,4096]{1,0:T(8,128)(2,1)S(1)}, u32[]{:S(2)}, u32[]{:S(2)}) collective-permute-start(bf16[64,4096]{1,0:T(8,128)(2,1)} %bitcast.34), channel_id=1, source_target_pairs={{0,8},{16,24},{32,40},{48,56},{64,72},{80,88},{96,104},{112,120},{... | collective-permute-start | bytes 1572872 | tf_op jit(solution)/shard_map/ppermute | solution.py:415
  2.3 17.6 %collective-permute-start = (bf16[64,4096]{1,0:T(8,128)(2,1)}, bf16[64,4096]{1,0:T(8,128)(2,1)S(1)}, u32[]{:S(2)}, u32[]{:S(2)}) collective-permute-start(bf16[64,4096]{1,0:T(8,128)(2,1)} %bitcast.35), channel_id=1, source_target_pairs={{8,16},{24,32},{40,48},{56,64},{72,80},{88,96},{104,112},{120,128}... | collective-permute-start | bytes 1572872 | tf_op jit(solution)/shard_map/ppermute | solution.py:415
  22.0 6.3 %collective-permute-start.6 = (f32[32,128]{1,0:T(8,128)S(1)}, f32[32,128]{1,0:T(8,128)S(1)}, u32[]{:S(2)}, u32[]{:S(2)}) collective-permute-start(f32[32,128]{1,0:T(8,128)S(1)} %get-tuple-element.28), channel_id=1, source_target_pairs={{0,8},{8,0},{16,24},{24,16},{32,40},{40,32},{48,56},{56,48},{64,72... | collective-permute-start | bytes 49160 | tf_op jit(solution)/shard_map/ppermute | solution.py:410
  22.1 6.3 %collective-permute-start.7 = (f32[32,128]{1,0:T(8,128)S(1)}, f32[32,128]{1,0:T(8,128)S(1)}, u32[]{:S(2)}, u32[]{:S(2)}) collective-permute-start(f32[32,128]{1,0:T(8,128)S(1)} %get-tuple-element.28), channel_id=1, source_target_pairs={{0,16},{8,24},{16,0},{24,8},{32,48},{40,56},{48,32},{56,40},{64,80... | collective-permute-start | bytes 49160 | tf_op jit(solution)/shard_map/ppermute | solution.py:410
  25.5 4.9 %collective-permute-start.8 = (f32[32,128]{1,0:T(8,128)S(1)}, f32[32,128]{1,0:T(8,128)S(1)}, u32[]{:S(2)}, u32[]{:S(2)}) collective-permute-start(f32[32,128]{1,0:T(8,128)S(1)} %get-tuple-element.28), channel_id=1, source_target_pairs={{0,24},{8,16},{16,8},{24,0},{32,56},{40,48},{48,40},{56,32},{64,88... | collective-permute-start | bytes 49160 | tf_op jit(solution)/shard_map/ppermute | solution.py:410
  28.3 2.9 %collective-permute-start.2 = (f32[4,8,16,128]{3,2,1,0:T(8,128)S(1)}, f32[4,8,16,128]{3,2,1,0:T(8,128)S(1)}, u32[]{:S(2)}, u32[]{:S(2)}) collective-permute-start(f32[4,8,16,128]{3,2,1,0:T(8,128)S(1)} %get-tuple-element.27), channel_id=1, source_target_pairs={{0,1},{1,0},{2,3},{3,2},{4,5},{5,4},{6,7},{7,6},{8,9},{9,8},{10,11... | collective-permute-start | bytes 786440 | tf_op jit(solution)/shard_map/ppermute | solution.py:410
  30.9 3.8 %collective-permute-start.9 = (f32[32,128]{1,0:T(8,128)S(1)}, f32[32,128]{1,0:T(8,128)S(1)}, u32[]{:S(2)}, u32[]{:S(2)}) collective-permute-start(f32[32,128]{1,0:T(8,128)S(1)} %fusion.7), channel_id=1, source_target_pairs={{0,32},{8,40},{16,48},{24,56},{32,0},{40,8},{48,16},{56,24},{64,96... | collective-permute-start | bytes 49160 | tf_op jit(solution)/shard_map/ppermute | solution.py:410
  31.2 12.6 %collective-permute-start.3 = (f32[8,16,128]{2,1,0:T(8,128)S(1)}, f32[8,16,128]{2,1,0:T(8,128)S(1)}, u32[]{:S(2)}, u32[]{:S(2)}) collective-permute-start(f32[8,16,128]{2,1,0:T(8,128)S(1)} %get-tuple-element.35), channel_id=1, source_target_pairs={{0,2},{1,3},{2,0},{3,1},{4,6},{5,7},{6,4},{7,5},{8,10},{9,11},{10,... | collective-permute-start | bytes 196616 | tf_op jit(solution)/shard_map/ppermute | solution.py:410
  34.9 8.9 %collective-permute-start.10 = (f32[32,128]{1,0:T(8,128)S(1)}, f32[32,128]{1,0:T(8,128)S(1)}, u32[]{:S(2)}, u32[]{:S(2)}) collective-permute-start(f32[32,128]{1,0:T(8,128)S(1)} %fusion.5), channel_id=1, source_target_pairs={{0,64},{8,72},{16,80},{24,88},{32,96},{40,104},{48,112},{56,120},{... | collective-permute-start | bytes 49160 | tf_op jit(solution)/shard_map/ppermute | solution.py:410
  39.7 6.3 %collective-permute-start.4 = (f32[8,16,128]{2,1,0:T(8,128)S(1)}, f32[8,16,128]{2,1,0:T(8,128)S(1)}, u32[]{:S(2)}, u32[]{:S(2)}) collective-permute-start(f32[8,16,128]{2,1,0:T(8,128)S(1)} %get-tuple-element.34), channel_id=1, source_target_pairs={{0,4},{1,5},{2,6},{3,7},{4,0},{5,1},{6,2},{7,3},{8,12},{9,13},{10,... | collective-permute-start | bytes 196616 | tf_op jit(solution)/shard_map/ppermute | solution.py:410
  42.6 5.5 %collective-permute-start.5 = (f32[8,16,128]{2,1,0:T(8,128)S(1)}, f32[8,16,128]{2,1,0:T(8,128)S(1)}, u32[]{:S(2)}, u32[]{:S(2)}) collective-permute-start(f32[8,16,128]{2,1,0:T(8,128)S(1)} %get-tuple-element.33), channel_id=1, source_target_pairs={{0,6},{1,7},{2,4},{3,5},{4,2},{5,3},{6,0},{7,1},{8,14},{9,15},{10,... | collective-permute-start | bytes 196616 | tf_op jit(solution)/shard_map/ppermute | solution.py:410
  44.0 5.9 %collective-permute-start.11 = (f32[32,128]{1,0:T(8,128)S(1)}, f32[32,128]{1,0:T(8,128)S(1)}, u32[]{:S(2)}, u32[]{:S(2)}) collective-permute-start(f32[32,128]{1,0:T(8,128)S(1)} %fusion.3), channel_id=1, source_target_pairs={{0,192},{8,200},{16,208},{24,216},{32,224},{40,232},{48,240},{56,2... | collective-permute-start | bytes 49160 | tf_op jit(solution)/shard_map/ppermute | solution.py:410

commit v8 on v6

--- a/solution.py
+++ b/solution.py
@@ -170,10 +170,10 @@
     pairs = (
         (index_any, index_ref),
         (number_any, number_ref),
+        (basis_any, basis_ref),
         (own_any, own_ref),
         (samples_any, samples_ref),
         (blocks_any, blocks_ref),
-        (basis_any, basis_ref),
         (lists.at[0], own_task),
         (lists.at[1], first_task_ref),
         (lists.at[2], second_task_ref),
@@ -192,20 +192,21 @@
     list_tasks(index_ref[...], number_ref[...], lax.axis_index("leaf"), lists)
     for copy in copies[6:]:
         copy.start()
+    copies[2].wait()
+    path_products(upper_ref, mats_ref, basis_ref, weight_ref)
     for height in range(1, upper_ref.shape[0]):
         matrix = upper_ref[height].astype(jnp.float32)
         blank = jnp.zeros_like(matrix)
         twice_ref[height - 1, :rank] = jnp.concatenate([matrix, blank], axis=1)
         twice_ref[height - 1, rank:] = jnp.concatenate([blank, matrix], axis=1)
-    copies[2].wait()
+    copies[3].wait()
     spread(source, 0, own_ref, size)
     source[count] = jnp.zeros_like(source[count])
-    copies[3].wait()
+    copies[4].wait()
     for leaf in range(count):
         acc_ref[leaf] = samples_ref[:, leaf * size : (leaf + 1) * size].astype(jnp.float32)
-    for copy in copies[4:]:
+    for copy in copies[5:]:
         copy.wait()
-    path_products(upper_ref, mats_ref, basis_ref, weight_ref)
     subtract_near(count, own_task, source, blocks_ref, acc_ref, slots)
 
 
@@ -273,15 +274,18 @@
         copy.wait()
 
 
-def finish_kernel(keep_ref, got_ref, *refs):
-    others, out_ref = refs[:-1], refs[-1]
+def finish_kernel(keep_ref, got_ref, received_ref, last_ref, out_ref):
     _, rows, pairs, width = keep_ref.shape
     half = width // 2
     lane = lax.broadcasted_iota(jnp.int32, (pairs, width), 1)
     for row in range(0, rows, 2):
-        even, odd = (keep_ref[0, at] + got_ref[0, at] for at in (row, row + 1))
-        for other in others:
-            even, odd = even + other[row], odd + other[row + 1]
+        even, odd = (
+            keep_ref[0, at]
+            + got_ref[0, at]
+            + received_ref[0, at].astype(jnp.float32)
+            + last_ref[at]
+            for at in (row, row + 1)
+        )
         at = slice(row * half, (row + 2) * half)
         out_ref[:pairs, at] = jnp.where(lane < half, even, pltpu.roll(odd, half, 1))
         out_ref[pairs:, at] = jnp.where(lane < half, pltpu.roll(even, half, 1), odd)
@@ -467,21 +471,22 @@
             coeffs, keep, send = gram_pass(place.reshape(1), far, basis, parts)
             got = exchange(send, "samp", 1)
         elif height == 2:
-            leaving = keep[1] + got[1]
+            leaving = (keep[1:3] + got[1:3]).astype(jnp.bfloat16)
             other, _ = lax.optimization_barrier((other, leaving))
-            received = [exchange(leaving, "samp", 2)]
+            received = exchange(leaving, "samp", 2)
         elif height == 3:
-            received += [exchange(keep[x] + got[x], "samp", 2 * x) for x in (2, 3)]
-            other, _ = lax.optimization_barrier((other, received[0]))
+            leaving = keep[3] + got[3] + received[1].astype(jnp.float32)
+            other, _ = lax.optimization_barrier((other, leaving))
+            last = exchange(leaving, "samp", 6)
         elif height == 4:
             leaf_gram = pl.pallas_call(
                 finish_kernel,
-                in_specs=[VMEM] * 5,
+                in_specs=[VMEM] * 4,
                 out_specs=VMEM,
                 out_shape=jax.ShapeDtypeStruct((count, rank * rank // parts), jnp.float32),
                 compiler_params=params(8),
                 name="finish",
-            )(keep, *map(resident, [got] + received))
+            )(keep, *map(resident, [got, received, last]))
             other, _ = lax.optimization_barrier((other, leaf_gram))
         accum = accum + other
         levels.append(accum)

time: 51.7 us -> 49.2 us (0.952); the launches traced: 50.8 us -> 49 us
  Pallas kernels: 15.8 us -> 13.4 us
  waiting for transfers between devices: 4.14 us -> 5.29 us
    pallas_call x1, Pallas kernels: 10.2 us -> 7.78 us  [own_pass(): pl.pallas_call(own_kernel, in_specs=[ANY, ANY, VMEM, VMEM, ANY, ANY, ANY,...]
    ppermute x9 -> x8, waiting for transfers between devices: 4.13 us -> 4.81 us  [exchange(): lax.ppermute(value, axis, [(i, i ^ flip) for i in range(lax.axis_size(axi...]
    ppermute x9 -> x8, starting transfers between devices: 23.8 us -> 23.2 us  [exchange(): lax.ppermute(value, axis, [(i, i ^ flip) for i in range(lax.axis_size(axi...]
  transfers between devices with their start and end apart: 11 -> 10, of which waited for: 4 -> 6; matrix products, arithmetic and copies ran while one was open for 8% -> 8% of each run, Pallas kernels for 28% -> 24%
where the time goes in v8:
time: 49.2 us; the launch traced here: 49 us
  starting transfers between devices  25.6 us (52%)
  Pallas kernels  13.4 us (27%)
  waiting for transfers between devices  5.29 us (11%)
  local copies, waits for them, and re-layouts  3.32 us (7%)
  between operations  0.75 us (2%)
  matrix products  0.62 us (1%)
    ppermute x8, starting transfers between devices, exchange(): lax.ppermute(value, axis, [(i, i ^ flip) for i in range(lax.axis_size(axi...  23.2 us
    pallas_call x1, Pallas kernels, own_pass(): pl.pallas_call(own_kernel, in_specs=[ANY, ANY, VMEM, VMEM, ANY, ANY, ANY,...  7.78 us
    ppermute x8, waiting for transfers between devices, exchange(): lax.ppermute(value, axis, [(i, i ^ flip) for i in range(lax.axis_size(axi...  4.81 us
    ppermute x2, starting transfers between devices, swap(): return lax.ppermute(value, axis, pairs + [(j, i) for i, j in pairs])  2.35 us
    reshape x1, local copies, waits for them, and re-layouts, shards(): inner_transfer.reshape(-1, rank)  2.03 us
    pallas_call x1, Pallas kernels, side_pass(): pl.pallas_call(kernel, in_specs=[SMEM] + [VMEM] * 3, out_specs=VMEM, out_...  1.92 us
    pallas_call x1, Pallas kernels, gram_pass(): pl.pallas_call(functools.partial(gram_kernel, 1.0 / (columns * parts)), i...  1.44 us
    dynamic_slice x1, local copies, waits for them, and re-layouts, shards(): lax.dynamic_slice_in_dim(upper_transfer, offset + jnp.right_shift(device,...  1.07 us
  transfers between devices with their start and end apart: 10, of which 6 were waited for; matrix products, arithmetic and copies ran while one was open for 8% of the time, Pallas kernels for 24%

profile of v8, /device:TPU:6, one launch (start us, length us, event | category | flops | bytes accessed | tf_op | source)
XLA Modules:
  0.0 49.0 jit_solution(3045649235147035950)
XLA Ops:
  0.6 1.7 %collective-permute-start.1 = (bf16[64,4096]{1,0:T(8,128)(2,1)}, bf16[64,4096]{1,0:T(8,128)(2,1)S(1)}, u32[]{:S(2)}, u32[]{:S(2)}) collective-permute-start(bf16[64,4096]{1,0:T(8,128)(2,1)} %bitcast.27), channel_id=1, source_target_pairs={{0,8},{16,24},{32,40},{48,56},{64,72},{80,88},{96,104},{112,120},{... | collective-permute-start | bytes 1572872 | tf_op jit(solution)/shard_map/ppermute | solution.py:418
  2.3 0.7 %collective-permute-start = (bf16[64,4096]{1,0:T(8,128)(2,1)}, bf16[64,4096]{1,0:T(8,128)(2,1)S(1)}, u32[]{:S(2)}, u32[]{:S(2)}) collective-permute-start(bf16[64,4096]{1,0:T(8,128)(2,1)} %bitcast.28), channel_id=1, source_target_pairs={{8,16},{24,32},{40,48},{56,64},{72,80},{88,96},{104,112},{120,128}... | collective-permute-start | bytes 1572872 | tf_op jit(solution)/shard_map/ppermute | solution.py:418
  3.0 1.1 %constant_dynamic-slice_fusion = (bf16[1,4096]{1,0:T(2,128)(2,1)S(1)}, bf16[1,4096]{1,0:T(2,128)(2,1)S(1)}, bf16[1,4096]{1,0:T(2,128)(2,1)S(1)}, bf16[1,4096]{1,0:T(2,128)(2,1)S(1)}, bf16[1,4096]{1,0:T(2,128)(2,1)S(1)}) fusion(bf16[62,4096]{1,0:T(8,128)(2,1)} %param.15, s32[]{:T(128)S(6)} %select_n.19, s32[]{:T(128)S(6)} %select_n.17, s32[]{:T(128)S(6)} %select_n.16, ...), kind=kLoop, calls=%fused_computation.17 | loop fusion | bytes 81940 | tf_op jit(solution)/shard_map/dynamic_slice | solution.py:442
  4.3 2.0 %reshape.27.mats_ref = bf16[3968,64]{1,0:T(8,128)(2,1)S(1)} reshape(bf16[62,4096]{1,0:T(8,128)(2,1)} %param.14) | data formatting | bytes 1015808 | tf_op jit(solution)/shard_map/reshape | solution.py:454
  6.3 7.8 %own_pass.1 = (f32[32,64,128]{2,1,0:T(8,128)S(1)}, bf16[256,128,128]{2,1,0:T(8,128)(2,1)S(1)}, bf16[32,64,128]{2,1,0:T(8,128)(2,1)S(1)}, bf16[128,4096]{1,0:T(8,...) custom-call(s32[8,32]{1,0:T(8,128)} %bitcast.31, s32[1,32]{1,0:T(1,128)} %bitcast.32, ...), custom_call_target="tpu_custom_call" | custom-call | tf_op jit(solution)/shard_map/own_pass/pallas_call | solution.py:313
  14.1 0.5 collective-permute-done.1.side_ref
  14.6 1.9 %side_pass.1.near_ref = f32[32,64,128]{2,1,0:T(8,128)S(1)} custom-call(s32[8,128]{1,0:T(8,128)S(4)} %get-tuple-element.19.task_ref, bf16[64,4096]{1,0:T(8,128)(2,1)S(1)} %collective-permute-done.1.side_ref, f32[32,64,128]{2,1,0:T(8,128)S(1)} %get-tuple-element.20.near_ref, ...), custom_call_target="tpu_custom_call", output_to_operand_aliasing={{}: (2, {})} | custom-call | tf_op jit(solution)/shard_map/side_pass/pallas_call | solution.py:357
  16.5 0.6 %far_pass.1 = (bf16[64,4096]{1,0:T(8,128)(2,1)S(1)}, f32[32,128]{1,0:T(8,128)S(1)}, f32[32,64,128]{2,1,0:T(8,128)S(1)}) custom-call(s32[8,128]{1,0:T(8,128)S(4)} %get-tuple-element.18.task_ref, bf16[64,4096]{1,0:T(8,128)(2,1)S(1)} %collective-permute-done.side_ref, f32[32,64,128]{2,1,0:T(8,128)S(1)} %side_pass.1.near_ref, ...), custom_call_target="tpu_custom_call", output_to_operand_aliasing={{2}: (2, {})} | custom-call | tf_op jit(solution)/shard_map/far_pass/pallas_call | solution.py:372
  17.2 3.4 %collective-permute-start.5 = (f32[32,128]{1,0:T(8,128)S(1)}, f32[32,128]{1,0:T(8,128)S(1)}, u32[]{:S(2)}, u32[]{:S(2)}) collective-permute-start(f32[32,128]{1,0:T(8,128)S(1)} %get-tuple-element.28), channel_id=1, source_target_pairs={{0,8},{8,0},{16,24},{24,16},{32,40},{40,32},{48,56},{56,48},{64,72... | collective-permute-start | bytes 49160 | tf_op jit(solution)/shard_map/ppermute | solution.py:413
  20.6 1.4 %gram_pass.1 = (f32[32,64,64]{2,1,0:T(8,128)}, f32[4,8,16,128]{3,2,1,0:T(8,128)S(1)}, f32[4,8,16,128]{3,2,1,0:T(8,128)S(1)}) custom-call(s32[1]{0:T(128)} %bitcast.place_ref, bf16[64,4096]{1,0:T(8,128)(2,1)S(1)} %get-tuple-element.23.far_ref, bf16[32,64,128]{2,1,0:T(8,128)(2,1)S(1)} %get-tuple-element.24.basis_ref), custom_call_target="tpu_custom_call" | custom-call | tf_op jit(solution)/shard_map/gram_pass/pallas_call | solution.py:393
  22.1 0.2 collective-permute-done.5
  22.4 5.9 %collective-permute-start.6 = (f32[32,128]{1,0:T(8,128)S(1)}, f32[32,128]{1,0:T(8,128)S(1)}, u32[]{:S(2)}, u32[]{:S(2)}) collective-permute-start(f32[32,128]{1,0:T(8,128)S(1)} %fusion.9), channel_id=1, source_target_pairs={{0,24},{8,16},{16,8},{24,0},{32,56},{40,48},{48,40},{56,32},{64,88... | collective-permute-start | bytes 49160 | tf_op jit(solution)/shard_map/ppermute | solution.py:413
  28.3 1.7 %collective-permute-done.6 = f32[32,128]{1,0:T(8,128)S(1)} collective-permute-done((f32[32,128]{1,0:T(8,128)S(1)}, f32[32,128]{1,0:T(8,128)S(1)}, u32[]{:S(2)}, u32[]{:S(2)}) %collective-permute-start.6) | collective-permute-done | bytes 16416 | tf_op jit(solution)/shard_map/ppermute | solution.py:413
  30.2 2.7 %collective-permute-start.7 = (f32[32,128]{1,0:T(8,128)S(1)}, f32[32,128]{1,0:T(8,128)S(1)}, u32[]{:S(2)}, u32[]{:S(2)}) collective-permute-start(f32[32,128]{1,0:T(8,128)S(1)} %fusion.7), channel_id=1, source_target_pairs={{0,32},{8,40},{16,48},{24,56},{32,0},{40,8},{48,16},{56,24},{64,96... | collective-permute-start | bytes 49160 | tf_op jit(solution)/shard_map/ppermute | solution.py:413
  33.0 0.9 %collective-permute-start.3 = (bf16[2,8,16,128]{3,2,1,0:T(8,128)(2,1)S(1)}, bf16[2,8,16,128]{3,2,1,0:T(8,128)(2,1)S(1)}, u32[]{:S(2)}, u32[]{:S(2)}) collective-permute-start(bf16[2,8,16,128]{3,2,1,0:T(8,128)(2,1)S(1)} %fusion), channel_id=1, source_target_pairs={{0,2},{1,3},{2,0},{3,1},{4,6},{5,7},{6,4},{7,5},{8,10},{9,11},{10,... | collective-permute-start | bytes 196616 | tf_op jit(solution)/shard_map/ppermute | solution.py:413
  33.9 0.8 %collective-permute-done.7 = f32[32,128]{1,0:T(8,128)S(1)} collective-permute-done((f32[32,128]{1,0:T(8,128)S(1)}, f32[32,128]{1,0:T(8,128)S(1)}, u32[]{:S(2)}, u32[]{:S(2)}) %collective-permute-start.7) | collective-permute-done | bytes 16416 | tf_op jit(solution)/shard_map/ppermute | solution.py:413
  34.7 0.2 fusion.5
  34.8 3.5 %collective-permute-start.8 = (f32[32,128]{1,0:T(8,128)S(1)}, f32[32,128]{1,0:T(8,128)S(1)}, u32[]{:S(2)}, u32[]{:S(2)}) collective-permute-start(f32[32,128]{1,0:T(8,128)S(1)} %fusion.5), channel_id=1, source_target_pairs={{0,64},{8,72},{16,80},{24,88},{32,96},{40,104},{48,112},{56,120},{... | collective-permute-start | bytes 49160 | tf_op jit(solution)/shard_map/ppermute | solution.py:413
  38.4 0.6 %collective-permute-start.4 = (f32[8,16,128]{2,1,0:T(8,128)S(1)}, f32[8,16,128]{2,1,0:T(8,128)S(1)}, u32[]{:S(2)}, u32[]{:S(2)}) collective-permute-start(f32[8,16,128]{2,1,0:T(8,128)S(1)} %fusion.2), channel_id=1, source_target_pairs={{0,6},{1,7},{2,4},{3,5},{4,2},{5,3},{6,0},{7,1},{8,14},{9,15},{10,... | collective-permute-start | bytes 196616 | tf_op jit(solution)/shard_map/ppermute | solution.py:413
  38.9 1.1 %collective-permute-done.8 = f32[32,128]{1,0:T(8,128)S(1)} collective-permute-done((f32[32,128]{1,0:T(8,128)S(1)}, f32[32,128]{1,0:T(8,128)S(1)}, u32[]{:S(2)}, u32[]{:S(2)}) %collective-permute-start.8) | collective-permute-done | bytes 16416 | tf_op jit(solution)/shard_map/ppermute | solution.py:413
  40.2 6.1 %collective-permute-start.9 = (f32[32,128]{1,0:T(8,128)S(1)}, f32[32,128]{1,0:T(8,128)S(1)}, u32[]{:S(2)}, u32[]{:S(2)}) collective-permute-start(f32[32,128]{1,0:T(8,128)S(1)} %fusion.3), channel_id=1, source_target_pairs={{0,192},{8,200},{16,208},{24,216},{32,224},{40,232},{48,240},{56,2... | collective-permute-start | bytes 49160 | tf_op jit(solution)/shard_map/ppermute | solution.py:413
  46.4 0.7 %finish.1 = f32[32,512]{1,0:T(8,128)} custom-call(f32[4,8,16,128]{3,2,1,0:T(8,128)S(1)} %get-tuple-element.26.keep_ref, f32[4,8,16,128]{3,2,1,0:T(8,128)S(1)} %collective-permute-done.2.got_ref, bf16[2,8,16,128]{3,2,1,0:T(8,128)(2,1)S(1)} %collective-permute-done.3.received_ref, f32[8,16,128]{2,1,0:T(8,128)S(1)} %collective-permute-done.4.last_ref), custom_call_target="tpu_custom_call" | custom-call | tf_op jit(solution)/shard_map/finish/pallas_call | solution.py:482
  47.1 1.0 %collective-permute-done.9 = f32[32,128]{1,0:T(8,128)S(1)} collective-permute-done((f32[32,128]{1,0:T(8,128)S(1)}, f32[32,128]{1,0:T(8,128)S(1)}, u32[]{:S(2)}, u32[]{:S(2)}) %collective-permute-start.9) | collective-permute-done | bytes 16416 | tf_op jit(solution)/shard_map/ppermute | solution.py:413
  48.1 0.9 %turn.1 = f32[5,64,64]{2,1,0:T(8,128)} custom-call(f32[32,128]{1,0:T(8,128)S(1)} %add.60.refs_0_, f32[32,128]{1,0:T(8,128)S(1)} %add.61.refs_1_, f32[32,128]{1,0:T(8,128)S(1)} %add.62.refs_2_, f32[32,128]{1,0:T(8,128)S(1)} %add.63.refs_3_, f32[32,128]{1,0:T(8,128)S(1)} %add.64.refs_4_), custom_call_target="tpu_custom_call" | custom-call | tf_op jit(solution)/shard_map/turn/pallas_call | solution.py:493
  (17 shorter events, 0.8 us)
Async XLA Ops:
  0.6 14.0 %collective-permute-start.1 = (bf16[64,4096]{1,0:T(8,128)(2,1)}, bf16[64,4096]{1,0:T(8,128)(2,1)S(1)}, u32[]{:S(2)}, u32[]{:S(2)}) collective-permute-start(bf16[64,4096]{1,0:T(8,128)(2,1)} %bitcast.27), channel_id=1, source_target_pairs={{0,8},{16,24},{32,40},{48,56},{64,72},{80,88},{96,104},{112,120},{... | collective-permute-start | bytes 1572872 | tf_op jit(solution)/shard_map/ppermute | solution.py:418
  2.3 14.2 %collective-permute-start = (bf16[64,4096]{1,0:T(8,128)(2,1)}, bf16[64,4096]{1,0:T(8,128)(2,1)S(1)}, u32[]{:S(2)}, u32[]{:S(2)}) collective-permute-start(bf16[64,4096]{1,0:T(8,128)(2,1)} %bitcast.28), channel_id=1, source_target_pairs={{8,16},{24,32},{40,48},{56,64},{72,80},{88,96},{104,112},{120,128}... | collective-permute-start | bytes 1572872 | tf_op jit(solution)/shard_map/ppermute | solution.py:418
  17.2 5.1 %collective-permute-start.5 = (f32[32,128]{1,0:T(8,128)S(1)}, f32[32,128]{1,0:T(8,128)S(1)}, u32[]{:S(2)}, u32[]{:S(2)}) collective-permute-start(f32[32,128]{1,0:T(8,128)S(1)} %get-tuple-element.28), channel_id=1, source_target_pairs={{0,8},{8,0},{16,24},{24,16},{32,40},{40,32},{48,56},{56,48},{64,72... | collective-permute-start | bytes 49160 | tf_op jit(solution)/shard_map/ppermute | solution.py:413
  22.0 10.9 %collective-permute-start.2 = (f32[4,8,16,128]{3,2,1,0:T(8,128)S(1)}, f32[4,8,16,128]{3,2,1,0:T(8,128)S(1)}, u32[]{:S(2)}, u32[]{:S(2)}) collective-permute-start(f32[4,8,16,128]{3,2,1,0:T(8,128)S(1)} %get-tuple-element.27), channel_id=1, source_target_pairs={{0,1},{1,0},{2,3},{3,2},{4,5},{5,4},{6,7},{7,6},{8,9},{9,8},{10,11... | collective-permute-start | bytes 786440 | tf_op jit(solution)/shard_map/ppermute | solution.py:413
  22.4 7.6 %collective-permute-start.6 = (f32[32,128]{1,0:T(8,128)S(1)}, f32[32,128]{1,0:T(8,128)S(1)}, u32[]{:S(2)}, u32[]{:S(2)}) collective-permute-start(f32[32,128]{1,0:T(8,128)S(1)} %fusion.9), channel_id=1, source_target_pairs={{0,24},{8,16},{16,8},{24,0},{32,56},{40,48},{48,40},{56,32},{64,88... | collective-permute-start | bytes 49160 | tf_op jit(solution)/shard_map/ppermute | solution.py:413
  30.2 4.5 %collective-permute-start.7 = (f32[32,128]{1,0:T(8,128)S(1)}, f32[32,128]{1,0:T(8,128)S(1)}, u32[]{:S(2)}, u32[]{:S(2)}) collective-permute-start(f32[32,128]{1,0:T(8,128)S(1)} %fusion.7), channel_id=1, source_target_pairs={{0,32},{8,40},{16,48},{24,56},{32,0},{40,8},{48,16},{56,24},{64,96... | collective-permute-start | bytes 49160 | tf_op jit(solution)/shard_map/ppermute | solution.py:413
  33.0 5.4 %collective-permute-start.3 = (bf16[2,8,16,128]{3,2,1,0:T(8,128)(2,1)S(1)}, bf16[2,8,16,128]{3,2,1,0:T(8,128)(2,1)S(1)}, u32[]{:S(2)}, u32[]{:S(2)}) collective-permute-start(bf16[2,8,16,128]{3,2,1,0:T(8,128)(2,1)S(1)} %fusion), channel_id=1, source_target_pairs={{0,2},{1,3},{2,0},{3,1},{4,6},{5,7},{6,4},{7,5},{8,10},{9,11},{10,... | collective-permute-start | bytes 196616 | tf_op jit(solution)/shard_map/ppermute | solution.py:413
  34.8 5.2 %collective-permute-start.8 = (f32[32,128]{1,0:T(8,128)S(1)}, f32[32,128]{1,0:T(8,128)S(1)}, u32[]{:S(2)}, u32[]{:S(2)}) collective-permute-start(f32[32,128]{1,0:T(8,128)S(1)} %fusion.5), channel_id=1, source_target_pairs={{0,64},{8,72},{16,80},{24,88},{32,96},{40,104},{48,112},{56,120},{... | collective-permute-start | bytes 49160 | tf_op jit(solution)/shard_map/ppermute | solution.py:413
  38.4 8.0 %collective-permute-start.4 = (f32[8,16,128]{2,1,0:T(8,128)S(1)}, f32[8,16,128]{2,1,0:T(8,128)S(1)}, u32[]{:S(2)}, u32[]{:S(2)}) collective-permute-start(f32[8,16,128]{2,1,0:T(8,128)S(1)} %fusion.2), channel_id=1, source_target_pairs={{0,6},{1,7},{2,4},{3,5},{4,2},{5,3},{6,0},{7,1},{8,14},{9,15},{10,... | collective-permute-start | bytes 196616 | tf_op jit(solution)/shard_map/ppermute | solution.py:413
  40.2 7.8 %collective-permute-start.9 = (f32[32,128]{1,0:T(8,128)S(1)}, f32[32,128]{1,0:T(8,128)S(1)}, u32[]{:S(2)}, u32[]{:S(2)}) collective-permute-start(f32[32,128]{1,0:T(8,128)S(1)} %fusion.3), channel_id=1, source_target_pairs={{0,192},{8,200},{16,208},{24,216},{32,224},{40,232},{48,240},{56,2... | collective-permute-start | bytes 49160 | tf_op jit(solution)/shard_map/ppermute | solution.py:413

commit v9 on v8

--- a/solution.py
+++ b/solution.py
@@ -269,7 +269,7 @@
         target = send_ref if relative % 2 else keep_ref
         for row in range(rows):
             at = pl.multiple_of((first + row) * pairs, pairs)
-            target[relative // 2, row] = gram[pl.ds(at, pairs), :]
+            target[relative // 2, row] = gram[pl.ds(at, pairs), :].astype(target.dtype)
     for copy in copies:
         copy.wait()
 
@@ -281,7 +281,7 @@
     for row in range(0, rows, 2):
         even, odd = (
             keep_ref[0, at]
-            + got_ref[0, at]
+            + got_ref[0, at].astype(jnp.float32)
             + received_ref[0, at].astype(jnp.float32)
             + last_ref[at]
             for at in (row, row + 1)
@@ -397,7 +397,7 @@
         out_shape=(
             pltpu.HBM((count, rank, columns), jnp.float32),
             pltpu.VMEM(shape, jnp.float32),
-            pltpu.VMEM(shape, jnp.float32),
+            pltpu.VMEM(shape, jnp.bfloat16),
         ),
         scratch_shapes=[
             pltpu.VMEM((rank * pairs, 2 * rank), jnp.float32),
@@ -471,11 +471,11 @@
             coeffs, keep, send = gram_pass(place.reshape(1), far, basis, parts)
             got = exchange(send, "samp", 1)
         elif height == 2:
-            leaving = (keep[1:3] + got[1:3]).astype(jnp.bfloat16)
+            leaving = (keep[1:3] + got[1:3].astype(jnp.float32)).astype(jnp.bfloat16)
             other, _ = lax.optimization_barrier((other, leaving))
             received = exchange(leaving, "samp", 2)
         elif height == 3:
-            leaving = keep[3] + got[3] + received[1].astype(jnp.float32)
+            leaving = keep[3] + got[3].astype(jnp.float32) + received[1].astype(jnp.float32)
             other, _ = lax.optimization_barrier((other, leaving))
             last = exchange(leaving, "samp", 6)
         elif height == 4:

time: 49.2 us -> 49 us (level)
  no operation moved by 1% of the time
where the time goes in v9:
time: 49 us; the launch traced here: 48.8 us
  starting transfers between devices  25.6 us (52%)
  Pallas kernels  13.4 us (27%)
  waiting for transfers between devices  5.09 us (10%)
  local copies, waits for them, and re-layouts  3.32 us (7%)
  between operations  0.75 us (2%)
  matrix products  0.62 us (1%)
    ppermute x8, starting transfers between devices, exchange(): lax.ppermute(value, axis, [(i, i ^ flip) for i in range(lax.axis_size(axi...  23.3 us
    pallas_call x1, Pallas kernels, own_pass(): pl.pallas_call(own_kernel, in_specs=[ANY, ANY, VMEM, VMEM, ANY, ANY, ANY,...  8.09 us
    ppermute x8, waiting for transfers between devices, exchange(): lax.ppermute(value, axis, [(i, i ^ flip) for i in range(lax.axis_size(axi...  4.92 us
    ppermute x2, starting transfers between devices, swap(): return lax.ppermute(value, axis, pairs + [(j, i) for i, j in pairs])  2.35 us
    reshape x1, local copies, waits for them, and re-layouts, shards(): inner_transfer.reshape(-1, rank)  2.03 us
    pallas_call x1, Pallas kernels, side_pass(): pl.pallas_call(kernel, in_specs=[SMEM] + [VMEM] * 3, out_specs=VMEM, out_...  1.62 us
    pallas_call x1, Pallas kernels, gram_pass(): pl.pallas_call(functools.partial(gram_kernel, 1.0 / (columns * parts)), i...  1.44 us
    dynamic_slice x1, local copies, waits for them, and re-layouts, shards(): lax.dynamic_slice_in_dim(upper_transfer, offset + jnp.right_shift(device,...  1.07 us
  transfers between devices with their start and end apart: 10, of which 6 were waited for; matrix products, arithmetic and copies ran while one was open for 8% of the time, Pallas kernels for 24%

profile of v9, /device:TPU:6, one launch (start us, length us, event | category | flops | bytes accessed | tf_op | source)
XLA Modules:
  0.0 48.8 jit_solution(18306067809061766239)
XLA Ops:
  0.6 1.7 %collective-permute-start.1 = (bf16[64,4096]{1,0:T(8,128)(2,1)}, bf16[64,4096]{1,0:T(8,128)(2,1)S(1)}, u32[]{:S(2)}, u32[]{:S(2)}) collective-permute-start(bf16[64,4096]{1,0:T(8,128)(2,1)} %bitcast.27), channel_id=1, source_target_pairs={{0,8},{16,24},{32,40},{48,56},{64,72},{80,88},{96,104},{112,120},{... | collective-permute-start | bytes 1572872 | tf_op jit(solution)/shard_map/ppermute | solution.py:418
  2.3 0.7 %collective-permute-start = (bf16[64,4096]{1,0:T(8,128)(2,1)}, bf16[64,4096]{1,0:T(8,128)(2,1)S(1)}, u32[]{:S(2)}, u32[]{:S(2)}) collective-permute-start(bf16[64,4096]{1,0:T(8,128)(2,1)} %bitcast.28), channel_id=1, source_target_pairs={{8,16},{24,32},{40,48},{56,64},{72,80},{88,96},{104,112},{120,128}... | collective-permute-start | bytes 1572872 | tf_op jit(solution)/shard_map/ppermute | solution.py:418
  3.0 1.1 %constant_dynamic-slice_fusion = (bf16[1,4096]{1,0:T(2,128)(2,1)S(1)}, bf16[1,4096]{1,0:T(2,128)(2,1)S(1)}, bf16[1,4096]{1,0:T(2,128)(2,1)S(1)}, bf16[1,4096]{1,0:T(2,128)(2,1)S(1)}, bf16[1,4096]{1,0:T(2,128)(2,1)S(1)}) fusion(bf16[62,4096]{1,0:T(8,128)(2,1)} %param.15, s32[]{:T(128)S(6)} %select_n.19, s32[]{:T(128)S(6)} %select_n.17, s32[]{:T(128)S(6)} %select_n.16, ...), kind=kLoop, calls=%fused_computation.14 | loop fusion | bytes 81940 | tf_op jit(solution)/shard_map/dynamic_slice | solution.py:442
  4.3 2.0 %reshape.28.mats_ref = bf16[3968,64]{1,0:T(8,128)(2,1)S(1)} reshape(bf16[62,4096]{1,0:T(8,128)(2,1)} %param.14) | data formatting | bytes 1015808 | tf_op jit(solution)/shard_map/reshape | solution.py:454
  6.3 8.1 %own_pass.1 = (f32[32,64,128]{2,1,0:T(8,128)S(1)}, bf16[256,128,128]{2,1,0:T(8,128)(2,1)S(1)}, bf16[32,64,128]{2,1,0:T(8,128)(2,1)S(1)}, bf16[128,4096]{1,0:T(8,...) custom-call(s32[8,32]{1,0:T(8,128)} %bitcast.31, s32[1,32]{1,0:T(1,128)} %bitcast.32, ...), custom_call_target="tpu_custom_call" | custom-call | tf_op jit(solution)/shard_map/own_pass/pallas_call | solution.py:313
  14.4 0.2 collective-permute-done.1.side_ref
  14.6 1.6 %side_pass.1.near_ref = f32[32,64,128]{2,1,0:T(8,128)S(1)} custom-call(s32[8,128]{1,0:T(8,128)S(4)} %get-tuple-element.19.task_ref, bf16[64,4096]{1,0:T(8,128)(2,1)S(1)} %collective-permute-done.1.side_ref, f32[32,64,128]{2,1,0:T(8,128)S(1)} %get-tuple-element.20.near_ref, ...), custom_call_target="tpu_custom_call", output_to_operand_aliasing={{}: (2, {})} | custom-call | tf_op jit(solution)/shard_map/side_pass/pallas_call | solution.py:357
  16.2 0.6 %far_pass.1 = (bf16[64,4096]{1,0:T(8,128)(2,1)S(1)}, f32[32,128]{1,0:T(8,128)S(1)}, f32[32,64,128]{2,1,0:T(8,128)S(1)}) custom-call(s32[8,128]{1,0:T(8,128)S(4)} %get-tuple-element.18.task_ref, bf16[64,4096]{1,0:T(8,128)(2,1)S(1)} %collective-permute-done.side_ref, f32[32,64,128]{2,1,0:T(8,128)S(1)} %side_pass.1.near_ref, ...), custom_call_target="tpu_custom_call", output_to_operand_aliasing={{2}: (2, {})} | custom-call | tf_op jit(solution)/shard_map/far_pass/pallas_call | solution.py:372
  16.8 4.3 %collective-permute-start.5 = (f32[32,128]{1,0:T(8,128)S(1)}, f32[32,128]{1,0:T(8,128)S(1)}, u32[]{:S(2)}, u32[]{:S(2)}) collective-permute-start(f32[32,128]{1,0:T(8,128)S(1)} %get-tuple-element.28), channel_id=1, source_target_pairs={{0,8},{8,0},{16,24},{24,16},{32,40},{40,32},{48,56},{56,48},{64,72... | collective-permute-start | bytes 49160 | tf_op jit(solution)/shard_map/ppermute | solution.py:413
  21.2 1.7 %collective-permute-done.5 = f32[32,128]{1,0:T(8,128)S(1)} collective-permute-done((f32[32,128]{1,0:T(8,128)S(1)}, f32[32,128]{1,0:T(8,128)S(1)}, u32[]{:S(2)}, u32[]{:S(2)}) %collective-permute-start.5) | collective-permute-done | bytes 16416 | tf_op jit(solution)/shard_map/ppermute | solution.py:413
  23.1 4.9 %collective-permute-start.6 = (f32[32,128]{1,0:T(8,128)S(1)}, f32[32,128]{1,0:T(8,128)S(1)}, u32[]{:S(2)}, u32[]{:S(2)}) collective-permute-start(f32[32,128]{1,0:T(8,128)S(1)} %fusion.6), channel_id=1, source_target_pairs={{0,24},{8,16},{16,8},{24,0},{32,56},{40,48},{48,40},{56,32},{64,88... | collective-permute-start | bytes 49160 | tf_op jit(solution)/shard_map/ppermute | solution.py:413
  28.0 1.4 %gram_pass.1 = (f32[32,64,64]{2,1,0:T(8,128)}, f32[4,8,16,128]{3,2,1,0:T(8,128)S(1)}, bf16[4,8,16,128]{3,2,1,0:T(8,128)(2,1)S(1)}) custom-call(s32[1]{0:T(128)} %bitcast.place_ref, bf16[64,4096]{1,0:T(8,128)(2,1)S(1)} %get-tuple-element.23.far_ref, bf16[32,64,128]{2,1,0:T(8,128)(2,1)S(1)} %get-tuple-element.24.basis_ref), custom_call_target="tpu_custom_call" | custom-call | tf_op jit(solution)/shard_map/gram_pass/pallas_call | solution.py:393
  29.5 0.2 collective-permute-done.6
  29.9 3.1 %collective-permute-start.7 = (f32[32,128]{1,0:T(8,128)S(1)}, f32[32,128]{1,0:T(8,128)S(1)}, u32[]{:S(2)}, u32[]{:S(2)}) collective-permute-start(f32[32,128]{1,0:T(8,128)S(1)} %fusion.4), channel_id=1, source_target_pairs={{0,32},{8,40},{16,48},{24,56},{32,0},{40,8},{48,16},{56,24},{64,96... | collective-permute-start | bytes 49160 | tf_op jit(solution)/shard_map/ppermute | solution.py:413
  33.0 0.9 %collective-permute-start.3 = (bf16[2,8,16,128]{3,2,1,0:T(8,128)(2,1)S(1)}, bf16[2,8,16,128]{3,2,1,0:T(8,128)(2,1)S(1)}, u32[]{:S(2)}, u32[]{:S(2)}) collective-permute-start(bf16[2,8,16,128]{3,2,1,0:T(8,128)(2,1)S(1)} %add_convert_fusion), channel_id=1, source_target_pairs={{0,2},{1,3},{2,0},{3,1},{4,6},{5,7},{6,4},{7,5},{8,10},{9,11},{10,... | collective-permute-start | bytes 196616 | tf_op jit(solution)/shard_map/ppermute | solution.py:413
  33.9 0.8 %collective-permute-done.7 = f32[32,128]{1,0:T(8,128)S(1)} collective-permute-done((f32[32,128]{1,0:T(8,128)S(1)}, f32[32,128]{1,0:T(8,128)S(1)}, u32[]{:S(2)}, u32[]{:S(2)}) %collective-permute-start.7) | collective-permute-done | bytes 16416 | tf_op jit(solution)/shard_map/ppermute | solution.py:413
  34.8 3.5 %collective-permute-start.8 = (f32[32,128]{1,0:T(8,128)S(1)}, f32[32,128]{1,0:T(8,128)S(1)}, u32[]{:S(2)}, u32[]{:S(2)}) collective-permute-start(f32[32,128]{1,0:T(8,128)S(1)} %fusion.2), channel_id=1, source_target_pairs={{0,64},{8,72},{16,80},{24,88},{32,96},{40,104},{48,112},{56,120},{... | collective-permute-start | bytes 49160 | tf_op jit(solution)/shard_map/ppermute | solution.py:413
  38.4 0.6 %collective-permute-start.4 = (f32[8,16,128]{2,1,0:T(8,128)S(1)}, f32[8,16,128]{2,1,0:T(8,128)S(1)}, u32[]{:S(2)}, u32[]{:S(2)}) collective-permute-start(f32[8,16,128]{2,1,0:T(8,128)S(1)} %add_bitcast_fusion), channel_id=1, source_target_pairs={{0,6},{1,7},{2,4},{3,5},{4,2},{5,3},{6,0},{7,1},{8,14},{9,15},{10,... | collective-permute-start | bytes 196616 | tf_op jit(solution)/shard_map/ppermute | solution.py:413
  38.9 1.2 %collective-permute-done.8 = f32[32,128]{1,0:T(8,128)S(1)} collective-permute-done((f32[32,128]{1,0:T(8,128)S(1)}, f32[32,128]{1,0:T(8,128)S(1)}, u32[]{:S(2)}, u32[]{:S(2)}) %collective-permute-start.8) | collective-permute-done | bytes 16416 | tf_op jit(solution)/shard_map/ppermute | solution.py:413
  40.2 0.2 fusion
  40.3 5.9 %collective-permute-start.9 = (f32[32,128]{1,0:T(8,128)S(1)}, f32[32,128]{1,0:T(8,128)S(1)}, u32[]{:S(2)}, u32[]{:S(2)}) collective-permute-start(f32[32,128]{1,0:T(8,128)S(1)} %fusion), channel_id=1, source_target_pairs={{0,192},{8,200},{16,208},{24,216},{32,224},{40,232},{48,240},{56,2... | collective-permute-start | bytes 49160 | tf_op jit(solution)/shard_map/ppermute | solution.py:413
  46.2 0.7 %finish.1 = f32[32,512]{1,0:T(8,128)} custom-call(f32[4,8,16,128]{3,2,1,0:T(8,128)S(1)} %get-tuple-element.26.keep_ref, bf16[4,8,16,128]{3,2,1,0:T(8,128)(2,1)S(1)} %collective-permute-done.2.got_ref, bf16[2,8,16,128]{3,2,1,0:T(8,128)(2,1)S(1)} %collective-permute-done.3.received_ref, f32[8,16,128]{2,1,0:T(8,128)S(1)} %collective-permute-done.4.last_ref), custom_call_target="tpu_custom_call" | custom-call | tf_op jit(solution)/shard_map/finish/pallas_call | solution.py:482
  46.9 1.0 %collective-permute-done.9 = f32[32,128]{1,0:T(8,128)S(1)} collective-permute-done((f32[32,128]{1,0:T(8,128)S(1)}, f32[32,128]{1,0:T(8,128)S(1)}, u32[]{:S(2)}, u32[]{:S(2)}) %collective-permute-start.9) | collective-permute-done | bytes 16416 | tf_op jit(solution)/shard_map/ppermute | solution.py:413
  47.9 0.9 %turn.1 = f32[5,64,64]{2,1,0:T(8,128)} custom-call(f32[32,128]{1,0:T(8,128)S(1)} %add.60.refs_0_, f32[32,128]{1,0:T(8,128)S(1)} %add.61.refs_1_, f32[32,128]{1,0:T(8,128)S(1)} %add.62.refs_2_, f32[32,128]{1,0:T(8,128)S(1)} %add.63.refs_3_, f32[32,128]{1,0:T(8,128)S(1)} %add.64.refs_4_), custom_call_target="tpu_custom_call" | custom-call | tf_op jit(solution)/shard_map/turn/pallas_call | solution.py:493
  (17 shorter events, 0.8 us)
Async XLA Ops:
  0.6 14.0 %collective-permute-start.1 = (bf16[64,4096]{1,0:T(8,128)(2,1)}, bf16[64,4096]{1,0:T(8,128)(2,1)S(1)}, u32[]{:S(2)}, u32[]{:S(2)}) collective-permute-start(bf16[64,4096]{1,0:T(8,128)(2,1)} %bitcast.27), channel_id=1, source_target_pairs={{0,8},{16,24},{32,40},{48,56},{64,72},{80,88},{96,104},{112,120},{... | collective-permute-start | bytes 1572872 | tf_op jit(solution)/shard_map/ppermute | solution.py:418
  2.3 13.9 %collective-permute-start = (bf16[64,4096]{1,0:T(8,128)(2,1)}, bf16[64,4096]{1,0:T(8,128)(2,1)S(1)}, u32[]{:S(2)}, u32[]{:S(2)}) collective-permute-start(bf16[64,4096]{1,0:T(8,128)(2,1)} %bitcast.28), channel_id=1, source_target_pairs={{8,16},{24,32},{40,48},{56,64},{72,80},{88,96},{104,112},{120,128}... | collective-permute-start | bytes 1572872 | tf_op jit(solution)/shard_map/ppermute | solution.py:418
  16.8 6.0 %collective-permute-start.5 = (f32[32,128]{1,0:T(8,128)S(1)}, f32[32,128]{1,0:T(8,128)S(1)}, u32[]{:S(2)}, u32[]{:S(2)}) collective-permute-start(f32[32,128]{1,0:T(8,128)S(1)} %get-tuple-element.28), channel_id=1, source_target_pairs={{0,8},{8,0},{16,24},{24,16},{32,40},{40,32},{48,56},{56,48},{64,72... | collective-permute-start | bytes 49160 | tf_op jit(solution)/shard_map/ppermute | solution.py:413
  23.1 6.7 %collective-permute-start.6 = (f32[32,128]{1,0:T(8,128)S(1)}, f32[32,128]{1,0:T(8,128)S(1)}, u32[]{:S(2)}, u32[]{:S(2)}) collective-permute-start(f32[32,128]{1,0:T(8,128)S(1)} %fusion.6), channel_id=1, source_target_pairs={{0,24},{8,16},{16,8},{24,0},{32,56},{40,48},{48,40},{56,32},{64,88... | collective-permute-start | bytes 49160 | tf_op jit(solution)/shard_map/ppermute | solution.py:413
  29.4 3.5 %collective-permute-start.2 = (bf16[4,8,16,128]{3,2,1,0:T(8,128)(2,1)S(1)}, bf16[4,8,16,128]{3,2,1,0:T(8,128)(2,1)S(1)}, u32[]{:S(2)}, u32[]{:S(2)}) collective-permute-start(bf16[4,8,16,128]{3,2,1,0:T(8,128)(2,1)S(1)} %get-tuple-element.27), channel_id=1, source_target_pairs={{0,1},{1,0},{2,3},{3,2},{4,5},{5,4},{6,7},{7,6},{8,9},{9,8},{10,11... | collective-permute-start | bytes 393224 | tf_op jit(solution)/shard_map/ppermute | solution.py:413
  29.9 4.8 %collective-permute-start.7 = (f32[32,128]{1,0:T(8,128)S(1)}, f32[32,128]{1,0:T(8,128)S(1)}, u32[]{:S(2)}, u32[]{:S(2)}) collective-permute-start(f32[32,128]{1,0:T(8,128)S(1)} %fusion.4), channel_id=1, source_target_pairs={{0,32},{8,40},{16,48},{24,56},{32,0},{40,8},{48,16},{56,24},{64,96... | collective-permute-start | bytes 49160 | tf_op jit(solution)/shard_map/ppermute | solution.py:413
  33.0 5.4 %collective-permute-start.3 = (bf16[2,8,16,128]{3,2,1,0:T(8,128)(2,1)S(1)}, bf16[2,8,16,128]{3,2,1,0:T(8,128)(2,1)S(1)}, u32[]{:S(2)}, u32[]{:S(2)}) collective-permute-start(bf16[2,8,16,128]{3,2,1,0:T(8,128)(2,1)S(1)} %add_convert_fusion), channel_id=1, source_target_pairs={{0,2},{1,3},{2,0},{3,1},{4,6},{5,7},{6,4},{7,5},{8,10},{9,11},{10,... | collective-permute-start | bytes 196616 | tf_op jit(solution)/shard_map/ppermute | solution.py:413
  34.8 5.4 %collective-permute-start.8 = (f32[32,128]{1,0:T(8,128)S(1)}, f32[32,128]{1,0:T(8,128)S(1)}, u32[]{:S(2)}, u32[]{:S(2)}) collective-permute-start(f32[32,128]{1,0:T(8,128)S(1)} %fusion.2), channel_id=1, source_target_pairs={{0,64},{8,72},{16,80},{24,88},{32,96},{40,104},{48,112},{56,120},{... | collective-permute-start | bytes 49160 | tf_op jit(solution)/shard_map/ppermute | solution.py:413
  38.4 7.8 %collective-permute-start.4 = (f32[8,16,128]{2,1,0:T(8,128)S(1)}, f32[8,16,128]{2,1,0:T(8,128)S(1)}, u32[]{:S(2)}, u32[]{:S(2)}) collective-permute-start(f32[8,16,128]{2,1,0:T(8,128)S(1)} %add_bitcast_fusion), channel_id=1, source_target_pairs={{0,6},{1,7},{2,4},{3,5},{4,2},{5,3},{6,0},{7,1},{8,14},{9,15},{10,... | collective-permute-start | bytes 196616 | tf_op jit(solution)/shard_map/ppermute | solution.py:413
  40.3 7.6 %collective-permute-start.9 = (f32[32,128]{1,0:T(8,128)S(1)}, f32[32,128]{1,0:T(8,128)S(1)}, u32[]{:S(2)}, u32[]{:S(2)}) collective-permute-start(f32[32,128]{1,0:T(8,128)S(1)} %fusion), channel_id=1, source_target_pairs={{0,192},{8,200},{16,208},{24,216},{32,224},{40,232},{48,240},{56,2... | collective-permute-start | bytes 49160 | tf_op jit(solution)/shard_map/ppermute | solution.py:413

commit v10 on v9

--- a/solution.py
+++ b/solution.py
@@ -470,11 +470,11 @@
         if height == 0:
             coeffs, keep, send = gram_pass(place.reshape(1), far, basis, parts)
             got = exchange(send, "samp", 1)
-        elif height == 2:
+        elif height == 1:
             leaving = (keep[1:3] + got[1:3].astype(jnp.float32)).astype(jnp.bfloat16)
             other, _ = lax.optimization_barrier((other, leaving))
             received = exchange(leaving, "samp", 2)
-        elif height == 3:
+        elif height == 2:
             leaving = keep[3] + got[3].astype(jnp.float32) + received[1].astype(jnp.float32)
             other, _ = lax.optimization_barrier((other, leaving))
             last = exchange(leaving, "samp", 6)

time: 49 us -> 49.1 us (level)
  transfers between devices with their start and end apart: 10 -> 10, of which waited for: 6 -> 6; matrix products, arithmetic and copies ran while one was open for 8% -> 8% of each run, Pallas kernels for 24% -> 25%
where the time goes in v10:
time: 49.1 us
  starting transfers between devices  25.6 us (52%)
  Pallas kernels  13.7 us (28%)
  waiting for transfers between devices  5.07 us (10%)
  local copies, waits for them, and re-layouts  3.32 us (7%)
  between operations  0.75 us (2%)
  matrix products  0.62 us (1%)
    ppermute x8, starting transfers between devices, exchange(): lax.ppermute(value, axis, [(i, i ^ flip) for i in range(lax.axis_size(axi...  23.3 us
    pallas_call x1, Pallas kernels, own_pass(): pl.pallas_call(own_kernel, in_specs=[ANY, ANY, VMEM, VMEM, ANY, ANY, ANY,...  8.09 us
    ppermute x8, waiting for transfers between devices, exchange(): lax.ppermute(value, axis, [(i, i ^ flip) for i in range(lax.axis_size(axi...  4.9 us
    ppermute x2, starting transfers between devices, swap(): return lax.ppermute(value, axis, pairs + [(j, i) for i, j in pairs])  2.35 us
    reshape x1, local copies, waits for them, and re-layouts, shards(): inner_transfer.reshape(-1, rank)  2.03 us
    pallas_call x1, Pallas kernels, side_pass(): pl.pallas_call(kernel, in_specs=[SMEM] + [VMEM] * 3, out_specs=VMEM, out_...  1.92 us
    pallas_call x1, Pallas kernels, gram_pass(): pl.pallas_call(functools.partial(gram_kernel, 1.0 / (columns * parts)), i...  1.44 us
    dynamic_slice x1, local copies, waits for them, and re-layouts, shards(): lax.dynamic_slice_in_dim(upper_transfer, offset + jnp.right_shift(device,...  1.07 us
  transfers between devices with their start and end apart: 10, of which 6 were waited for; matrix products, arithmetic and copies ran while one was open for 8% of the time, Pallas kernels for 25%

profile of v10, /device:TPU:6, one launch (start us, length us, event | category | flops | bytes accessed | tf_op | source)
XLA Modules:
  0.0 49.1 jit_solution(3530298275317708864)
XLA Ops:
  0.6 1.7 %collective-permute-start.1 = (bf16[64,4096]{1,0:T(8,128)(2,1)}, bf16[64,4096]{1,0:T(8,128)(2,1)S(1)}, u32[]{:S(2)}, u32[]{:S(2)}) collective-permute-start(bf16[64,4096]{1,0:T(8,128)(2,1)} %bitcast.27), channel_id=1, source_target_pairs={{0,8},{16,24},{32,40},{48,56},{64,72},{80,88},{96,104},{112,120},{... | collective-permute-start | bytes 1572872 | tf_op jit(solution)/shard_map/ppermute | solution.py:418
  2.3 0.7 %collective-permute-start = (bf16[64,4096]{1,0:T(8,128)(2,1)}, bf16[64,4096]{1,0:T(8,128)(2,1)S(1)}, u32[]{:S(2)}, u32[]{:S(2)}) collective-permute-start(bf16[64,4096]{1,0:T(8,128)(2,1)} %bitcast.28), channel_id=1, source_target_pairs={{8,16},{24,32},{40,48},{56,64},{72,80},{88,96},{104,112},{120,128}... | collective-permute-start | bytes 1572872 | tf_op jit(solution)/shard_map/ppermute | solution.py:418
  3.0 1.1 %constant_dynamic-slice_fusion = (bf16[1,4096]{1,0:T(2,128)(2,1)S(1)}, bf16[1,4096]{1,0:T(2,128)(2,1)S(1)}, bf16[1,4096]{1,0:T(2,128)(2,1)S(1)}, bf16[1,4096]{1,0:T(2,128)(2,1)S(1)}, bf16[1,4096]{1,0:T(2,128)(2,1)S(1)}) fusion(bf16[62,4096]{1,0:T(8,128)(2,1)} %param.15, s32[]{:T(128)S(6)} %select_n.19, s32[]{:T(128)S(6)} %select_n.17, s32[]{:T(128)S(6)} %select_n.16, ...), kind=kLoop, calls=%fused_computation.14 | loop fusion | bytes 81940 | tf_op jit(solution)/shard_map/dynamic_slice | solution.py:442
  4.3 2.0 %reshape.28.mats_ref = bf16[3968,64]{1,0:T(8,128)(2,1)S(1)} reshape(bf16[62,4096]{1,0:T(8,128)(2,1)} %param.14) | data formatting | bytes 1015808 | tf_op jit(solution)/shard_map/reshape | solution.py:454
  6.3 8.1 %own_pass.1 = (f32[32,64,128]{2,1,0:T(8,128)S(1)}, bf16[256,128,128]{2,1,0:T(8,128)(2,1)S(1)}, bf16[32,64,128]{2,1,0:T(8,128)(2,1)S(1)}, bf16[128,4096]{1,0:T(8,...) custom-call(s32[8,32]{1,0:T(8,128)} %bitcast.31, s32[1,32]{1,0:T(1,128)} %bitcast.32, ...), custom_call_target="tpu_custom_call" | custom-call | tf_op jit(solution)/shard_map/own_pass/pallas_call | solution.py:313
  14.4 0.2 collective-permute-done.1.side_ref
  14.6 1.9 %side_pass.1.near_ref = f32[32,64,128]{2,1,0:T(8,128)S(1)} custom-call(s32[8,128]{1,0:T(8,128)S(4)} %get-tuple-element.19.task_ref, bf16[64,4096]{1,0:T(8,128)(2,1)S(1)} %collective-permute-done.1.side_ref, f32[32,64,128]{2,1,0:T(8,128)S(1)} %get-tuple-element.20.near_ref, ...), custom_call_target="tpu_custom_call", output_to_operand_aliasing={{}: (2, {})} | custom-call | tf_op jit(solution)/shard_map/side_pass/pallas_call | solution.py:357
  16.5 0.6 %far_pass.1 = (bf16[64,4096]{1,0:T(8,128)(2,1)S(1)}, f32[32,128]{1,0:T(8,128)S(1)}, f32[32,64,128]{2,1,0:T(8,128)S(1)}) custom-call(s32[8,128]{1,0:T(8,128)S(4)} %get-tuple-element.18.task_ref, bf16[64,4096]{1,0:T(8,128)(2,1)S(1)} %collective-permute-done.side_ref, f32[32,64,128]{2,1,0:T(8,128)S(1)} %side_pass.1.near_ref, ...), custom_call_target="tpu_custom_call", output_to_operand_aliasing={{2}: (2, {})} | custom-call | tf_op jit(solution)/shard_map/far_pass/pallas_call | solution.py:372
  17.2 4.3 %collective-permute-start.5 = (f32[32,128]{1,0:T(8,128)S(1)}, f32[32,128]{1,0:T(8,128)S(1)}, u32[]{:S(2)}, u32[]{:S(2)}) collective-permute-start(f32[32,128]{1,0:T(8,128)S(1)} %get-tuple-element.28), channel_id=1, source_target_pairs={{0,8},{8,0},{16,24},{24,16},{32,40},{40,32},{48,56},{56,48},{64,72... | collective-permute-start | bytes 49160 | tf_op jit(solution)/shard_map/ppermute | solution.py:413
  21.5 1.4 %gram_pass.1 = (f32[32,64,64]{2,1,0:T(8,128)}, f32[4,8,16,128]{3,2,1,0:T(8,128)S(1)}, bf16[4,8,16,128]{3,2,1,0:T(8,128)(2,1)S(1)}) custom-call(s32[1]{0:T(128)} %bitcast.place_ref, bf16[64,4096]{1,0:T(8,128)(2,1)S(1)} %get-tuple-element.23.far_ref, bf16[32,64,128]{2,1,0:T(8,128)(2,1)S(1)} %get-tuple-element.24.basis_ref), custom_call_target="tpu_custom_call" | custom-call | tf_op jit(solution)/shard_map/gram_pass/pallas_call | solution.py:393
  23.0 0.2 collective-permute-done.5
  23.4 4.6 %collective-permute-start.6 = (f32[32,128]{1,0:T(8,128)S(1)}, f32[32,128]{1,0:T(8,128)S(1)}, u32[]{:S(2)}, u32[]{:S(2)}) collective-permute-start(f32[32,128]{1,0:T(8,128)S(1)} %fusion.6), channel_id=1, source_target_pairs={{0,24},{8,16},{16,8},{24,0},{32,56},{40,48},{48,40},{56,32},{64,88... | collective-permute-start | bytes 49160 | tf_op jit(solution)/shard_map/ppermute | solution.py:413
  28.0 0.9 %collective-permute-start.3 = (bf16[2,8,16,128]{3,2,1,0:T(8,128)(2,1)S(1)}, bf16[2,8,16,128]{3,2,1,0:T(8,128)(2,1)S(1)}, u32[]{:S(2)}, u32[]{:S(2)}) collective-permute-start(bf16[2,8,16,128]{3,2,1,0:T(8,128)(2,1)S(1)} %add_convert_fusion), channel_id=1, source_target_pairs={{0,2},{1,3},{2,0},{3,1},{4,6},{5,7},{6,4},{7,5},{8,10},{9,11},{10,... | collective-permute-start | bytes 196616 | tf_op jit(solution)/shard_map/ppermute | solution.py:413
  28.9 0.8 %collective-permute-done.6 = f32[32,128]{1,0:T(8,128)S(1)} collective-permute-done((f32[32,128]{1,0:T(8,128)S(1)}, f32[32,128]{1,0:T(8,128)S(1)}, u32[]{:S(2)}, u32[]{:S(2)}) %collective-permute-start.6) | collective-permute-done | bytes 16416 | tf_op jit(solution)/shard_map/ppermute | solution.py:413
  29.7 0.2 fusion.4
  29.9 3.1 %collective-permute-start.7 = (f32[32,128]{1,0:T(8,128)S(1)}, f32[32,128]{1,0:T(8,128)S(1)}, u32[]{:S(2)}, u32[]{:S(2)}) collective-permute-start(f32[32,128]{1,0:T(8,128)S(1)} %fusion.4), channel_id=1, source_target_pairs={{0,32},{8,40},{16,48},{24,56},{32,0},{40,8},{48,16},{56,24},{64,96... | collective-permute-start | bytes 49160 | tf_op jit(solution)/shard_map/ppermute | solution.py:413
  33.0 1.7 %collective-permute-done.7 = f32[32,128]{1,0:T(8,128)S(1)} collective-permute-done((f32[32,128]{1,0:T(8,128)S(1)}, f32[32,128]{1,0:T(8,128)S(1)}, u32[]{:S(2)}, u32[]{:S(2)}) %collective-permute-start.7) | collective-permute-done | bytes 16416 | tf_op jit(solution)/shard_map/ppermute | solution.py:413
  34.8 3.5 %collective-permute-start.8 = (f32[32,128]{1,0:T(8,128)S(1)}, f32[32,128]{1,0:T(8,128)S(1)}, u32[]{:S(2)}, u32[]{:S(2)}) collective-permute-start(f32[32,128]{1,0:T(8,128)S(1)} %fusion.2), channel_id=1, source_target_pairs={{0,64},{8,72},{16,80},{24,88},{32,96},{40,104},{48,112},{56,120},{... | collective-permute-start | bytes 49160 | tf_op jit(solution)/shard_map/ppermute | solution.py:413
  38.3 0.5 collective-permute-start.4
  38.8 1.2 %collective-permute-done.8 = f32[32,128]{1,0:T(8,128)S(1)} collective-permute-done((f32[32,128]{1,0:T(8,128)S(1)}, f32[32,128]{1,0:T(8,128)S(1)}, u32[]{:S(2)}, u32[]{:S(2)}) %collective-permute-start.8) | collective-permute-done | bytes 16416 | tf_op jit(solution)/shard_map/ppermute | solution.py:413
  40.2 6.3 %collective-permute-start.9 = (f32[32,128]{1,0:T(8,128)S(1)}, f32[32,128]{1,0:T(8,128)S(1)}, u32[]{:S(2)}, u32[]{:S(2)}) collective-permute-start(f32[32,128]{1,0:T(8,128)S(1)} %fusion), channel_id=1, source_target_pairs={{0,192},{8,200},{16,208},{24,216},{32,224},{40,232},{48,240},{56,2... | collective-permute-start | bytes 49160 | tf_op jit(solution)/shard_map/ppermute | solution.py:413
  46.5 0.7 %finish.1 = f32[32,512]{1,0:T(8,128)} custom-call(f32[4,8,16,128]{3,2,1,0:T(8,128)S(1)} %get-tuple-element.26.keep_ref, bf16[4,8,16,128]{3,2,1,0:T(8,128)(2,1)S(1)} %collective-permute-done.2.got_ref, bf16[2,8,16,128]{3,2,1,0:T(8,128)(2,1)S(1)} %collective-permute-done.3.received_ref, f32[8,16,128]{2,1,0:T(8,128)S(1)} %collective-permute-done.4.last_ref), custom_call_target="tpu_custom_call" | custom-call | tf_op jit(solution)/shard_map/finish/pallas_call | solution.py:482
  47.2 1.0 %collective-permute-done.9 = f32[32,128]{1,0:T(8,128)S(1)} collective-permute-done((f32[32,128]{1,0:T(8,128)S(1)}, f32[32,128]{1,0:T(8,128)S(1)}, u32[]{:S(2)}, u32[]{:S(2)}) %collective-permute-start.9) | collective-permute-done | bytes 16416 | tf_op jit(solution)/shard_map/ppermute | solution.py:413
  48.2 0.9 %turn.1 = f32[5,64,64]{2,1,0:T(8,128)} custom-call(f32[32,128]{1,0:T(8,128)S(1)} %add.60.refs_0_, f32[32,128]{1,0:T(8,128)S(1)} %add.61.refs_1_, f32[32,128]{1,0:T(8,128)S(1)} %add.62.refs_2_, f32[32,128]{1,0:T(8,128)S(1)} %add.63.refs_3_, f32[32,128]{1,0:T(8,128)S(1)} %add.64.refs_4_), custom_call_target="tpu_custom_call" | custom-call | tf_op jit(solution)/shard_map/turn/pallas_call | solution.py:493
  (17 shorter events, 0.8 us)
Async XLA Ops:
  0.6 14.0 %collective-permute-start.1 = (bf16[64,4096]{1,0:T(8,128)(2,1)}, bf16[64,4096]{1,0:T(8,128)(2,1)S(1)}, u32[]{:S(2)}, u32[]{:S(2)}) collective-permute-start(bf16[64,4096]{1,0:T(8,128)(2,1)} %bitcast.27), channel_id=1, source_target_pairs={{0,8},{16,24},{32,40},{48,56},{64,72},{80,88},{96,104},{112,120},{... | collective-permute-start | bytes 1572872 | tf_op jit(solution)/shard_map/ppermute | solution.py:418
  2.3 14.2 %collective-permute-start = (bf16[64,4096]{1,0:T(8,128)(2,1)}, bf16[64,4096]{1,0:T(8,128)(2,1)S(1)}, u32[]{:S(2)}, u32[]{:S(2)}) collective-permute-start(bf16[64,4096]{1,0:T(8,128)(2,1)} %bitcast.28), channel_id=1, source_target_pairs={{8,16},{24,32},{40,48},{56,64},{72,80},{88,96},{104,112},{120,128}... | collective-permute-start | bytes 1572872 | tf_op jit(solution)/shard_map/ppermute | solution.py:418
  17.2 6.0 %collective-permute-start.5 = (f32[32,128]{1,0:T(8,128)S(1)}, f32[32,128]{1,0:T(8,128)S(1)}, u32[]{:S(2)}, u32[]{:S(2)}) collective-permute-start(f32[32,128]{1,0:T(8,128)S(1)} %get-tuple-element.28), channel_id=1, source_target_pairs={{0,8},{8,0},{16,24},{24,16},{32,40},{40,32},{48,56},{56,48},{64,72... | collective-permute-start | bytes 49160 | tf_op jit(solution)/shard_map/ppermute | solution.py:413
  22.9 5.1 %collective-permute-start.2 = (bf16[4,8,16,128]{3,2,1,0:T(8,128)(2,1)S(1)}, bf16[4,8,16,128]{3,2,1,0:T(8,128)(2,1)S(1)}, u32[]{:S(2)}, u32[]{:S(2)}) collective-permute-start(bf16[4,8,16,128]{3,2,1,0:T(8,128)(2,1)S(1)} %get-tuple-element.27), channel_id=1, source_target_pairs={{0,1},{1,0},{2,3},{3,2},{4,5},{5,4},{6,7},{7,6},{8,9},{9,8},{10,11... | collective-permute-start | bytes 393224 | tf_op jit(solution)/shard_map/ppermute | solution.py:413
  23.4 6.4 %collective-permute-start.6 = (f32[32,128]{1,0:T(8,128)S(1)}, f32[32,128]{1,0:T(8,128)S(1)}, u32[]{:S(2)}, u32[]{:S(2)}) collective-permute-start(f32[32,128]{1,0:T(8,128)S(1)} %fusion.6), channel_id=1, source_target_pairs={{0,24},{8,16},{16,8},{24,0},{32,56},{40,48},{48,40},{56,32},{64,88... | collective-permute-start | bytes 49160 | tf_op jit(solution)/shard_map/ppermute | solution.py:413
  28.0 4.9 %collective-permute-start.3 = (bf16[2,8,16,128]{3,2,1,0:T(8,128)(2,1)S(1)}, bf16[2,8,16,128]{3,2,1,0:T(8,128)(2,1)S(1)}, u32[]{:S(2)}, u32[]{:S(2)}) collective-permute-start(bf16[2,8,16,128]{3,2,1,0:T(8,128)(2,1)S(1)} %add_convert_fusion), channel_id=1, source_target_pairs={{0,2},{1,3},{2,0},{3,1},{4,6},{5,7},{6,4},{7,5},{8,10},{9,11},{10,... | collective-permute-start | bytes 196616 | tf_op jit(solution)/shard_map/ppermute | solution.py:413
  29.9 4.8 %collective-permute-start.7 = (f32[32,128]{1,0:T(8,128)S(1)}, f32[32,128]{1,0:T(8,128)S(1)}, u32[]{:S(2)}, u32[]{:S(2)}) collective-permute-start(f32[32,128]{1,0:T(8,128)S(1)} %fusion.4), channel_id=1, source_target_pairs={{0,32},{8,40},{16,48},{24,56},{32,0},{40,8},{48,16},{56,24},{64,96... | collective-permute-start | bytes 49160 | tf_op jit(solution)/shard_map/ppermute | solution.py:413
  34.8 5.2 %collective-permute-start.8 = (f32[32,128]{1,0:T(8,128)S(1)}, f32[32,128]{1,0:T(8,128)S(1)}, u32[]{:S(2)}, u32[]{:S(2)}) collective-permute-start(f32[32,128]{1,0:T(8,128)S(1)} %fusion.2), channel_id=1, source_target_pairs={{0,64},{8,72},{16,80},{24,88},{32,96},{40,104},{48,112},{56,120},{... | collective-permute-start | bytes 49160 | tf_op jit(solution)/shard_map/ppermute | solution.py:413
  38.3 8.2 %collective-permute-start.4 = (f32[8,16,128]{2,1,0:T(8,128)S(1)}, f32[8,16,128]{2,1,0:T(8,128)S(1)}, u32[]{:S(2)}, u32[]{:S(2)}) collective-permute-start(f32[8,16,128]{2,1,0:T(8,128)S(1)} %add_bitcast_fusion), channel_id=1, source_target_pairs={{0,6},{1,7},{2,4},{3,5},{4,2},{5,3},{6,0},{7,1},{8,14},{9,15},{10,... | collective-permute-start | bytes 196616 | tf_op jit(solution)/shard_map/ppermute | solution.py:413
  40.2 8.0 %collective-permute-start.9 = (f32[32,128]{1,0:T(8,128)S(1)}, f32[32,128]{1,0:T(8,128)S(1)}, u32[]{:S(2)}, u32[]{:S(2)}) collective-permute-start(f32[32,128]{1,0:T(8,128)S(1)} %fusion), channel_id=1, source_target_pairs={{0,192},{8,200},{16,208},{24,216},{32,224},{40,232},{48,240},{56,2... | collective-permute-start | bytes 49160 | tf_op jit(solution)/shard_map/ppermute | solution.py:413

commit v11 on v10

--- a/solution.py
+++ b/solution.py
@@ -435,16 +435,15 @@
     second = swap(own, "leaf", 0)
 
     heights = groups.bit_length() - 1
-    rows = []
+    nodes = []
     offset, width = 0, groups
     for height in range(heights):
-        rows.append(
-            lax.dynamic_slice_in_dim(
-                upper_transfer, offset + jnp.right_shift(device, height), 1, axis=0
-            )
-        )
+        node = jnp.right_shift(device, height)
+        nodes.append(offset + node)
+        sibling = offset + jnp.bitwise_xor(node, 1)
         offset, width = offset + width, width // 2
-    upper = jnp.concatenate(rows, axis=0).reshape(heights, rank, rank)
+    rows = [lax.dynamic_slice_in_dim(upper_transfer, n, 1, axis=0) for n in nodes + [sibling]]
+    upper = jnp.concatenate(rows, axis=0).reshape(heights + 1, rank, rank)
 
     blocks = near_blocks.reshape(count * slots, size, size)
     near, blocks, basis, weight, twice, crossing_tasks, tasks = own_pass(
@@ -460,36 +459,43 @@
     near = side_pass(tasks, second, near, blocks)
     far, part, _ = far_pass(crossing_tasks, first, near, blocks, weight)
 
-    flips = (1, 3, 4, 8, 24)
+    def step(value, matrix):
+        return jnp.dot(value, matrix, precision=lax.Precision.HIGHEST)
+
     levels = []
     accum = part
-    for height in range(heights):
+    for height, flip in enumerate((1, 3, 4)):
         if height:
-            accum = jnp.dot(accum, twice[height - 1], precision=lax.Precision.HIGHEST)
-        other = exchange(accum, "leaf", flips[height])
+            accum = step(accum, twice[height - 1])
+        other = exchange(accum, "leaf", flip)
         if height == 0:
             coeffs, keep, send = gram_pass(place.reshape(1), far, basis, parts)
             got = exchange(send, "samp", 1)
         elif height == 1:
-            leaving = (keep[1:3] + got[1:3].astype(jnp.float32)).astype(jnp.bfloat16)
+            leaving = keep[1:3] + got[1:3].astype(jnp.float32)
+            leaving = leaving.astype(jnp.bfloat16)
             other, _ = lax.optimization_barrier((other, leaving))
             received = exchange(leaving, "samp", 2)
         elif height == 2:
             leaving = keep[3] + got[3].astype(jnp.float32) + received[1].astype(jnp.float32)
             other, _ = lax.optimization_barrier((other, leaving))
             last = exchange(leaving, "samp", 6)
-        elif height == 4:
-            leaf_gram = pl.pallas_call(
-                finish_kernel,
-                in_specs=[VMEM] * 4,
-                out_specs=VMEM,
-                out_shape=jax.ShapeDtypeStruct((count, rank * rank // parts), jnp.float32),
-                compiler_params=params(8),
-                name="finish",
-            )(keep, *map(resident, [got, received, last]))
-            other, _ = lax.optimization_barrier((other, leaf_gram))
         accum = accum + other
         levels.append(accum)
+    accum = step(accum, twice[2])
+    others = [exchange(accum, "leaf", flip) for flip in (24, 8, 20)]
+    leaf_gram = pl.pallas_call(
+        finish_kernel,
+        in_specs=[VMEM] * 4,
+        out_specs=VMEM,
+        out_shape=jax.ShapeDtypeStruct((count, rank * rank // parts), jnp.float32),
+        compiler_params=params(8),
+        name="finish",
+    )(keep, *map(resident, [got, received, last]))
+    *others, _ = lax.optimization_barrier((*others, leaf_gram))
+    third, sibling, fourth = others
+    levels.append(accum + sibling)
+    levels.append(step(levels[-1], twice[3]) + step(third + fourth, twice[4]))
     ancestors = pl.pallas_call(
         turn_kernel,
         in_specs=[VMEM] * heights,

time: 49.1 us -> 49.4 us (level)
  starting transfers between devices: 25.6 us -> 24.9 us
    ppermute x8 -> x9, starting transfers between devices: 23.3 us -> 22.5 us  [exchange(): lax.ppermute(value, axis, [(i, i ^ flip) for i in range(lax.axis_size(axi...]
    ppermute x8 -> x9, waiting for transfers between devices: 4.9 us -> 5.1 us  [exchange(): lax.ppermute(value, axis, [(i, i ^ flip) for i in range(lax.axis_size(axi...]
  transfers between devices with their start and end apart: 10 -> 11, of which waited for: 6 -> 5; matrix products, arithmetic and copies ran while one was open for 8% -> 8% of each run, Pallas kernels for 25% -> 25%
where the time goes in v11:
time: 49.4 us; the launch traced here: 49.1 us
  starting transfers between devices  24.9 us (50%)
  Pallas kernels  13.7 us (28%)
  waiting for transfers between devices  5.48 us (11%)
  local copies, waits for them, and re-layouts  3.4 us (7%)
  matrix products  0.79 us (2%)
  between operations  0.77 us (2%)
    ppermute x9, starting transfers between devices, exchange(): lax.ppermute(value, axis, [(i, i ^ flip) for i in range(lax.axis_size(axi...  22.5 us
    pallas_call x1, Pallas kernels, own_pass(): pl.pallas_call(own_kernel, in_specs=[ANY, ANY, VMEM, VMEM, ANY, ANY, ANY,...  7.78 us
    ppermute x9, waiting for transfers between devices, exchange(): lax.ppermute(value, axis, [(i, i ^ flip) for i in range(lax.axis_size(axi...  5.1 us
    ppermute x2, starting transfers between devices, swap(): return lax.ppermute(value, axis, pairs + [(j, i) for i, j in pairs])  2.35 us
    pallas_call x1, Pallas kernels, side_pass(): pl.pallas_call(kernel, in_specs=[SMEM] + [VMEM] * 3, out_specs=VMEM, out_...  2.23 us
    reshape x1, local copies, waits for them, and re-layouts, shards(): inner_transfer.reshape(-1, rank)  2.03 us
    pallas_call x1, Pallas kernels, gram_pass(): pl.pallas_call(functools.partial(gram_kernel, 1.0 / (columns * parts)), i...  1.44 us
    dynamic_slice x1, local copies, waits for them, and re-layouts, shards(): lax.dynamic_slice_in_dim(upper_transfer, n, 1, axis=0)  1.12 us
  transfers between devices with their start and end apart: 11, of which 5 were waited for; matrix products, arithmetic and copies ran while one was open for 8% of the time, Pallas kernels for 25%

profile of v11, /device:TPU:6, one launch (start us, length us, event | category | flops | bytes accessed | tf_op | source)
XLA Modules:
  0.0 49.1 jit_solution(3940647354920816332)
XLA Ops:
  0.6 1.7 %collective-permute-start.1 = (bf16[64,4096]{1,0:T(8,128)(2,1)}, bf16[64,4096]{1,0:T(8,128)(2,1)S(1)}, u32[]{:S(2)}, u32[]{:S(2)}) collective-permute-start(bf16[64,4096]{1,0:T(8,128)(2,1)} %bitcast.30), channel_id=1, source_target_pairs={{0,8},{16,24},{32,40},{48,56},{64,72},{80,88},{96,104},{112,120},{... | collective-permute-start | bytes 1572872 | tf_op jit(solution)/shard_map/ppermute | solution.py:418
  2.3 0.7 %collective-permute-start = (bf16[64,4096]{1,0:T(8,128)(2,1)}, bf16[64,4096]{1,0:T(8,128)(2,1)S(1)}, u32[]{:S(2)}, u32[]{:S(2)}) collective-permute-start(bf16[64,4096]{1,0:T(8,128)(2,1)} %bitcast.31), channel_id=1, source_target_pairs={{8,16},{24,32},{40,48},{56,64},{72,80},{88,96},{104,112},{120,128}... | collective-permute-start | bytes 1572872 | tf_op jit(solution)/shard_map/ppermute | solution.py:418
  3.0 1.1 %constant_dynamic-slice_fusion = (bf16[1,4096]{1,0:T(2,128)(2,1)S(1)}, bf16[1,4096]{1,0:T(2,128)(2,1)S(1)}, bf16[1,4096]{1,0:T(2,128)(2,1)S(1)}, bf16[1,4096]{1,...) fusion(bf16[62,4096]{1,0:T(8,128)(2,1)} %param.15, s32[]{:T(128)S(6)} %select_n.23, ...), kind=kLoop, calls=%fused_computation.18 | loop fusion | bytes 98328 | tf_op jit(solution)/shard_map/dynamic_slice | solution.py:445
  4.4 2.0 %reshape.28.mats_ref = bf16[3968,64]{1,0:T(8,128)(2,1)S(1)} reshape(bf16[62,4096]{1,0:T(8,128)(2,1)} %param.14) | data formatting | bytes 1015808 | tf_op jit(solution)/shard_map/reshape | solution.py:453
  6.4 7.8 %own_pass.1 = (f32[32,64,128]{2,1,0:T(8,128)S(1)}, bf16[256,128,128]{2,1,0:T(8,128)(2,1)S(1)}, bf16[32,64,128]{2,1,0:T(8,128)(2,1)S(1)}, bf16[128,4096]{1,0:T(8,...) custom-call(s32[8,32]{1,0:T(8,128)} %bitcast.34, s32[1,32]{1,0:T(1,128)} %bitcast.35, ...), custom_call_target="tpu_custom_call" | custom-call | tf_op jit(solution)/shard_map/own_pass/pallas_call | solution.py:313
  14.2 0.4 collective-permute-done.1.side_ref
  14.6 2.2 %side_pass.1.near_ref = f32[32,64,128]{2,1,0:T(8,128)S(1)} custom-call(s32[8,128]{1,0:T(8,128)S(4)} %get-tuple-element.21.task_ref, bf16[64,4096]{1,0:T(8,128)(2,1)S(1)} %collective-permute-done.1.side_ref, f32[32,64,128]{2,1,0:T(8,128)S(1)} %get-tuple-element.22.near_ref, ...), custom_call_target="tpu_custom_call", output_to_operand_aliasing={{}: (2, {})} | custom-call | tf_op jit(solution)/shard_map/side_pass/pallas_call | solution.py:357
  16.8 0.6 %far_pass.1 = (bf16[64,4096]{1,0:T(8,128)(2,1)S(1)}, f32[32,128]{1,0:T(8,128)S(1)}, f32[32,64,128]{2,1,0:T(8,128)S(1)}) custom-call(s32[8,128]{1,0:T(8,128)S(4)} %get-tuple-element.20.task_ref, bf16[64,4096]{1,0:T(8,128)(2,1)S(1)} %collective-permute-done.side_ref, f32[32,64,128]{2,1,0:T(8,128)S(1)} %side_pass.1.near_ref, ...), custom_call_target="tpu_custom_call", output_to_operand_aliasing={{2}: (2, {})} | custom-call | tf_op jit(solution)/shard_map/far_pass/pallas_call | solution.py:372
  17.5 4.1 %collective-permute-start.5 = (f32[32,128]{1,0:T(8,128)S(1)}, f32[32,128]{1,0:T(8,128)S(1)}, u32[]{:S(2)}, u32[]{:S(2)}) collective-permute-start(f32[32,128]{1,0:T(8,128)S(1)} %get-tuple-element.30), channel_id=1, source_target_pairs={{0,8},{8,0},{16,24},{24,16},{32,40},{40,32},{48,56},{56,48},{64,72... | collective-permute-start | bytes 49160 | tf_op jit(solution)/shard_map/ppermute | solution.py:413
  21.6 1.4 %gram_pass.1 = (f32[32,64,64]{2,1,0:T(8,128)}, f32[4,8,16,128]{3,2,1,0:T(8,128)S(1)}, bf16[4,8,16,128]{3,2,1,0:T(8,128)(2,1)S(1)}) custom-call(s32[1]{0:T(128)} %bitcast.place_ref, bf16[64,4096]{1,0:T(8,128)(2,1)S(1)} %get-tuple-element.25.far_ref, bf16[32,64,128]{2,1,0:T(8,128)(2,1)S(1)} %get-tuple-element.26.basis_ref), custom_call_target="tpu_custom_call" | custom-call | tf_op jit(solution)/shard_map/gram_pass/pallas_call | solution.py:393
  23.1 0.2 collective-permute-done.5
  23.5 4.8 %collective-permute-start.6 = (f32[32,128]{1,0:T(8,128)S(1)}, f32[32,128]{1,0:T(8,128)S(1)}, u32[]{:S(2)}, u32[]{:S(2)}) collective-permute-start(f32[32,128]{1,0:T(8,128)S(1)} %fusion.7), channel_id=1, source_target_pairs={{0,24},{8,16},{16,8},{24,0},{32,56},{40,48},{48,40},{56,32},{64,88... | collective-permute-start | bytes 49160 | tf_op jit(solution)/shard_map/ppermute | solution.py:413
  28.3 0.9 %collective-permute-start.3 = (bf16[2,8,16,128]{3,2,1,0:T(8,128)(2,1)S(1)}, bf16[2,8,16,128]{3,2,1,0:T(8,128)(2,1)S(1)}, u32[]{:S(2)}, u32[]{:S(2)}) collective-permute-start(bf16[2,8,16,128]{3,2,1,0:T(8,128)(2,1)S(1)} %add_convert_fusion), channel_id=1, source_target_pairs={{0,2},{1,3},{2,0},{3,1},{4,6},{5,7},{6,4},{7,5},{8,10},{9,11},{10,... | collective-permute-start | bytes 196616 | tf_op jit(solution)/shard_map/ppermute | solution.py:413
  29.2 0.8 %collective-permute-done.6 = f32[32,128]{1,0:T(8,128)S(1)} collective-permute-done((f32[32,128]{1,0:T(8,128)S(1)}, f32[32,128]{1,0:T(8,128)S(1)}, u32[]{:S(2)}, u32[]{:S(2)}) %collective-permute-start.6) | collective-permute-done | bytes 16416 | tf_op jit(solution)/shard_map/ppermute | solution.py:413
  30.2 2.7 %collective-permute-start.7 = (f32[32,128]{1,0:T(8,128)S(1)}, f32[32,128]{1,0:T(8,128)S(1)}, u32[]{:S(2)}, u32[]{:S(2)}) collective-permute-start(f32[32,128]{1,0:T(8,128)S(1)} %fusion.5), channel_id=1, source_target_pairs={{0,32},{8,40},{16,48},{24,56},{32,0},{40,8},{48,16},{56,24},{64,96... | collective-permute-start | bytes 49160 | tf_op jit(solution)/shard_map/ppermute | solution.py:413
  33.0 0.6 %collective-permute-start.4 = (f32[8,16,128]{2,1,0:T(8,128)S(1)}, f32[8,16,128]{2,1,0:T(8,128)S(1)}, u32[]{:S(2)}, u32[]{:S(2)}) collective-permute-start(f32[8,16,128]{2,1,0:T(8,128)S(1)} %add_bitcast_fusion), channel_id=1, source_target_pairs={{0,6},{1,7},{2,4},{3,5},{4,2},{5,3},{6,0},{7,1},{8,14},{9,15},{10,... | collective-permute-start | bytes 196616 | tf_op jit(solution)/shard_map/ppermute | solution.py:413
  33.5 1.1 %collective-permute-done.7 = f32[32,128]{1,0:T(8,128)S(1)} collective-permute-done((f32[32,128]{1,0:T(8,128)S(1)}, f32[32,128]{1,0:T(8,128)S(1)}, u32[]{:S(2)}, u32[]{:S(2)}) %collective-permute-start.7) | collective-permute-done | bytes 16416 | tf_op jit(solution)/shard_map/ppermute | solution.py:413
  34.8 7.1 %collective-permute-start.10 = (f32[32,128]{1,0:T(8,128)S(1)}, f32[32,128]{1,0:T(8,128)S(1)}, u32[]{:S(2)}, u32[]{:S(2)}) collective-permute-start(f32[32,128]{1,0:T(8,128)S(1)} %fusion.3), channel_id=1, source_target_pairs={{0,160},{8,168},{16,176},{24,184},{32,128},{40,136},{48,144},{56,1... | collective-permute-start | bytes 49160 | tf_op jit(solution)/shard_map/ppermute | solution.py:413
  42.0 0.5 %collective-permute-start.8 = (f32[32,128]{1,0:T(8,128)S(1)}, f32[32,128]{1,0:T(8,128)S(1)}, u32[]{:S(2)}, u32[]{:S(2)}) collective-permute-start(f32[32,128]{1,0:T(8,128)S(1)} %fusion.3), channel_id=1, source_target_pairs={{0,192},{8,200},{16,208},{24,216},{32,224},{40,232},{48,240},{56,2... | collective-permute-start | bytes 49160 | tf_op jit(solution)/shard_map/ppermute | solution.py:413
  42.5 1.6 %collective-permute-start.9 = (f32[32,128]{1,0:T(8,128)S(1)}, f32[32,128]{1,0:T(8,128)S(1)}, u32[]{:S(2)}, u32[]{:S(2)}) collective-permute-start(f32[32,128]{1,0:T(8,128)S(1)} %fusion.3), channel_id=1, source_target_pairs={{0,64},{8,72},{16,80},{24,88},{32,96},{40,104},{48,112},{56,120},{... | collective-permute-start | bytes 49160 | tf_op jit(solution)/shard_map/ppermute | solution.py:413
  44.1 0.7 %finish.1 = f32[32,512]{1,0:T(8,128)} custom-call(f32[4,8,16,128]{3,2,1,0:T(8,128)S(1)} %get-tuple-element.28.keep_ref, bf16[4,8,16,128]{3,2,1,0:T(8,128)(2,1)S(1)} %collective-permute-done.2.got_ref, bf16[2,8,16,128]{3,2,1,0:T(8,128)(2,1)S(1)} %collective-permute-done.3.received_ref, f32[8,16,128]{2,1,0:T(8,128)S(1)} %collective-permute-done.4.last_ref), custom_call_target="tpu_custom_call" | custom-call | tf_op jit(solution)/shard_map/finish/pallas_call | solution.py:487
  44.8 3.0 %collective-permute-done.8 = f32[32,128]{1,0:T(8,128)S(1)} collective-permute-done((f32[32,128]{1,0:T(8,128)S(1)}, f32[32,128]{1,0:T(8,128)S(1)}, u32[]{:S(2)}, u32[]{:S(2)}) %collective-permute-start.8) | collective-permute-done | bytes 16416 | tf_op jit(solution)/shard_map/ppermute | solution.py:413
  48.0 0.2 convolution_add_fusion.refs_4_
  48.2 0.9 %turn.1 = f32[5,64,64]{2,1,0:T(8,128)} custom-call(f32[32,128]{1,0:T(8,128)S(1)} %add.77.refs_0_, f32[32,128]{1,0:T(8,128)S(1)} %add.78.refs_1_, f32[32,128]{1,0:T(8,128)S(1)} %add.79.refs_2_, f32[32,128]{1,0:T(8,128)S(1)} %add.80.refs_3_, f32[32,128]{1,0:T(8,128)S(1)} %convolution_add_fusion.refs_4_), custom_call_target="tpu_custom_call" | custom-call | tf_op jit(solution)/shard_map/turn/pallas_call | solution.py:499
  (19 shorter events, 1.0 us)
Async XLA Ops:
  0.6 14.0 %collective-permute-start.1 = (bf16[64,4096]{1,0:T(8,128)(2,1)}, bf16[64,4096]{1,0:T(8,128)(2,1)S(1)}, u32[]{:S(2)}, u32[]{:S(2)}) collective-permute-start(bf16[64,4096]{1,0:T(8,128)(2,1)} %bitcast.30), channel_id=1, source_target_pairs={{0,8},{16,24},{32,40},{48,56},{64,72},{80,88},{96,104},{112,120},{... | collective-permute-start | bytes 1572872 | tf_op jit(solution)/shard_map/ppermute | solution.py:418
  2.3 14.5 %collective-permute-start = (bf16[64,4096]{1,0:T(8,128)(2,1)}, bf16[64,4096]{1,0:T(8,128)(2,1)S(1)}, u32[]{:S(2)}, u32[]{:S(2)}) collective-permute-start(bf16[64,4096]{1,0:T(8,128)(2,1)} %bitcast.31), channel_id=1, source_target_pairs={{8,16},{24,32},{40,48},{56,64},{72,80},{88,96},{104,112},{120,128}... | collective-permute-start | bytes 1572872 | tf_op jit(solution)/shard_map/ppermute | solution.py:418
  17.5 5.8 %collective-permute-start.5 = (f32[32,128]{1,0:T(8,128)S(1)}, f32[32,128]{1,0:T(8,128)S(1)}, u32[]{:S(2)}, u32[]{:S(2)}) collective-permute-start(f32[32,128]{1,0:T(8,128)S(1)} %get-tuple-element.30), channel_id=1, source_target_pairs={{0,8},{8,0},{16,24},{24,16},{32,40},{40,32},{48,56},{56,48},{64,72... | collective-permute-start | bytes 49160 | tf_op jit(solution)/shard_map/ppermute | solution.py:413
  23.0 5.3 %collective-permute-start.2 = (bf16[4,8,16,128]{3,2,1,0:T(8,128)(2,1)S(1)}, bf16[4,8,16,128]{3,2,1,0:T(8,128)(2,1)S(1)}, u32[]{:S(2)}, u32[]{:S(2)}) collective-permute-start(bf16[4,8,16,128]{3,2,1,0:T(8,128)(2,1)S(1)} %get-tuple-element.29), channel_id=1, source_target_pairs={{0,1},{1,0},{2,3},{3,2},{4,5},{5,4},{6,7},{7,6},{8,9},{9,8},{10,11... | collective-permute-start | bytes 393224 | tf_op jit(solution)/shard_map/ppermute | solution.py:413
  23.5 6.6 %collective-permute-start.6 = (f32[32,128]{1,0:T(8,128)S(1)}, f32[32,128]{1,0:T(8,128)S(1)}, u32[]{:S(2)}, u32[]{:S(2)}) collective-permute-start(f32[32,128]{1,0:T(8,128)S(1)} %fusion.7), channel_id=1, source_target_pairs={{0,24},{8,16},{16,8},{24,0},{32,56},{40,48},{48,40},{56,32},{64,88... | collective-permute-start | bytes 49160 | tf_op jit(solution)/shard_map/ppermute | solution.py:413
  28.3 4.6 %collective-permute-start.3 = (bf16[2,8,16,128]{3,2,1,0:T(8,128)(2,1)S(1)}, bf16[2,8,16,128]{3,2,1,0:T(8,128)(2,1)S(1)}, u32[]{:S(2)}, u32[]{:S(2)}) collective-permute-start(bf16[2,8,16,128]{3,2,1,0:T(8,128)(2,1)S(1)} %add_convert_fusion), channel_id=1, source_target_pairs={{0,2},{1,3},{2,0},{3,1},{4,6},{5,7},{6,4},{7,5},{8,10},{9,11},{10,... | collective-permute-start | bytes 196616 | tf_op jit(solution)/shard_map/ppermute | solution.py:413
  30.2 4.5 %collective-permute-start.7 = (f32[32,128]{1,0:T(8,128)S(1)}, f32[32,128]{1,0:T(8,128)S(1)}, u32[]{:S(2)}, u32[]{:S(2)}) collective-permute-start(f32[32,128]{1,0:T(8,128)S(1)} %fusion.5), channel_id=1, source_target_pairs={{0,32},{8,40},{16,48},{24,56},{32,0},{40,8},{48,16},{56,24},{64,96... | collective-permute-start | bytes 49160 | tf_op jit(solution)/shard_map/ppermute | solution.py:413
  33.0 11.1 %collective-permute-start.4 = (f32[8,16,128]{2,1,0:T(8,128)S(1)}, f32[8,16,128]{2,1,0:T(8,128)S(1)}, u32[]{:S(2)}, u32[]{:S(2)}) collective-permute-start(f32[8,16,128]{2,1,0:T(8,128)S(1)} %add_bitcast_fusion), channel_id=1, source_target_pairs={{0,6},{1,7},{2,4},{3,5},{4,2},{5,3},{6,0},{7,1},{8,14},{9,15},{10,... | collective-permute-start | bytes 196616 | tf_op jit(solution)/shard_map/ppermute | solution.py:413
  34.8 10.0 %collective-permute-start.10 = (f32[32,128]{1,0:T(8,128)S(1)}, f32[32,128]{1,0:T(8,128)S(1)}, u32[]{:S(2)}, u32[]{:S(2)}) collective-permute-start(f32[32,128]{1,0:T(8,128)S(1)} %fusion.3), channel_id=1, source_target_pairs={{0,160},{8,168},{16,176},{24,184},{32,128},{40,136},{48,144},{56,1... | collective-permute-start | bytes 49160 | tf_op jit(solution)/shard_map/ppermute | solution.py:413
  42.0 5.8 %collective-permute-start.8 = (f32[32,128]{1,0:T(8,128)S(1)}, f32[32,128]{1,0:T(8,128)S(1)}, u32[]{:S(2)}, u32[]{:S(2)}) collective-permute-start(f32[32,128]{1,0:T(8,128)S(1)} %fusion.3), channel_id=1, source_target_pairs={{0,192},{8,200},{16,208},{24,216},{32,224},{40,232},{48,240},{56,2... | collective-permute-start | bytes 49160 | tf_op jit(solution)/shard_map/ppermute | solution.py:413
  42.5 5.3 %collective-permute-start.9 = (f32[32,128]{1,0:T(8,128)S(1)}, f32[32,128]{1,0:T(8,128)S(1)}, u32[]{:S(2)}, u32[]{:S(2)}) collective-permute-start(f32[32,128]{1,0:T(8,128)S(1)} %fusion.3), channel_id=1, source_target_pairs={{0,64},{8,72},{16,80},{24,88},{32,96},{40,104},{48,112},{56,120},{... | collective-permute-start | bytes 49160 | tf_op jit(solution)/shard_map/ppermute | solution.py:413

commit v12 on v8

--- a/solution.py
+++ b/solution.py
@@ -233,33 +233,36 @@
     part_ref[...] = jnp.concatenate([turned[:half], turned[half:]], axis=1)
 
 
-def gram_kernel(
-    scale, place_ref, far_ref, basis_ref, coeff_any, keep_ref, send_ref, gram, coeff_ref, sems
-):
+def coeff_kernel(far_ref, basis_ref, coeff_any, coeff_ref, sems):
+    count, _, size = basis_ref.shape
+    copies = []
+    for first in range(0, count, PER_STEP):
+        for leaf in range(first, first + PER_STEP):
+            far = far_ref[:, leaf * size : (leaf + 1) * size]
+            coeff_ref[leaf] = dot(basis_ref[leaf], far, NT)
+        these = pl.ds(first, PER_STEP)
+        copies.append(
+            pltpu.make_async_copy(coeff_ref.at[these], coeff_any.at[these], sems.at[len(copies)])
+        )
+        copies[-1].start()
+    for copy in copies:
+        copy.wait()
+
+
+def gram_kernel(scale, place_ref, far_ref, basis_ref, keep_ref, send_ref, gram):
     parts, rows, pairs, width = keep_ref.shape
     parts = 2 * parts
     rank = width // 2
     size = basis_ref.shape[2]
     lane = lax.broadcasted_iota(jnp.int32, (rank, width), 1)
-    copies = []
     for first in range(0, pairs, PER_STEP):
         stacks = []
         for pair in range(first, first + PER_STEP):
-            both = []
-            for leaf in (pair, pair + pairs):
-                far = far_ref[:, leaf * size : (leaf + 1) * size]
-                coeff = dot(basis_ref[leaf], far, NT)
-                coeff_ref[leaf] = coeff
-                both.append(coeff.astype(jnp.bfloat16))
-            stacks.append(jnp.concatenate(both, axis=0))
-        for start in (first, first + pairs):
-            these = pl.ds(start, PER_STEP)
-            copies.append(
-                pltpu.make_async_copy(
-                    coeff_ref.at[these], coeff_any.at[these], sems.at[len(copies)]
-                )
-            )
-            copies[-1].start()
+            both = [
+                dot(basis_ref[leaf], far_ref[:, leaf * size : (leaf + 1) * size], NT)
+                for leaf in (pair, pair + pairs)
+            ]
+            stacks.append(jnp.concatenate(both, axis=0).astype(jnp.bfloat16))
         for pair, stacked in enumerate(stacks, first):
             product = dot(stacked, stacked, NT)
             value = jnp.where(lane < rank, product[:rank], product[rank:]) * scale
@@ -270,8 +273,6 @@
         for row in range(rows):
             at = pl.multiple_of((first + row) * pairs, pairs)
             target[relative // 2, row] = gram[pl.ds(at, pairs), :]
-    for copy in copies:
-        copy.wait()
 
 
 def finish_kernel(keep_ref, got_ref, received_ref, last_ref, out_ref):
@@ -385,6 +386,23 @@
     )(tasks, resident(side), near, blocks, weight)
 
 
+def coeff_pass(far, basis):
+    count, rank, _ = basis.shape
+    columns = far.shape[0]
+    return pl.pallas_call(
+        coeff_kernel,
+        in_specs=[VMEM, VMEM],
+        out_specs=ANY,
+        out_shape=pltpu.HBM((count, rank, columns), jnp.float32),
+        scratch_shapes=[
+            pltpu.VMEM((count, rank, columns), jnp.float32),
+            pltpu.SemaphoreType.DMA((count // PER_STEP,)),
+        ],
+        compiler_params=params(8),
+        name="coeff_pass",
+    )(far, basis)
+
+
 def gram_pass(place, far, basis, parts):
     count, rank, _ = basis.shape
     columns = far.shape[0]
@@ -393,17 +411,9 @@
     return pl.pallas_call(
         functools.partial(gram_kernel, 1.0 / (columns * parts)),
         in_specs=[SMEM, VMEM, VMEM],
-        out_specs=(ANY, VMEM, VMEM),
-        out_shape=(
-            pltpu.HBM((count, rank, columns), jnp.float32),
-            pltpu.VMEM(shape, jnp.float32),
-            pltpu.VMEM(shape, jnp.float32),
-        ),
-        scratch_shapes=[
-            pltpu.VMEM((rank * pairs, 2 * rank), jnp.float32),
-            pltpu.VMEM((count, rank, columns), jnp.float32),
-            pltpu.SemaphoreType.DMA((count // PER_STEP,)),
-        ],
+        out_specs=(VMEM, VMEM),
+        out_shape=(pltpu.VMEM(shape, jnp.float32), pltpu.VMEM(shape, jnp.float32)),
+        scratch_shapes=[pltpu.VMEM((rank * pairs, 2 * rank), jnp.float32)],
         compiler_params=params(8),
         name="gram_pass",
     )(place, far, basis)
@@ -466,9 +476,12 @@
     for height in range(heights):
         if height:
             accum = jnp.dot(accum, twice[height - 1], precision=lax.Precision.HIGHEST)
+        if height == heights - 1:
+            accum, far = lax.optimization_barrier((accum, far))
+            coeffs = coeff_pass(far, basis)
         other = exchange(accum, "leaf", flips[height])
         if height == 0:
-            coeffs, keep, send = gram_pass(place.reshape(1), far, basis, parts)
+            keep, send = gram_pass(place.reshape(1), far, basis, parts)
             got = exchange(send, "samp", 1)
         elif height == 2:
             leaving = (keep[1:3] + got[1:3]).astype(jnp.bfloat16)

time: 49.2 us -> 49.4 us (level)
  Pallas kernels: 13.4 us -> 14.3 us
  starting transfers between devices: 25.6 us -> 25.1 us
    pallas_call x0 -> x1, Pallas kernels: none -> 1.19 us  [coeff_pass(): pl.pallas_call(coeff_kernel, in_specs=[VMEM, VMEM], out_specs=ANY, out_sh...]
    pallas_call x1, Pallas kernels: 1.44 us -> 0.83 us  [gram_pass(): pl.pallas_call(functools.partial(gram_kernel, 1.0 / (columns * parts)), i...]
  transfers between devices with their start and end apart: 10 -> 10, of which waited for: 6 -> 5; matrix products, arithmetic and copies ran while one was open for 8% -> 8% of each run, Pallas kernels for 24% -> 26%
where the time goes in v12:
time: 49.4 us; the launch traced here: 49.1 us
  starting transfers between devices  25.1 us (51%)
  Pallas kernels  14.3 us (29%)
  waiting for transfers between devices  4.9 us (10%)
  local copies, waits for them, and re-layouts  3.32 us (7%)
  between operations  0.76 us (2%)
  matrix products  0.62 us (1%)
    ppermute x8, starting transfers between devices, exchange(): lax.ppermute(value, axis, [(i, i ^ flip) for i in range(lax.axis_size(axi...  22.8 us
    pallas_call x1, Pallas kernels, own_pass(): pl.pallas_call(own_kernel, in_specs=[ANY, ANY, VMEM, VMEM, ANY, ANY, ANY,...  7.78 us
    ppermute x8, waiting for transfers between devices, exchange(): lax.ppermute(value, axis, [(i, i ^ flip) for i in range(lax.axis_size(axi...  4.42 us
    ppermute x2, starting transfers between devices, swap(): return lax.ppermute(value, axis, pairs + [(j, i) for i, j in pairs])  2.35 us
    pallas_call x1, Pallas kernels, side_pass(): pl.pallas_call(kernel, in_specs=[SMEM] + [VMEM] * 3, out_specs=VMEM, out_...  2.23 us
    reshape x1, local copies, waits for them, and re-layouts, shards(): inner_transfer.reshape(-1, rank)  2.03 us
    pallas_call x1, Pallas kernels, coeff_pass(): pl.pallas_call(coeff_kernel, in_specs=[VMEM, VMEM], out_specs=ANY, out_sh...  1.19 us
    dynamic_slice x1, local copies, waits for them, and re-layouts, shards(): lax.dynamic_slice_in_dim(upper_transfer, offset + jnp.right_shift(device,...  1.07 us
  transfers between devices with their start and end apart: 10, of which 5 were waited for; matrix products, arithmetic and copies ran while one was open for 8% of the time, Pallas kernels for 26%

profile of v12, /device:TPU:6, one launch (start us, length us, event | category | flops | bytes accessed | tf_op | source)
XLA Modules:
  0.0 49.1 jit_solution(11323650146160360760)
XLA Ops:
  0.6 1.7 %collective-permute-start.1 = (bf16[64,4096]{1,0:T(8,128)(2,1)}, bf16[64,4096]{1,0:T(8,128)(2,1)S(1)}, u32[]{:S(2)}, u32[]{:S(2)}) collective-permute-start(bf16[64,4096]{1,0:T(8,128)(2,1)} %bitcast.27), channel_id=1, source_target_pairs={{0,8},{16,24},{32,40},{48,56},{64,72},{80,88},{96,104},{112,120},{... | collective-permute-start | bytes 1572872 | tf_op jit(solution)/shard_map/ppermute | solution.py:428
  2.3 0.7 %collective-permute-start = (bf16[64,4096]{1,0:T(8,128)(2,1)}, bf16[64,4096]{1,0:T(8,128)(2,1)S(1)}, u32[]{:S(2)}, u32[]{:S(2)}) collective-permute-start(bf16[64,4096]{1,0:T(8,128)(2,1)} %bitcast.28), channel_id=1, source_target_pairs={{8,16},{24,32},{40,48},{56,64},{72,80},{88,96},{104,112},{120,128}... | collective-permute-start | bytes 1572872 | tf_op jit(solution)/shard_map/ppermute | solution.py:428
  3.0 1.1 %constant_dynamic-slice_fusion = (bf16[1,4096]{1,0:T(2,128)(2,1)S(1)}, bf16[1,4096]{1,0:T(2,128)(2,1)S(1)}, bf16[1,4096]{1,0:T(2,128)(2,1)S(1)}, bf16[1,4096]{1,0:T(2,128)(2,1)S(1)}, bf16[1,4096]{1,0:T(2,128)(2,1)S(1)}) fusion(bf16[62,4096]{1,0:T(8,128)(2,1)} %param.15, s32[]{:T(128)S(6)} %select_n.19, s32[]{:T(128)S(6)} %select_n.17, s32[]{:T(128)S(6)} %select_n.16, ...), kind=kLoop, calls=%fused_computation.17 | loop fusion | bytes 81940 | tf_op jit(solution)/shard_map/dynamic_slice | solution.py:452
  4.3 2.0 %reshape.26.mats_ref = bf16[3968,64]{1,0:T(8,128)(2,1)S(1)} reshape(bf16[62,4096]{1,0:T(8,128)(2,1)} %param.14) | data formatting | bytes 1015808 | tf_op jit(solution)/shard_map/reshape | solution.py:464
  6.3 7.8 %own_pass.1 = (f32[32,64,128]{2,1,0:T(8,128)S(1)}, bf16[256,128,128]{2,1,0:T(8,128)(2,1)S(1)}, bf16[32,64,128]{2,1,0:T(8,128)(2,1)S(1)}, bf16[128,4096]{1,0:T(8,...) custom-call(s32[8,32]{1,0:T(8,128)} %bitcast.31, s32[1,32]{1,0:T(1,128)} %bitcast.32, ...), custom_call_target="tpu_custom_call" | custom-call | tf_op jit(solution)/shard_map/own_pass/pallas_call | solution.py:314
  14.1 0.5 collective-permute-done.1.side_ref
  14.6 2.2 %side_pass.1.near_ref = f32[32,64,128]{2,1,0:T(8,128)S(1)} custom-call(s32[8,128]{1,0:T(8,128)S(4)} %get-tuple-element.20.task_ref, bf16[64,4096]{1,0:T(8,128)(2,1)S(1)} %collective-permute-done.1.side_ref, f32[32,64,128]{2,1,0:T(8,128)S(1)} %get-tuple-element.21.near_ref, ...), custom_call_target="tpu_custom_call", output_to_operand_aliasing={{}: (2, {})} | custom-call | tf_op jit(solution)/shard_map/side_pass/pallas_call | solution.py:358
  16.8 0.6 %far_pass.1 = (bf16[64,4096]{1,0:T(8,128)(2,1)S(1)}, f32[32,128]{1,0:T(8,128)S(1)}, f32[32,64,128]{2,1,0:T(8,128)S(1)}) custom-call(s32[8,128]{1,0:T(8,128)S(4)} %get-tuple-element.19.task_ref, bf16[64,4096]{1,0:T(8,128)(2,1)S(1)} %collective-permute-done.side_ref, f32[32,64,128]{2,1,0:T(8,128)S(1)} %side_pass.1.near_ref, ...), custom_call_target="tpu_custom_call", output_to_operand_aliasing={{2}: (2, {})} | custom-call | tf_op jit(solution)/shard_map/far_pass/pallas_call | solution.py:373
  17.5 3.7 %collective-permute-start.2 = (f32[32,128]{1,0:T(8,128)S(1)}, f32[32,128]{1,0:T(8,128)S(1)}, u32[]{:S(2)}, u32[]{:S(2)}) collective-permute-start(f32[32,128]{1,0:T(8,128)S(1)} %get-tuple-element.24), channel_id=1, source_target_pairs={{0,8},{8,0},{16,24},{24,16},{32,40},{40,32},{48,56},{56,48},{64,72... | collective-permute-start | bytes 49160 | tf_op jit(solution)/shard_map/ppermute | solution.py:423
  21.2 0.8 %gram_pass.1 = (f32[4,8,16,128]{3,2,1,0:T(8,128)S(1)}, f32[4,8,16,128]{3,2,1,0:T(8,128)S(1)}) custom-call(s32[1]{0:T(128)} %bitcast.7.place_ref, bf16[64,4096]{1,0:T(8,128)(2,1)S(1)} %get-tuple-element.32.far_ref, bf16[32,64,128]{2,1,0:T(8,128)(2,1)S(1)} %get-tuple-element.27.basis_ref), custom_call_target="tpu_custom_call" | custom-call | tf_op jit(solution)/shard_map/gram_pass/pallas_call | solution.py:411
  22.1 0.8 %collective-permute-done.2 = f32[32,128]{1,0:T(8,128)S(1)} collective-permute-done((f32[32,128]{1,0:T(8,128)S(1)}, f32[32,128]{1,0:T(8,128)S(1)}, u32[]{:S(2)}, u32[]{:S(2)}) %collective-permute-start.2) | collective-permute-done | bytes 16416 | tf_op jit(solution)/shard_map/ppermute | solution.py:423
  23.1 4.6 %collective-permute-start.3 = (f32[32,128]{1,0:T(8,128)S(1)}, f32[32,128]{1,0:T(8,128)S(1)}, u32[]{:S(2)}, u32[]{:S(2)}) collective-permute-start(f32[32,128]{1,0:T(8,128)S(1)} %fusion.9), channel_id=1, source_target_pairs={{0,24},{8,16},{16,8},{24,0},{32,56},{40,48},{48,40},{56,32},{64,88... | collective-permute-start | bytes 49160 | tf_op jit(solution)/shard_map/ppermute | solution.py:423
  27.7 1.7 %collective-permute-done.3 = f32[32,128]{1,0:T(8,128)S(1)} collective-permute-done((f32[32,128]{1,0:T(8,128)S(1)}, f32[32,128]{1,0:T(8,128)S(1)}, u32[]{:S(2)}, u32[]{:S(2)}) %collective-permute-start.3) | collective-permute-done | bytes 16416 | tf_op jit(solution)/shard_map/ppermute | solution.py:423
  29.4 0.2 fusion.7
  29.6 3.4 %collective-permute-start.4 = (f32[32,128]{1,0:T(8,128)S(1)}, f32[32,128]{1,0:T(8,128)S(1)}, u32[]{:S(2)}, u32[]{:S(2)}) collective-permute-start(f32[32,128]{1,0:T(8,128)S(1)} %fusion.7), channel_id=1, source_target_pairs={{0,32},{8,40},{16,48},{24,56},{32,0},{40,8},{48,16},{56,24},{64,96... | collective-permute-start | bytes 49160 | tf_op jit(solution)/shard_map/ppermute | solution.py:423
  33.0 0.9 %collective-permute-start.7 = (bf16[2,8,16,128]{3,2,1,0:T(8,128)(2,1)S(1)}, bf16[2,8,16,128]{3,2,1,0:T(8,128)(2,1)S(1)}, u32[]{:S(2)}, u32[]{:S(2)}) collective-permute-start(bf16[2,8,16,128]{3,2,1,0:T(8,128)(2,1)S(1)} %fusion), channel_id=1, source_target_pairs={{0,2},{1,3},{2,0},{3,1},{4,6},{5,7},{6,4},{7,5},{8,10},{9,11},{10,... | collective-permute-start | bytes 196616 | tf_op jit(solution)/shard_map/ppermute | solution.py:423
  33.9 0.8 %collective-permute-done.4 = f32[32,128]{1,0:T(8,128)S(1)} collective-permute-done((f32[32,128]{1,0:T(8,128)S(1)}, f32[32,128]{1,0:T(8,128)S(1)}, u32[]{:S(2)}, u32[]{:S(2)}) %collective-permute-start.4) | collective-permute-done | bytes 16416 | tf_op jit(solution)/shard_map/ppermute | solution.py:423
  34.8 3.5 %collective-permute-start.6 = (f32[32,128]{1,0:T(8,128)S(1)}, f32[32,128]{1,0:T(8,128)S(1)}, u32[]{:S(2)}, u32[]{:S(2)}) collective-permute-start(f32[32,128]{1,0:T(8,128)S(1)} %fusion.5), channel_id=1, source_target_pairs={{0,64},{8,72},{16,80},{24,88},{32,96},{40,104},{48,112},{56,120},{... | collective-permute-start | bytes 49160 | tf_op jit(solution)/shard_map/ppermute | solution.py:423
  38.4 0.6 %collective-permute-start.8 = (f32[8,16,128]{2,1,0:T(8,128)S(1)}, f32[8,16,128]{2,1,0:T(8,128)S(1)}, u32[]{:S(2)}, u32[]{:S(2)}) collective-permute-start(f32[8,16,128]{2,1,0:T(8,128)S(1)} %fusion.2), channel_id=1, source_target_pairs={{0,6},{1,7},{2,4},{3,5},{4,2},{5,3},{6,0},{7,1},{8,14},{9,15},{10,... | collective-permute-start | bytes 196616 | tf_op jit(solution)/shard_map/ppermute | solution.py:423
  38.9 1.1 %collective-permute-done.6 = f32[32,128]{1,0:T(8,128)S(1)} collective-permute-done((f32[32,128]{1,0:T(8,128)S(1)}, f32[32,128]{1,0:T(8,128)S(1)}, u32[]{:S(2)}, u32[]{:S(2)}) %collective-permute-start.6) | collective-permute-done | bytes 16416 | tf_op jit(solution)/shard_map/ppermute | solution.py:423
  40.2 6.0 %collective-permute-start.9 = (f32[32,128]{1,0:T(8,128)S(1)}, f32[32,128]{1,0:T(8,128)S(1)}, u32[]{:S(2)}, u32[]{:S(2)}) collective-permute-start(f32[32,128]{1,0:T(8,128)S(1)} %fusion.3), channel_id=1, source_target_pairs={{0,192},{8,200},{16,208},{24,216},{32,224},{40,232},{48,240},{56,2... | collective-permute-start | bytes 49160 | tf_op jit(solution)/shard_map/ppermute | solution.py:423
  46.2 1.2 %coeff_pass.1 = f32[32,64,64]{2,1,0:T(8,128)} custom-call(bf16[64,4096]{1,0:T(8,128)(2,1)S(1)} %get-tuple-element.32.far_ref, bf16[32,64,128]{2,1,0:T(8,128)(2,1)S(1)} %get-tuple-element.27.basis_ref), custom_call_target="tpu_custom_call" | custom-call | tf_op jit(solution)/shard_map/coeff_pass/pallas_call | solution.py:392
  47.4 0.7 %finish.1 = f32[32,512]{1,0:T(8,128)} custom-call(f32[4,8,16,128]{3,2,1,0:T(8,128)S(1)} %get-tuple-element.28.keep_ref, f32[4,8,16,128]{3,2,1,0:T(8,128)S(1)} %collective-permute-done.5.got_ref, bf16[2,8,16,128]{3,2,1,0:T(8,128)(2,1)S(1)} %collective-permute-done.7.received_ref, f32[8,16,128]{2,1,0:T(8,128)S(1)} %collective-permute-done.8.last_ref), custom_call_target="tpu_custom_call" | custom-call | tf_op jit(solution)/shard_map/finish/pallas_call | solution.py:495
  48.2 0.9 %turn.1 = f32[5,64,64]{2,1,0:T(8,128)} custom-call(f32[32,128]{1,0:T(8,128)S(1)} %add.56.refs_0_, f32[32,128]{1,0:T(8,128)S(1)} %add.57.refs_1_, f32[32,128]{1,0:T(8,128)S(1)} %add.59.refs_2_, f32[32,128]{1,0:T(8,128)S(1)} %add.63.refs_3_, f32[32,128]{1,0:T(8,128)S(1)} %add.64.refs_4_), custom_call_target="tpu_custom_call" | custom-call | tf_op jit(solution)/shard_map/turn/pallas_call | solution.py:506
  (18 shorter events, 0.9 us)
Async XLA Ops:
  0.6 14.0 %collective-permute-start.1 = (bf16[64,4096]{1,0:T(8,128)(2,1)}, bf16[64,4096]{1,0:T(8,128)(2,1)S(1)}, u32[]{:S(2)}, u32[]{:S(2)}) collective-permute-start(bf16[64,4096]{1,0:T(8,128)(2,1)} %bitcast.27), channel_id=1, source_target_pairs={{0,8},{16,24},{32,40},{48,56},{64,72},{80,88},{96,104},{112,120},{... | collective-permute-start | bytes 1572872 | tf_op jit(solution)/shard_map/ppermute | solution.py:428
  2.3 14.5 %collective-permute-start = (bf16[64,4096]{1,0:T(8,128)(2,1)}, bf16[64,4096]{1,0:T(8,128)(2,1)S(1)}, u32[]{:S(2)}, u32[]{:S(2)}) collective-permute-start(bf16[64,4096]{1,0:T(8,128)(2,1)} %bitcast.28), channel_id=1, source_target_pairs={{8,16},{24,32},{40,48},{56,64},{72,80},{88,96},{104,112},{120,128}... | collective-permute-start | bytes 1572872 | tf_op jit(solution)/shard_map/ppermute | solution.py:428
  17.5 5.4 %collective-permute-start.2 = (f32[32,128]{1,0:T(8,128)S(1)}, f32[32,128]{1,0:T(8,128)S(1)}, u32[]{:S(2)}, u32[]{:S(2)}) collective-permute-start(f32[32,128]{1,0:T(8,128)S(1)} %get-tuple-element.24), channel_id=1, source_target_pairs={{0,8},{8,0},{16,24},{24,16},{32,40},{40,32},{48,56},{56,48},{64,72... | collective-permute-start | bytes 49160 | tf_op jit(solution)/shard_map/ppermute | solution.py:423
  22.0 10.9 %collective-permute-start.5 = (f32[4,8,16,128]{3,2,1,0:T(8,128)S(1)}, f32[4,8,16,128]{3,2,1,0:T(8,128)S(1)}, u32[]{:S(2)}, u32[]{:S(2)}) collective-permute-start(f32[4,8,16,128]{3,2,1,0:T(8,128)S(1)} %get-tuple-element.29), channel_id=1, source_target_pairs={{0,1},{1,0},{2,3},{3,2},{4,5},{5,4},{6,7},{7,6},{8,9},{9,8},{10,11... | collective-permute-start | bytes 786440 | tf_op jit(solution)/shard_map/ppermute | solution.py:423
  23.1 6.4 %collective-permute-start.3 = (f32[32,128]{1,0:T(8,128)S(1)}, f32[32,128]{1,0:T(8,128)S(1)}, u32[]{:S(2)}, u32[]{:S(2)}) collective-permute-start(f32[32,128]{1,0:T(8,128)S(1)} %fusion.9), channel_id=1, source_target_pairs={{0,24},{8,16},{16,8},{24,0},{32,56},{40,48},{48,40},{56,32},{64,88... | collective-permute-start | bytes 49160 | tf_op jit(solution)/shard_map/ppermute | solution.py:423
  29.6 5.1 %collective-permute-start.4 = (f32[32,128]{1,0:T(8,128)S(1)}, f32[32,128]{1,0:T(8,128)S(1)}, u32[]{:S(2)}, u32[]{:S(2)}) collective-permute-start(f32[32,128]{1,0:T(8,128)S(1)} %fusion.7), channel_id=1, source_target_pairs={{0,32},{8,40},{16,48},{24,56},{32,0},{40,8},{48,16},{56,24},{64,96... | collective-permute-start | bytes 49160 | tf_op jit(solution)/shard_map/ppermute | solution.py:423
  33.0 5.4 %collective-permute-start.7 = (bf16[2,8,16,128]{3,2,1,0:T(8,128)(2,1)S(1)}, bf16[2,8,16,128]{3,2,1,0:T(8,128)(2,1)S(1)}, u32[]{:S(2)}, u32[]{:S(2)}) collective-permute-start(bf16[2,8,16,128]{3,2,1,0:T(8,128)(2,1)S(1)} %fusion), channel_id=1, source_target_pairs={{0,2},{1,3},{2,0},{3,1},{4,6},{5,7},{6,4},{7,5},{8,10},{9,11},{10,... | collective-permute-start | bytes 196616 | tf_op jit(solution)/shard_map/ppermute | solution.py:423
  34.8 5.2 %collective-permute-start.6 = (f32[32,128]{1,0:T(8,128)S(1)}, f32[32,128]{1,0:T(8,128)S(1)}, u32[]{:S(2)}, u32[]{:S(2)}) collective-permute-start(f32[32,128]{1,0:T(8,128)S(1)} %fusion.5), channel_id=1, source_target_pairs={{0,64},{8,72},{16,80},{24,88},{32,96},{40,104},{48,112},{56,120},{... | collective-permute-start | bytes 49160 | tf_op jit(solution)/shard_map/ppermute | solution.py:423
  38.4 9.1 %collective-permute-start.8 = (f32[8,16,128]{2,1,0:T(8,128)S(1)}, f32[8,16,128]{2,1,0:T(8,128)S(1)}, u32[]{:S(2)}, u32[]{:S(2)}) collective-permute-start(f32[8,16,128]{2,1,0:T(8,128)S(1)} %fusion.2), channel_id=1, source_target_pairs={{0,6},{1,7},{2,4},{3,5},{4,2},{5,3},{6,0},{7,1},{8,14},{9,15},{10,... | collective-permute-start | bytes 196616 | tf_op jit(solution)/shard_map/ppermute | solution.py:423
  40.2 7.9 %collective-permute-start.9 = (f32[32,128]{1,0:T(8,128)S(1)}, f32[32,128]{1,0:T(8,128)S(1)}, u32[]{:S(2)}, u32[]{:S(2)}) collective-permute-start(f32[32,128]{1,0:T(8,128)S(1)} %fusion.3), channel_id=1, source_target_pairs={{0,192},{8,200},{16,208},{24,216},{32,224},{40,232},{48,240},{56,2... | collective-permute-start | bytes 49160 | tf_op jit(solution)/shard_map/ppermute | solution.py:423

commit v13 on v12

--- a/solution.py
+++ b/solution.py
@@ -476,10 +476,12 @@
     for height in range(heights):
         if height:
             accum = jnp.dot(accum, twice[height - 1], precision=lax.Precision.HIGHEST)
-        if height == heights - 1:
+        if height == 1:
             accum, far = lax.optimization_barrier((accum, far))
             coeffs = coeff_pass(far, basis)
         other = exchange(accum, "leaf", flips[height])
+        if height == 1:
+            other, coeffs = lax.optimization_barrier((other, coeffs))
         if height == 0:
             keep, send = gram_pass(place.reshape(1), far, basis, parts)
             got = exchange(send, "samp", 1)

time: 49.4 us -> 49.1 us (level)
  waiting for transfers between devices: 4.9 us -> 4.37 us
  transfers between devices with their start and end apart: 10 -> 10, of which waited for: 5 -> 6; matrix products, arithmetic and copies ran while one was open for 8% -> 8% of each run, Pallas kernels for 26% -> 27%
where the time goes in v13:
time: 49.1 us; the launch traced here: 48.9 us
  starting transfers between devices  25.2 us (51%)
  Pallas kernels  14.6 us (30%)
  waiting for transfers between devices  4.37 us (9%)
  local copies, waits for them, and re-layouts  3.32 us (7%)
  between operations  0.76 us (2%)
  matrix products  0.62 us (1%)
    ppermute x8, starting transfers between devices, exchange(): lax.ppermute(value, axis, [(i, i ^ flip) for i in range(lax.axis_size(axi...  22.8 us
    pallas_call x1, Pallas kernels, own_pass(): pl.pallas_call(own_kernel, in_specs=[ANY, ANY, VMEM, VMEM, ANY, ANY, ANY,...  8.09 us
    ppermute x8, waiting for transfers between devices, exchange(): lax.ppermute(value, axis, [(i, i ^ flip) for i in range(lax.axis_size(axi...  4.2 us
    ppermute x2, starting transfers between devices, swap(): return lax.ppermute(value, axis, pairs + [(j, i) for i, j in pairs])  2.35 us
    pallas_call x1, Pallas kernels, side_pass(): pl.pallas_call(kernel, in_specs=[SMEM] + [VMEM] * 3, out_specs=VMEM, out_...  2.23 us
    reshape x1, local copies, waits for them, and re-layouts, shards(): inner_transfer.reshape(-1, rank)  2.03 us
    pallas_call x1, Pallas kernels, coeff_pass(): pl.pallas_call(coeff_kernel, in_specs=[VMEM, VMEM], out_specs=ANY, out_sh...  1.19 us
    dynamic_slice x1, local copies, waits for them, and re-layouts, shards(): lax.dynamic_slice_in_dim(upper_transfer, offset + jnp.right_shift(device,...  1.07 us
  transfers between devices with their start and end apart: 10, of which 6 were waited for; matrix products, arithmetic and copies ran while one was open for 8% of the time, Pallas kernels for 27%

profile of v13, /device:TPU:6, one launch (start us, length us, event | category | flops | bytes accessed | tf_op | source)
XLA Modules:
  0.0 48.9 jit_solution(10035999484332408523)
XLA Ops:
  0.6 1.7 %collective-permute-start.1 = (bf16[64,4096]{1,0:T(8,128)(2,1)}, bf16[64,4096]{1,0:T(8,128)(2,1)S(1)}, u32[]{:S(2)}, u32[]{:S(2)}) collective-permute-start(bf16[64,4096]{1,0:T(8,128)(2,1)} %bitcast.27), channel_id=1, source_target_pairs={{0,8},{16,24},{32,40},{48,56},{64,72},{80,88},{96,104},{112,120},{... | collective-permute-start | bytes 1572872 | tf_op jit(solution)/shard_map/ppermute | solution.py:428
  2.3 0.7 %collective-permute-start = (bf16[64,4096]{1,0:T(8,128)(2,1)}, bf16[64,4096]{1,0:T(8,128)(2,1)S(1)}, u32[]{:S(2)}, u32[]{:S(2)}) collective-permute-start(bf16[64,4096]{1,0:T(8,128)(2,1)} %bitcast.28), channel_id=1, source_target_pairs={{8,16},{24,32},{40,48},{56,64},{72,80},{88,96},{104,112},{120,128}... | collective-permute-start | bytes 1572872 | tf_op jit(solution)/shard_map/ppermute | solution.py:428
  3.0 1.1 %constant_dynamic-slice_fusion = (bf16[1,4096]{1,0:T(2,128)(2,1)S(1)}, bf16[1,4096]{1,0:T(2,128)(2,1)S(1)}, bf16[1,4096]{1,0:T(2,128)(2,1)S(1)}, bf16[1,4096]{1,0:T(2,128)(2,1)S(1)}, bf16[1,4096]{1,0:T(2,128)(2,1)S(1)}) fusion(bf16[62,4096]{1,0:T(8,128)(2,1)} %param.15, s32[]{:T(128)S(6)} %select_n.19, s32[]{:T(128)S(6)} %select_n.17, s32[]{:T(128)S(6)} %select_n.16, ...), kind=kLoop, calls=%fused_computation.17 | loop fusion | bytes 81940 | tf_op jit(solution)/shard_map/dynamic_slice | solution.py:452
  4.3 2.0 %reshape.26.mats_ref = bf16[3968,64]{1,0:T(8,128)(2,1)S(1)} reshape(bf16[62,4096]{1,0:T(8,128)(2,1)} %param.14) | data formatting | bytes 1015808 | tf_op jit(solution)/shard_map/reshape | solution.py:464
  6.3 8.1 %own_pass.1 = (f32[32,64,128]{2,1,0:T(8,128)S(1)}, bf16[256,128,128]{2,1,0:T(8,128)(2,1)S(1)}, bf16[32,64,128]{2,1,0:T(8,128)(2,1)S(1)}, bf16[128,4096]{1,0:T(8,...) custom-call(s32[8,32]{1,0:T(8,128)} %bitcast.31, s32[1,32]{1,0:T(1,128)} %bitcast.32, ...), custom_call_target="tpu_custom_call" | custom-call | tf_op jit(solution)/shard_map/own_pass/pallas_call | solution.py:314
  14.4 0.2 collective-permute-done.1.side_ref
  14.6 2.2 %side_pass.1.near_ref = f32[32,64,128]{2,1,0:T(8,128)S(1)} custom-call(s32[8,128]{1,0:T(8,128)S(4)} %get-tuple-element.22.task_ref, bf16[64,4096]{1,0:T(8,128)(2,1)S(1)} %collective-permute-done.1.side_ref, f32[32,64,128]{2,1,0:T(8,128)S(1)} %get-tuple-element.23.near_ref, ...), custom_call_target="tpu_custom_call", output_to_operand_aliasing={{}: (2, {})} | custom-call | tf_op jit(solution)/shard_map/side_pass/pallas_call | solution.py:358
  16.8 0.6 %far_pass.1 = (bf16[64,4096]{1,0:T(8,128)(2,1)S(1)}, f32[32,128]{1,0:T(8,128)S(1)}, f32[32,64,128]{2,1,0:T(8,128)S(1)}) custom-call(s32[8,128]{1,0:T(8,128)S(4)} %get-tuple-element.21.task_ref, bf16[64,4096]{1,0:T(8,128)(2,1)S(1)} %collective-permute-done.side_ref, f32[32,64,128]{2,1,0:T(8,128)S(1)} %side_pass.1.near_ref, ...), custom_call_target="tpu_custom_call", output_to_operand_aliasing={{2}: (2, {})} | custom-call | tf_op jit(solution)/shard_map/far_pass/pallas_call | solution.py:373
  17.5 4.3 %collective-permute-start.2 = (f32[32,128]{1,0:T(8,128)S(1)}, f32[32,128]{1,0:T(8,128)S(1)}, u32[]{:S(2)}, u32[]{:S(2)}) collective-permute-start(f32[32,128]{1,0:T(8,128)S(1)} %get-tuple-element.26), channel_id=1, source_target_pairs={{0,8},{8,0},{16,24},{24,16},{32,40},{40,32},{48,56},{56,48},{64,72... | collective-permute-start | bytes 49160 | tf_op jit(solution)/shard_map/ppermute | solution.py:423
  21.8 0.8 %gram_pass.1 = (f32[4,8,16,128]{3,2,1,0:T(8,128)S(1)}, f32[4,8,16,128]{3,2,1,0:T(8,128)S(1)}) custom-call(s32[1]{0:T(128)} %bitcast.6.place_ref, bf16[64,4096]{1,0:T(8,128)(2,1)S(1)} %get-tuple-element.30.far_ref, bf16[32,64,128]{2,1,0:T(8,128)(2,1)S(1)} %get-tuple-element.31.basis_ref), custom_call_target="tpu_custom_call" | custom-call | tf_op jit(solution)/shard_map/gram_pass/pallas_call | solution.py:411
  22.7 0.8 %collective-permute-done.2 = f32[32,128]{1,0:T(8,128)S(1)} collective-permute-done((f32[32,128]{1,0:T(8,128)S(1)}, f32[32,128]{1,0:T(8,128)S(1)}, u32[]{:S(2)}, u32[]{:S(2)}) %collective-permute-start.2) | collective-permute-done | bytes 16416 | tf_op jit(solution)/shard_map/ppermute | solution.py:423
  23.7 4.3 %collective-permute-start.3 = (f32[32,128]{1,0:T(8,128)S(1)}, f32[32,128]{1,0:T(8,128)S(1)}, u32[]{:S(2)}, u32[]{:S(2)}) collective-permute-start(f32[32,128]{1,0:T(8,128)S(1)} %fusion.9), channel_id=1, source_target_pairs={{0,24},{8,16},{16,8},{24,0},{32,56},{40,48},{48,40},{56,32},{64,88... | collective-permute-start | bytes 49160 | tf_op jit(solution)/shard_map/ppermute | solution.py:423
  28.0 1.2 %coeff_pass.1 = f32[32,64,64]{2,1,0:T(8,128)} custom-call(bf16[64,4096]{1,0:T(8,128)(2,1)S(1)} %get-tuple-element.30.far_ref, bf16[32,64,128]{2,1,0:T(8,128)(2,1)S(1)} %get-tuple-element.31.basis_ref), custom_call_target="tpu_custom_call" | custom-call | tf_op jit(solution)/shard_map/coeff_pass/pallas_call | solution.py:392
  29.2 0.5 %collective-permute-done.3 = f32[32,128]{1,0:T(8,128)S(1)} collective-permute-done((f32[32,128]{1,0:T(8,128)S(1)}, f32[32,128]{1,0:T(8,128)S(1)}, u32[]{:S(2)}, u32[]{:S(2)}) %collective-permute-start.3) | collective-permute-done | bytes 16416 | tf_op jit(solution)/shard_map/ppermute | solution.py:423
  29.9 3.1 %collective-permute-start.7 = (f32[32,128]{1,0:T(8,128)S(1)}, f32[32,128]{1,0:T(8,128)S(1)}, u32[]{:S(2)}, u32[]{:S(2)}) collective-permute-start(f32[32,128]{1,0:T(8,128)S(1)} %fusion.7), channel_id=1, source_target_pairs={{0,32},{8,40},{16,48},{24,56},{32,0},{40,8},{48,16},{56,24},{64,96... | collective-permute-start | bytes 49160 | tf_op jit(solution)/shard_map/ppermute | solution.py:423
  33.0 0.9 %collective-permute-start.5 = (bf16[2,8,16,128]{3,2,1,0:T(8,128)(2,1)S(1)}, bf16[2,8,16,128]{3,2,1,0:T(8,128)(2,1)S(1)}, u32[]{:S(2)}, u32[]{:S(2)}) collective-permute-start(bf16[2,8,16,128]{3,2,1,0:T(8,128)(2,1)S(1)} %fusion), channel_id=1, source_target_pairs={{0,2},{1,3},{2,0},{3,1},{4,6},{5,7},{6,4},{7,5},{8,10},{9,11},{10,... | collective-permute-start | bytes 196616 | tf_op jit(solution)/shard_map/ppermute | solution.py:423
  33.9 0.8 %collective-permute-done.7 = f32[32,128]{1,0:T(8,128)S(1)} collective-permute-done((f32[32,128]{1,0:T(8,128)S(1)}, f32[32,128]{1,0:T(8,128)S(1)}, u32[]{:S(2)}, u32[]{:S(2)}) %collective-permute-start.7) | collective-permute-done | bytes 16416 | tf_op jit(solution)/shard_map/ppermute | solution.py:423
  34.8 3.5 %collective-permute-start.8 = (f32[32,128]{1,0:T(8,128)S(1)}, f32[32,128]{1,0:T(8,128)S(1)}, u32[]{:S(2)}, u32[]{:S(2)}) collective-permute-start(f32[32,128]{1,0:T(8,128)S(1)} %fusion.5), channel_id=1, source_target_pairs={{0,64},{8,72},{16,80},{24,88},{32,96},{40,104},{48,112},{56,120},{... | collective-permute-start | bytes 49160 | tf_op jit(solution)/shard_map/ppermute | solution.py:423
  38.4 0.6 %collective-permute-start.6 = (f32[8,16,128]{2,1,0:T(8,128)S(1)}, f32[8,16,128]{2,1,0:T(8,128)S(1)}, u32[]{:S(2)}, u32[]{:S(2)}) collective-permute-start(f32[8,16,128]{2,1,0:T(8,128)S(1)} %fusion.2), channel_id=1, source_target_pairs={{0,6},{1,7},{2,4},{3,5},{4,2},{5,3},{6,0},{7,1},{8,14},{9,15},{10,... | collective-permute-start | bytes 196616 | tf_op jit(solution)/shard_map/ppermute | solution.py:423
  38.9 1.1 %collective-permute-done.8 = f32[32,128]{1,0:T(8,128)S(1)} collective-permute-done((f32[32,128]{1,0:T(8,128)S(1)}, f32[32,128]{1,0:T(8,128)S(1)}, u32[]{:S(2)}, u32[]{:S(2)}) %collective-permute-start.8) | collective-permute-done | bytes 16416 | tf_op jit(solution)/shard_map/ppermute | solution.py:423
  40.2 6.0 %collective-permute-start.9 = (f32[32,128]{1,0:T(8,128)S(1)}, f32[32,128]{1,0:T(8,128)S(1)}, u32[]{:S(2)}, u32[]{:S(2)}) collective-permute-start(f32[32,128]{1,0:T(8,128)S(1)} %fusion.3), channel_id=1, source_target_pairs={{0,192},{8,200},{16,208},{24,216},{32,224},{40,232},{48,240},{56,2... | collective-permute-start | bytes 49160 | tf_op jit(solution)/shard_map/ppermute | solution.py:423
  46.3 0.7 %finish.1 = f32[32,512]{1,0:T(8,128)} custom-call(f32[4,8,16,128]{3,2,1,0:T(8,128)S(1)} %get-tuple-element.33.keep_ref, f32[4,8,16,128]{3,2,1,0:T(8,128)S(1)} %collective-permute-done.4.got_ref, bf16[2,8,16,128]{3,2,1,0:T(8,128)(2,1)S(1)} %collective-permute-done.5.received_ref, f32[8,16,128]{2,1,0:T(8,128)S(1)} %collective-permute-done.6.last_ref), custom_call_target="tpu_custom_call" | custom-call | tf_op jit(solution)/shard_map/finish/pallas_call | solution.py:497
  47.0 1.0 %collective-permute-done.9 = f32[32,128]{1,0:T(8,128)S(1)} collective-permute-done((f32[32,128]{1,0:T(8,128)S(1)}, f32[32,128]{1,0:T(8,128)S(1)}, u32[]{:S(2)}, u32[]{:S(2)}) %collective-permute-start.9) | collective-permute-done | bytes 16416 | tf_op jit(solution)/shard_map/ppermute | solution.py:423
  48.0 0.9 %turn.1 = f32[5,64,64]{2,1,0:T(8,128)} custom-call(f32[32,128]{1,0:T(8,128)S(1)} %add.56.refs_0_, f32[32,128]{1,0:T(8,128)S(1)} %add.61.refs_1_, f32[32,128]{1,0:T(8,128)S(1)} %add.62.refs_2_, f32[32,128]{1,0:T(8,128)S(1)} %add.63.refs_3_, f32[32,128]{1,0:T(8,128)S(1)} %add.64.refs_4_), custom_call_target="tpu_custom_call" | custom-call | tf_op jit(solution)/shard_map/turn/pallas_call | solution.py:508
  (18 shorter events, 1.0 us)
Async XLA Ops:
  0.6 14.0 %collective-permute-start.1 = (bf16[64,4096]{1,0:T(8,128)(2,1)}, bf16[64,4096]{1,0:T(8,128)(2,1)S(1)}, u32[]{:S(2)}, u32[]{:S(2)}) collective-permute-start(bf16[64,4096]{1,0:T(8,128)(2,1)} %bitcast.27), channel_id=1, source_target_pairs={{0,8},{16,24},{32,40},{48,56},{64,72},{80,88},{96,104},{112,120},{... | collective-permute-start | bytes 1572872 | tf_op jit(solution)/shard_map/ppermute | solution.py:428
  2.3 14.5 %collective-permute-start = (bf16[64,4096]{1,0:T(8,128)(2,1)}, bf16[64,4096]{1,0:T(8,128)(2,1)S(1)}, u32[]{:S(2)}, u32[]{:S(2)}) collective-permute-start(bf16[64,4096]{1,0:T(8,128)(2,1)} %bitcast.28), channel_id=1, source_target_pairs={{8,16},{24,32},{40,48},{56,64},{72,80},{88,96},{104,112},{120,128}... | collective-permute-start | bytes 1572872 | tf_op jit(solution)/shard_map/ppermute | solution.py:428
  17.5 6.0 %collective-permute-start.2 = (f32[32,128]{1,0:T(8,128)S(1)}, f32[32,128]{1,0:T(8,128)S(1)}, u32[]{:S(2)}, u32[]{:S(2)}) collective-permute-start(f32[32,128]{1,0:T(8,128)S(1)} %get-tuple-element.26), channel_id=1, source_target_pairs={{0,8},{8,0},{16,24},{24,16},{32,40},{40,32},{48,56},{56,48},{64,72... | collective-permute-start | bytes 49160 | tf_op jit(solution)/shard_map/ppermute | solution.py:423
  22.6 10.3 %collective-permute-start.4 = (f32[4,8,16,128]{3,2,1,0:T(8,128)S(1)}, f32[4,8,16,128]{3,2,1,0:T(8,128)S(1)}, u32[]{:S(2)}, u32[]{:S(2)}) collective-permute-start(f32[4,8,16,128]{3,2,1,0:T(8,128)S(1)} %get-tuple-element.34), channel_id=1, source_target_pairs={{0,1},{1,0},{2,3},{3,2},{4,5},{5,4},{6,7},{7,6},{8,9},{9,8},{10,11... | collective-permute-start | bytes 786440 | tf_op jit(solution)/shard_map/ppermute | solution.py:423
  23.7 6.0 %collective-permute-start.3 = (f32[32,128]{1,0:T(8,128)S(1)}, f32[32,128]{1,0:T(8,128)S(1)}, u32[]{:S(2)}, u32[]{:S(2)}) collective-permute-start(f32[32,128]{1,0:T(8,128)S(1)} %fusion.9), channel_id=1, source_target_pairs={{0,24},{8,16},{16,8},{24,0},{32,56},{40,48},{48,40},{56,32},{64,88... | collective-permute-start | bytes 49160 | tf_op jit(solution)/shard_map/ppermute | solution.py:423
  29.9 4.8 %collective-permute-start.7 = (f32[32,128]{1,0:T(8,128)S(1)}, f32[32,128]{1,0:T(8,128)S(1)}, u32[]{:S(2)}, u32[]{:S(2)}) collective-permute-start(f32[32,128]{1,0:T(8,128)S(1)} %fusion.7), channel_id=1, source_target_pairs={{0,32},{8,40},{16,48},{24,56},{32,0},{40,8},{48,16},{56,24},{64,96... | collective-permute-start | bytes 49160 | tf_op jit(solution)/shard_map/ppermute | solution.py:423
  33.0 5.4 %collective-permute-start.5 = (bf16[2,8,16,128]{3,2,1,0:T(8,128)(2,1)S(1)}, bf16[2,8,16,128]{3,2,1,0:T(8,128)(2,1)S(1)}, u32[]{:S(2)}, u32[]{:S(2)}) collective-permute-start(bf16[2,8,16,128]{3,2,1,0:T(8,128)(2,1)S(1)} %fusion), channel_id=1, source_target_pairs={{0,2},{1,3},{2,0},{3,1},{4,6},{5,7},{6,4},{7,5},{8,10},{9,11},{10,... | collective-permute-start | bytes 196616 | tf_op jit(solution)/shard_map/ppermute | solution.py:423
  34.8 5.2 %collective-permute-start.8 = (f32[32,128]{1,0:T(8,128)S(1)}, f32[32,128]{1,0:T(8,128)S(1)}, u32[]{:S(2)}, u32[]{:S(2)}) collective-permute-start(f32[32,128]{1,0:T(8,128)S(1)} %fusion.5), channel_id=1, source_target_pairs={{0,64},{8,72},{16,80},{24,88},{32,96},{40,104},{48,112},{56,120},{... | collective-permute-start | bytes 49160 | tf_op jit(solution)/shard_map/ppermute | solution.py:423
  38.4 7.9 %collective-permute-start.6 = (f32[8,16,128]{2,1,0:T(8,128)S(1)}, f32[8,16,128]{2,1,0:T(8,128)S(1)}, u32[]{:S(2)}, u32[]{:S(2)}) collective-permute-start(f32[8,16,128]{2,1,0:T(8,128)S(1)} %fusion.2), channel_id=1, source_target_pairs={{0,6},{1,7},{2,4},{3,5},{4,2},{5,3},{6,0},{7,1},{8,14},{9,15},{10,... | collective-permute-start | bytes 196616 | tf_op jit(solution)/shard_map/ppermute | solution.py:423
  40.2 7.7 %collective-permute-start.9 = (f32[32,128]{1,0:T(8,128)S(1)}, f32[32,128]{1,0:T(8,128)S(1)}, u32[]{:S(2)}, u32[]{:S(2)}) collective-permute-start(f32[32,128]{1,0:T(8,128)S(1)} %fusion.3), channel_id=1, source_target_pairs={{0,192},{8,200},{16,208},{24,216},{32,224},{40,232},{48,240},{56,2... | collective-permute-start | bytes 49160 | tf_op jit(solution)/shard_map/ppermute | solution.py:423
